TPU v7x, 32 devices: a whole 2x2x4 slice. The times are simulated.
32 devices in a mesh: sec: 32 (over z, y, x, core).
Axes of the slice: x: 2, y: 2, z: 4, core: 2. Of those that a mesh axis runs over, the one named last changes fastest.
Arguments:
- front_reflect: float32 [32, 384, 384], P('sec'), may hold values from -0.125 to 0.125
- front_through: float32 [32, 384, 384], P('sec'), may hold values from -1 to 1
- back_reflect: float32 [32, 384, 384], P('sec'), may hold values from -0.125 to 0.125
- back_through: float32 [32, 384, 384], P('sec'), may hold values from -1 to 1
- depth_maps: float32 [32, 4, 384, 384], P('sec'), may hold values from -1 to 1
- incident: float32 [384, 128], replicated, may hold values from -6 to 6
Outputs:
- through_field: float32 [32, 384, 128], P('sec')
- reflected: float32 [32, 384, 128], P('sec')
- depth_fields: float32 [32, 4, 384, 128], P('sec')
All inputs are finite; a program needn't handle non-finite values.
Results may differ from a plain program's by a relative error of at most 0.00013.
Values sent between devices are 32-bit elements; how exact they have to be, the bound alone decides.
No kernel may reach another device: no remote copies, remote signals or barrier semaphores. Data moves between devices by JAX's collectives and lax.ppermute only.
A program may use at most 64 MiB of HBM per device.

v0:
```python
import jax
import jax.numpy as jnp
from jax import lax
from jax.experimental import pallas as pl
from jax.experimental.pallas import tpu as pltpu
from jax.sharding import PartitionSpec as P

SEGMENTS = 3
NODES = 2**SEGMENTS
F32 = jnp.float32


def split(value):
    high = value.astype(jnp.bfloat16)
    return high, (value - high.astype(F32)).astype(jnp.bfloat16)


def left(value):
    high, low = split(value)
    return jnp.concatenate([high, high, low], axis=1)


def right(value):
    high, low = split(value)
    return jnp.concatenate([high, low, high], axis=0)


def product(former, latter):
    return jnp.dot(left(former), right(latter), preferred_element_type=F32)


def summed(bounce, value):
    factor = left(bounce)
    total = value
    for _ in range(3):
        total = value + jnp.dot(factor, right(total), preferred_element_type=F32)
    return total


def staged(body, stride, inputs, outputs, products):
    def kernel(*refs):
        body(lax.axis_index("sec") // stride, *refs)

    vmem = pl.BlockSpec(memory_space=pltpu.VMEM)
    side = inputs[0].shape[0]
    moved_bytes = 4 * side * side * (len(inputs) + len(outputs))
    return pl.pallas_call(
        kernel,
        out_shape=[jax.ShapeDtypeStruct(shape, F32) for shape in outputs],
        in_specs=[vmem] * len(inputs),
        out_specs=[vmem] * len(outputs),
        compiler_params=pltpu.CompilerParams(vmem_limit_bytes=24 * 2**20),
        cost_estimate=pl.CostEstimate(flops=int(products * 6 * side**3), bytes_accessed=moved_bytes, transcendentals=0),
    )(*inputs)


def per_device(front_reflect, front_through, back_reflect, back_through, depth_maps, incident):
    length = lax.axis_size("sec")
    stride = length // NODES
    position = lax.axis_index("sec")
    k = position // stride
    square, field = front_reflect.shape[1:], incident.shape

    def moved(value, routes):
        pairs = [(a * stride + i, b * stride + i) for a, b in routes for i in range(stride)]
        return lax.ppermute(value, "sec", pairs)

    r, t, q, u = front_reflect[0], front_through[0], back_reflect[0], back_through[0]
    onward = [(0, 1), (1, 2), (2, 3), (3, 4), (4, 5)]
    low = [(0, 2), (1, 3)]
    back = [(4, 2), (5, 3)]

    q0 = moved(q, onward)
    swapped = moved(r, [(7, 6), (6, 7), (1, 0)])
    t0 = moved(t, onward)
    u0 = moved(u, onward)

    def pair_reflect(at):
        def body(k, came, r, t, q, u, *rest):
            out, gt_out = rest[-2:]

            @pl.when(k == at)
            def _():
                gt = summed(product(q[...], came[...]), t[...])
                gt_out[...] = gt
                out[...] = r[...] + product(u[...], product(came[...], gt))

            @pl.when(k != at)
            def _():
                out[...] = came[...]
                if len(rest) == 3:
                    gt_out[...] = rest[0][...]

        return body

    (relay, gt) = staged(pair_reflect(6), stride, [swapped, r, t, q, u], [square] * 2, 6)
    hopped = moved(relay, [(6, 7), (7, 5), (0, 2)])

    def forward_q(k, q0, r, t, q, u, q1, hu_out):
        @pl.when(k == 0)
        def _():
            q1[...] = q[...]

        @pl.when((k > 0) & (k < 6))
        def _():
            hu = summed(product(r[...], q0[...]), u[...])
            hu_out[...] = hu
            q1[...] = q[...] + product(t[...], product(q0[...], hu))

    (q1, hu) = staged(forward_q, stride, [q0, r, t, q, u], [square] * 2, 6)
    qa = moved(q1, low)

    r_late = moved(r, [(0, 1), (2, 3), (3, 2)])

    def forward_t(k, q0, t0, r, t, t1, rgt):
        @pl.when(k == 0)
        def _():
            t1[...] = t[...]

        @pl.when((k > 0) & (k < 6))
        def _():
            gt = summed(product(q0[...], r[...]), t0[...])
            rgt[...] = product(r[...], gt)
            t1[...] = product(t[...], gt)

    (t1, rgt) = staged(forward_t, stride, [q0, t0, r, t], [square] * 2, 6)

    (relay, gt) = staged(pair_reflect(5), stride, [hopped, r, t, q, u, gt], [square] * 2, 6)
    bounced = moved(relay, [(5, 4), (7, 5)])
    gt_came = moved(gt, [(5, 6), (6, 7)])
    r_next = moved(lax.optimization_barrier((r, relay))[0], [(4, 3)])

    def forward_u(k, u0, u, hu, rgt, u1, w):
        @pl.when(k == 0)
        def _():
            u1[...] = u[...]

        @pl.when((k > 0) & (k < 6))
        def _():
            factor = left(u0[...])
            w[...] = jnp.dot(factor, right(rgt[...]), preferred_element_type=F32)
            u1[...] = jnp.dot(factor, right(hu[...]), preferred_element_type=F32)

    (u1, w) = staged(forward_u, stride, [u0, u, hu, rgt], [square] * 2, 2)
    w_came = moved(w, back)
    ua = moved(u1, low)

    def second_reflect(k, bounced, q1, t1, u1, w, total, gt_out):
        @pl.when((k == 4) | (k == 5))
        def _():
            gt = summed(product(q1[...], bounced[...]), t1[...])
            gt_out[...] = gt
            total[...] = w[...] + product(u1[...], product(bounced[...], gt))

    (total, gt2) = staged(second_reflect, stride, [bounced, q1, t1, u1, w], [square] * 2, 6
    )
    total_came = moved(total, back)
    gt2_came = moved(gt2, [(4, 6), (5, 7)])

    def own_fields(k, r_late, hopped, r, w, t1, incident, r1, f1, s1):
        @pl.when(k == 0)
        def _():
            r1[...] = r[...]

        @pl.when(k == 2)
        def _():
            r1[...] = hopped[...] + w[...]

        @pl.when((k == 1) | (k == 3))
        def _():
            r1[...] = r_late[...] + w[...]

        @pl.when(k < 2)
        def _():
            f1[...] = product(t1[...], incident[...])
            s1[...] = product(r1[...], incident[...])

    (r1, f1, s1) = staged(own_fields, stride, [r_late, hopped, r, w, t1, incident], [square, field, field], 1
    )
    fa = moved(f1, low)
    sa = moved(s1, low)

    def second_q(k, r1, qa, q1, t1, u1, q2, hu_out):
        @pl.when((k == 2) | (k == 3))
        def _():
            hu = summed(product(r1[...], qa[...]), u1[...])
            hu_out[...] = hu
            q2[...] = q1[...] + product(t1[...], product(qa[...], hu))

    (q2, hu2) = staged(second_q, stride, [r1, qa, q1, t1, u1], [square] * 2, 6)

    def second_fields(k, qa, ua, fa, sa, hu2, r1, t1, u2, f2, s2):
        @pl.when((k == 2) | (k == 3))
        def _():
            g = summed(product(qa[...], r1[...]), fa[...])
            f2[...] = product(t1[...], g)
            s2[...] = sa[...] + product(ua[...], product(r1[...], g))
            u2[...] = product(ua[...], hu2[...])

    (u2, f2, s2) = staged(second_fields, stride, [qa, ua, fa, sa, hu2, r1, t1], [square, field, field], 4
    )

    def third_fields(k, r_late, r_next, w_came, q1, t1, u1, r1, qa, ua, fa, sa, w4, s4):
        @pl.when((k == 2) | (k == 3))
        def _():
            came = jnp.where(k == 2, r_late[...], r_next[...]) + w_came[...]
            gt = summed(product(q1[...], came), t1[...])
            rc = r1[...] + product(u1[...], product(came, gt))
            g = summed(product(qa[...], rc), fa[...])
            w4[...] = product(gt, g)
            s4[...] = sa[...] + product(ua[...], product(rc, g))

    (w4, s4) = staged(third_fields, stride,
        [r_late, r_next, w_came, q1, t1, u1, r1, qa, ua, fa, sa],
        [field] * 2,
        9,
    )
    w4_came = moved(w4, [(2, 4), (3, 5)])
    s4_came = moved(s4, [(2, 4), (3, 5)])

    def second_through(k, t, gt_came, gt2_came, t2):
        @pl.when(k > 5)
        def _():
            t2[...] = product(product(t[...], gt_came[...]), gt2_came[...])

    (t2,) = staged(second_through, stride, [t, gt_came, gt2_came], [square], 2)

    def last_fields(k, r_late, r_next, total_came, q2, f2, g6, rg6):
        @pl.when((k == 2) | (k == 3))
        def _():
            rc = jnp.where(k == 2, r_late[...], r_next[...]) + total_came[...]
            g = summed(product(q2[...], rc), f2[...])
            g6[...] = g
            rg6[...] = product(rc, g)

    (g6, rg6) = staged(last_fields, stride, [r_late, r_next, total_came, q2, f2], [field] * 2, 3
    )
    g6_came = moved(g6, [(2, 6), (3, 7)])

    def last_reflected(k, s2, u2, rg6, s6):
        @pl.when((k == 2) | (k == 3))
        def _():
            s6[...] = s2[...] + product(u2[...], rg6[...])

    (s6,) = staged(last_reflected, stride, [s2, u2, rg6], [field], 1)
    s6_came = moved(s6, [(2, 6), (3, 7)])

    def through(k, f1, f2, t1, w4, t2, g6, out):
        @pl.when(k < 2)
        def _():
            out[...] = f1[...]

        @pl.when((k == 2) | (k == 3))
        def _():
            out[...] = f2[...]

        @pl.when((k == 4) | (k == 5))
        def _():
            out[...] = product(t1[...], w4[...])

        @pl.when(k > 5)
        def _():
            out[...] = product(t2[...], g6[...])

    (through_field,) = staged(through, stride, [f1, f2, t1, w4_came, t2, g6_came], [field], 1
    )
    entering = lax.ppermute(through_field, "sec", [(i, i + 1) for i in range(length - 1)])
    reflected = jnp.where(
        k < 2, s1, jnp.where(k < 4, s2, jnp.where(k < 6, s4_came, s6_came))
    )

    def depths(place, maps, entering, incident, out):
        value = right(jnp.where(place == 0, incident[...], entering[...]))
        for j in range(depth_maps.shape[1]):
            out[j] = jnp.dot(left(maps[j]), value, preferred_element_type=F32)

    (depth_fields,) = staged(depths, 1, [depth_maps[0], entering, incident], [depth_maps.shape[1:3] + field[1:]], 1)
    return (through_field[None], reflected[None], depth_fields[None])


def solution(mesh):
    in_specs = (
        P("sec", None, None),
        P("sec", None, None),
        P("sec", None, None),
        P("sec", None, None),
        P("sec", None, None, None),
        P(),
    )
    out_specs = (P("sec", None, None), P("sec", None, None), P("sec", None, None, None))

    return jax.shard_map(per_device, mesh=mesh, in_specs=in_specs, out_specs=out_specs, check_vma=False)
```

profile of v0, /device:TPU:28, one launch (start us, length us, event | category | flops | bytes accessed | tf_op | source)
XLA Modules:
  0.0 120.1 jit_solution(4196381013031005012)
XLA Ops:
  0.6 2.4 %collective-permute-start.1 = (f32[384,384]{1,0:T(8,128)}, f32[384,384]{1,0:T(8,128)S(1)}, u32[]{:S(2)}, u32[]{:S(2)}) collective-permute-start(f32[384,384]{1,0:T(8,128)} %bitcast.refs_1_.refs_2_), channel_id=1, source_target_pairs={{28,24},{29,25},{30,26},{31,27},{24,28},{25,29},{26,30},{27,31},{4... | collective-permute-start | bytes 1769480 | tf_op jit(solution)/shard_map/ppermute | solution.py:66
  3.1 0.7 collective-permute-start.4
  3.8 14.0 %collective-permute-done.1.refs_0_ = f32[384,384]{1,0:T(8,128)S(1)} collective-permute-done((f32[384,384]{1,0:T(8,128)}, f32[384,384]{1,0:T(8,128)S(1)}, u32[]{:S(2)}, u32[]{:S(2)}) %collective-permute-start.1) | collective-permute-done | bytes 589856 | tf_op jit(solution)/shard_map/ppermute | solution.py:66
  17.8 1.1 copy-done.2
  18.9 1.1 copy-done.4
  19.9 1.3 %shard_map.85 = (f32[384,384]{1,0:T(8,128)S(1)}, f32[384,384]{1,0:T(8,128)S(1)}) custom-call(f32[384,384]{1,0:T(8,128)S(1)} %collective-permute-done.1.refs_0_, f32[384,384]{1,0:T(8,128)} %bitcast.refs_1_.refs_2_, f32[384,384]{1,0:T(8,128)S(1)} %bitcast.14, f32[384,384]{1,0:T(8,128)S(1)} %bitcast.11, f32[384,384]{1,0:T(8,128)} %bitcast.3.refs_4_.refs_1_), custom_call_target="tpu_custom_call" | custom-call | flops 2038431744 | bytes 4128768 | tf_op jit(solution)/shard_map/pallas_call | solution.py:47
  21.3 1.9 %collective-permute-start.2 = (f32[384,384]{1,0:T(8,128)S(1)}, f32[384,384]{1,0:T(8,128)S(1)}, u32[]{:S(2)}, u32[]{:S(2)}) collective-permute-start(f32[384,384]{1,0:T(8,128)S(1)} %get-tuple-element.28), channel_id=1, source_target_pairs={{24,28},{25,29},{26,30},{27,31},{28,20},{29,21},{30,22},{31,23},{0... | collective-permute-start | bytes 1769480 | tf_op jit(solution)/shard_map/ppermute | solution.py:66
  23.2 0.7 collective-permute-start.5
  23.9 0.7 collective-permute-start.3
  24.6 0.7 collective-permute-start
  25.3 0.0 collective-permute-done.4.refs_0_
  25.4 1.2 %shard_map.86 = (f32[384,384]{1,0:T(8,128)S(1)}, f32[384,384]{1,0:T(8,128)S(1)}) custom-call(f32[384,384]{1,0:T(8,128)S(1)} %collective-permute-done.4.refs_0_, f32[384,384]{1,0:T(8,128)} %bitcast.refs_1_.refs_2_, f32[384,384]{1,0:T(8,128)S(1)} %bitcast.16, f32[384,384]{1,0:T(8,128)S(1)} %bitcast.12, f32[384,384]{1,0:T(8,128)} %bitcast.3.refs_4_.refs_1_), custom_call_target="tpu_custom_call" | custom-call | flops 2038431744 | bytes 4128768 | tf_op jit(solution)/shard_map/pallas_call | solution.py:47
  26.6 0.7 collective-permute-start.6
  27.3 11.9 %collective-permute-done.2.refs_1_.refs_0_ = f32[384,384]{1,0:T(8,128)S(1)} collective-permute-done((f32[384,384]{1,0:T(8,128)S(1)}, f32[384,384]{1,0:T(8,128)S(1)}, u32[]{:S(2)}, u32[]{:S(2)}) %collective-permute-start.2) | collective-permute-done | bytes 589856 | tf_op jit(solution)/shard_map/ppermute | solution.py:66
  39.1 1.4 %shard_map.92 = (f32[384,384]{1,0:T(8,128)S(1)}, f32[384,384]{1,0:T(8,128)S(1)}) custom-call(f32[384,384]{1,0:T(8,128)S(1)} %collective-permute-done.2.refs_1_.refs_0_, f32[384,384]{1,0:T(8,128)} %bitcast.refs_1_.refs_2_, f32[384,384]{1,0:T(8,128)S(1)} %bitcast.17, f32[384,384]{1,0:T(8,128)S(1)} %bitcast.13, f32[384,384]{1,0:T(8,128)} %bitcast.3.refs_4_.refs_1_, ...), custom_call_target="tpu_custom_call" | custom-call | flops 2038431744 | bytes 4718592 | tf_op jit(solution)/shard_map/pallas_call | solution.py:47
  40.5 4.0 %collective-permute-start.14 = (f32[384,384]{1,0:T(8,128)S(1)}, f32[384,384]{1,0:T(8,128)S(1)}, u32[]{:S(2)}, u32[]{:S(2)}) collective-permute-start(f32[384,384]{1,0:T(8,128)S(1)} %get-tuple-element.41), channel_id=1, source_target_pairs={{20,16},{21,17},{22,18},{23,19},{28,20},{29,21},{30,22},{31,23}} | collective-permute-start | bytes 1769480 | tf_op jit(solution)/shard_map/ppermute | solution.py:66
  44.6 0.0 collective-permute-done.5.refs_1_
  44.6 1.1 shard_map.87
  45.7 1.1 shard_map.88
  46.8 0.7 collective-permute-start.7
  47.5 0.7 collective-permute-start.11
  48.2 0.7 collective-permute-start.10
  48.9 1.1 shard_map.89
  50.0 0.7 collective-permute-start.8
  50.7 5.0 %collective-permute-done.14.refs_0_ = f32[384,384]{1,0:T(8,128)S(1)} collective-permute-done((f32[384,384]{1,0:T(8,128)S(1)}, f32[384,384]{1,0:T(8,128)S(1)}, u32[]{:S(2)}, u32[]{:S(2)}) %collective-permute-start.14) | collective-permute-done | bytes 589856 | tf_op jit(solution)/shard_map/ppermute | solution.py:66
  55.7 0.7 collective-permute-start.9
  56.4 1.3 %collective-permute-start.13 = (f32[384,384]{1,0:T(8,128)S(1)}, f32[384,384]{1,0:T(8,128)S(1)}, u32[]{:S(2)}, u32[]{:S(2)}) collective-permute-start(f32[384,384]{1,0:T(8,128)S(1)} %get-tuple-element.44), channel_id=1, source_target_pairs={{20,24},{21,25},{22,26},{23,27},{24,28},{25,29},{26,30},{27,31}} | collective-permute-start | bytes 1769480 | tf_op jit(solution)/shard_map/ppermute | solution.py:66
  57.7 0.7 collective-permute-start.16
  58.5 1.3 %collective-permute-start.15 = (f32[384,384]{1,0:T(8,128)S(1)}, f32[384,384]{1,0:T(8,128)}, u32[]{:S(2)}, u32[]{:S(2)}) collective-permute-start(f32[384,384]{1,0:T(8,128)S(1)} %get-tuple-element.45), channel_id=1, source_target_pairs={{16,24},{17,25},{18,26},{19,27},{20,28},{21,29},{22,30},{23,31}} | collective-permute-start | bytes 1769480 | tf_op jit(solution)/shard_map/ppermute | solution.py:66
  59.8 0.2 shard_map.91
  60.1 0.7 collective-permute-start.12
  60.7 1.3 %collective-permute-start.18 = (f32[384,128]{1,0:T(8,128)S(1)}, f32[384,128]{1,0:T(8,128)}, u32[]{:S(2)}, u32[]{:S(2)}) collective-permute-start(f32[384,128]{1,0:T(8,128)S(1)} %get-tuple-element.50), channel_id=1, source_target_pairs={{8,16},{9,17},{10,18},{11,19},{12,20},{13,21},{14,22},{15,23}} | collective-permute-start | bytes 589832 | tf_op jit(solution)/shard_map/ppermute | solution.py:66
  62.1 0.7 shard_map.96
  62.8 1.3 %collective-permute-start.17 = (f32[384,128]{1,0:T(8,128)}, f32[384,128]{1,0:T(8,128)S(1)}, u32[]{:S(2)}, u32[]{:S(2)}) collective-permute-start(f32[384,128]{1,0:T(8,128)} %get-tuple-element.48), channel_id=1, source_target_pairs={{8,24},{9,25},{10,26},{11,27},{12,28},{13,29},{14,30},{15,31}} | collective-permute-start | bytes 589832 | tf_op jit(solution)/shard_map/ppermute | solution.py:66
  64.0 0.7 shard_map.98
  64.7 6.3 %collective-permute-done.13.refs_1_ = f32[384,384]{1,0:T(8,128)S(1)} collective-permute-done((f32[384,384]{1,0:T(8,128)S(1)}, f32[384,384]{1,0:T(8,128)S(1)}, u32[]{:S(2)}, u32[]{:S(2)}) %collective-permute-start.13) | collective-permute-done | bytes 589856 | tf_op jit(solution)/shard_map/ppermute | solution.py:66
  71.1 0.8 copy-done.6
  71.9 1.3 %collective-permute-start.19 = (f32[384,128]{1,0:T(8,128)}, f32[384,128]{1,0:T(8,128)}, u32[]{:S(2)}, u32[]{:S(2)}) collective-permute-start(f32[384,128]{1,0:T(8,128)} %shard_map.98), channel_id=1, source_target_pairs={{8,24},{9,25},{10,26},{11,27},{12,28},{13,29},{14,30},{15,31}} | collective-permute-start | bytes 589832 | tf_op jit(solution)/shard_map/ppermute | solution.py:66
  73.2 0.0 copy-start
  73.2 19.6 %collective-permute-done.15.refs_2_ = f32[384,384]{1,0:T(8,128)} collective-permute-done((f32[384,384]{1,0:T(8,128)S(1)}, f32[384,384]{1,0:T(8,128)}, u32[]{:S(2)}, u32[]{:S(2)}) %collective-permute-start.15) | collective-permute-done | bytes 589856 | tf_op jit(solution)/shard_map/ppermute | solution.py:66
  92.8 1.1 copy-done.7
  93.9 2.3 %shard_map.95.refs_4_ = f32[384,384]{1,0:T(8,128)S(1)} custom-call(f32[384,384]{1,0:T(8,128)S(1)} %bitcast.19, f32[384,384]{1,0:T(8,128)S(1)} %copy-done.7, f32[384,384]{1,0:T(8,128)} %collective-permute-done.15.refs_2_), custom_call_target="tpu_custom_call" | custom-call | flops 679477248 | bytes 2359296 | tf_op jit(solution)/shard_map/pallas_call | solution.py:47
  96.2 12.8 %collective-permute-done.17.refs_5_ = f32[384,128]{1,0:T(8,128)S(1)} collective-permute-done((f32[384,128]{1,0:T(8,128)}, f32[384,128]{1,0:T(8,128)S(1)}, u32[]{:S(2)}, u32[]{:S(2)}) %collective-permute-start.17) | collective-permute-done | bytes 196640 | tf_op jit(solution)/shard_map/ppermute | solution.py:66
  109.0 1.1 shard_map.97
  110.1 1.9 %collective-permute-start.20 = (f32[384,128]{1,0:T(8,128)}, f32[384,128]{1,0:T(8,128)S(1)}, u32[]{:S(2)}, u32[]{:S(2)}) collective-permute-start(f32[384,128]{1,0:T(8,128)} %shard_map.97), channel_id=1, source_target_pairs={{0,1},{1,2},{2,3},{3,4},{4,5},{5,6},{6,7},{7,8},{8,9},{9,10},{10,1... | collective-permute-start | bytes 589832 | tf_op jit(solution)/shard_map/ppermute | solution.py:267
  112.0 1.7 %select_bitcast_fusion = f32[1,384,128]{2,1,0:T(8,128)} fusion(f32[384,128]{1,0:T(8,128)S(1)} %get-tuple-element.36, f32[384,128]{1,0:T(8,128)S(1)} %get-tuple-element.49.refs_0_, f32[384,128]{1,0:T(8,128)} %collective-permute-done.18, f32[384,128]{1,0:T(8,128)} %collective-permute-done.19, pred[]{:T(512)S(6)} %lt.11, pred[]{:T(512)S(6)} %lt.10, pred[]{:T(512)S(6)} %lt.9), kind=kLoop, calls=%fused_computation | loop fusion | flops 147456 | bytes 983043 | tf_op jit(solution)/shard_map/broadcast_in_dim | solution.py:278
  113.7 4.5 %collective-permute-done.20.refs_1_ = f32[384,128]{1,0:T(8,128)S(1)} collective-permute-done((f32[384,128]{1,0:T(8,128)}, f32[384,128]{1,0:T(8,128)S(1)}, u32[]{:S(2)}, u32[]{:S(2)}) %collective-permute-start.20) | collective-permute-done | bytes 196640 | tf_op jit(solution)/shard_map/ppermute | solution.py:267
  118.2 2.0 %shard_map.99 = f32[4,384,128]{2,1,0:T(8,128)} custom-call(f32[4,384,384]{2,1,0:T(8,128)S(1)} %bitcast.9, f32[384,128]{1,0:T(8,128)S(1)} %collective-permute-done.20.refs_1_, f32[384,128]{1,0:T(8,128)S(1)} %copy-done.1), custom_call_target="tpu_custom_call" | custom-call | flops 384 | bytes 256 | tf_op jit(solution)/shard_map/pallas_call | solution.py:47
  (26 shorter events, 0.1 us)
Async XLA Ops:
  0.6 17.2 %collective-permute-start.1 = (f32[384,384]{1,0:T(8,128)}, f32[384,384]{1,0:T(8,128)S(1)}, u32[]{:S(2)}, u32[]{:S(2)}) collective-permute-start(f32[384,384]{1,0:T(8,128)} %bitcast.refs_1_.refs_2_), channel_id=1, source_target_pairs={{28,24},{29,25},{30,26},{31,27},{24,28},{25,29},{26,30},{27,31},{4... | collective-permute-start | bytes 1769480 | tf_op jit(solution)/shard_map/ppermute | solution.py:66
  3.1 22.3 %collective-permute-start.4 = (f32[384,384]{1,0:T(8,128)}, f32[384,384]{1,0:T(8,128)S(1)}, u32[]{:S(2)}, u32[]{:S(2)}) collective-permute-start(f32[384,384]{1,0:T(8,128)} %bitcast.10), channel_id=1, source_target_pairs={{0,4},{1,5},{2,6},{3,7},{4,8},{5,9},{6,10},{7,11},{8,12},{9,13},{1... | collective-permute-start | bytes 1769480 | tf_op jit(solution)/shard_map/ppermute | solution.py:66
  17.8 1.1 copy-start.2
  18.9 1.1 copy-start.4
  19.9 5.4 %copy-start.3 = (f32[1,384,384]{2,1,0:T(8,128)S(1)}, f32[1,384,384]{2,1,0:T(8,128)}, u32[]{:S(2)}) copy-start(f32[1,384,384]{2,1,0:T(8,128)} %param.8) | copy-start | bytes 1769476
  21.3 17.9 %collective-permute-start.2 = (f32[384,384]{1,0:T(8,128)S(1)}, f32[384,384]{1,0:T(8,128)S(1)}, u32[]{:S(2)}, u32[]{:S(2)}) collective-permute-start(f32[384,384]{1,0:T(8,128)S(1)} %get-tuple-element.28), channel_id=1, source_target_pairs={{24,28},{25,29},{26,30},{27,31},{28,20},{29,21},{30,22},{31,23},{0... | collective-permute-start | bytes 1769480 | tf_op jit(solution)/shard_map/ppermute | solution.py:66
  23.2 21.4 %collective-permute-start.5 = (f32[384,384]{1,0:T(8,128)S(1)}, f32[384,384]{1,0:T(8,128)S(1)}, u32[]{:S(2)}, u32[]{:S(2)}) collective-permute-start(f32[384,384]{1,0:T(8,128)S(1)} %bitcast.15), channel_id=1, source_target_pairs={{0,4},{1,5},{2,6},{3,7},{4,8},{5,9},{6,10},{7,11},{8,12},{9,13},{1... | collective-permute-start | bytes 1769480 | tf_op jit(solution)/shard_map/ppermute | solution.py:66
  23.9 21.8 %collective-permute-start.3 = (f32[384,384]{1,0:T(8,128)}, f32[384,384]{1,0:T(8,128)S(1)}, u32[]{:S(2)}, u32[]{:S(2)}) collective-permute-start(f32[384,384]{1,0:T(8,128)} %bitcast.3.refs_4_.refs_1_), channel_id=1, source_target_pairs={{0,4},{1,5},{2,6},{3,7},{4,8},{5,9},{6,10},{7,11},{8,12},{9,13},{1... | collective-permute-start | bytes 1769480 | tf_op jit(solution)/shard_map/ppermute | solution.py:66
  24.6 23.6 %collective-permute-start = (f32[384,384]{1,0:T(8,128)}, f32[384,384]{1,0:T(8,128)S(1)}, u32[]{:S(2)}, u32[]{:S(2)}) collective-permute-start(f32[384,384]{1,0:T(8,128)} %bitcast.refs_1_.refs_2_), channel_id=1, source_target_pairs={{0,4},{1,5},{2,6},{3,7},{8,12},{9,13},{10,14},{11,15},{12,8},{13,9... | collective-permute-start | bytes 1769480 | tf_op jit(solution)/shard_map/ppermute | solution.py:66
  26.6 23.4 %collective-permute-start.6 = (f32[384,384]{1,0:T(8,128)S(1)}, f32[384,384]{1,0:T(8,128)S(1)}, u32[]{:S(2)}, u32[]{:S(2)}) collective-permute-start(f32[384,384]{1,0:T(8,128)S(1)} %get-tuple-element.34.refs_2_.refs_3_.refs_1_), channel_id=1, source_target_pairs={{0,8},{1,9},{2,10},{3,11},{4,12},{5,13},{6,14},{7,15}} | collective-permute-start | bytes 1769480 | tf_op jit(solution)/shard_map/ppermute | solution.py:66
  39.1 5.5 %copy-start.5 = (f32[1,384,384]{2,1,0:T(8,128)S(1)}, f32[1,384,384]{2,1,0:T(8,128)}, u32[]{:S(2)}) copy-start(f32[1,384,384]{2,1,0:T(8,128)} %param.7) | copy-start | bytes 1769476
  40.5 15.2 %collective-permute-start.14 = (f32[384,384]{1,0:T(8,128)S(1)}, f32[384,384]{1,0:T(8,128)S(1)}, u32[]{:S(2)}, u32[]{:S(2)}) collective-permute-start(f32[384,384]{1,0:T(8,128)S(1)} %get-tuple-element.41), channel_id=1, source_target_pairs={{20,16},{21,17},{22,18},{23,19},{28,20},{29,21},{30,22},{31,23}} | collective-permute-start | bytes 1769480 | tf_op jit(solution)/shard_map/ppermute | solution.py:66
  45.7 3.2 %copy-start.1 = (f32[384,128]{1,0:T(8,128)S(1)}, f32[384,128]{1,0:T(8,128)}, u32[]{:S(2)}) copy-start(f32[384,128]{1,0:T(8,128)} %refs_2_.1) | copy-start | bytes 589828
  46.8 9.6 %collective-permute-start.7 = (f32[384,384]{1,0:T(8,128)S(1)}, f32[384,384]{1,0:T(8,128)S(1)}, u32[]{:S(2)}, u32[]{:S(2)}) collective-permute-start(f32[384,384]{1,0:T(8,128)S(1)} %get-tuple-element.35.refs_4_.refs_5_.refs_3_), channel_id=1, source_target_pairs={{0,8},{1,9},{2,10},{3,11},{4,12},{5,13},{6,14},{7,15}} | collective-permute-start | bytes 1769480 | tf_op jit(solution)/shard_map/ppermute | solution.py:66
  47.5 12.5 %collective-permute-start.11 = (f32[384,384]{1,0:T(8,128)S(1)}, f32[384,384]{1,0:T(8,128)S(1)}, u32[]{:S(2)}, u32[]{:S(2)}) collective-permute-start(f32[384,384]{1,0:T(8,128)S(1)} %get-tuple-element.31.refs_3_.refs_4_), channel_id=1, source_target_pairs={{16,8},{17,9},{18,10},{19,11},{20,12},{21,13},{22,14},{23,15}} | collective-permute-start | bytes 1769480 | tf_op jit(solution)/shard_map/ppermute | solution.py:66
  48.2 11.8 %collective-permute-start.10 = (f32[384,384]{1,0:T(8,128)}, f32[384,384]{1,0:T(8,128)S(1)}, u32[]{:S(2)}, u32[]{:S(2)}) collective-permute-start(f32[384,384]{1,0:T(8,128)} %bitcast.refs_1_.refs_2_), channel_id=1, source_target_pairs={{16,12},{17,13},{18,14},{19,15}} | collective-permute-start | bytes 1769480 | tf_op jit(solution)/shard_map/ppermute | solution.py:66
  50.0 7.7 %collective-permute-start.8 = (f32[384,128]{1,0:T(8,128)S(1)}, f32[384,128]{1,0:T(8,128)S(1)}, u32[]{:S(2)}, u32[]{:S(2)}) collective-permute-start(f32[384,128]{1,0:T(8,128)S(1)} %get-tuple-element.33.refs_0_), channel_id=1, source_target_pairs={{0,8},{1,9},{2,10},{3,11},{4,12},{5,13},{6,14},{7,15}} | collective-permute-start | bytes 589832 | tf_op jit(solution)/shard_map/ppermute | solution.py:66
  55.7 2.8 %collective-permute-start.9 = (f32[384,128]{1,0:T(8,128)S(1)}, f32[384,128]{1,0:T(8,128)S(1)}, u32[]{:S(2)}, u32[]{:S(2)}) collective-permute-start(f32[384,128]{1,0:T(8,128)S(1)} %get-tuple-element.36), channel_id=1, source_target_pairs={{0,8},{1,9},{2,10},{3,11},{4,12},{5,13},{6,14},{7,15}} | collective-permute-start | bytes 589832 | tf_op jit(solution)/shard_map/ppermute | solution.py:66
  56.4 14.7 %collective-permute-start.13 = (f32[384,384]{1,0:T(8,128)S(1)}, f32[384,384]{1,0:T(8,128)S(1)}, u32[]{:S(2)}, u32[]{:S(2)}) collective-permute-start(f32[384,384]{1,0:T(8,128)S(1)} %get-tuple-element.44), channel_id=1, source_target_pairs={{20,24},{21,25},{22,26},{23,27},{24,28},{25,29},{26,30},{27,31}} | collective-permute-start | bytes 1769480 | tf_op jit(solution)/shard_map/ppermute | solution.py:66
  57.7 4.4 %collective-permute-start.16 = (f32[384,384]{1,0:T(8,128)S(1)}, f32[384,384]{1,0:T(8,128)S(1)}, u32[]{:S(2)}, u32[]{:S(2)}) collective-permute-start(f32[384,384]{1,0:T(8,128)S(1)} %get-tuple-element.46), channel_id=1, source_target_pairs={{16,8},{17,9},{18,10},{19,11},{20,12},{21,13},{22,14},{23,15}} | collective-permute-start | bytes 1769480 | tf_op jit(solution)/shard_map/ppermute | solution.py:66
  58.5 34.4 %collective-permute-start.15 = (f32[384,384]{1,0:T(8,128)S(1)}, f32[384,384]{1,0:T(8,128)}, u32[]{:S(2)}, u32[]{:S(2)}) collective-permute-start(f32[384,384]{1,0:T(8,128)S(1)} %get-tuple-element.45), channel_id=1, source_target_pairs={{16,24},{17,25},{18,26},{19,27},{20,28},{21,29},{22,30},{23,31}} | collective-permute-start | bytes 1769480 | tf_op jit(solution)/shard_map/ppermute | solution.py:66
  60.1 36.1 %collective-permute-start.12 = (f32[384,128]{1,0:T(8,128)S(1)}, f32[384,128]{1,0:T(8,128)S(1)}, u32[]{:S(2)}, u32[]{:S(2)}) collective-permute-start(f32[384,128]{1,0:T(8,128)S(1)} %get-tuple-element.43), channel_id=1, source_target_pairs={{8,16},{9,17},{10,18},{11,19},{12,20},{13,21},{14,22},{15,23}} | collective-permute-start | bytes 589832 | tf_op jit(solution)/shard_map/ppermute | solution.py:66
  60.7 51.3 %collective-permute-start.18 = (f32[384,128]{1,0:T(8,128)S(1)}, f32[384,128]{1,0:T(8,128)}, u32[]{:S(2)}, u32[]{:S(2)}) collective-permute-start(f32[384,128]{1,0:T(8,128)S(1)} %get-tuple-element.50), channel_id=1, source_target_pairs={{8,16},{9,17},{10,18},{11,19},{12,20},{13,21},{14,22},{15,23}} | collective-permute-start | bytes 589832 | tf_op jit(solution)/shard_map/ppermute | solution.py:66
  62.8 46.2 %collective-permute-start.17 = (f32[384,128]{1,0:T(8,128)}, f32[384,128]{1,0:T(8,128)S(1)}, u32[]{:S(2)}, u32[]{:S(2)}) collective-permute-start(f32[384,128]{1,0:T(8,128)} %get-tuple-element.48), channel_id=1, source_target_pairs={{8,24},{9,25},{10,26},{11,27},{12,28},{13,29},{14,30},{15,31}} | collective-permute-start | bytes 589832 | tf_op jit(solution)/shard_map/ppermute | solution.py:66
  71.1 0.8 copy-start.6
  71.9 40.1 %collective-permute-start.19 = (f32[384,128]{1,0:T(8,128)}, f32[384,128]{1,0:T(8,128)}, u32[]{:S(2)}, u32[]{:S(2)}) collective-permute-start(f32[384,128]{1,0:T(8,128)} %shard_map.98), channel_id=1, source_target_pairs={{8,24},{9,25},{10,26},{11,27},{12,28},{13,29},{14,30},{15,31}} | collective-permute-start | bytes 589832 | tf_op jit(solution)/shard_map/ppermute | solution.py:66
  73.2 45.0 %copy-start = (f32[1,4,384,384]{3,2,1,0:T(8,128)S(1)}, f32[1,4,384,384]{3,2,1,0:T(8,128)}, u32[]{:S(2)}) copy-start(f32[1,4,384,384]{3,2,1,0:T(8,128)} %param.10) | copy-start | bytes 7077892
  92.8 1.1 copy-start.7
  110.1 8.1 %collective-permute-start.20 = (f32[384,128]{1,0:T(8,128)}, f32[384,128]{1,0:T(8,128)S(1)}, u32[]{:S(2)}, u32[]{:S(2)}) collective-permute-start(f32[384,128]{1,0:T(8,128)} %shard_map.97), channel_id=1, source_target_pairs={{0,1},{1,2},{2,3},{3,4},{4,5},{5,6},{6,7},{7,8},{8,9},{9,10},{10,1... | collective-permute-start | bytes 589832 | tf_op jit(solution)/shard_map/ppermute | solution.py:267
where the time goes:
time: 121 us; the launch traced here: 120 us
  waiting for transfers between devices  74.2 us (61%)
  starting transfers between devices  25 us (21%)
  Pallas kernels  14.2 us (12%)
  local copies, waits for them, and re-layouts  4.02 us (3%)
  other arithmetic  1.66 us (1%)
    ppermute x20, waiting for transfers between devices, moved(): return lax.ppermute(value, 'sec', pairs)  69.7 us
    ppermute x20, starting transfers between devices, moved(): return lax.ppermute(value, 'sec', pairs)  23.1 us
    pallas_call x15, Pallas kernels, staged(): pl.pallas_call(kernel, out_shape=[jax.ShapeDtypeStruct(shape, F32) for sh...  14.2 us
    ppermute x1, waiting for transfers between devices, per_device(): lax.ppermute(through_field, 'sec', [(i, i + 1) for i in range(length - 1)])  4.49 us
    unnamed x16, local copies, waits for them, and re-layouts  4.02 us
  transfers between devices with their start and end apart: 21, of which 7 were waited for; matrix products, arithmetic and copies ran while one was open for 1% of the time, Pallas kernels for 10%

commit v1 on v0

--- a/solution.py
+++ b/solution.py
@@ -71,9 +71,15 @@
     back = [(4, 2), (5, 3)]
 
     q0 = moved(q, onward)
-    swapped = moved(r, [(7, 6), (6, 7), (1, 0)])
+    swapped = moved(r, [(7, 6), (6, 7), (1, 0), (0, 1)])
     t0 = moved(t, onward)
     u0 = moved(u, onward)
+
+    def load(k, *refs):
+        for i in range(4):
+            refs[4 + i][...] = refs[i][...]
+
+    r_in, (r, t, q, u) = r, staged(load, stride, [r, t, q, u], [square] * 4, 0.1)
 
     def pair_reflect(at):
         def body(k, came, r, t, q, u, *rest):
@@ -110,7 +116,6 @@
     (q1, hu) = staged(forward_q, stride, [q0, r, t, q, u], [square] * 2, 6)
     qa = moved(q1, low)
 
-    r_late = moved(r, [(0, 1), (2, 3), (3, 2)])
 
     def forward_t(k, q0, t0, r, t, t1, rgt):
         @pl.when(k == 0)
@@ -128,7 +133,8 @@
     (relay, gt) = staged(pair_reflect(5), stride, [hopped, r, t, q, u, gt], [square] * 2, 6)
     bounced = moved(relay, [(5, 4), (7, 5)])
     gt_came = moved(gt, [(5, 6), (6, 7)])
-    r_next = moved(lax.optimization_barrier((r, relay))[0], [(4, 3)])
+    r_late = moved(r_in, [(2, 3), (3, 2)])
+    r_next = moved(r_in, [(4, 3)])
 
     def forward_u(k, u0, u, hu, rgt, u1, w):
         @pl.when(k == 0)
@@ -145,40 +151,45 @@
     w_came = moved(w, back)
     ua = moved(u1, low)
 
-    def second_reflect(k, bounced, q1, t1, u1, w, total, gt_out):
+    def low_fields(k, swapped, r, w, t1, incident, f1, s1):
+        @pl.when(k < 2)
+        def _():
+            whole = jnp.where(k == 0, r[...], swapped[...] + w[...])
+            value = right(incident[...])
+            f1[...] = jnp.dot(left(t1[...]), value, preferred_element_type=F32)
+            s1[...] = jnp.dot(left(whole), value, preferred_element_type=F32)
+
+    (f1, s1) = staged(low_fields, stride, [swapped, r, w, t1, incident], [field, field], 1)
+    fa = moved(f1, low)
+    sa = moved(s1, low)
+
+    def open_gate(k, w, out):
+        out[...] = w[:8, :128]
+
+    (gate,) = staged(open_gate, stride, [w], [(8, 128)], 0.1)
+
+    def second_reflect(k, bounced, q1, t1, u1, w, gate, total, gt_out):
         @pl.when((k == 4) | (k == 5))
         def _():
             gt = summed(product(q1[...], bounced[...]), t1[...])
             gt_out[...] = gt
             total[...] = w[...] + product(u1[...], product(bounced[...], gt))
 
-    (total, gt2) = staged(second_reflect, stride, [bounced, q1, t1, u1, w], [square] * 2, 6
+    (total, gt2) = staged(second_reflect, stride, [bounced, q1, t1, u1, w, gate], [square] * 2, 6
     )
     total_came = moved(total, back)
     gt2_came = moved(gt2, [(4, 6), (5, 7)])
 
-    def own_fields(k, r_late, hopped, r, w, t1, incident, r1, f1, s1):
-        @pl.when(k == 0)
-        def _():
-            r1[...] = r[...]
-
+    def own_fields(k, r_late, hopped, w, r1):
         @pl.when(k == 2)
         def _():
             r1[...] = hopped[...] + w[...]
 
-        @pl.when((k == 1) | (k == 3))
+        @pl.when(k == 3)
         def _():
             r1[...] = r_late[...] + w[...]
 
-        @pl.when(k < 2)
-        def _():
-            f1[...] = product(t1[...], incident[...])
-            s1[...] = product(r1[...], incident[...])
-
-    (r1, f1, s1) = staged(own_fields, stride, [r_late, hopped, r, w, t1, incident], [square, field, field], 1
-    )
-    fa = moved(f1, low)
-    sa = moved(s1, low)
+    (r1,) = staged(own_fields, stride, [r_late, hopped, w], [square], 0.1)
 
     def second_q(k, r1, qa, q1, t1, u1, q2, hu_out):
         @pl.when((k == 2) | (k == 3))

time: 121 us -> 138 us (1.14)
  waiting for transfers between devices: 74.2 us -> 94.8 us
  Pallas kernels: 14.2 us -> 7.81 us
  local copies, waits for them, and re-layouts: 4.02 us -> 6.15 us
    ppermute x20, waiting for transfers between devices: 69.7 us -> 90.3 us  [moved(): return lax.ppermute(value, 'sec', pairs)]
    pallas_call x15 -> x18, Pallas kernels: 14.2 us -> 7.81 us  [staged(): pl.pallas_call(kernel, out_shape=[jax.ShapeDtypeStruct(shape, F32) for sh...]
    unnamed x16 -> x22, local copies, waits for them, and re-layouts: 4.02 us -> 6.15 us
  transfers between devices with their start and end apart: 21 -> 21, of which waited for: 7 -> 7; matrix products, arithmetic and copies ran while one was open for 1% -> 1% of each run, Pallas kernels for 10% -> 4%
where the time goes in v1:
time: 138 us; the launch traced here: 137 us
  waiting for transfers between devices  94.8 us (69%)
  starting transfers between devices  25.5 us (18%)
  Pallas kernels  7.81 us (6%)
  local copies, waits for them, and re-layouts  6.15 us (4%)
  other arithmetic  1.66 us (1%)
    ppermute x20, waiting for transfers between devices, moved(): return lax.ppermute(value, 'sec', pairs)  90.3 us
    ppermute x20, starting transfers between devices, moved(): return lax.ppermute(value, 'sec', pairs)  23.6 us
    pallas_call x18, Pallas kernels, staged(): pl.pallas_call(kernel, out_shape=[jax.ShapeDtypeStruct(shape, F32) for sh...  7.81 us
    unnamed x22, local copies, waits for them, and re-layouts  6.15 us
    ppermute x1, waiting for transfers between devices, per_device(): lax.ppermute(through_field, 'sec', [(i, i + 1) for i in range(length - 1)])  4.49 us
  transfers between devices with their start and end apart: 21, of which 7 were waited for; matrix products, arithmetic and copies ran while one was open for 1% of the time, Pallas kernels for 4%

profile of v1, /device:TPU:28, one launch (start us, length us, event | category | flops | bytes accessed | tf_op | source)
XLA Modules:
  0.0 137.0 jit_solution(265326467304031196)
XLA Ops:
  0.6 2.4 %collective-permute-start = (f32[384,384]{1,0:T(8,128)}, f32[384,384]{1,0:T(8,128)S(1)}, u32[]{:S(2)}, u32[]{:S(2)}) collective-permute-start(f32[384,384]{1,0:T(8,128)} %bitcast.16), channel_id=1, source_target_pairs={{28,24},{29,25},{30,26},{31,27},{24,28},{25,29},{26,30},{27,31},{4... | collective-permute-start | bytes 1769480 | tf_op jit(solution)/shard_map/ppermute | solution.py:66
  3.1 0.7 collective-permute-start.2
  3.8 1.1 copy-done.2
  4.8 1.1 copy-done.3
  5.9 1.1 copy-done.5
  7.0 1.1 copy-done.7
  8.0 0.2 shard_map.85
  8.2 9.6 %collective-permute-done.refs_0_ = f32[384,384]{1,0:T(8,128)S(1)} collective-permute-done((f32[384,384]{1,0:T(8,128)}, f32[384,384]{1,0:T(8,128)S(1)}, u32[]{:S(2)}, u32[]{:S(2)}) %collective-permute-start) | collective-permute-done | bytes 589856 | tf_op jit(solution)/shard_map/ppermute | solution.py:66
  17.9 2.1 %collective-permute-start.9 = (f32[384,384]{1,0:T(8,128)S(1)}, f32[384,384]{1,0:T(8,128)S(1)}, u32[]{:S(2)}, u32[]{:S(2)}) collective-permute-start(f32[384,384]{1,0:T(8,128)S(1)} %get-tuple-element.42), channel_id=1, source_target_pairs={{24,28},{25,29},{26,30},{27,31},{28,20},{29,21},{30,22},{31,23},{0... | collective-permute-start | bytes 1769480 | tf_op jit(solution)/shard_map/ppermute | solution.py:66
  19.9 0.7 collective-permute-start.3
  20.6 0.7 collective-permute-start.1
  21.4 0.7 collective-permute-start.10
  22.1 0.7 collective-permute-start.8
  22.8 12.9 %collective-permute-done.9.refs_1_.refs_0_ = f32[384,384]{1,0:T(8,128)S(1)} collective-permute-done((f32[384,384]{1,0:T(8,128)S(1)}, f32[384,384]{1,0:T(8,128)S(1)}, u32[]{:S(2)}, u32[]{:S(2)}) %collective-permute-start.9) | collective-permute-done | bytes 589856 | tf_op jit(solution)/shard_map/ppermute | solution.py:66
  35.7 0.1 shard_map.95
  35.8 4.2 %collective-permute-start.14 = (f32[384,384]{1,0:T(8,128)S(1)}, f32[384,384]{1,0:T(8,128)S(1)}, u32[]{:S(2)}, u32[]{:S(2)}) collective-permute-start(f32[384,384]{1,0:T(8,128)S(1)} %get-tuple-element.48), channel_id=1, source_target_pairs={{20,16},{21,17},{22,18},{23,19},{28,20},{29,21},{30,22},{31,23}} | collective-permute-start | bytes 1769480 | tf_op jit(solution)/shard_map/ppermute | solution.py:66
  40.0 0.0 collective-permute-done.3.refs_1_
  40.0 0.2 shard_map.87
  40.2 0.0 copy-start.1
  40.3 0.8 collective-permute-start.5
  41.1 0.7 collective-permute-start.11
  41.8 0.0 collective-permute-done.10.refs_1_
  41.8 0.7 collective-permute-start.4
  42.6 0.7 collective-permute-start.6
  43.3 7.8 %collective-permute-done.14.refs_0_ = f32[384,384]{1,0:T(8,128)S(1)} collective-permute-done((f32[384,384]{1,0:T(8,128)S(1)}, f32[384,384]{1,0:T(8,128)S(1)}, u32[]{:S(2)}, u32[]{:S(2)}) %collective-permute-start.14) | collective-permute-done | bytes 589856 | tf_op jit(solution)/shard_map/ppermute | solution.py:66
  51.1 0.7 collective-permute-start.7
  51.8 1.3 collective-permute-start.13
  53.1 1.3 collective-permute-start.15
  54.5 0.7 collective-permute-start.16
  55.2 0.2 shard_map.94
  55.4 0.7 collective-permute-start.12
  56.1 1.3 collective-permute-start.18
  57.5 0.7 shard_map.99
  58.1 1.3 collective-permute-start.17
  59.4 1.0 shard_map.101
  60.4 6.1 %collective-permute-done.13.refs_1_ = f32[384,384]{1,0:T(8,128)S(1)} collective-permute-done((f32[384,384]{1,0:T(8,128)S(1)}, f32[384,384]{1,0:T(8,128)S(1)}, u32[]{:S(2)}, u32[]{:S(2)}) %collective-permute-start.13) | collective-permute-done | bytes 589856 | tf_op jit(solution)/shard_map/ppermute | solution.py:66
  66.5 0.8 copy-done.9
  67.3 1.3 collective-permute-start.19
  68.6 0.0 copy-start
  68.6 25.1 %collective-permute-done.15.refs_2_ = f32[384,384]{1,0:T(8,128)} collective-permute-done((f32[384,384]{1,0:T(8,128)S(1)}, f32[384,384]{1,0:T(8,128)}, u32[]{:S(2)}, u32[]{:S(2)}) %collective-permute-start.15) | collective-permute-done | bytes 589856 | tf_op jit(solution)/shard_map/ppermute | solution.py:66
  93.8 1.1 copy-done.10
  94.8 2.3 %shard_map.98.refs_4_ = f32[384,384]{1,0:T(8,128)S(1)} custom-call(f32[384,384]{1,0:T(8,128)S(1)} %get-tuple-element.32.refs_2_.refs_3_.refs_0_, f32[384,384]{1,0:T(8,128)S(1)} %copy-done.10, f32[384,384]{1,0:T(8,128)} %collective-permute-done.15.refs_2_), custom_call_target="tpu_custom_call" | custom-call | flops 679477248 | bytes 2359296 | tf_op jit(solution)/shard_map/pallas_call | solution.py:47
  97.1 28.7 %collective-permute-done.17.refs_5_ = f32[384,128]{1,0:T(8,128)S(1)} collective-permute-done((f32[384,128]{1,0:T(8,128)}, f32[384,128]{1,0:T(8,128)S(1)}, u32[]{:S(2)}, u32[]{:S(2)}) %collective-permute-start.17) | collective-permute-done | bytes 196640 | tf_op jit(solution)/shard_map/ppermute | solution.py:66
  125.8 1.1 shard_map.100
  126.9 1.9 %collective-permute-start.20 = (f32[384,128]{1,0:T(8,128)}, f32[384,128]{1,0:T(8,128)S(1)}, u32[]{:S(2)}, u32[]{:S(2)}) collective-permute-start(f32[384,128]{1,0:T(8,128)} %shard_map.100), channel_id=1, source_target_pairs={{0,1},{1,2},{2,3},{3,4},{4,5},{5,6},{6,7},{7,8},{8,9},{9,10},{10,1... | collective-permute-start | bytes 589832 | tf_op jit(solution)/shard_map/ppermute | solution.py:278
  128.8 1.7 %select_bitcast_fusion = f32[1,384,128]{2,1,0:T(8,128)} fusion(f32[384,128]{1,0:T(8,128)S(1)} %get-tuple-element.41, f32[384,128]{1,0:T(8,128)S(1)} %get-tuple-element.53.refs_0_, f32[384,128]{1,0:T(8,128)} %collective-permute-done.18, f32[384,128]{1,0:T(8,128)} %collective-permute-done.19, pred[]{:T(512)S(6)} %lt.11, pred[]{:T(512)S(6)} %lt.10, pred[]{:T(512)S(6)} %lt.9), kind=kLoop, calls=%fused_computation | loop fusion | flops 147456 | bytes 983043 | tf_op jit(solution)/shard_map/broadcast_in_dim | solution.py:289
  130.5 4.5 %collective-permute-done.20.refs_1_ = f32[384,128]{1,0:T(8,128)S(1)} collective-permute-done((f32[384,128]{1,0:T(8,128)}, f32[384,128]{1,0:T(8,128)S(1)}, u32[]{:S(2)}, u32[]{:S(2)}) %collective-permute-start.20) | collective-permute-done | bytes 196640 | tf_op jit(solution)/shard_map/ppermute | solution.py:278
  135.0 2.0 %shard_map.102 = f32[4,384,128]{2,1,0:T(8,128)} custom-call(f32[4,384,384]{2,1,0:T(8,128)S(1)} %bitcast.9, f32[384,128]{1,0:T(8,128)S(1)} %collective-permute-done.20.refs_1_, f32[384,128]{1,0:T(8,128)S(1)} %copy-done.1), custom_call_target="tpu_custom_call" | custom-call | flops 384 | bytes 256 | tf_op jit(solution)/shard_map/pallas_call | solution.py:47
  (35 shorter events, 0.2 us)
Async XLA Ops:
  0.6 17.2 %collective-permute-start = (f32[384,384]{1,0:T(8,128)}, f32[384,384]{1,0:T(8,128)S(1)}, u32[]{:S(2)}, u32[]{:S(2)}) collective-permute-start(f32[384,384]{1,0:T(8,128)} %bitcast.16), channel_id=1, source_target_pairs={{28,24},{29,25},{30,26},{31,27},{24,28},{25,29},{26,30},{27,31},{4... | collective-permute-start | bytes 1769480 | tf_op jit(solution)/shard_map/ppermute | solution.py:66
  3.1 19.0 %collective-permute-start.2 = (f32[384,384]{1,0:T(8,128)}, f32[384,384]{1,0:T(8,128)S(1)}, u32[]{:S(2)}, u32[]{:S(2)}) collective-permute-start(f32[384,384]{1,0:T(8,128)} %bitcast.10), channel_id=1, source_target_pairs={{0,4},{1,5},{2,6},{3,7},{4,8},{5,9},{6,10},{7,11},{8,12},{9,13},{1... | collective-permute-start | bytes 1769480 | tf_op jit(solution)/shard_map/ppermute | solution.py:66
  3.8 1.1 copy-start.2
  4.8 1.1 copy-start.3
  5.9 1.1 copy-start.5
  7.0 1.1 copy-start.7
  17.8 2.1 %copy-start.4 = (f32[1,384,384]{2,1,0:T(8,128)S(1)}, f32[1,384,384]{2,1,0:T(8,128)}, u32[]{:S(2)}) copy-start(f32[1,384,384]{2,1,0:T(8,128)} %param.7) | copy-start | bytes 1769476
  17.8 2.8 %copy-start.6 = (f32[1,384,384]{2,1,0:T(8,128)S(1)}, f32[1,384,384]{2,1,0:T(8,128)}, u32[]{:S(2)}) copy-start(f32[1,384,384]{2,1,0:T(8,128)} %param.9) | copy-start | bytes 1769476
  17.8 3.5 %copy-start.8 = (f32[1,384,384]{2,1,0:T(8,128)S(1)}, f32[1,384,384]{2,1,0:T(8,128)}, u32[]{:S(2)}) copy-start(f32[1,384,384]{2,1,0:T(8,128)} %param.6) | copy-start | bytes 1769476
  17.9 17.9 %collective-permute-start.9 = (f32[384,384]{1,0:T(8,128)S(1)}, f32[384,384]{1,0:T(8,128)S(1)}, u32[]{:S(2)}, u32[]{:S(2)}) collective-permute-start(f32[384,384]{1,0:T(8,128)S(1)} %get-tuple-element.42), channel_id=1, source_target_pairs={{24,28},{25,29},{26,30},{27,31},{28,20},{29,21},{30,22},{31,23},{0... | collective-permute-start | bytes 1769480 | tf_op jit(solution)/shard_map/ppermute | solution.py:66
  19.9 20.1 %collective-permute-start.3 = (f32[384,384]{1,0:T(8,128)S(1)}, f32[384,384]{1,0:T(8,128)S(1)}, u32[]{:S(2)}, u32[]{:S(2)}) collective-permute-start(f32[384,384]{1,0:T(8,128)S(1)} %bitcast.13), channel_id=1, source_target_pairs={{0,4},{1,5},{2,6},{3,7},{4,8},{5,9},{6,10},{7,11},{8,12},{9,13},{1... | collective-permute-start | bytes 1769480 | tf_op jit(solution)/shard_map/ppermute | solution.py:66
  20.6 19.6 %collective-permute-start.1 = (f32[384,384]{1,0:T(8,128)S(1)}, f32[384,384]{1,0:T(8,128)S(1)}, u32[]{:S(2)}, u32[]{:S(2)}) collective-permute-start(f32[384,384]{1,0:T(8,128)S(1)} %bitcast.15), channel_id=1, source_target_pairs={{0,4},{1,5},{2,6},{3,7},{4,8},{5,9},{6,10},{7,11},{8,12},{9,13},{1... | collective-permute-start | bytes 1769480 | tf_op jit(solution)/shard_map/ppermute | solution.py:66
  21.4 20.5 %collective-permute-start.10 = (f32[384,384]{1,0:T(8,128)S(1)}, f32[384,384]{1,0:T(8,128)S(1)}, u32[]{:S(2)}, u32[]{:S(2)}) collective-permute-start(f32[384,384]{1,0:T(8,128)S(1)} %bitcast.18), channel_id=1, source_target_pairs={{16,12},{17,13},{18,14},{19,15}} | collective-permute-start | bytes 1769480 | tf_op jit(solution)/shard_map/ppermute | solution.py:66
  22.1 20.5 %collective-permute-start.8 = (f32[384,384]{1,0:T(8,128)S(1)}, f32[384,384]{1,0:T(8,128)S(1)}, u32[]{:S(2)}, u32[]{:S(2)}) collective-permute-start(f32[384,384]{1,0:T(8,128)S(1)} %bitcast.19), channel_id=1, source_target_pairs={{8,12},{9,13},{10,14},{11,15},{12,8},{13,9},{14,10},{15,11}} | collective-permute-start | bytes 1769480 | tf_op jit(solution)/shard_map/ppermute | solution.py:66
  35.8 15.3 %collective-permute-start.14 = (f32[384,384]{1,0:T(8,128)S(1)}, f32[384,384]{1,0:T(8,128)S(1)}, u32[]{:S(2)}, u32[]{:S(2)}) collective-permute-start(f32[384,384]{1,0:T(8,128)S(1)} %get-tuple-element.48), channel_id=1, source_target_pairs={{20,16},{21,17},{22,18},{23,19},{28,20},{29,21},{30,22},{31,23}} | collective-permute-start | bytes 1769480 | tf_op jit(solution)/shard_map/ppermute | solution.py:66
  40.2 2.3 %copy-start.1 = (f32[384,128]{1,0:T(8,128)S(1)}, f32[384,128]{1,0:T(8,128)}, u32[]{:S(2)}) copy-start(f32[384,128]{1,0:T(8,128)} %refs_2_.1) | copy-start | bytes 589828
  40.3 14.2 %collective-permute-start.5 = (f32[384,384]{1,0:T(8,128)S(1)}, f32[384,384]{1,0:T(8,128)S(1)}, u32[]{:S(2)}, u32[]{:S(2)}) collective-permute-start(f32[384,384]{1,0:T(8,128)S(1)} %get-tuple-element.40.refs_4_.refs_5_.refs_3_), channel_id=1, source_target_pairs={{0,8},{1,9},{2,10},{3,11},{4,12},{5,13},{6,14},{7,15}} | collective-permute-start | bytes 1769480 | tf_op jit(solution)/shard_map/ppermute | solution.py:66
  41.1 14.1 %collective-permute-start.11 = (f32[384,384]{1,0:T(8,128)S(1)}, f32[384,384]{1,0:T(8,128)S(1)}, u32[]{:S(2)}, u32[]{:S(2)}) collective-permute-start(f32[384,384]{1,0:T(8,128)S(1)} %get-tuple-element.36.refs_2_.refs_0_.refs_4_), channel_id=1, source_target_pairs={{16,8},{17,9},{18,10},{19,11},{20,12},{21,13},{22,14},{23,15}} | collective-permute-start | bytes 1769480 | tf_op jit(solution)/shard_map/ppermute | solution.py:66
  41.8 13.4 %collective-permute-start.4 = (f32[384,384]{1,0:T(8,128)S(1)}, f32[384,384]{1,0:T(8,128)S(1)}, u32[]{:S(2)}, u32[]{:S(2)}) collective-permute-start(f32[384,384]{1,0:T(8,128)S(1)} %get-tuple-element.39.refs_2_.refs_3_.refs_1_), channel_id=1, source_target_pairs={{0,8},{1,9},{2,10},{3,11},{4,12},{5,13},{6,14},{7,15}} | collective-permute-start | bytes 1769480 | tf_op jit(solution)/shard_map/ppermute | solution.py:66
  42.6 9.3 %collective-permute-start.6 = (f32[384,128]{1,0:T(8,128)S(1)}, f32[384,128]{1,0:T(8,128)S(1)}, u32[]{:S(2)}, u32[]{:S(2)}) collective-permute-start(f32[384,128]{1,0:T(8,128)S(1)} %get-tuple-element.38.refs_0_), channel_id=1, source_target_pairs={{0,8},{1,9},{2,10},{3,11},{4,12},{5,13},{6,14},{7,15}} | collective-permute-start | bytes 589832 | tf_op jit(solution)/shard_map/ppermute | solution.py:66
  51.1 2.1 %collective-permute-start.7 = (f32[384,128]{1,0:T(8,128)S(1)}, f32[384,128]{1,0:T(8,128)S(1)}, u32[]{:S(2)}, u32[]{:S(2)}) collective-permute-start(f32[384,128]{1,0:T(8,128)S(1)} %get-tuple-element.41), channel_id=1, source_target_pairs={{0,8},{1,9},{2,10},{3,11},{4,12},{5,13},{6,14},{7,15}} | collective-permute-start | bytes 589832 | tf_op jit(solution)/shard_map/ppermute | solution.py:66
  51.8 14.7 %collective-permute-start.13 = (f32[384,384]{1,0:T(8,128)S(1)}, f32[384,384]{1,0:T(8,128)S(1)}, u32[]{:S(2)}, u32[]{:S(2)}) collective-permute-start(f32[384,384]{1,0:T(8,128)S(1)} %get-tuple-element.47), channel_id=1, source_target_pairs={{20,24},{21,25},{22,26},{23,27},{24,28},{25,29},{26,30},{27,31}} | collective-permute-start | bytes 1769480 | tf_op jit(solution)/shard_map/ppermute | solution.py:66
  53.1 40.6 %collective-permute-start.15 = (f32[384,384]{1,0:T(8,128)S(1)}, f32[384,384]{1,0:T(8,128)}, u32[]{:S(2)}, u32[]{:S(2)}) collective-permute-start(f32[384,384]{1,0:T(8,128)S(1)} %get-tuple-element.49), channel_id=1, source_target_pairs={{16,24},{17,25},{18,26},{19,27},{20,28},{21,29},{22,30},{23,31}} | collective-permute-start | bytes 1769480 | tf_op jit(solution)/shard_map/ppermute | solution.py:66
  54.5 3.0 %collective-permute-start.16 = (f32[384,384]{1,0:T(8,128)S(1)}, f32[384,384]{1,0:T(8,128)S(1)}, u32[]{:S(2)}, u32[]{:S(2)}) collective-permute-start(f32[384,384]{1,0:T(8,128)S(1)} %get-tuple-element.50), channel_id=1, source_target_pairs={{16,8},{17,9},{18,10},{19,11},{20,12},{21,13},{22,14},{23,15}} | collective-permute-start | bytes 1769480 | tf_op jit(solution)/shard_map/ppermute | solution.py:66
  55.4 41.7 %collective-permute-start.12 = (f32[384,128]{1,0:T(8,128)S(1)}, f32[384,128]{1,0:T(8,128)S(1)}, u32[]{:S(2)}, u32[]{:S(2)}) collective-permute-start(f32[384,128]{1,0:T(8,128)S(1)} %get-tuple-element.45), channel_id=1, source_target_pairs={{8,16},{9,17},{10,18},{11,19},{12,20},{13,21},{14,22},{15,23}} | collective-permute-start | bytes 589832 | tf_op jit(solution)/shard_map/ppermute | solution.py:66
  56.1 72.7 %collective-permute-start.18 = (f32[384,128]{1,0:T(8,128)S(1)}, f32[384,128]{1,0:T(8,128)}, u32[]{:S(2)}, u32[]{:S(2)}) collective-permute-start(f32[384,128]{1,0:T(8,128)S(1)} %get-tuple-element.54), channel_id=1, source_target_pairs={{8,16},{9,17},{10,18},{11,19},{12,20},{13,21},{14,22},{15,23}} | collective-permute-start | bytes 589832 | tf_op jit(solution)/shard_map/ppermute | solution.py:66
  58.1 67.7 %collective-permute-start.17 = (f32[384,128]{1,0:T(8,128)}, f32[384,128]{1,0:T(8,128)S(1)}, u32[]{:S(2)}, u32[]{:S(2)}) collective-permute-start(f32[384,128]{1,0:T(8,128)} %get-tuple-element.52), channel_id=1, source_target_pairs={{8,24},{9,25},{10,26},{11,27},{12,28},{13,29},{14,30},{15,31}} | collective-permute-start | bytes 589832 | tf_op jit(solution)/shard_map/ppermute | solution.py:66
  66.5 0.8 copy-start.9
  67.3 61.5 %collective-permute-start.19 = (f32[384,128]{1,0:T(8,128)}, f32[384,128]{1,0:T(8,128)}, u32[]{:S(2)}, u32[]{:S(2)}) collective-permute-start(f32[384,128]{1,0:T(8,128)} %shard_map.101), channel_id=1, source_target_pairs={{8,24},{9,25},{10,26},{11,27},{12,28},{13,29},{14,30},{15,31}} | collective-permute-start | bytes 589832 | tf_op jit(solution)/shard_map/ppermute | solution.py:66
  68.6 66.3 %copy-start = (f32[1,4,384,384]{3,2,1,0:T(8,128)S(1)}, f32[1,4,384,384]{3,2,1,0:T(8,128)}, u32[]{:S(2)}) copy-start(f32[1,4,384,384]{3,2,1,0:T(8,128)} %param.10) | copy-start | bytes 7077892
  93.8 1.1 copy-start.10
  126.9 8.1 %collective-permute-start.20 = (f32[384,128]{1,0:T(8,128)}, f32[384,128]{1,0:T(8,128)S(1)}, u32[]{:S(2)}, u32[]{:S(2)}) collective-permute-start(f32[384,128]{1,0:T(8,128)} %shard_map.100), channel_id=1, source_target_pairs={{0,1},{1,2},{2,3},{3,4},{4,5},{5,6},{6,7},{7,8},{8,9},{9,10},{10,1... | collective-permute-start | bytes 589832 | tf_op jit(solution)/shard_map/ppermute | solution.py:278

commit v2 on v1

--- a/solution.py
+++ b/solution.py
@@ -50,7 +50,9 @@
         in_specs=[vmem] * len(inputs),
         out_specs=[vmem] * len(outputs),
         compiler_params=pltpu.CompilerParams(vmem_limit_bytes=24 * 2**20),
-        cost_estimate=pl.CostEstimate(flops=int(products * 6 * side**3), bytes_accessed=moved_bytes, transcendentals=0),
+        cost_estimate=pl.CostEstimate(
+            flops=int(products * 6 * side**3), bytes_accessed=moved_bytes, transcendentals=0
+        ),
     )(*inputs)
 
 
@@ -159,7 +161,8 @@
             f1[...] = jnp.dot(left(t1[...]), value, preferred_element_type=F32)
             s1[...] = jnp.dot(left(whole), value, preferred_element_type=F32)
 
-    (f1, s1) = staged(low_fields, stride, [swapped, r, w, t1, incident], [field, field], 1)
+    (f1, s1) = staged(low_fields, stride, [swapped, r, w, t1, incident], [field, field], 1
+    )
     fa = moved(f1, low)
     sa = moved(s1, low)
 
@@ -200,18 +203,16 @@
 
     (q2, hu2) = staged(second_q, stride, [r1, qa, q1, t1, u1], [square] * 2, 6)
 
-    def second_fields(k, qa, ua, fa, sa, hu2, r1, t1, u2, f2, s2):
+    def second_fields(k, qa, fa, r1, t1, f2, rg2):
         @pl.when((k == 2) | (k == 3))
         def _():
             g = summed(product(qa[...], r1[...]), fa[...])
             f2[...] = product(t1[...], g)
-            s2[...] = sa[...] + product(ua[...], product(r1[...], g))
-            u2[...] = product(ua[...], hu2[...])
-
-    (u2, f2, s2) = staged(second_fields, stride, [qa, ua, fa, sa, hu2, r1, t1], [square, field, field], 4
-    )
-
-    def third_fields(k, r_late, r_next, w_came, q1, t1, u1, r1, qa, ua, fa, sa, w4, s4):
+            rg2[...] = product(r1[...], g)
+
+    (f2, rg2) = staged(second_fields, stride, [qa, fa, r1, t1], [field, field], 2)
+
+    def third_fields(k, r_late, r_next, w_came, q1, t1, u1, r1, qa, fa, w4, rg4):
         @pl.when((k == 2) | (k == 3))
         def _():
             came = jnp.where(k == 2, r_late[...], r_next[...]) + w_came[...]
@@ -219,15 +220,12 @@
             rc = r1[...] + product(u1[...], product(came, gt))
             g = summed(product(qa[...], rc), fa[...])
             w4[...] = product(gt, g)
-            s4[...] = sa[...] + product(ua[...], product(rc, g))
-
-    (w4, s4) = staged(third_fields, stride,
-        [r_late, r_next, w_came, q1, t1, u1, r1, qa, ua, fa, sa],
-        [field] * 2,
-        9,
+            rg4[...] = product(rc, g)
+
+    (w4, rg4) = staged(
+        third_fields, stride, [r_late, r_next, w_came, q1, t1, u1, r1, qa, fa], [field] * 2, 9
     )
     w4_came = moved(w4, [(2, 4), (3, 5)])
-    s4_came = moved(s4, [(2, 4), (3, 5)])
 
     def second_through(k, t, gt_came, gt2_came, t2):
         @pl.when(k > 5)
@@ -248,13 +246,18 @@
     )
     g6_came = moved(g6, [(2, 6), (3, 7)])
 
-    def last_reflected(k, s2, u2, rg6, s6):
-        @pl.when((k == 2) | (k == 3))
-        def _():
-            s6[...] = s2[...] + product(u2[...], rg6[...])
-
-    (s6,) = staged(last_reflected, stride, [s2, u2, rg6], [field], 1)
+    def all_reflected(k, sa, ua, rg2, rg4, rg6, hu2, s2, s4, s6):
+        @pl.when((k == 2) | (k == 3))
+        def _():
+            sums = rg2[...] + product(hu2[...], rg6[...])
+            value = product(ua[...], jnp.concatenate([rg2[...], rg4[...], sums], axis=1))
+            width = sa.shape[1]
+            for i, out in enumerate((s2, s4, s6)):
+                out[...] = sa[...] + value[:, i * width : (i + 1) * width]
+
+    (s2, s4, s6) = staged(all_reflected, stride, [sa, ua, rg2, rg4, rg6, hu2], [field] * 3, 2)
     s6_came = moved(s6, [(2, 6), (3, 7)])
+    s4_came = moved(s4, [(2, 4), (3, 5)])
 
     def through(k, f1, f2, t1, w4, t2, g6, out):
         @pl.when(k < 2)
@@ -285,7 +288,12 @@
         for j in range(depth_maps.shape[1]):
             out[j] = jnp.dot(left(maps[j]), value, preferred_element_type=F32)
 
-    (depth_fields,) = staged(depths, 1, [depth_maps[0], entering, incident], [depth_maps.shape[1:3] + field[1:]], 1)
+    (depth_fields,) = staged(depths,
+        1,
+        [depth_maps[0], entering, incident],
+        [depth_maps.shape[1:3] + field[1:]],
+        1,
+    )
     return (through_field[None], reflected[None], depth_fields[None])
 
 
@@ -300,4 +308,6 @@
     )
     out_specs = (P("sec", None, None), P("sec", None, None), P("sec", None, None, None))
 
-    return jax.shard_map(per_device, mesh=mesh, in_specs=in_specs, out_specs=out_specs, check_vma=False)
+    return jax.shard_map(
+        per_device, mesh=mesh, in_specs=in_specs, out_specs=out_specs, check_vma=False
+    )

time: 138 us -> 124 us (0.90)
  the two profiles are of different devices: /device:TPU:28 before, /device:TPU:12 now
where the time goes in v2:
time: 124 us; the launch traced here: 123 us
  waiting for transfers between devices  51.9 us (42%)
  starting transfers between devices  32.8 us (26%)
  Pallas kernels  29.6 us (24%)
  local copies, waits for them, and re-layouts  6.44 us (5%)
  other arithmetic  1.65 us (1%)
    ppermute x20, waiting for transfers between devices, moved(): return lax.ppermute(value, 'sec', pairs)  47.4 us
    ppermute x20, starting transfers between devices, moved(): return lax.ppermute(value, 'sec', pairs)  30.9 us
    pallas_call x18, Pallas kernels, staged(): pl.pallas_call(kernel, out_shape=[jax.ShapeDtypeStruct(shape, F32) for sh...  29.6 us
    unnamed x22, local copies, waits for them, and re-layouts  6.44 us
    ppermute x1, waiting for transfers between devices, per_device(): lax.ppermute(through_field, 'sec', [(i, i + 1) for i in range(length - 1)])  4.5 us
  transfers between devices with their start and end apart: 21, of which 6 were waited for; matrix products, arithmetic and copies ran while one was open for 1% of the time, Pallas kernels for 22%

profile of v2, /device:TPU:12, one launch (start us, length us, event | category | flops | bytes accessed | tf_op | source)
XLA Modules:
  0.0 123.4 jit_solution(8483067262830212132)
XLA Ops:
  0.6 0.7 collective-permute-start
  1.3 3.4 %collective-permute-start.2 = (f32[384,384]{1,0:T(8,128)}, f32[384,384]{1,0:T(8,128)S(1)}, u32[]{:S(2)}, u32[]{:S(2)}) collective-permute-start(f32[384,384]{1,0:T(8,128)} %bitcast.10), channel_id=1, source_target_pairs={{0,4},{1,5},{2,6},{3,7},{4,8},{5,9},{6,10},{7,11},{8,12},{9,13},{1... | collective-permute-start | bytes 1769480 | tf_op jit(solution)/shard_map/ppermute | solution.py:68
  4.8 1.1 copy-done.2
  5.8 1.1 copy-done.3
  6.9 1.1 copy-done.5
  8.0 1.1 copy-done.7
  9.0 0.2 shard_map.85
  9.3 0.8 collective-permute-start.7
  10.1 0.1 copy-done.4
  10.3 3.4 %collective-permute-start.3 = (f32[384,384]{1,0:T(8,128)S(1)}, f32[384,384]{1,0:T(8,128)S(1)}, u32[]{:S(2)}, u32[]{:S(2)}) collective-permute-start(f32[384,384]{1,0:T(8,128)S(1)} %bitcast.13), channel_id=1, source_target_pairs={{0,4},{1,5},{2,6},{3,7},{4,8},{5,9},{6,10},{7,11},{8,12},{9,13},{1... | collective-permute-start | bytes 1769480 | tf_op jit(solution)/shard_map/ppermute | solution.py:68
  13.7 1.9 %collective-permute-start.1 = (f32[384,384]{1,0:T(8,128)S(1)}, f32[384,384]{1,0:T(8,128)S(1)}, u32[]{:S(2)}, u32[]{:S(2)}) collective-permute-start(f32[384,384]{1,0:T(8,128)S(1)} %bitcast.15), channel_id=1, source_target_pairs={{0,4},{1,5},{2,6},{3,7},{4,8},{5,9},{6,10},{7,11},{8,12},{9,13},{1... | collective-permute-start | bytes 1769480 | tf_op jit(solution)/shard_map/ppermute | solution.py:68
  15.6 1.3 %collective-permute-start.8 = (f32[384,384]{1,0:T(8,128)S(1)}, f32[384,384]{1,0:T(8,128)S(1)}, u32[]{:S(2)}, u32[]{:S(2)}) collective-permute-start(f32[384,384]{1,0:T(8,128)S(1)} %bitcast.18), channel_id=1, source_target_pairs={{16,12},{17,13},{18,14},{19,15}} | collective-permute-start | bytes 1769480 | tf_op jit(solution)/shard_map/ppermute | solution.py:68
  16.9 2.7 %collective-permute-done.2.refs_0_ = f32[384,384]{1,0:T(8,128)S(1)} collective-permute-done((f32[384,384]{1,0:T(8,128)}, f32[384,384]{1,0:T(8,128)S(1)}, u32[]{:S(2)}, u32[]{:S(2)}) %collective-permute-start.2) | collective-permute-done | bytes 589856 | tf_op jit(solution)/shard_map/ppermute | solution.py:68
  19.6 2.2 %collective-permute-start.6 = (f32[384,384]{1,0:T(8,128)S(1)}, f32[384,384]{1,0:T(8,128)S(1)}, u32[]{:S(2)}, u32[]{:S(2)}) collective-permute-start(f32[384,384]{1,0:T(8,128)S(1)} %bitcast.19), channel_id=1, source_target_pairs={{8,12},{9,13},{10,14},{11,15},{12,8},{13,9},{14,10},{15,11}} | collective-permute-start | bytes 1769480 | tf_op jit(solution)/shard_map/ppermute | solution.py:68
  21.8 3.7 %shard_map.86 = (f32[384,384]{1,0:T(8,128)S(1)}, f32[384,384]{1,0:T(8,128)S(1)}) custom-call(f32[384,384]{1,0:T(8,128)S(1)} %collective-permute-done.2.refs_0_, f32[384,384]{1,0:T(8,128)S(1)} %get-tuple-element.32.refs_1_.refs_2_, f32[384,384]{1,0:T(8,128)S(1)} %get-tuple-element.34.refs_2_.refs_3_.refs_0_, f32[384,384]{1,0:T(8,128)S(1)} %get-tuple-element.35.refs_3_, ...), custom_call_target="tpu_custom_call" | custom-call | flops 2038431744 | bytes 4128768 | tf_op jit(solution)/shard_map/pallas_call | solution.py:47
  25.5 0.1 shard_map.94
  25.6 0.7 collective-permute-start.12
  26.3 18.6 %collective-permute-done.3.refs_1_ = f32[384,384]{1,0:T(8,128)S(1)} collective-permute-done((f32[384,384]{1,0:T(8,128)S(1)}, f32[384,384]{1,0:T(8,128)S(1)}, u32[]{:S(2)}, u32[]{:S(2)}) %collective-permute-start.3) | collective-permute-done | bytes 589856 | tf_op jit(solution)/shard_map/ppermute | solution.py:68
  44.9 3.5 %shard_map.87 = (f32[384,384]{1,0:T(8,128)S(1)}, f32[384,384]{1,0:T(8,128)S(1)}) custom-call(f32[384,384]{1,0:T(8,128)S(1)} %collective-permute-done.2.refs_0_, f32[384,384]{1,0:T(8,128)S(1)} %collective-permute-done.3.refs_1_, f32[384,384]{1,0:T(8,128)S(1)} %get-tuple-element.32.refs_1_.refs_2_, f32[384,384]{1,0:T(8,128)S(1)} %get-tuple-element.34.refs_2_.refs_3_.refs_0_), custom_call_target="tpu_custom_call" | custom-call | flops 2038431744 | bytes 3538944 | tf_op jit(solution)/shard_map/pallas_call | solution.py:47
  48.4 9.1 %collective-permute-done.1.refs_0_ = f32[384,384]{1,0:T(8,128)S(1)} collective-permute-done((f32[384,384]{1,0:T(8,128)S(1)}, f32[384,384]{1,0:T(8,128)S(1)}, u32[]{:S(2)}, u32[]{:S(2)}) %collective-permute-start.1) | collective-permute-done | bytes 589856 | tf_op jit(solution)/shard_map/ppermute | solution.py:68
  57.6 1.1 shard_map.88
  58.7 1.3 %collective-permute-start.9 = (f32[384,384]{1,0:T(8,128)S(1)}, f32[384,384]{1,0:T(8,128)S(1)}, u32[]{:S(2)}, u32[]{:S(2)}) collective-permute-start(f32[384,384]{1,0:T(8,128)S(1)} %get-tuple-element.38.refs_2_.refs_0_.refs_4_), channel_id=1, source_target_pairs={{16,8},{17,9},{18,10},{19,11},{20,12},{21,13},{22,14},{23,15}} | collective-permute-start | bytes 1769480 | tf_op jit(solution)/shard_map/ppermute | solution.py:68
  60.0 1.3 %collective-permute-start.4 = (f32[384,384]{1,0:T(8,128)S(1)}, f32[384,384]{1,0:T(8,128)S(1)}, u32[]{:S(2)}, u32[]{:S(2)}) collective-permute-start(f32[384,384]{1,0:T(8,128)S(1)} %get-tuple-element.41.refs_3_.refs_1_.refs_2_), channel_id=1, source_target_pairs={{0,8},{1,9},{2,10},{3,11},{4,12},{5,13},{6,14},{7,15}} | collective-permute-start | bytes 1769480 | tf_op jit(solution)/shard_map/ppermute | solution.py:68
  61.4 1.3 %collective-permute-start.5 = (f32[384,128]{1,0:T(8,128)S(1)}, f32[384,128]{1,0:T(8,128)S(1)}, u32[]{:S(2)}, u32[]{:S(2)}) collective-permute-start(f32[384,128]{1,0:T(8,128)S(1)} %get-tuple-element.40.refs_0_), channel_id=1, source_target_pairs={{0,8},{1,9},{2,10},{3,11},{4,12},{5,13},{6,14},{7,15}} | collective-permute-start | bytes 589832 | tf_op jit(solution)/shard_map/ppermute | solution.py:68
  62.7 6.4 %collective-permute-done.6.refs_0_ = f32[384,384]{1,0:T(8,128)S(1)} collective-permute-done((f32[384,384]{1,0:T(8,128)S(1)}, f32[384,384]{1,0:T(8,128)S(1)}, u32[]{:S(2)}, u32[]{:S(2)}) %collective-permute-start.6) | collective-permute-done | bytes 589856 | tf_op jit(solution)/shard_map/ppermute | solution.py:68
  69.1 1.3 %collective-permute-start.14 = (f32[384,384]{1,0:T(8,128)S(1)}, f32[384,384]{1,0:T(8,128)S(1)}, u32[]{:S(2)}, u32[]{:S(2)}) collective-permute-start(f32[384,384]{1,0:T(8,128)S(1)} %get-tuple-element.50), channel_id=1, source_target_pairs={{16,8},{17,9},{18,10},{19,11},{20,12},{21,13},{22,14},{23,15}} | collective-permute-start | bytes 1769480 | tf_op jit(solution)/shard_map/ppermute | solution.py:68
  70.5 1.3 %collective-permute-start.17 = (f32[384,384]{1,0:T(8,128)S(1)}, f32[384,384]{1,0:T(8,128)S(1)}, u32[]{:S(2)}, u32[]{:S(2)}) collective-permute-start(f32[384,384]{1,0:T(8,128)S(1)} %get-tuple-element.44.refs_5_.refs_3_.refs_4_), channel_id=1, source_target_pairs={{0,8},{1,9},{2,10},{3,11},{4,12},{5,13},{6,14},{7,15}} | collective-permute-start | bytes 1769480 | tf_op jit(solution)/shard_map/ppermute | solution.py:68
  71.8 10.5 %collective-permute-done.5.refs_1_.refs_8_ = f32[384,128]{1,0:T(8,128)S(1)} collective-permute-done((f32[384,128]{1,0:T(8,128)S(1)}, f32[384,128]{1,0:T(8,128)S(1)}, u32[]{:S(2)}, u32[]{:S(2)}) %collective-permute-start.5) | collective-permute-done | bytes 196640 | tf_op jit(solution)/shard_map/ppermute | solution.py:68
  82.3 1.3 %collective-permute-start.16 = (f32[384,128]{1,0:T(8,128)S(1)}, f32[384,128]{1,0:T(8,128)S(1)}, u32[]{:S(2)}, u32[]{:S(2)}) collective-permute-start(f32[384,128]{1,0:T(8,128)S(1)} %get-tuple-element.53), channel_id=1, source_target_pairs={{0,8},{1,9},{2,10},{3,11},{4,12},{5,13},{6,14},{7,15}} | collective-permute-start | bytes 589832 | tf_op jit(solution)/shard_map/ppermute | solution.py:68
  83.6 0.7 collective-permute-start.11
  84.3 1.5 %collective-permute-start.13 = (f32[384,384]{1,0:T(8,128)S(1)}, f32[384,384]{1,0:T(8,128)}, u32[]{:S(2)}, u32[]{:S(2)}) collective-permute-start(f32[384,384]{1,0:T(8,128)S(1)} %get-tuple-element.49), channel_id=1, source_target_pairs={{16,24},{17,25},{18,26},{19,27},{20,28},{21,29},{22,30},{23,31}} | collective-permute-start | bytes 1769480 | tf_op jit(solution)/shard_map/ppermute | solution.py:68
  85.8 6.3 %shard_map.93 = (f32[384,128]{1,0:T(8,128)S(1)}, f32[384,128]{1,0:T(8,128)S(1)}) custom-call(f32[384,384]{1,0:T(8,128)S(1)} %collective-permute-done.6.refs_0_, f32[384,384]{1,0:T(8,128)S(1)} %collective-permute-done.8.refs_1_, f32[384,384]{1,0:T(8,128)S(1)} %collective-permute-done.9.refs_2_, f32[384,384]{1,0:T(8,128)S(1)} %get-tuple-element.41.refs_3_.refs_1_.refs_2_, ...), custom_call_target="tpu_custom_call" | custom-call | flops 3057647616 | bytes 6488064 | tf_op jit(solution)/shard_map/pallas_call | solution.py:47
  92.1 3.7 %shard_map.98 = (f32[384,384]{1,0:T(8,128)S(1)}, f32[384,384]{1,0:T(8,128)S(1)}) custom-call(f32[384,384]{1,0:T(8,128)S(1)} %shard_map.91.refs_2_.refs_6_.refs_0_, f32[384,384]{1,0:T(8,128)S(1)} %collective-permute-done.4.refs_0_.refs_7_.refs_1_, f32[384,384]{1,0:T(8,128)S(1)} %get-tuple-element.41.refs_3_.refs_1_.refs_2_, ...), custom_call_target="tpu_custom_call" | custom-call | flops 2038431744 | bytes 4128768 | tf_op jit(solution)/shard_map/pallas_call | solution.py:47
  95.8 2.8 %shard_map.92 = (f32[384,128]{1,0:T(8,128)S(1)}, f32[384,128]{1,0:T(8,128)S(1)}) custom-call(f32[384,384]{1,0:T(8,128)S(1)} %collective-permute-done.4.refs_0_.refs_7_.refs_1_, f32[384,128]{1,0:T(8,128)S(1)} %collective-permute-done.5.refs_1_.refs_8_, f32[384,384]{1,0:T(8,128)S(1)} %shard_map.91.refs_2_.refs_6_.refs_0_, ...), custom_call_target="tpu_custom_call" | custom-call | flops 679477248 | bytes 3538944 | tf_op jit(solution)/shard_map/pallas_call | solution.py:47
  98.6 1.3 %collective-permute-start.10 = (f32[384,128]{1,0:T(8,128)S(1)}, f32[384,128]{1,0:T(8,128)S(1)}, u32[]{:S(2)}, u32[]{:S(2)}) collective-permute-start(f32[384,128]{1,0:T(8,128)S(1)} %get-tuple-element.45), channel_id=1, source_target_pairs={{8,16},{9,17},{10,18},{11,19},{12,20},{13,21},{14,22},{15,23}} | collective-permute-start | bytes 589832 | tf_op jit(solution)/shard_map/ppermute | solution.py:68
  99.9 2.6 %shard_map.99 = (f32[384,128]{1,0:T(8,128)S(1)}, f32[384,128]{1,0:T(8,128)S(1)}) custom-call(f32[384,384]{1,0:T(8,128)S(1)} %collective-permute-done.6.refs_0_, f32[384,384]{1,0:T(8,128)S(1)} %collective-permute-done.8.refs_1_, f32[384,384]{1,0:T(8,128)S(1)} %collective-permute-done.14.refs_2_, f32[384,384]{1,0:T(8,128)S(1)} %get-tuple-element.51.refs_3_, ...), custom_call_target="tpu_custom_call" | custom-call | flops 1019215872 | bytes 4128768 | tf_op jit(solution)/shard_map/pallas_call | solution.py:47
  102.6 1.3 %collective-permute-start.15 = (f32[384,128]{1,0:T(8,128)S(1)}, f32[384,128]{1,0:T(8,128)S(1)}, u32[]{:S(2)}, u32[]{:S(2)}) collective-permute-start(f32[384,128]{1,0:T(8,128)S(1)} %get-tuple-element.52), channel_id=1, source_target_pairs={{8,24},{9,25},{10,26},{11,27},{12,28},{13,29},{14,30},{15,31}} | collective-permute-start | bytes 589832 | tf_op jit(solution)/shard_map/ppermute | solution.py:68
  103.9 1.7 %shard_map.101 = (f32[384,128]{1,0:T(8,128)S(1)}, f32[384,128]{1,0:T(8,128)}, f32[384,128]{1,0:T(8,128)}) custom-call(f32[384,128]{1,0:T(8,128)S(1)} %collective-permute-done.16.refs_0_, f32[384,384]{1,0:T(8,128)S(1)} %collective-permute-done.17.refs_1_, f32[384,128]{1,0:T(8,128)S(1)} %get-tuple-element.54.refs_2_, ...), custom_call_target="tpu_custom_call" | custom-call | flops 679477248 | bytes 5308416 | tf_op jit(solution)/shard_map/pallas_call | solution.py:47
  105.6 2.0 %collective-permute-start.18 = (f32[384,128]{1,0:T(8,128)}, f32[384,128]{1,0:T(8,128)}, u32[]{:S(2)}, u32[]{:S(2)}) collective-permute-start(f32[384,128]{1,0:T(8,128)} %get-tuple-element.59), channel_id=1, source_target_pairs={{8,16},{9,17},{10,18},{11,19},{12,20},{13,21},{14,22},{15,23}} | collective-permute-start | bytes 589832 | tf_op jit(solution)/shard_map/ppermute | solution.py:68
  107.6 0.8 copy-done.9
  108.4 2.0 %collective-permute-start.19 = (f32[384,128]{1,0:T(8,128)}, f32[384,128]{1,0:T(8,128)}, u32[]{:S(2)}, u32[]{:S(2)}) collective-permute-start(f32[384,128]{1,0:T(8,128)} %get-tuple-element.60), channel_id=1, source_target_pairs={{8,24},{9,25},{10,26},{11,27},{12,28},{13,29},{14,30},{15,31}} | collective-permute-start | bytes 589832 | tf_op jit(solution)/shard_map/ppermute | solution.py:68
  110.4 1.2 copy-done.10
  111.6 1.1 shard_map.97.refs_4_
  112.7 0.7 shard_map.100
  113.4 1.9 %collective-permute-start.20 = (f32[384,128]{1,0:T(8,128)}, f32[384,128]{1,0:T(8,128)S(1)}, u32[]{:S(2)}, u32[]{:S(2)}) collective-permute-start(f32[384,128]{1,0:T(8,128)} %shard_map.100), channel_id=1, source_target_pairs={{0,1},{1,2},{2,3},{3,4},{4,5},{5,6},{6,7},{7,8},{8,9},{9,10},{10,1... | collective-permute-start | bytes 589832 | tf_op jit(solution)/shard_map/ppermute | solution.py:281
  115.3 1.7 %select_bitcast_fusion = f32[1,384,128]{2,1,0:T(8,128)} fusion(f32[384,128]{1,0:T(8,128)S(1)} %get-tuple-element.53, f32[384,128]{1,0:T(8,128)S(1)} %get-tuple-element.58, f32[384,128]{1,0:T(8,128)} %collective-permute-done.18, f32[384,128]{1,0:T(8,128)} %collective-permute-done.19, pred[]{:T(512)S(6)} %lt.11, pred[]{:T(512)S(6)} %lt.10, pred[]{:T(512)S(6)} %lt.9), kind=kLoop, calls=%fused_computation | loop fusion | flops 147456 | bytes 983043 | tf_op jit(solution)/shard_map/broadcast_in_dim | solution.py:297
  116.9 4.5 %collective-permute-done.20.refs_1_ = f32[384,128]{1,0:T(8,128)S(1)} collective-permute-done((f32[384,128]{1,0:T(8,128)}, f32[384,128]{1,0:T(8,128)S(1)}, u32[]{:S(2)}, u32[]{:S(2)}) %collective-permute-start.20) | collective-permute-done | bytes 196640 | tf_op jit(solution)/shard_map/ppermute | solution.py:281
  121.4 2.0 %shard_map.102 = f32[4,384,128]{2,1,0:T(8,128)} custom-call(f32[4,384,384]{2,1,0:T(8,128)S(1)} %bitcast.9, f32[384,128]{1,0:T(8,128)S(1)} %collective-permute-done.20.refs_1_, f32[384,128]{1,0:T(8,128)S(1)} %copy-done.1), custom_call_target="tpu_custom_call" | custom-call | flops 384 | bytes 256 | tf_op jit(solution)/shard_map/pallas_call | solution.py:47
  (35 shorter events, 0.3 us)
Async XLA Ops:
  0.6 8.6 %collective-permute-start = (f32[384,384]{1,0:T(8,128)}, f32[384,384]{1,0:T(8,128)S(1)}, u32[]{:S(2)}, u32[]{:S(2)}) collective-permute-start(f32[384,384]{1,0:T(8,128)} %bitcast.16), channel_id=1, source_target_pairs={{28,24},{29,25},{30,26},{31,27},{24,28},{25,29},{26,30},{27,31},{4... | collective-permute-start | bytes 1769480 | tf_op jit(solution)/shard_map/ppermute | solution.py:68
  1.3 18.3 %collective-permute-start.2 = (f32[384,384]{1,0:T(8,128)}, f32[384,384]{1,0:T(8,128)S(1)}, u32[]{:S(2)}, u32[]{:S(2)}) collective-permute-start(f32[384,384]{1,0:T(8,128)} %bitcast.10), channel_id=1, source_target_pairs={{0,4},{1,5},{2,6},{3,7},{4,8},{5,9},{6,10},{7,11},{8,12},{9,13},{1... | collective-permute-start | bytes 1769480 | tf_op jit(solution)/shard_map/ppermute | solution.py:68
  4.8 1.1 copy-start.2
  5.8 1.1 copy-start.3
  6.9 1.1 copy-start.5
  8.0 1.1 copy-start.7
  9.2 1.1 copy-start.4
  9.2 4.5 %copy-start.6 = (f32[1,384,384]{2,1,0:T(8,128)S(1)}, f32[1,384,384]{2,1,0:T(8,128)}, u32[]{:S(2)}) copy-start(f32[1,384,384]{2,1,0:T(8,128)} %param.9) | copy-start | bytes 1769476
  9.2 6.4 %copy-start.8 = (f32[1,384,384]{2,1,0:T(8,128)S(1)}, f32[1,384,384]{2,1,0:T(8,128)}, u32[]{:S(2)}) copy-start(f32[1,384,384]{2,1,0:T(8,128)} %param.6) | copy-start | bytes 1769476
  9.3 16.2 %collective-permute-start.7 = (f32[384,384]{1,0:T(8,128)S(1)}, f32[384,384]{1,0:T(8,128)S(1)}, u32[]{:S(2)}, u32[]{:S(2)}) collective-permute-start(f32[384,384]{1,0:T(8,128)S(1)} %get-tuple-element.42), channel_id=1, source_target_pairs={{24,28},{25,29},{26,30},{27,31},{28,20},{29,21},{30,22},{31,23},{0... | collective-permute-start | bytes 1769480 | tf_op jit(solution)/shard_map/ppermute | solution.py:68
  10.3 34.6 %collective-permute-start.3 = (f32[384,384]{1,0:T(8,128)S(1)}, f32[384,384]{1,0:T(8,128)S(1)}, u32[]{:S(2)}, u32[]{:S(2)}) collective-permute-start(f32[384,384]{1,0:T(8,128)S(1)} %bitcast.13), channel_id=1, source_target_pairs={{0,4},{1,5},{2,6},{3,7},{4,8},{5,9},{6,10},{7,11},{8,12},{9,13},{1... | collective-permute-start | bytes 1769480 | tf_op jit(solution)/shard_map/ppermute | solution.py:68
  13.7 43.8 %collective-permute-start.1 = (f32[384,384]{1,0:T(8,128)S(1)}, f32[384,384]{1,0:T(8,128)S(1)}, u32[]{:S(2)}, u32[]{:S(2)}) collective-permute-start(f32[384,384]{1,0:T(8,128)S(1)} %bitcast.15), channel_id=1, source_target_pairs={{0,4},{1,5},{2,6},{3,7},{4,8},{5,9},{6,10},{7,11},{8,12},{9,13},{1... | collective-permute-start | bytes 1769480 | tf_op jit(solution)/shard_map/ppermute | solution.py:68
  15.6 54.8 %collective-permute-start.8 = (f32[384,384]{1,0:T(8,128)S(1)}, f32[384,384]{1,0:T(8,128)S(1)}, u32[]{:S(2)}, u32[]{:S(2)}) collective-permute-start(f32[384,384]{1,0:T(8,128)S(1)} %bitcast.18), channel_id=1, source_target_pairs={{16,12},{17,13},{18,14},{19,15}} | collective-permute-start | bytes 1769480 | tf_op jit(solution)/shard_map/ppermute | solution.py:68
  19.6 49.4 %collective-permute-start.6 = (f32[384,384]{1,0:T(8,128)S(1)}, f32[384,384]{1,0:T(8,128)S(1)}, u32[]{:S(2)}, u32[]{:S(2)}) collective-permute-start(f32[384,384]{1,0:T(8,128)S(1)} %bitcast.19), channel_id=1, source_target_pairs={{8,12},{9,13},{10,14},{11,15},{12,8},{13,9},{14,10},{15,11}} | collective-permute-start | bytes 1769480 | tf_op jit(solution)/shard_map/ppermute | solution.py:68
  25.6 35.7 %collective-permute-start.12 = (f32[384,384]{1,0:T(8,128)S(1)}, f32[384,384]{1,0:T(8,128)S(1)}, u32[]{:S(2)}, u32[]{:S(2)}) collective-permute-start(f32[384,384]{1,0:T(8,128)S(1)} %get-tuple-element.48), channel_id=1, source_target_pairs={{20,16},{21,17},{22,18},{23,19},{28,20},{29,21},{30,22},{31,23}} | collective-permute-start | bytes 1769480 | tf_op jit(solution)/shard_map/ppermute | solution.py:68
  48.4 12.9 %copy-start.1 = (f32[384,128]{1,0:T(8,128)S(1)}, f32[384,128]{1,0:T(8,128)}, u32[]{:S(2)}) copy-start(f32[384,128]{1,0:T(8,128)} %refs_2_.1) | copy-start | bytes 589828
  58.7 24.9 %collective-permute-start.9 = (f32[384,384]{1,0:T(8,128)S(1)}, f32[384,384]{1,0:T(8,128)S(1)}, u32[]{:S(2)}, u32[]{:S(2)}) collective-permute-start(f32[384,384]{1,0:T(8,128)S(1)} %get-tuple-element.38.refs_2_.refs_0_.refs_4_), channel_id=1, source_target_pairs={{16,8},{17,9},{18,10},{19,11},{20,12},{21,13},{22,14},{23,15}} | collective-permute-start | bytes 1769480 | tf_op jit(solution)/shard_map/ppermute | solution.py:68
  60.0 24.3 %collective-permute-start.4 = (f32[384,384]{1,0:T(8,128)S(1)}, f32[384,384]{1,0:T(8,128)S(1)}, u32[]{:S(2)}, u32[]{:S(2)}) collective-permute-start(f32[384,384]{1,0:T(8,128)S(1)} %get-tuple-element.41.refs_3_.refs_1_.refs_2_), channel_id=1, source_target_pairs={{0,8},{1,9},{2,10},{3,11},{4,12},{5,13},{6,14},{7,15}} | collective-permute-start | bytes 1769480 | tf_op jit(solution)/shard_map/ppermute | solution.py:68
  61.4 20.9 %collective-permute-start.5 = (f32[384,128]{1,0:T(8,128)S(1)}, f32[384,128]{1,0:T(8,128)S(1)}, u32[]{:S(2)}, u32[]{:S(2)}) collective-permute-start(f32[384,128]{1,0:T(8,128)S(1)} %get-tuple-element.40.refs_0_), channel_id=1, source_target_pairs={{0,8},{1,9},{2,10},{3,11},{4,12},{5,13},{6,14},{7,15}} | collective-permute-start | bytes 589832 | tf_op jit(solution)/shard_map/ppermute | solution.py:68
  69.1 29.5 %collective-permute-start.14 = (f32[384,384]{1,0:T(8,128)S(1)}, f32[384,384]{1,0:T(8,128)S(1)}, u32[]{:S(2)}, u32[]{:S(2)}) collective-permute-start(f32[384,384]{1,0:T(8,128)S(1)} %get-tuple-element.50), channel_id=1, source_target_pairs={{16,8},{17,9},{18,10},{19,11},{20,12},{21,13},{22,14},{23,15}} | collective-permute-start | bytes 1769480 | tf_op jit(solution)/shard_map/ppermute | solution.py:68
  70.5 33.4 %collective-permute-start.17 = (f32[384,384]{1,0:T(8,128)S(1)}, f32[384,384]{1,0:T(8,128)S(1)}, u32[]{:S(2)}, u32[]{:S(2)}) collective-permute-start(f32[384,384]{1,0:T(8,128)S(1)} %get-tuple-element.44.refs_5_.refs_3_.refs_4_), channel_id=1, source_target_pairs={{0,8},{1,9},{2,10},{3,11},{4,12},{5,13},{6,14},{7,15}} | collective-permute-start | bytes 1769480 | tf_op jit(solution)/shard_map/ppermute | solution.py:68
  82.3 20.2 %collective-permute-start.16 = (f32[384,128]{1,0:T(8,128)S(1)}, f32[384,128]{1,0:T(8,128)S(1)}, u32[]{:S(2)}, u32[]{:S(2)}) collective-permute-start(f32[384,128]{1,0:T(8,128)S(1)} %get-tuple-element.53), channel_id=1, source_target_pairs={{0,8},{1,9},{2,10},{3,11},{4,12},{5,13},{6,14},{7,15}} | collective-permute-start | bytes 589832 | tf_op jit(solution)/shard_map/ppermute | solution.py:68
  83.6 24.0 %collective-permute-start.11 = (f32[384,384]{1,0:T(8,128)S(1)}, f32[384,384]{1,0:T(8,128)S(1)}, u32[]{:S(2)}, u32[]{:S(2)}) collective-permute-start(f32[384,384]{1,0:T(8,128)S(1)} %get-tuple-element.47), channel_id=1, source_target_pairs={{20,24},{21,25},{22,26},{23,27},{24,28},{25,29},{26,30},{27,31}} | collective-permute-start | bytes 1769480 | tf_op jit(solution)/shard_map/ppermute | solution.py:68
  84.3 26.1 %collective-permute-start.13 = (f32[384,384]{1,0:T(8,128)S(1)}, f32[384,384]{1,0:T(8,128)}, u32[]{:S(2)}, u32[]{:S(2)}) collective-permute-start(f32[384,384]{1,0:T(8,128)S(1)} %get-tuple-element.49), channel_id=1, source_target_pairs={{16,24},{17,25},{18,26},{19,27},{20,28},{21,29},{22,30},{23,31}} | collective-permute-start | bytes 1769480 | tf_op jit(solution)/shard_map/ppermute | solution.py:68
  98.6 14.1 %collective-permute-start.10 = (f32[384,128]{1,0:T(8,128)S(1)}, f32[384,128]{1,0:T(8,128)S(1)}, u32[]{:S(2)}, u32[]{:S(2)}) collective-permute-start(f32[384,128]{1,0:T(8,128)S(1)} %get-tuple-element.45), channel_id=1, source_target_pairs={{8,16},{9,17},{10,18},{11,19},{12,20},{13,21},{14,22},{15,23}} | collective-permute-start | bytes 589832 | tf_op jit(solution)/shard_map/ppermute | solution.py:68
  102.6 10.1 %collective-permute-start.15 = (f32[384,128]{1,0:T(8,128)S(1)}, f32[384,128]{1,0:T(8,128)S(1)}, u32[]{:S(2)}, u32[]{:S(2)}) collective-permute-start(f32[384,128]{1,0:T(8,128)S(1)} %get-tuple-element.52), channel_id=1, source_target_pairs={{8,24},{9,25},{10,26},{11,27},{12,28},{13,29},{14,30},{15,31}} | collective-permute-start | bytes 589832 | tf_op jit(solution)/shard_map/ppermute | solution.py:68
  105.6 9.7 %collective-permute-start.18 = (f32[384,128]{1,0:T(8,128)}, f32[384,128]{1,0:T(8,128)}, u32[]{:S(2)}, u32[]{:S(2)}) collective-permute-start(f32[384,128]{1,0:T(8,128)} %get-tuple-element.59), channel_id=1, source_target_pairs={{8,16},{9,17},{10,18},{11,19},{12,20},{13,21},{14,22},{15,23}} | collective-permute-start | bytes 589832 | tf_op jit(solution)/shard_map/ppermute | solution.py:68
  107.6 0.8 copy-start.9
  108.4 6.9 %collective-permute-start.19 = (f32[384,128]{1,0:T(8,128)}, f32[384,128]{1,0:T(8,128)}, u32[]{:S(2)}, u32[]{:S(2)}) collective-permute-start(f32[384,128]{1,0:T(8,128)} %get-tuple-element.60), channel_id=1, source_target_pairs={{8,24},{9,25},{10,26},{11,27},{12,28},{13,29},{14,30},{15,31}} | collective-permute-start | bytes 589832 | tf_op jit(solution)/shard_map/ppermute | solution.py:68
  110.4 11.1 %copy-start = (f32[1,4,384,384]{3,2,1,0:T(8,128)S(1)}, f32[1,4,384,384]{3,2,1,0:T(8,128)}, u32[]{:S(2)}) copy-start(f32[1,4,384,384]{3,2,1,0:T(8,128)} %param.10) | copy-start | bytes 7077892
  110.4 1.2 copy-start.10
  113.4 8.1 %collective-permute-start.20 = (f32[384,128]{1,0:T(8,128)}, f32[384,128]{1,0:T(8,128)S(1)}, u32[]{:S(2)}, u32[]{:S(2)}) collective-permute-start(f32[384,128]{1,0:T(8,128)} %shard_map.100), channel_id=1, source_target_pairs={{0,1},{1,2},{2,3},{3,4},{4,5},{5,6},{6,7},{7,8},{8,9},{9,10},{10,1... | collective-permute-start | bytes 589832 | tf_op jit(solution)/shard_map/ppermute | solution.py:281

commit v3 on v2

--- a/solution.py
+++ b/solution.py
@@ -29,12 +29,13 @@
     return jnp.dot(left(former), right(latter), preferred_element_type=F32)
 
 
-def summed(bounce, value):
+def summed(bounce, value, rolled=False):
     factor = left(bounce)
-    total = value
-    for _ in range(3):
-        total = value + jnp.dot(factor, right(total), preferred_element_type=F32)
-    return total
+
+    def step(_, total):
+        return value + jnp.dot(factor, right(total), preferred_element_type=F32)
+
+    return lax.fori_loop(0, 3, step, value, unroll=not rolled)
 
 
 def staged(body, stride, inputs, outputs, products):
@@ -68,20 +69,33 @@
         return lax.ppermute(value, "sec", pairs)
 
     r, t, q, u = front_reflect[0], front_through[0], back_reflect[0], back_through[0]
-    onward = [(0, 1), (1, 2), (2, 3), (3, 4), (4, 5)]
+    width = field[1]
+    fields = (field[0], 2 * width)
     low = [(0, 2), (1, 3)]
     back = [(4, 2), (5, 3)]
-
-    q0 = moved(q, onward)
-    swapped = moved(r, [(7, 6), (6, 7), (1, 0), (0, 1)])
-    t0 = moved(t, onward)
-    u0 = moved(u, onward)
-
-    def load(k, *refs):
-        for i in range(4):
-            refs[4 + i][...] = refs[i][...]
-
-    r_in, (r, t, q, u) = r, staged(load, stride, [r, t, q, u], [square] * 4, 0.1)
+    middle = [(2, 3), (3, 4), (4, 5)]
+
+    swapped = moved(r, [(7, 6), (6, 7), (1, 0)])
+    r2_down = moved(r, [(2, 0)])
+    q0 = moved(q, [(0, 1), (1, 2)] + middle)
+    t0 = moved(t, [(1, 2)] + middle)
+    u1_over = moved(u, [(1, 0)])
+    u0 = moved(u, [(0, 1)] + middle)
+    r_late = moved(r, [(3, 2)])
+    r_next = moved(r, [(4, 3)])
+
+    def load(k, r, t, q, u, incident, *out):
+        for i, ref in enumerate((r, t, q, u)):
+            out[i][...] = ref[...]
+
+        @pl.when(k == 0)
+        def _():
+            value = right(incident[...])
+            out[4][:, :width] = jnp.dot(left(t[...]), value, preferred_element_type=F32)
+            out[4][:, width:] = jnp.dot(left(r[...]), value, preferred_element_type=F32)
+
+    r, t, q, u, first = staged(load, stride, [r, t, q, u, incident], [square] * 4 + [fields], 1)
+    first_came = moved(first, [(0, 1)])
 
     def pair_reflect(at):
         def body(k, came, r, t, q, u, *rest):
@@ -89,7 +103,7 @@
 
             @pl.when(k == at)
             def _():
-                gt = summed(product(q[...], came[...]), t[...])
+                gt = summed(product(q[...], came[...]), t[...], True)
                 gt_out[...] = gt
                 out[...] = r[...] + product(u[...], product(came[...], gt))
 
@@ -103,6 +117,9 @@
 
     (relay, gt) = staged(pair_reflect(6), stride, [swapped, r, t, q, u], [square] * 2, 6)
     hopped = moved(relay, [(6, 7), (7, 5), (0, 2)])
+    r2_over = moved(r2_down, [(0, 1)])
+    u1_up = moved(u1_over, [(0, 2)])
+    r2_up = moved(r2_over, [(1, 3)])
 
     def forward_q(k, q0, r, t, q, u, q1, hu_out):
         @pl.when(k == 0)
@@ -111,7 +128,7 @@
 
         @pl.when((k > 0) & (k < 6))
         def _():
-            hu = summed(product(r[...], q0[...]), u[...])
+            hu = summed(product(r[...], q0[...]), u[...], True)
             hu_out[...] = hu
             q1[...] = q[...] + product(t[...], product(q0[...], hu))
 
@@ -120,13 +137,9 @@
 
 
     def forward_t(k, q0, t0, r, t, t1, rgt):
-        @pl.when(k == 0)
-        def _():
-            t1[...] = t[...]
-
-        @pl.when((k > 0) & (k < 6))
-        def _():
-            gt = summed(product(q0[...], r[...]), t0[...])
+        @pl.when((k > 1) & (k < 6))
+        def _():
+            gt = summed(product(q0[...], r[...]), t0[...], True)
             rgt[...] = product(r[...], gt)
             t1[...] = product(t[...], gt)
 
@@ -135,36 +148,38 @@
     (relay, gt) = staged(pair_reflect(5), stride, [hopped, r, t, q, u, gt], [square] * 2, 6)
     bounced = moved(relay, [(5, 4), (7, 5)])
     gt_came = moved(gt, [(5, 6), (6, 7)])
-    r_late = moved(r_in, [(2, 3), (3, 2)])
-    r_next = moved(r_in, [(4, 3)])
-
-    def forward_u(k, u0, u, hu, rgt, u1, w):
+
+    def forward_u(k, u0, u1_up, u, hu, rgt, u1, w):
         @pl.when(k == 0)
         def _():
             u1[...] = u[...]
 
         @pl.when((k > 0) & (k < 6))
         def _():
-            factor = left(u0[...])
-            w[...] = jnp.dot(factor, right(rgt[...]), preferred_element_type=F32)
+            factor = left(jnp.where(k == 2, u1_up[...], u0[...]))
             u1[...] = jnp.dot(factor, right(hu[...]), preferred_element_type=F32)
 
-    (u1, w) = staged(forward_u, stride, [u0, u, hu, rgt], [square] * 2, 2)
+            @pl.when(k > 1)
+            def _():
+                w[...] = jnp.dot(factor, right(rgt[...]), preferred_element_type=F32)
+
+    (u1, w) = staged(forward_u, stride, [u0, u1_up, u, hu, rgt], [square] * 2, 2)
     w_came = moved(w, back)
     ua = moved(u1, low)
 
-    def low_fields(k, swapped, r, w, t1, incident, f1, s1):
-        @pl.when(k < 2)
-        def _():
-            whole = jnp.where(k == 0, r[...], swapped[...] + w[...])
-            value = right(incident[...])
-            f1[...] = jnp.dot(left(t1[...]), value, preferred_element_type=F32)
-            s1[...] = jnp.dot(left(whole), value, preferred_element_type=F32)
-
-    (f1, s1) = staged(low_fields, stride, [swapped, r, w, t1, incident], [field, field], 1
-    )
-    fa = moved(f1, low)
-    sa = moved(s1, low)
+    def low_fields(k, first, came, q0, r, t, u0, out):
+        @pl.when(k == 0)
+        def _():
+            out[...] = first[...]
+
+        @pl.when(k == 1)
+        def _():
+            g = summed(product(q0[...], r[...]), came[:, :width], True)
+            out[:, :width] = product(t[...], g)
+            out[:, width:] = came[:, width:] + product(u0[...], product(r[...], g))
+
+    (first,) = staged(low_fields, stride, [first, first_came, q0, r, t, u0], [fields], 2)
+    fa = moved(first, low)
 
     def open_gate(k, w, out):
         out[...] = w[:8, :128]
@@ -183,21 +198,21 @@
     total_came = moved(total, back)
     gt2_came = moved(gt2, [(4, 6), (5, 7)])
 
-    def own_fields(k, r_late, hopped, w, r1):
+    def own_fields(k, r2_up, hopped, w, r1):
         @pl.when(k == 2)
         def _():
             r1[...] = hopped[...] + w[...]
 
         @pl.when(k == 3)
         def _():
-            r1[...] = r_late[...] + w[...]
-
-    (r1,) = staged(own_fields, stride, [r_late, hopped, w], [square], 0.1)
+            r1[...] = r2_up[...] + w[...]
+
+    (r1,) = staged(own_fields, stride, [r2_up, hopped, w], [square], 0.1)
 
     def second_q(k, r1, qa, q1, t1, u1, q2, hu_out):
         @pl.when((k == 2) | (k == 3))
         def _():
-            hu = summed(product(r1[...], qa[...]), u1[...])
+            hu = summed(product(r1[...], qa[...]), u1[...], True)
             hu_out[...] = hu
             q2[...] = q1[...] + product(t1[...], product(qa[...], hu))
 
@@ -206,7 +221,7 @@
     def second_fields(k, qa, fa, r1, t1, f2, rg2):
         @pl.when((k == 2) | (k == 3))
         def _():
-            g = summed(product(qa[...], r1[...]), fa[...])
+            g = summed(product(qa[...], r1[...]), fa[:, :width])
             f2[...] = product(t1[...], g)
             rg2[...] = product(r1[...], g)
 
@@ -218,7 +233,7 @@
             came = jnp.where(k == 2, r_late[...], r_next[...]) + w_came[...]
             gt = summed(product(q1[...], came), t1[...])
             rc = r1[...] + product(u1[...], product(came, gt))
-            g = summed(product(qa[...], rc), fa[...])
+            g = summed(product(qa[...], rc), fa[:, :width])
             w4[...] = product(gt, g)
             rg4[...] = product(rc, g)
 
@@ -246,23 +261,22 @@
     )
     g6_came = moved(g6, [(2, 6), (3, 7)])
 
-    def all_reflected(k, sa, ua, rg2, rg4, rg6, hu2, s2, s4, s6):
+    def all_reflected(k, fa, ua, rg2, rg4, rg6, hu2, s2, s4, s6):
         @pl.when((k == 2) | (k == 3))
         def _():
             sums = rg2[...] + product(hu2[...], rg6[...])
             value = product(ua[...], jnp.concatenate([rg2[...], rg4[...], sums], axis=1))
-            width = sa.shape[1]
             for i, out in enumerate((s2, s4, s6)):
-                out[...] = sa[...] + value[:, i * width : (i + 1) * width]
-
-    (s2, s4, s6) = staged(all_reflected, stride, [sa, ua, rg2, rg4, rg6, hu2], [field] * 3, 2)
+                out[...] = fa[:, width:] + value[:, i * width : (i + 1) * width]
+
+    (s2, s4, s6) = staged(all_reflected, stride, [fa, ua, rg2, rg4, rg6, hu2], [field] * 3, 2)
     s6_came = moved(s6, [(2, 6), (3, 7)])
     s4_came = moved(s4, [(2, 4), (3, 5)])
 
-    def through(k, f1, f2, t1, w4, t2, g6, out):
+    def through(k, first, f2, t1, w4, t2, g6, out):
         @pl.when(k < 2)
         def _():
-            out[...] = f1[...]
+            out[...] = first[:, :width]
 
         @pl.when((k == 2) | (k == 3))
         def _():
@@ -276,11 +290,11 @@
         def _():
             out[...] = product(t2[...], g6[...])
 
-    (through_field,) = staged(through, stride, [f1, f2, t1, w4_came, t2, g6_came], [field], 1
+    (through_field,) = staged(through, stride, [first, f2, t1, w4_came, t2, g6_came], [field], 1
     )
     entering = lax.ppermute(through_field, "sec", [(i, i + 1) for i in range(length - 1)])
     reflected = jnp.where(
-        k < 2, s1, jnp.where(k < 4, s2, jnp.where(k < 6, s4_came, s6_came))
+        k < 2, first[:, width:], jnp.where(k < 4, s2, jnp.where(k < 6, s4_came, s6_came))
     )
 
     def depths(place, maps, entering, incident, out):

time: 124 us -> 134 us (1.081)
  the two profiles are of different devices: /device:TPU:12 before, /device:TPU:28 now
where the time goes in v3:
time: 134 us; the launch traced here: 133 us
  waiting for transfers between devices  83.1 us (62%)
  starting transfers between devices  33.1 us (25%)
  Pallas kernels  8.38 us (6%)
  local copies, waits for them, and re-layouts  5.2 us (4%)
  other arithmetic  1.64 us (1%)
    ppermute x25, waiting for transfers between devices, moved(): return lax.ppermute(value, 'sec', pairs)  81 us
    ppermute x25, starting transfers between devices, moved(): return lax.ppermute(value, 'sec', pairs)  31.2 us
    pallas_call x18, Pallas kernels, staged(): pl.pallas_call(kernel, out_shape=[jax.ShapeDtypeStruct(shape, F32) for sh...  8.38 us
    unnamed x20, local copies, waits for them, and re-layouts  5.2 us
  transfers between devices with their start and end apart: 26, of which 8 were waited for; matrix products, arithmetic and copies ran while one was open for 1% of the time, Pallas kernels for 5%

profile of v3, /device:TPU:28, one launch (start us, length us, event | category | flops | bytes accessed | tf_op | source)
XLA Modules:
  0.0 132.6 jit_solution(11219995538004045513)
XLA Ops:
  0.6 2.4 %collective-permute-start.8 = (f32[384,384]{1,0:T(8,128)}, f32[384,384]{1,0:T(8,128)S(1)}, u32[]{:S(2)}, u32[]{:S(2)}) collective-permute-start(f32[384,384]{1,0:T(8,128)} %bitcast.17), channel_id=1, source_target_pairs={{28,24},{29,25},{30,26},{31,27},{24,28},{25,29},{26,30},{27,31},{4... | collective-permute-start | bytes 1769480 | tf_op jit(solution)/shard_map/ppermute | solution.py:69
  3.1 0.7 collective-permute-start.1
  3.8 0.7 collective-permute-start.5
  4.5 0.7 collective-permute-start.10
  5.2 0.9 copy-done.1
  6.1 1.1 copy-done.3
  7.2 1.1 copy-done.4
  8.2 1.1 copy-done.6
  9.3 1.1 copy-done.8
  10.5 7.3 %collective-permute-done.8.refs_0_ = f32[384,384]{1,0:T(8,128)S(1)} collective-permute-done((f32[384,384]{1,0:T(8,128)}, f32[384,384]{1,0:T(8,128)S(1)}, u32[]{:S(2)}, u32[]{:S(2)}) %collective-permute-start.8) | collective-permute-done | bytes 589856 | tf_op jit(solution)/shard_map/ppermute | solution.py:69
  17.9 2.1 %collective-permute-start.9 = (f32[384,384]{1,0:T(8,128)S(1)}, f32[384,384]{1,0:T(8,128)S(1)}, u32[]{:S(2)}, u32[]{:S(2)}) collective-permute-start(f32[384,384]{1,0:T(8,128)S(1)} %get-tuple-element.37), channel_id=1, source_target_pairs={{24,28},{25,29},{26,30},{27,31},{28,20},{29,21},{30,22},{31,23},{0... | collective-permute-start | bytes 1769480 | tf_op jit(solution)/shard_map/ppermute | solution.py:69
  19.9 0.7 collective-permute-start.12
  20.7 0.7 collective-permute-start.2
  21.4 0.7 collective-permute-start.11
  22.1 0.7 collective-permute-start.6
  22.8 13.4 %collective-permute-done.9.refs_1_.refs_0_ = f32[384,384]{1,0:T(8,128)S(1)} collective-permute-done((f32[384,384]{1,0:T(8,128)S(1)}, f32[384,384]{1,0:T(8,128)S(1)}, u32[]{:S(2)}, u32[]{:S(2)}) %collective-permute-start.9) | collective-permute-done | bytes 589856 | tf_op jit(solution)/shard_map/ppermute | solution.py:69
  36.1 0.7 collective-permute-start.13
  37.0 0.7 collective-permute-start
  37.7 8.5 %collective-permute-start.18 = (f32[384,384]{1,0:T(8,128)S(1)}, f32[384,384]{1,0:T(8,128)S(1)}, u32[]{:S(2)}, u32[]{:S(2)}) collective-permute-start(f32[384,384]{1,0:T(8,128)S(1)} %get-tuple-element.47), channel_id=1, source_target_pairs={{20,16},{21,17},{22,18},{23,19},{28,20},{29,21},{30,22},{31,23}} | collective-permute-start | bytes 1769480 | tf_op jit(solution)/shard_map/ppermute | solution.py:69
  46.2 0.7 collective-permute-start.14
  47.0 0.7 collective-permute-start.7
  47.7 0.2 shard_map.90
  47.9 0.7 collective-permute-start.3
  48.6 0.7 collective-permute-start.15
  49.4 8.5 %collective-permute-done.18.refs_0_ = f32[384,384]{1,0:T(8,128)S(1)} collective-permute-done((f32[384,384]{1,0:T(8,128)S(1)}, f32[384,384]{1,0:T(8,128)S(1)}, u32[]{:S(2)}, u32[]{:S(2)}) %collective-permute-start.18) | collective-permute-done | bytes 589856 | tf_op jit(solution)/shard_map/ppermute | solution.py:69
  57.9 0.7 collective-permute-start.4
  58.6 0.7 collective-permute-start.20
  59.3 0.7 collective-permute-start.22
  60.0 1.3 collective-permute-start.17
  61.4 1.3 collective-permute-start.19
  62.7 0.7 shard_map.93
  63.4 0.7 collective-permute-start.16
  64.0 0.2 shard_map.92
  64.3 0.7 shard_map.99
  65.0 1.3 collective-permute-start.21
  66.3 0.8 shard_map.101
  67.1 1.3 collective-permute-start.23
  68.4 6.9 %collective-permute-done.17.refs_1_ = f32[384,384]{1,0:T(8,128)S(1)} collective-permute-done((f32[384,384]{1,0:T(8,128)S(1)}, f32[384,384]{1,0:T(8,128)S(1)}, u32[]{:S(2)}, u32[]{:S(2)}) %collective-permute-start.17) | collective-permute-done | bytes 589856 | tf_op jit(solution)/shard_map/ppermute | solution.py:69
  75.3 1.3 collective-permute-start.24
  76.6 22.7 %collective-permute-done.19.refs_2_ = f32[384,384]{1,0:T(8,128)} collective-permute-done((f32[384,384]{1,0:T(8,128)S(1)}, f32[384,384]{1,0:T(8,128)}, u32[]{:S(2)}, u32[]{:S(2)}) %collective-permute-start.19) | collective-permute-done | bytes 589856 | tf_op jit(solution)/shard_map/ppermute | solution.py:69
  99.4 2.3 %shard_map.97.refs_4_ = f32[384,384]{1,0:T(8,128)S(1)} custom-call(f32[384,384]{1,0:T(8,128)S(1)} %get-tuple-element.33.refs_4_.refs_2_.refs_3_.refs_0_, f32[384,384]{1,0:T(8,128)S(1)} %collective-permute-done.17.refs_1_, f32[384,384]{1,0:T(8,128)} %collective-permute-done.19.refs_2_), custom_call_target="tpu_custom_call" | custom-call | flops 679477248 | bytes 2359296 | tf_op jit(solution)/shard_map/pallas_call | solution.py:48
  101.7 19.8 %collective-permute-done.21.refs_5_ = f32[384,128]{1,0:T(8,128)S(1)} collective-permute-done((f32[384,128]{1,0:T(8,128)}, f32[384,128]{1,0:T(8,128)S(1)}, u32[]{:S(2)}, u32[]{:S(2)}) %collective-permute-start.21) | collective-permute-done | bytes 196640 | tf_op jit(solution)/shard_map/ppermute | solution.py:69
  121.5 1.1 shard_map.100
  122.6 1.9 %collective-permute-start.25 = (f32[384,128]{1,0:T(8,128)}, f32[384,128]{1,0:T(8,128)S(1)}, u32[]{:S(2)}, u32[]{:S(2)}) collective-permute-start(f32[384,128]{1,0:T(8,128)} %shard_map.100), channel_id=1, source_target_pairs={{0,1},{1,2},{2,3},{3,4},{4,5},{5,6},{6,7},{7,8},{8,9},{9,10},{10,1... | collective-permute-start | bytes 589832 | tf_op jit(solution)/shard_map/ppermute | solution.py:295
  124.5 2.4 %collective-permute-done.24 = f32[384,128]{1,0:T(8,128)} collective-permute-done((f32[384,128]{1,0:T(8,128)}, f32[384,128]{1,0:T(8,128)}, u32[]{:S(2)}, u32[]{:S(2)}) %collective-permute-start.24) | collective-permute-done | bytes 196640 | tf_op jit(solution)/shard_map/ppermute | solution.py:69
  126.9 1.6 %fusion = f32[1,384,128]{2,1,0:T(8,128)} fusion(f32[384,256]{1,0:T(8,128)S(1)} %shard_map.86.refs_0_, f32[384,128]{1,0:T(8,128)S(1)} %get-tuple-element.56, f32[384,128]{1,0:T(8,128)} %collective-permute-done.23, f32[384,128]{1,0:T(8,128)} %collective-permute-done.24, pred[]{:T(512)S(6)} %lt.11, pred[]{:T(512)S(6)} %lt.10, pred[]{:T(512)S(6)} %lt.9), kind=kLoop, calls=%fused_computation.1 | loop fusion | flops 147456 | bytes 983043 | tf_op jit(solution)/shard_map/broadcast_in_dim | solution.py:311
  128.5 2.1 %collective-permute-done.25.refs_1_ = f32[384,128]{1,0:T(8,128)S(1)} collective-permute-done((f32[384,128]{1,0:T(8,128)}, f32[384,128]{1,0:T(8,128)S(1)}, u32[]{:S(2)}, u32[]{:S(2)}) %collective-permute-start.25) | collective-permute-done | bytes 196640 | tf_op jit(solution)/shard_map/ppermute | solution.py:295
  130.6 2.0 %shard_map.102 = f32[4,384,128]{2,1,0:T(8,128)} custom-call(f32[4,384,384]{2,1,0:T(8,128)S(1)} %bitcast.9, f32[384,128]{1,0:T(8,128)S(1)} %collective-permute-done.25.refs_1_, f32[384,128]{1,0:T(8,128)S(1)} %copy-done.2), custom_call_target="tpu_custom_call" | custom-call | flops 384 | bytes 256 | tf_op jit(solution)/shard_map/pallas_call | solution.py:48
  (43 shorter events, 0.5 us)
Async XLA Ops:
  0.6 17.2 %collective-permute-start.8 = (f32[384,384]{1,0:T(8,128)}, f32[384,384]{1,0:T(8,128)S(1)}, u32[]{:S(2)}, u32[]{:S(2)}) collective-permute-start(f32[384,384]{1,0:T(8,128)} %bitcast.17), channel_id=1, source_target_pairs={{28,24},{29,25},{30,26},{31,27},{24,28},{25,29},{26,30},{27,31},{4... | collective-permute-start | bytes 1769480 | tf_op jit(solution)/shard_map/ppermute | solution.py:69
  3.1 17.6 %collective-permute-start.1 = (f32[384,384]{1,0:T(8,128)}, f32[384,384]{1,0:T(8,128)S(1)}, u32[]{:S(2)}, u32[]{:S(2)}) collective-permute-start(f32[384,384]{1,0:T(8,128)} %bitcast.10), channel_id=1, source_target_pairs={{0,4},{1,5},{2,6},{3,7},{4,8},{5,9},{6,10},{7,11},{8,12},{9,13},{1... | collective-permute-start | bytes 1769480 | tf_op jit(solution)/shard_map/ppermute | solution.py:69
  3.8 18.3 %collective-permute-start.5 = (f32[384,384]{1,0:T(8,128)}, f32[384,384]{1,0:T(8,128)S(1)}, u32[]{:S(2)}, u32[]{:S(2)}) collective-permute-start(f32[384,384]{1,0:T(8,128)} %bitcast.18), channel_id=1, source_target_pairs={{8,0},{9,1},{10,2},{11,3}} | collective-permute-start | bytes 1769480 | tf_op jit(solution)/shard_map/ppermute | solution.py:69
  4.5 16.9 %collective-permute-start.10 = (f32[384,384]{1,0:T(8,128)}, f32[384,384]{1,0:T(8,128)S(1)}, u32[]{:S(2)}, u32[]{:S(2)}) collective-permute-start(f32[384,384]{1,0:T(8,128)} %bitcast.14), channel_id=1, source_target_pairs={{4,0},{5,1},{6,2},{7,3}} | collective-permute-start | bytes 1769480 | tf_op jit(solution)/shard_map/ppermute | solution.py:69
  5.2 0.9 copy-start.1
  6.1 1.1 copy-start.3
  7.2 1.1 copy-start.4
  8.2 1.1 copy-start.6
  9.3 1.1 copy-start.8
  17.8 2.1 %copy-start.5 = (f32[1,384,384]{2,1,0:T(8,128)S(1)}, f32[1,384,384]{2,1,0:T(8,128)}, u32[]{:S(2)}) copy-start(f32[1,384,384]{2,1,0:T(8,128)} %param.7) | copy-start | bytes 1769476
  17.8 2.8 %copy-start.7 = (f32[1,384,384]{2,1,0:T(8,128)S(1)}, f32[1,384,384]{2,1,0:T(8,128)}, u32[]{:S(2)}) copy-start(f32[1,384,384]{2,1,0:T(8,128)} %param.9) | copy-start | bytes 1769476
  17.8 18.3 %copy-start.9 = (f32[1,384,384]{2,1,0:T(8,128)S(1)}, f32[1,384,384]{2,1,0:T(8,128)}, u32[]{:S(2)}) copy-start(f32[1,384,384]{2,1,0:T(8,128)} %param.6) | copy-start | bytes 1769476
  17.9 18.3 %collective-permute-start.9 = (f32[384,384]{1,0:T(8,128)S(1)}, f32[384,384]{1,0:T(8,128)S(1)}, u32[]{:S(2)}, u32[]{:S(2)}) collective-permute-start(f32[384,384]{1,0:T(8,128)S(1)} %get-tuple-element.37), channel_id=1, source_target_pairs={{24,28},{25,29},{26,30},{27,31},{28,20},{29,21},{30,22},{31,23},{0... | collective-permute-start | bytes 1769480 | tf_op jit(solution)/shard_map/ppermute | solution.py:69
  19.9 17.0 %collective-permute-start.12 = (f32[384,384]{1,0:T(8,128)S(1)}, f32[384,384]{1,0:T(8,128)S(1)}, u32[]{:S(2)}, u32[]{:S(2)}) collective-permute-start(f32[384,384]{1,0:T(8,128)S(1)} %bitcast.13), channel_id=1, source_target_pairs={{4,8},{5,9},{6,10},{7,11},{8,12},{9,13},{10,14},{11,15},{12,16},{1... | collective-permute-start | bytes 1769480 | tf_op jit(solution)/shard_map/ppermute | solution.py:69
  20.7 17.0 %collective-permute-start.2 = (f32[384,384]{1,0:T(8,128)S(1)}, f32[384,384]{1,0:T(8,128)S(1)}, u32[]{:S(2)}, u32[]{:S(2)}) collective-permute-start(f32[384,384]{1,0:T(8,128)S(1)} %bitcast.16), channel_id=1, source_target_pairs={{0,4},{1,5},{2,6},{3,7},{8,12},{9,13},{10,14},{11,15},{12,16},{13,... | collective-permute-start | bytes 1769480 | tf_op jit(solution)/shard_map/ppermute | solution.py:69
  21.4 24.9 %collective-permute-start.11 = (f32[384,384]{1,0:T(8,128)S(1)}, f32[384,384]{1,0:T(8,128)S(1)}, u32[]{:S(2)}, u32[]{:S(2)}) collective-permute-start(f32[384,384]{1,0:T(8,128)S(1)} %collective-permute-done.10), channel_id=1, source_target_pairs={{0,8},{1,9},{2,10},{3,11}} | collective-permute-start | bytes 1769480 | tf_op jit(solution)/shard_map/ppermute | solution.py:69
  22.1 24.9 %collective-permute-start.6 = (f32[384,384]{1,0:T(8,128)S(1)}, f32[384,384]{1,0:T(8,128)S(1)}, u32[]{:S(2)}, u32[]{:S(2)}) collective-permute-start(f32[384,384]{1,0:T(8,128)S(1)} %collective-permute-done.5), channel_id=1, source_target_pairs={{0,4},{1,5},{2,6},{3,7}} | collective-permute-start | bytes 1769480 | tf_op jit(solution)/shard_map/ppermute | solution.py:69
  36.1 12.5 %collective-permute-start.13 = (f32[384,384]{1,0:T(8,128)S(1)}, f32[384,384]{1,0:T(8,128)S(1)}, u32[]{:S(2)}, u32[]{:S(2)}) collective-permute-start(f32[384,384]{1,0:T(8,128)S(1)} %bitcast.20), channel_id=1, source_target_pairs={{12,8},{13,9},{14,10},{15,11}} | collective-permute-start | bytes 1769480 | tf_op jit(solution)/shard_map/ppermute | solution.py:69
  37.0 10.9 %collective-permute-start = (f32[384,256]{1,0:T(8,128)S(1)}, f32[384,256]{1,0:T(8,128)S(1)}, u32[]{:S(2)}, u32[]{:S(2)}) collective-permute-start(f32[384,256]{1,0:T(8,128)S(1)} %get-tuple-element.31.refs_0_), channel_id=1, source_target_pairs={{0,4},{1,5},{2,6},{3,7}} | collective-permute-start | bytes 1179656 | tf_op jit(solution)/shard_map/ppermute | solution.py:69
  37.7 20.2 %collective-permute-start.18 = (f32[384,384]{1,0:T(8,128)S(1)}, f32[384,384]{1,0:T(8,128)S(1)}, u32[]{:S(2)}, u32[]{:S(2)}) collective-permute-start(f32[384,384]{1,0:T(8,128)S(1)} %get-tuple-element.47), channel_id=1, source_target_pairs={{20,16},{21,17},{22,18},{23,19},{28,20},{29,21},{30,22},{31,23}} | collective-permute-start | bytes 1769480 | tf_op jit(solution)/shard_map/ppermute | solution.py:69
  46.2 13.1 %collective-permute-start.14 = (f32[384,384]{1,0:T(8,128)S(1)}, f32[384,384]{1,0:T(8,128)S(1)}, u32[]{:S(2)}, u32[]{:S(2)}) collective-permute-start(f32[384,384]{1,0:T(8,128)S(1)} %bitcast.21), channel_id=1, source_target_pairs={{16,12},{17,13},{18,14},{19,15}} | collective-permute-start | bytes 1769480 | tf_op jit(solution)/shard_map/ppermute | solution.py:69
  47.0 11.6 %collective-permute-start.7 = (f32[384,384]{1,0:T(8,128)S(1)}, f32[384,384]{1,0:T(8,128)S(1)}, u32[]{:S(2)}, u32[]{:S(2)}) collective-permute-start(f32[384,384]{1,0:T(8,128)S(1)} %collective-permute-done.6), channel_id=1, source_target_pairs={{4,12},{5,13},{6,14},{7,15}} | collective-permute-start | bytes 1769480 | tf_op jit(solution)/shard_map/ppermute | solution.py:69
  47.9 13.5 %collective-permute-start.3 = (f32[384,384]{1,0:T(8,128)S(1)}, f32[384,384]{1,0:T(8,128)S(1)}, u32[]{:S(2)}, u32[]{:S(2)}) collective-permute-start(f32[384,384]{1,0:T(8,128)S(1)} %get-tuple-element.36.refs_3_.refs_1_.refs_2_), channel_id=1, source_target_pairs={{0,8},{1,9},{2,10},{3,11},{4,12},{5,13},{6,14},{7,15}} | collective-permute-start | bytes 1769480 | tf_op jit(solution)/shard_map/ppermute | solution.py:69
  48.6 14.1 %collective-permute-start.15 = (f32[384,384]{1,0:T(8,128)S(1)}, f32[384,384]{1,0:T(8,128)S(1)}, u32[]{:S(2)}, u32[]{:S(2)}) collective-permute-start(f32[384,384]{1,0:T(8,128)S(1)} %get-tuple-element.40.refs_2_.refs_0_.refs_4_), channel_id=1, source_target_pairs={{16,8},{17,9},{18,10},{19,11},{20,12},{21,13},{22,14},{23,15}} | collective-permute-start | bytes 1769480 | tf_op jit(solution)/shard_map/ppermute | solution.py:69
  57.9 2.2 %collective-permute-start.4 = (f32[384,256]{1,0:T(8,128)S(1)}, f32[384,256]{1,0:T(8,128)S(1)}, u32[]{:S(2)}, u32[]{:S(2)}) collective-permute-start(f32[384,256]{1,0:T(8,128)S(1)} %shard_map.86.refs_0_), channel_id=1, source_target_pairs={{0,8},{1,9},{2,10},{3,11},{4,12},{5,13},{6,14},{7,15}} | collective-permute-start | bytes 1179656 | tf_op jit(solution)/shard_map/ppermute | solution.py:69
  58.6 5.7 %collective-permute-start.20 = (f32[384,384]{1,0:T(8,128)S(1)}, f32[384,384]{1,0:T(8,128)S(1)}, u32[]{:S(2)}, u32[]{:S(2)}) collective-permute-start(f32[384,384]{1,0:T(8,128)S(1)} %get-tuple-element.49), channel_id=1, source_target_pairs={{16,8},{17,9},{18,10},{19,11},{20,12},{21,13},{22,14},{23,15}} | collective-permute-start | bytes 1769480 | tf_op jit(solution)/shard_map/ppermute | solution.py:69
  59.3 7.0 %collective-permute-start.22 = (f32[384,384]{1,0:T(8,128)S(1)}, f32[384,384]{1,0:T(8,128)S(1)}, u32[]{:S(2)}, u32[]{:S(2)}) collective-permute-start(f32[384,384]{1,0:T(8,128)S(1)} %get-tuple-element.43.refs_5_.refs_3_.refs_4_), channel_id=1, source_target_pairs={{0,8},{1,9},{2,10},{3,11},{4,12},{5,13},{6,14},{7,15}} | collective-permute-start | bytes 1769480 | tf_op jit(solution)/shard_map/ppermute | solution.py:69
  60.0 15.3 %collective-permute-start.17 = (f32[384,384]{1,0:T(8,128)S(1)}, f32[384,384]{1,0:T(8,128)S(1)}, u32[]{:S(2)}, u32[]{:S(2)}) collective-permute-start(f32[384,384]{1,0:T(8,128)S(1)} %get-tuple-element.46), channel_id=1, source_target_pairs={{20,24},{21,25},{22,26},{23,27},{24,28},{25,29},{26,30},{27,31}} | collective-permute-start | bytes 1769480 | tf_op jit(solution)/shard_map/ppermute | solution.py:69
  61.4 38.0 %collective-permute-start.19 = (f32[384,384]{1,0:T(8,128)S(1)}, f32[384,384]{1,0:T(8,128)}, u32[]{:S(2)}, u32[]{:S(2)}) collective-permute-start(f32[384,384]{1,0:T(8,128)S(1)} %get-tuple-element.48), channel_id=1, source_target_pairs={{16,24},{17,25},{18,26},{19,27},{20,28},{21,29},{22,30},{23,31}} | collective-permute-start | bytes 1769480 | tf_op jit(solution)/shard_map/ppermute | solution.py:69
  63.4 38.3 %collective-permute-start.16 = (f32[384,128]{1,0:T(8,128)}, f32[384,128]{1,0:T(8,128)S(1)}, u32[]{:S(2)}, u32[]{:S(2)}) collective-permute-start(f32[384,128]{1,0:T(8,128)} %get-tuple-element.44), channel_id=1, source_target_pairs={{8,16},{9,17},{10,18},{11,19},{12,20},{13,21},{14,22},{15,23}} | collective-permute-start | bytes 589832 | tf_op jit(solution)/shard_map/ppermute | solution.py:69
  65.0 56.5 %collective-permute-start.21 = (f32[384,128]{1,0:T(8,128)}, f32[384,128]{1,0:T(8,128)S(1)}, u32[]{:S(2)}, u32[]{:S(2)}) collective-permute-start(f32[384,128]{1,0:T(8,128)} %get-tuple-element.51), channel_id=1, source_target_pairs={{8,24},{9,25},{10,26},{11,27},{12,28},{13,29},{14,30},{15,31}} | collective-permute-start | bytes 589832 | tf_op jit(solution)/shard_map/ppermute | solution.py:69
  67.1 57.4 %collective-permute-start.23 = (f32[384,128]{1,0:T(8,128)}, f32[384,128]{1,0:T(8,128)}, u32[]{:S(2)}, u32[]{:S(2)}) collective-permute-start(f32[384,128]{1,0:T(8,128)} %get-tuple-element.57), channel_id=1, source_target_pairs={{8,16},{9,17},{10,18},{11,19},{12,20},{13,21},{14,22},{15,23}} | collective-permute-start | bytes 589832 | tf_op jit(solution)/shard_map/ppermute | solution.py:69
  75.3 51.6 %collective-permute-start.24 = (f32[384,128]{1,0:T(8,128)}, f32[384,128]{1,0:T(8,128)}, u32[]{:S(2)}, u32[]{:S(2)}) collective-permute-start(f32[384,128]{1,0:T(8,128)} %get-tuple-element.58), channel_id=1, source_target_pairs={{8,24},{9,25},{10,26},{11,27},{12,28},{13,29},{14,30},{15,31}} | collective-permute-start | bytes 589832 | tf_op jit(solution)/shard_map/ppermute | solution.py:69
  76.6 54.0 %copy-start = (f32[1,4,384,384]{3,2,1,0:T(8,128)S(1)}, f32[1,4,384,384]{3,2,1,0:T(8,128)}, u32[]{:S(2)}) copy-start(f32[1,4,384,384]{3,2,1,0:T(8,128)} %param.10) | copy-start | bytes 7077892
  76.6 54.0 %copy-start.2 = (f32[384,128]{1,0:T(8,128)S(1)}, f32[384,128]{1,0:T(8,128)}, u32[]{:S(2)}) copy-start(f32[384,128]{1,0:T(8,128)} %refs_2_.1) | copy-start | bytes 589828
  122.6 8.1 %collective-permute-start.25 = (f32[384,128]{1,0:T(8,128)}, f32[384,128]{1,0:T(8,128)S(1)}, u32[]{:S(2)}, u32[]{:S(2)}) collective-permute-start(f32[384,128]{1,0:T(8,128)} %shard_map.100), channel_id=1, source_target_pairs={{0,1},{1,2},{2,3},{3,4},{4,5},{5,6},{6,7},{7,8},{8,9},{9,10},{10,1... | collective-permute-start | bytes 589832 | tf_op jit(solution)/shard_map/ppermute | solution.py:295

commit v4 on v3

--- a/solution.py
+++ b/solution.py
@@ -80,7 +80,8 @@
     q0 = moved(q, [(0, 1), (1, 2)] + middle)
     t0 = moved(t, [(1, 2)] + middle)
     u1_over = moved(u, [(1, 0)])
-    u0 = moved(u, [(0, 1)] + middle)
+    u0 = moved(u, [(3, 4), (4, 5)])
+    u0_low = moved(u, [(0, 1), (2, 3)])
     r_late = moved(r, [(3, 2)])
     r_next = moved(r, [(4, 3)])
 
@@ -149,54 +150,73 @@
     bounced = moved(relay, [(5, 4), (7, 5)])
     gt_came = moved(gt, [(5, 6), (6, 7)])
 
-    def forward_u(k, u0, u1_up, u, hu, rgt, u1, w):
+    def forward_u(k, u0, hu, rgt, u1, w):
+        @pl.when((k == 4) | (k == 5))
+        def _():
+            factor = left(u0[...])
+            w[...] = jnp.dot(factor, right(rgt[...]), preferred_element_type=F32)
+            u1[...] = jnp.dot(factor, right(hu[...]), preferred_element_type=F32)
+
+    (u1, w) = staged(forward_u, stride, [u0, hu, rgt], [square] * 2, 2)
+    w_came = moved(w, back)
+
+    def low_fields(k, first, came, q0, r, t, f1, rg):
         @pl.when(k == 0)
         def _():
-            u1[...] = u[...]
-
-        @pl.when((k > 0) & (k < 6))
+            f1[...] = first[:, :width]
+
+        @pl.when(k == 1)
+        def _():
+            g = summed(product(q0[...], r[...]), came[:, :width], True)
+            f1[...] = product(t[...], g)
+            rg[...] = product(r[...], g)
+
+    (f1, rg) = staged(low_fields, stride, [first, first_came, q0, r, t], [field] * 2, 2)
+    fa = moved(f1, low)
+
+    def second_reflect(k, bounced, q1, t1, u1, w, total, gt_out):
+        @pl.when((k == 4) | (k == 5))
+        def _():
+            gt = summed(product(q1[...], bounced[...]), t1[...])
+            gt_out[...] = gt
+            total[...] = w[...] + product(u1[...], product(bounced[...], gt))
+
+    (total, gt2) = staged(second_reflect, stride, [bounced, q1, t1, u1, w], [square] * 2, 6
+    )
+    total_came = moved(total, back)
+    gt2_came = moved(gt2, [(4, 6), (5, 7)])
+
+    def low_u(k, u0, u1_up, u, hu, rgt, rg, first, came, both, w):
+        side = u.shape[1]
+
+        @pl.when(k == 0)
+        def _():
+            both[:, :side] = u[...]
+            both[:, side:] = first[:, width:]
+
+        @pl.when((k > 0) & (k < 4))
         def _():
             factor = left(jnp.where(k == 2, u1_up[...], u0[...]))
-            u1[...] = jnp.dot(factor, right(hu[...]), preferred_element_type=F32)
+            both[:, :side] = jnp.dot(factor, right(hu[...]), preferred_element_type=F32)
+
+            @pl.when(k == 1)
+            def _():
+                both[:, side:] = came[:, width:] + jnp.dot(
+                    factor, right(rg[...]), preferred_element_type=F32
+                )
 
             @pl.when(k > 1)
             def _():
                 w[...] = jnp.dot(factor, right(rgt[...]), preferred_element_type=F32)
 
-    (u1, w) = staged(forward_u, stride, [u0, u1_up, u, hu, rgt], [square] * 2, 2)
-    w_came = moved(w, back)
-    ua = moved(u1, low)
-
-    def low_fields(k, first, came, q0, r, t, u0, out):
-        @pl.when(k == 0)
-        def _():
-            out[...] = first[...]
-
-        @pl.when(k == 1)
-        def _():
-            g = summed(product(q0[...], r[...]), came[:, :width], True)
-            out[:, :width] = product(t[...], g)
-            out[:, width:] = came[:, width:] + product(u0[...], product(r[...], g))
-
-    (first,) = staged(low_fields, stride, [first, first_came, q0, r, t, u0], [fields], 2)
-    fa = moved(first, low)
-
-    def open_gate(k, w, out):
-        out[...] = w[:8, :128]
-
-    (gate,) = staged(open_gate, stride, [w], [(8, 128)], 0.1)
-
-    def second_reflect(k, bounced, q1, t1, u1, w, gate, total, gt_out):
-        @pl.when((k == 4) | (k == 5))
-        def _():
-            gt = summed(product(q1[...], bounced[...]), t1[...])
-            gt_out[...] = gt
-            total[...] = w[...] + product(u1[...], product(bounced[...], gt))
-
-    (total, gt2) = staged(second_reflect, stride, [bounced, q1, t1, u1, w, gate], [square] * 2, 6
-    )
-    total_came = moved(total, back)
-    gt2_came = moved(gt2, [(4, 6), (5, 7)])
+    (both, w_low) = staged(
+        low_u,
+        stride,
+        [u0_low, u1_up, u, hu, rgt, rg, first, first_came],
+        [(square[0], square[1] + width), square],
+        2,
+    )
+    ua = moved(both, low)
 
     def own_fields(k, r2_up, hopped, w, r1):
         @pl.when(k == 2)
@@ -207,38 +227,38 @@
         def _():
             r1[...] = r2_up[...] + w[...]
 
-    (r1,) = staged(own_fields, stride, [r2_up, hopped, w], [square], 0.1)
-
-    def second_q(k, r1, qa, q1, t1, u1, q2, hu_out):
-        @pl.when((k == 2) | (k == 3))
-        def _():
-            hu = summed(product(r1[...], qa[...]), u1[...], True)
+    (r1,) = staged(own_fields, stride, [r2_up, hopped, w_low], [square], 0.1)
+
+    def second_q(k, r1, qa, q1, t1, both, q2, hu_out):
+        @pl.when((k == 2) | (k == 3))
+        def _():
+            hu = summed(product(r1[...], qa[...]), both[:, : q1.shape[1]], True)
             hu_out[...] = hu
             q2[...] = q1[...] + product(t1[...], product(qa[...], hu))
 
-    (q2, hu2) = staged(second_q, stride, [r1, qa, q1, t1, u1], [square] * 2, 6)
+    (q2, hu2) = staged(second_q, stride, [r1, qa, q1, t1, both], [square] * 2, 6)
 
     def second_fields(k, qa, fa, r1, t1, f2, rg2):
         @pl.when((k == 2) | (k == 3))
         def _():
-            g = summed(product(qa[...], r1[...]), fa[:, :width])
+            g = summed(product(qa[...], r1[...]), fa[...])
             f2[...] = product(t1[...], g)
             rg2[...] = product(r1[...], g)
 
     (f2, rg2) = staged(second_fields, stride, [qa, fa, r1, t1], [field, field], 2)
 
-    def third_fields(k, r_late, r_next, w_came, q1, t1, u1, r1, qa, fa, w4, rg4):
+    def third_fields(k, r_late, r_next, w_came, q1, t1, both, r1, qa, fa, w4, rg4):
         @pl.when((k == 2) | (k == 3))
         def _():
             came = jnp.where(k == 2, r_late[...], r_next[...]) + w_came[...]
-            gt = summed(product(q1[...], came), t1[...])
-            rc = r1[...] + product(u1[...], product(came, gt))
-            g = summed(product(qa[...], rc), fa[:, :width])
+            gt = summed(product(q1[...], came), t1[...], True)
+            rc = r1[...] + product(both[:, : q1.shape[1]], product(came, gt))
+            g = summed(product(qa[...], rc), fa[...])
             w4[...] = product(gt, g)
             rg4[...] = product(rc, g)
 
     (w4, rg4) = staged(
-        third_fields, stride, [r_late, r_next, w_came, q1, t1, u1, r1, qa, fa], [field] * 2, 9
+        third_fields, stride, [r_late, r_next, w_came, q1, t1, both, r1, qa, fa], [field] * 2, 9
     )
     w4_came = moved(w4, [(2, 4), (3, 5)])
 
@@ -261,22 +281,22 @@
     )
     g6_came = moved(g6, [(2, 6), (3, 7)])
 
-    def all_reflected(k, fa, ua, rg2, rg4, rg6, hu2, s2, s4, s6):
+    def all_reflected(k, ua, rg2, rg4, rg6, hu2, s2, s4, s6):
         @pl.when((k == 2) | (k == 3))
         def _():
             sums = rg2[...] + product(hu2[...], rg6[...])
-            value = product(ua[...], jnp.concatenate([rg2[...], rg4[...], sums], axis=1))
+            value = product(ua[:, : hu2.shape[1]], jnp.concatenate([rg2[...], rg4[...], sums], axis=1))
             for i, out in enumerate((s2, s4, s6)):
-                out[...] = fa[:, width:] + value[:, i * width : (i + 1) * width]
-
-    (s2, s4, s6) = staged(all_reflected, stride, [fa, ua, rg2, rg4, rg6, hu2], [field] * 3, 2)
+                out[...] = ua[:, hu2.shape[1] :] + value[:, i * width : (i + 1) * width]
+
+    (s2, s4, s6) = staged(all_reflected, stride, [ua, rg2, rg4, rg6, hu2], [field] * 3, 2)
     s6_came = moved(s6, [(2, 6), (3, 7)])
     s4_came = moved(s4, [(2, 4), (3, 5)])
 
-    def through(k, first, f2, t1, w4, t2, g6, out):
+    def through(k, f1, f2, t1, w4, t2, g6, out):
         @pl.when(k < 2)
         def _():
-            out[...] = first[:, :width]
+            out[...] = f1[...]
 
         @pl.when((k == 2) | (k == 3))
         def _():
@@ -290,11 +310,11 @@
         def _():
             out[...] = product(t2[...], g6[...])
 
-    (through_field,) = staged(through, stride, [first, f2, t1, w4_came, t2, g6_came], [field], 1
+    (through_field,) = staged(through, stride, [f1, f2, t1, w4_came, t2, g6_came], [field], 1
     )
     entering = lax.ppermute(through_field, "sec", [(i, i + 1) for i in range(length - 1)])
     reflected = jnp.where(
-        k < 2, first[:, width:], jnp.where(k < 4, s2, jnp.where(k < 6, s4_came, s6_came))
+        k < 2, both[:, square[1] :], jnp.where(k < 4, s2, jnp.where(k < 6, s4_came, s6_came))
     )
 
     def depths(place, maps, entering, incident, out):

time: 134 us -> 135 us (level)
  the two profiles are of different devices: /device:TPU:28 before, /device:TPU:12 now
where the time goes in v4:
time: 135 us; the launch traced here: 134 us
  waiting for transfers between devices  55.6 us (41%)
  starting transfers between devices  37.8 us (28%)
  Pallas kernels  34.9 us (26%)
  local copies, waits for them, and re-layouts  2.96 us (2%)
  other arithmetic  1.66 us (1%)
    ppermute x26, waiting for transfers between devices, moved(): return lax.ppermute(value, 'sec', pairs)  51.1 us
    ppermute x26, starting transfers between devices, moved(): return lax.ppermute(value, 'sec', pairs)  35.9 us
    pallas_call x18, Pallas kernels, staged(): pl.pallas_call(kernel, out_shape=[jax.ShapeDtypeStruct(shape, F32) for sh...  34.9 us
    ppermute x1, waiting for transfers between devices, per_device(): lax.ppermute(through_field, 'sec', [(i, i + 1) for i in range(length - 1)])  4.49 us
    unnamed x10, local copies, waits for them, and re-layouts  2.96 us
  transfers between devices with their start and end apart: 27, of which 8 were waited for; matrix products, arithmetic and copies ran while one was open for 1% of the time, Pallas kernels for 25%

profile of v4, /device:TPU:12, one launch (start us, length us, event | category | flops | bytes accessed | tf_op | source)
XLA Modules:
  0.0 134.0 jit_solution(13798264273227571298)
XLA Ops:
  0.6 0.7 collective-permute-start.7
  1.3 0.9 copy-done.1
  2.3 1.8 %shard_map.85 = (f32[384,384]{1,0:T(8,128)S(1)}, f32[384,384]{1,0:T(8,128)S(1)}, f32[384,384]{1,0:T(8,128)S(1)}, f32[384,384]{1,0:T(8,128)S(1)}, f32[384,256]{1,0:T(8,128)S(1)}) custom-call(f32[384,384]{1,0:T(8,128)} %bitcast.refs_0_, f32[384,384]{1,0:T(8,128)} %bitcast.1.refs_1_, f32[384,384]{1,0:T(8,128)} %bitcast.2.refs_2_, f32[384,384]{1,0:T(8,128)} %bitcast.3.refs_3_, ...), custom_call_target="tpu_custom_call" | custom-call | flops 339738624 | bytes 5898240 | tf_op jit(solution)/shard_map/pallas_call | solution.py:48
  4.7 3.4 %collective-permute-start.1 = (f32[384,384]{1,0:T(8,128)}, f32[384,384]{1,0:T(8,128)S(1)}, u32[]{:S(2)}, u32[]{:S(2)}) collective-permute-start(f32[384,384]{1,0:T(8,128)} %bitcast.2.refs_2_), channel_id=1, source_target_pairs={{0,4},{1,5},{2,6},{3,7},{4,8},{5,9},{6,10},{7,11},{8,12},{9,13},{1... | collective-permute-start | bytes 1769480 | tf_op jit(solution)/shard_map/ppermute | solution.py:69
  8.2 3.4 %collective-permute-start.12 = (f32[384,384]{1,0:T(8,128)}, f32[384,384]{1,0:T(8,128)S(1)}, u32[]{:S(2)}, u32[]{:S(2)}) collective-permute-start(f32[384,384]{1,0:T(8,128)} %bitcast.1.refs_1_), channel_id=1, source_target_pairs={{4,8},{5,9},{6,10},{7,11},{8,12},{9,13},{10,14},{11,15},{12,16},{1... | collective-permute-start | bytes 1769480 | tf_op jit(solution)/shard_map/ppermute | solution.py:69
  11.6 0.7 collective-permute-start.10
  12.3 0.7 collective-permute-start.4
  13.1 0.7 collective-permute-start.8
  13.8 9.2 %collective-permute-done.1.refs_2_.refs_0_ = f32[384,384]{1,0:T(8,128)S(1)} collective-permute-done((f32[384,384]{1,0:T(8,128)}, f32[384,384]{1,0:T(8,128)S(1)}, u32[]{:S(2)}, u32[]{:S(2)}) %collective-permute-start.1) | collective-permute-done | bytes 589856 | tf_op jit(solution)/shard_map/ppermute | solution.py:69
  23.0 1.3 collective-permute-start.9
  24.3 11.4 %collective-permute-done.12.refs_1_ = f32[384,384]{1,0:T(8,128)S(1)} collective-permute-done((f32[384,384]{1,0:T(8,128)}, f32[384,384]{1,0:T(8,128)S(1)}, u32[]{:S(2)}, u32[]{:S(2)}) %collective-permute-start.12) | collective-permute-done | bytes 589856 | tf_op jit(solution)/shard_map/ppermute | solution.py:69
  35.7 3.2 %collective-permute-start.15 = (f32[384,384]{1,0:T(8,128)}, f32[384,384]{1,0:T(8,128)S(1)}, u32[]{:S(2)}, u32[]{:S(2)}) collective-permute-start(f32[384,384]{1,0:T(8,128)} %bitcast.3.refs_3_), channel_id=1, source_target_pairs={{12,16},{13,17},{14,18},{15,19},{16,20},{17,21},{18,22},{19,23}} | collective-permute-start | bytes 1769480 | tf_op jit(solution)/shard_map/ppermute | solution.py:69
  38.9 0.7 collective-permute-start.5
  39.6 1.3 collective-permute-start.13
  41.0 0.7 collective-permute-start.11
  41.7 4.1 %shard_map.87 = (f32[384,384]{1,0:T(8,128)S(1)}, f32[384,384]{1,0:T(8,128)S(1)}) custom-call(f32[384,384]{1,0:T(8,128)S(1)} %collective-permute-done.1.refs_2_.refs_0_, f32[384,384]{1,0:T(8,128)S(1)} %get-tuple-element.36.refs_3_.refs_1_.refs_2_, f32[384,384]{1,0:T(8,128)S(1)} %get-tuple-element.37.refs_4_.refs_2_.refs_3_.refs_0_, ...), custom_call_target="tpu_custom_call" | custom-call | flops 2038431744 | bytes 4128768 | tf_op jit(solution)/shard_map/pallas_call | solution.py:48
  45.9 1.3 collective-permute-done.9.refs_0_
  47.2 1.3 collective-permute-start.14
  48.5 2.4 %collective-permute-done.15.refs_0_ = f32[384,384]{1,0:T(8,128)S(1)} collective-permute-done((f32[384,384]{1,0:T(8,128)}, f32[384,384]{1,0:T(8,128)S(1)}, u32[]{:S(2)}, u32[]{:S(2)}) %collective-permute-start.15) | collective-permute-done | bytes 589856 | tf_op jit(solution)/shard_map/ppermute | solution.py:69
  51.6 3.9 %shard_map.89 = (f32[384,384]{1,0:T(8,128)S(1)}, f32[384,384]{1,0:T(8,128)S(1)}) custom-call(f32[384,384]{1,0:T(8,128)S(1)} %collective-permute-done.1.refs_2_.refs_0_, f32[384,384]{1,0:T(8,128)S(1)} %collective-permute-done.12.refs_1_, f32[384,384]{1,0:T(8,128)S(1)} %get-tuple-element.36.refs_3_.refs_1_.refs_2_, ...), custom_call_target="tpu_custom_call" | custom-call | flops 2038431744 | bytes 3538944 | tf_op jit(solution)/shard_map/pallas_call | solution.py:48
  55.5 1.3 collective-permute-start.6
  57.0 1.3 collective-permute-start.2
  58.3 1.3 collective-permute-start.16
  59.7 1.3 shard_map.90
  61.0 5.4 %collective-permute-done.14.refs_1_ = f32[384,384]{1,0:T(8,128)S(1)} collective-permute-done((f32[384,384]{1,0:T(8,128)}, f32[384,384]{1,0:T(8,128)S(1)}, u32[]{:S(2)}, u32[]{:S(2)}) %collective-permute-start.14) | collective-permute-done | bytes 589856 | tf_op jit(solution)/shard_map/ppermute | solution.py:69
  66.4 1.3 collective-permute-start.3
  67.7 1.3 collective-permute-start.23
  69.0 5.9 %collective-permute-done.6.refs_0_ = f32[384,384]{1,0:T(8,128)S(1)} collective-permute-done((f32[384,384]{1,0:T(8,128)S(1)}, f32[384,384]{1,0:T(8,128)S(1)}, u32[]{:S(2)}, u32[]{:S(2)}) %collective-permute-start.6) | collective-permute-done | bytes 589856 | tf_op jit(solution)/shard_map/ppermute | solution.py:69
  74.9 1.3 collective-permute-start.21
  76.3 15.5 %collective-permute-done.3.refs_1_.refs_8_ = f32[384,128]{1,0:T(8,128)S(1)} collective-permute-done((f32[384,128]{1,0:T(8,128)S(1)}, f32[384,128]{1,0:T(8,128)S(1)}, u32[]{:S(2)}, u32[]{:S(2)}) %collective-permute-start.3) | collective-permute-done | bytes 196640 | tf_op jit(solution)/shard_map/ppermute | solution.py:69
  92.5 1.5 %collective-permute-start.20 = (f32[384,384]{1,0:T(8,128)S(1)}, f32[384,384]{1,0:T(8,128)}, u32[]{:S(2)}, u32[]{:S(2)}) collective-permute-start(f32[384,384]{1,0:T(8,128)S(1)} %get-tuple-element.56), channel_id=1, source_target_pairs={{16,24},{17,25},{18,26},{19,27},{20,28},{21,29},{22,30},{23,31}} | collective-permute-start | bytes 1769480 | tf_op jit(solution)/shard_map/ppermute | solution.py:69
  94.0 7.4 %shard_map.94 = (f32[384,128]{1,0:T(8,128)}, f32[384,128]{1,0:T(8,128)S(1)}) custom-call(f32[384,384]{1,0:T(8,128)S(1)} %collective-permute-done.13.refs_0_, f32[384,384]{1,0:T(8,128)S(1)} %collective-permute-done.14.refs_1_, f32[384,384]{1,0:T(8,128)S(1)} %collective-permute-done.16.refs_2_, f32[384,384]{1,0:T(8,128)S(1)} %get-tuple-element.41.refs_3_.refs_1_.refs_2_, ...), custom_call_target="tpu_custom_call" | custom-call | flops 3057647616 | bytes 6488064 | tf_op jit(solution)/shard_map/pallas_call | solution.py:48
  101.4 1.3 collective-permute-start.17
  102.7 3.0 %shard_map.92 = (f32[384,128]{1,0:T(8,128)S(1)}, f32[384,128]{1,0:T(8,128)S(1)}) custom-call(f32[384,384]{1,0:T(8,128)S(1)} %collective-permute-done.2.refs_0_.refs_7_.refs_1_, f32[384,128]{1,0:T(8,128)S(1)} %collective-permute-done.3.refs_1_.refs_8_, f32[384,384]{1,0:T(8,128)S(1)} %shard_map.91.refs_2_.refs_6_.refs_0_, ...), custom_call_target="tpu_custom_call" | custom-call | flops 679477248 | bytes 3538944 | tf_op jit(solution)/shard_map/pallas_call | solution.py:48
  105.7 4.1 %shard_map.98 = (f32[384,384]{1,0:T(8,128)S(1)}, f32[384,384]{1,0:T(8,128)S(1)}) custom-call(f32[384,384]{1,0:T(8,128)S(1)} %shard_map.91.refs_2_.refs_6_.refs_0_, f32[384,384]{1,0:T(8,128)S(1)} %collective-permute-done.2.refs_0_.refs_7_.refs_1_, f32[384,384]{1,0:T(8,128)S(1)} %get-tuple-element.41.refs_3_.refs_1_.refs_2_, ...), custom_call_target="tpu_custom_call" | custom-call | flops 2038431744 | bytes 4128768 | tf_op jit(solution)/shard_map/pallas_call | solution.py:48
  109.8 3.3 %shard_map.99 = (f32[384,128]{1,0:T(8,128)}, f32[384,128]{1,0:T(8,128)S(1)}) custom-call(f32[384,384]{1,0:T(8,128)S(1)} %collective-permute-done.13.refs_0_, f32[384,384]{1,0:T(8,128)S(1)} %collective-permute-done.14.refs_1_, f32[384,384]{1,0:T(8,128)S(1)} %collective-permute-done.21.refs_2_, f32[384,384]{1,0:T(8,128)S(1)} %get-tuple-element.58.refs_3_, ...), custom_call_target="tpu_custom_call" | custom-call | flops 1019215872 | bytes 4128768 | tf_op jit(solution)/shard_map/pallas_call | solution.py:48
  113.1 1.3 collective-permute-start.22
  114.5 1.8 %shard_map.101 = (f32[384,128]{1,0:T(8,128)S(1)}, f32[384,128]{1,0:T(8,128)}, f32[384,128]{1,0:T(8,128)}) custom-call(f32[384,512]{1,0:T(8,128)S(1)} %collective-permute-done.23.refs_0_, f32[384,128]{1,0:T(8,128)S(1)} %get-tuple-element.60.refs_1_, f32[384,128]{1,0:T(8,128)S(1)} %get-tuple-element.61.refs_2_, f32[384,128]{1,0:T(8,128)S(1)} %get-tuple-element.62.refs_3_, ...), custom_call_target="tpu_custom_call" | custom-call | flops 679477248 | bytes 4718592 | tf_op jit(solution)/shard_map/pallas_call | solution.py:48
  116.2 2.0 %collective-permute-start.24 = (f32[384,128]{1,0:T(8,128)}, f32[384,128]{1,0:T(8,128)}, u32[]{:S(2)}, u32[]{:S(2)}) collective-permute-start(f32[384,128]{1,0:T(8,128)} %get-tuple-element.65), channel_id=1, source_target_pairs={{8,16},{9,17},{10,18},{11,19},{12,20},{13,21},{14,22},{15,23}} | collective-permute-start | bytes 589832 | tf_op jit(solution)/shard_map/ppermute | solution.py:69
  118.2 0.8 copy-done.3
  119.0 2.0 %collective-permute-start.25 = (f32[384,128]{1,0:T(8,128)}, f32[384,128]{1,0:T(8,128)}, u32[]{:S(2)}, u32[]{:S(2)}) collective-permute-start(f32[384,128]{1,0:T(8,128)} %get-tuple-element.66), channel_id=1, source_target_pairs={{8,24},{9,25},{10,26},{11,27},{12,28},{13,29},{14,30},{15,31}} | collective-permute-start | bytes 589832 | tf_op jit(solution)/shard_map/ppermute | solution.py:69
  121.0 1.2 copy-done.4
  122.2 1.1 shard_map.97.refs_4_
  123.2 0.7 shard_map.100
  123.9 1.9 %collective-permute-start.26 = (f32[384,128]{1,0:T(8,128)}, f32[384,128]{1,0:T(8,128)S(1)}, u32[]{:S(2)}, u32[]{:S(2)}) collective-permute-start(f32[384,128]{1,0:T(8,128)} %shard_map.100), channel_id=1, source_target_pairs={{0,1},{1,2},{2,3},{3,4},{4,5},{5,6},{6,7},{7,8},{8,9},{9,10},{10,1... | collective-permute-start | bytes 589832 | tf_op jit(solution)/shard_map/ppermute | solution.py:315
  125.9 1.7 %select_bitcast_fusion = f32[1,384,128]{2,1,0:T(8,128)} fusion(f32[384,128]{1,0:T(8,128)S(1)} %get-tuple-element.64, f32[384,128]{1,0:T(8,128)} %collective-permute-done.24, f32[384,128]{1,0:T(8,128)} %collective-permute-done.25, f32[384,512]{1,0:T(8,128)S(1)} %get-tuple-element.50.refs_5_.refs_4_, pred[]{:T(512)S(6)} %lt.11, pred[]{:T(512)S(6)} %lt.10, pred[]{:T(512)S(6)} %lt.9), kind=kLoop, calls=%fused_computation | loop fusion | flops 147456 | bytes 983043 | tf_op jit(solution)/shard_map/broadcast_in_dim | solution.py:331
  127.5 4.5 %collective-permute-done.26.refs_1_ = f32[384,128]{1,0:T(8,128)S(1)} collective-permute-done((f32[384,128]{1,0:T(8,128)}, f32[384,128]{1,0:T(8,128)S(1)}, u32[]{:S(2)}, u32[]{:S(2)}) %collective-permute-start.26) | collective-permute-done | bytes 196640 | tf_op jit(solution)/shard_map/ppermute | solution.py:315
  132.0 2.0 %shard_map.102 = f32[4,384,128]{2,1,0:T(8,128)} custom-call(f32[4,384,384]{2,1,0:T(8,128)S(1)} %bitcast.9, f32[384,128]{1,0:T(8,128)S(1)} %collective-permute-done.26.refs_1_, f32[384,128]{1,0:T(8,128)S(1)} %copy-done.2), custom_call_target="tpu_custom_call" | custom-call | flops 384 | bytes 256 | tf_op jit(solution)/shard_map/pallas_call | solution.py:48
  (35 shorter events, 2.6 us)
Async XLA Ops:
  0.6 11.7 %collective-permute-start.7 = (f32[384,384]{1,0:T(8,128)}, f32[384,384]{1,0:T(8,128)S(1)}, u32[]{:S(2)}, u32[]{:S(2)}) collective-permute-start(f32[384,384]{1,0:T(8,128)} %bitcast.refs_0_), channel_id=1, source_target_pairs={{28,24},{29,25},{30,26},{31,27},{24,28},{25,29},{26,30},{27,31},{4... | collective-permute-start | bytes 1769480 | tf_op jit(solution)/shard_map/ppermute | solution.py:69
  1.3 0.9 copy-start.1
  4.0 9.1 %collective-permute-start = (f32[384,256]{1,0:T(8,128)S(1)}, f32[384,256]{1,0:T(8,128)S(1)}, u32[]{:S(2)}, u32[]{:S(2)}) collective-permute-start(f32[384,256]{1,0:T(8,128)S(1)} %get-tuple-element.35.refs_0_.refs_6_), channel_id=1, source_target_pairs={{0,4},{1,5},{2,6},{3,7}} | collective-permute-start | bytes 1179656 | tf_op jit(solution)/shard_map/ppermute | solution.py:69
  4.7 18.3 %collective-permute-start.1 = (f32[384,384]{1,0:T(8,128)}, f32[384,384]{1,0:T(8,128)S(1)}, u32[]{:S(2)}, u32[]{:S(2)}) collective-permute-start(f32[384,384]{1,0:T(8,128)} %bitcast.2.refs_2_), channel_id=1, source_target_pairs={{0,4},{1,5},{2,6},{3,7},{4,8},{5,9},{6,10},{7,11},{8,12},{9,13},{1... | collective-permute-start | bytes 1769480 | tf_op jit(solution)/shard_map/ppermute | solution.py:69
  8.2 27.5 %collective-permute-start.12 = (f32[384,384]{1,0:T(8,128)}, f32[384,384]{1,0:T(8,128)S(1)}, u32[]{:S(2)}, u32[]{:S(2)}) collective-permute-start(f32[384,384]{1,0:T(8,128)} %bitcast.1.refs_1_), channel_id=1, source_target_pairs={{4,8},{5,9},{6,10},{7,11},{8,12},{9,13},{10,14},{11,15},{12,16},{1... | collective-permute-start | bytes 1769480 | tf_op jit(solution)/shard_map/ppermute | solution.py:69
  11.6 28.0 %collective-permute-start.10 = (f32[384,384]{1,0:T(8,128)}, f32[384,384]{1,0:T(8,128)S(1)}, u32[]{:S(2)}, u32[]{:S(2)}) collective-permute-start(f32[384,384]{1,0:T(8,128)} %bitcast.3.refs_3_), channel_id=1, source_target_pairs={{4,0},{5,1},{6,2},{7,3}} | collective-permute-start | bytes 1769480 | tf_op jit(solution)/shard_map/ppermute | solution.py:69
  12.3 26.6 %collective-permute-start.4 = (f32[384,384]{1,0:T(8,128)}, f32[384,384]{1,0:T(8,128)S(1)}, u32[]{:S(2)}, u32[]{:S(2)}) collective-permute-start(f32[384,384]{1,0:T(8,128)} %bitcast.refs_0_), channel_id=1, source_target_pairs={{8,0},{9,1},{10,2},{11,3}} | collective-permute-start | bytes 1769480 | tf_op jit(solution)/shard_map/ppermute | solution.py:69
  13.1 27.9 %collective-permute-start.8 = (f32[384,384]{1,0:T(8,128)S(1)}, f32[384,384]{1,0:T(8,128)S(1)}, u32[]{:S(2)}, u32[]{:S(2)}) collective-permute-start(f32[384,384]{1,0:T(8,128)S(1)} %get-tuple-element.42), channel_id=1, source_target_pairs={{24,28},{25,29},{26,30},{27,31},{28,20},{29,21},{30,22},{31,23},{0... | collective-permute-start | bytes 1769480 | tf_op jit(solution)/shard_map/ppermute | solution.py:69
  23.0 24.1 %collective-permute-start.9 = (f32[384,384]{1,0:T(8,128)}, f32[384,384]{1,0:T(8,128)S(1)}, u32[]{:S(2)}, u32[]{:S(2)}) collective-permute-start(f32[384,384]{1,0:T(8,128)} %bitcast.3.refs_3_), channel_id=1, source_target_pairs={{0,4},{1,5},{2,6},{3,7},{8,12},{9,13},{10,14},{11,15}} | collective-permute-start | bytes 1769480 | tf_op jit(solution)/shard_map/ppermute | solution.py:69
  35.7 15.2 %collective-permute-start.15 = (f32[384,384]{1,0:T(8,128)}, f32[384,384]{1,0:T(8,128)S(1)}, u32[]{:S(2)}, u32[]{:S(2)}) collective-permute-start(f32[384,384]{1,0:T(8,128)} %bitcast.3.refs_3_), channel_id=1, source_target_pairs={{12,16},{13,17},{14,18},{15,19},{16,20},{17,21},{18,22},{19,23}} | collective-permute-start | bytes 1769480 | tf_op jit(solution)/shard_map/ppermute | solution.py:69
  38.9 16.6 %collective-permute-start.5 = (f32[384,384]{1,0:T(8,128)S(1)}, f32[384,384]{1,0:T(8,128)S(1)}, u32[]{:S(2)}, u32[]{:S(2)}) collective-permute-start(f32[384,384]{1,0:T(8,128)S(1)} %collective-permute-done.4), channel_id=1, source_target_pairs={{0,4},{1,5},{2,6},{3,7}} | collective-permute-start | bytes 1769480 | tf_op jit(solution)/shard_map/ppermute | solution.py:69
  39.6 17.4 %collective-permute-start.13 = (f32[384,384]{1,0:T(8,128)}, f32[384,384]{1,0:T(8,128)S(1)}, u32[]{:S(2)}, u32[]{:S(2)}) collective-permute-start(f32[384,384]{1,0:T(8,128)} %bitcast.refs_0_), channel_id=1, source_target_pairs={{12,8},{13,9},{14,10},{15,11}} | collective-permute-start | bytes 1769480 | tf_op jit(solution)/shard_map/ppermute | solution.py:69
  41.0 17.4 %collective-permute-start.11 = (f32[384,384]{1,0:T(8,128)S(1)}, f32[384,384]{1,0:T(8,128)S(1)}, u32[]{:S(2)}, u32[]{:S(2)}) collective-permute-start(f32[384,384]{1,0:T(8,128)S(1)} %collective-permute-done.10), channel_id=1, source_target_pairs={{0,8},{1,9},{2,10},{3,11}} | collective-permute-start | bytes 1769480 | tf_op jit(solution)/shard_map/ppermute | solution.py:69
  47.2 19.2 %collective-permute-start.14 = (f32[384,384]{1,0:T(8,128)}, f32[384,384]{1,0:T(8,128)S(1)}, u32[]{:S(2)}, u32[]{:S(2)}) collective-permute-start(f32[384,384]{1,0:T(8,128)} %bitcast.refs_0_), channel_id=1, source_target_pairs={{16,12},{17,13},{18,14},{19,15}} | collective-permute-start | bytes 1769480 | tf_op jit(solution)/shard_map/ppermute | solution.py:69
  50.9 16.8 %collective-permute-start.19 = (f32[384,384]{1,0:T(8,128)S(1)}, f32[384,384]{1,0:T(8,128)S(1)}, u32[]{:S(2)}, u32[]{:S(2)}) collective-permute-start(f32[384,384]{1,0:T(8,128)S(1)} %get-tuple-element.54), channel_id=1, source_target_pairs={{20,16},{21,17},{22,18},{23,19},{28,20},{29,21},{30,22},{31,23}} | collective-permute-start | bytes 1769480 | tf_op jit(solution)/shard_map/ppermute | solution.py:69
  55.5 19.4 %collective-permute-start.6 = (f32[384,384]{1,0:T(8,128)S(1)}, f32[384,384]{1,0:T(8,128)S(1)}, u32[]{:S(2)}, u32[]{:S(2)}) collective-permute-start(f32[384,384]{1,0:T(8,128)S(1)} %collective-permute-done.5), channel_id=1, source_target_pairs={{4,12},{5,13},{6,14},{7,15}} | collective-permute-start | bytes 1769480 | tf_op jit(solution)/shard_map/ppermute | solution.py:69
  57.0 35.5 %collective-permute-start.2 = (f32[384,384]{1,0:T(8,128)S(1)}, f32[384,384]{1,0:T(8,128)S(1)}, u32[]{:S(2)}, u32[]{:S(2)}) collective-permute-start(f32[384,384]{1,0:T(8,128)S(1)} %get-tuple-element.41.refs_3_.refs_1_.refs_2_), channel_id=1, source_target_pairs={{0,8},{1,9},{2,10},{3,11},{4,12},{5,13},{6,14},{7,15}} | collective-permute-start | bytes 1769480 | tf_op jit(solution)/shard_map/ppermute | solution.py:69
  58.3 35.7 %collective-permute-start.16 = (f32[384,384]{1,0:T(8,128)S(1)}, f32[384,384]{1,0:T(8,128)S(1)}, u32[]{:S(2)}, u32[]{:S(2)}) collective-permute-start(f32[384,384]{1,0:T(8,128)S(1)} %get-tuple-element.49.refs_4_), channel_id=1, source_target_pairs={{16,8},{17,9},{18,10},{19,11},{20,12},{21,13},{22,14},{23,15}} | collective-permute-start | bytes 1769480 | tf_op jit(solution)/shard_map/ppermute | solution.py:69
  66.4 25.4 %collective-permute-start.3 = (f32[384,128]{1,0:T(8,128)S(1)}, f32[384,128]{1,0:T(8,128)S(1)}, u32[]{:S(2)}, u32[]{:S(2)}) collective-permute-start(f32[384,128]{1,0:T(8,128)S(1)} %get-tuple-element.38.refs_0_), channel_id=1, source_target_pairs={{0,8},{1,9},{2,10},{3,11},{4,12},{5,13},{6,14},{7,15}} | collective-permute-start | bytes 589832 | tf_op jit(solution)/shard_map/ppermute | solution.py:69
  67.7 46.8 %collective-permute-start.23 = (f32[384,512]{1,0:T(8,128)S(1)}, f32[384,512]{1,0:T(8,128)S(1)}, u32[]{:S(2)}, u32[]{:S(2)}) collective-permute-start(f32[384,512]{1,0:T(8,128)S(1)} %get-tuple-element.50.refs_5_.refs_4_), channel_id=1, source_target_pairs={{0,8},{1,9},{2,10},{3,11},{4,12},{5,13},{6,14},{7,15}} | collective-permute-start | bytes 2359304 | tf_op jit(solution)/shard_map/ppermute | solution.py:69
  74.9 34.9 %collective-permute-start.21 = (f32[384,384]{1,0:T(8,128)S(1)}, f32[384,384]{1,0:T(8,128)S(1)}, u32[]{:S(2)}, u32[]{:S(2)}) collective-permute-start(f32[384,384]{1,0:T(8,128)S(1)} %get-tuple-element.57), channel_id=1, source_target_pairs={{16,8},{17,9},{18,10},{19,11},{20,12},{21,13},{22,14},{23,15}} | collective-permute-start | bytes 1769480 | tf_op jit(solution)/shard_map/ppermute | solution.py:69
  91.8 26.4 %collective-permute-start.18 = (f32[384,384]{1,0:T(8,128)S(1)}, f32[384,384]{1,0:T(8,128)S(1)}, u32[]{:S(2)}, u32[]{:S(2)}) collective-permute-start(f32[384,384]{1,0:T(8,128)S(1)} %get-tuple-element.53), channel_id=1, source_target_pairs={{20,24},{21,25},{22,26},{23,27},{24,28},{25,29},{26,30},{27,31}} | collective-permute-start | bytes 1769480 | tf_op jit(solution)/shard_map/ppermute | solution.py:69
  92.5 28.5 %collective-permute-start.20 = (f32[384,384]{1,0:T(8,128)S(1)}, f32[384,384]{1,0:T(8,128)}, u32[]{:S(2)}, u32[]{:S(2)}) collective-permute-start(f32[384,384]{1,0:T(8,128)S(1)} %get-tuple-element.56), channel_id=1, source_target_pairs={{16,24},{17,25},{18,26},{19,27},{20,28},{21,29},{22,30},{23,31}} | collective-permute-start | bytes 1769480 | tf_op jit(solution)/shard_map/ppermute | solution.py:69
  101.4 21.8 %collective-permute-start.17 = (f32[384,128]{1,0:T(8,128)}, f32[384,128]{1,0:T(8,128)S(1)}, u32[]{:S(2)}, u32[]{:S(2)}) collective-permute-start(f32[384,128]{1,0:T(8,128)} %get-tuple-element.51), channel_id=1, source_target_pairs={{8,16},{9,17},{10,18},{11,19},{12,20},{13,21},{14,22},{15,23}} | collective-permute-start | bytes 589832 | tf_op jit(solution)/shard_map/ppermute | solution.py:69
  113.1 10.1 %collective-permute-start.22 = (f32[384,128]{1,0:T(8,128)}, f32[384,128]{1,0:T(8,128)S(1)}, u32[]{:S(2)}, u32[]{:S(2)}) collective-permute-start(f32[384,128]{1,0:T(8,128)} %get-tuple-element.59), channel_id=1, source_target_pairs={{8,24},{9,25},{10,26},{11,27},{12,28},{13,29},{14,30},{15,31}} | collective-permute-start | bytes 589832 | tf_op jit(solution)/shard_map/ppermute | solution.py:69
  116.2 9.6 %collective-permute-start.24 = (f32[384,128]{1,0:T(8,128)}, f32[384,128]{1,0:T(8,128)}, u32[]{:S(2)}, u32[]{:S(2)}) collective-permute-start(f32[384,128]{1,0:T(8,128)} %get-tuple-element.65), channel_id=1, source_target_pairs={{8,16},{9,17},{10,18},{11,19},{12,20},{13,21},{14,22},{15,23}} | collective-permute-start | bytes 589832 | tf_op jit(solution)/shard_map/ppermute | solution.py:69
  118.2 0.8 copy-start.3
  119.0 6.9 %collective-permute-start.25 = (f32[384,128]{1,0:T(8,128)}, f32[384,128]{1,0:T(8,128)}, u32[]{:S(2)}, u32[]{:S(2)}) collective-permute-start(f32[384,128]{1,0:T(8,128)} %get-tuple-element.66), channel_id=1, source_target_pairs={{8,24},{9,25},{10,26},{11,27},{12,28},{13,29},{14,30},{15,31}} | collective-permute-start | bytes 589832 | tf_op jit(solution)/shard_map/ppermute | solution.py:69
  120.9 11.1 %copy-start = (f32[1,4,384,384]{3,2,1,0:T(8,128)S(1)}, f32[1,4,384,384]{3,2,1,0:T(8,128)}, u32[]{:S(2)}) copy-start(f32[1,4,384,384]{3,2,1,0:T(8,128)} %param.10) | copy-start | bytes 7077892
  120.9 11.1 %copy-start.2 = (f32[384,128]{1,0:T(8,128)S(1)}, f32[384,128]{1,0:T(8,128)}, u32[]{:S(2)}) copy-start(f32[384,128]{1,0:T(8,128)} %refs_2_.1) | copy-start | bytes 589828
  120.9 1.2 copy-start.4
  123.9 8.1 %collective-permute-start.26 = (f32[384,128]{1,0:T(8,128)}, f32[384,128]{1,0:T(8,128)S(1)}, u32[]{:S(2)}, u32[]{:S(2)}) collective-permute-start(f32[384,128]{1,0:T(8,128)} %shard_map.100), channel_id=1, source_target_pairs={{0,1},{1,2},{2,3},{3,4},{4,5},{5,6},{6,7},{7,8},{8,9},{9,10},{10,1... | collective-permute-start | bytes 589832 | tf_op jit(solution)/shard_map/ppermute | solution.py:315

commit v5 on v4

--- a/solution.py
+++ b/solution.py
@@ -38,16 +38,16 @@
     return lax.fori_loop(0, 3, step, value, unroll=not rolled)
 
 
-def staged(body, stride, inputs, outputs, products):
+def staged(body, stride, inputs, outputs, products, dtype=F32):
     def kernel(*refs):
         body(lax.axis_index("sec") // stride, *refs)
 
     vmem = pl.BlockSpec(memory_space=pltpu.VMEM)
-    side = inputs[0].shape[0]
+    side = inputs[0].shape[-1]
     moved_bytes = 4 * side * side * (len(inputs) + len(outputs))
     return pl.pallas_call(
         kernel,
-        out_shape=[jax.ShapeDtypeStruct(shape, F32) for shape in outputs],
+        out_shape=[jax.ShapeDtypeStruct(shape, dtype) for shape in outputs],
         in_specs=[vmem] * len(inputs),
         out_specs=[vmem] * len(outputs),
         compiler_params=pltpu.CompilerParams(vmem_limit_bytes=24 * 2**20),
@@ -64,8 +64,12 @@
     k = position // stride
     square, field = front_reflect.shape[1:], incident.shape
 
-    def moved(value, routes):
-        pairs = [(a * stride + i, b * stride + i) for a, b in routes for i in range(stride)]
+    def moved(value, routes, start=0, step=1):
+        pairs = [
+            (a * stride + i, b * stride + i)
+            for a, b in routes
+            for i in range(start, stride, step)
+        ]
         return lax.ppermute(value, "sec", pairs)
 
     r, t, q, u = front_reflect[0], front_through[0], back_reflect[0], back_through[0]
@@ -136,6 +140,20 @@
     (q1, hu) = staged(forward_q, stride, [q0, r, t, q, u], [square] * 2, 6)
     qa = moved(q1, low)
 
+    def split_maps(d, maps, out):
+        @pl.loop(0, depth_maps.shape[1])
+        def _(j):
+            out[j] = left(maps[j])
+
+    (maps,) = staged(
+        split_maps,
+        1,
+        [depth_maps[0]],
+        [depth_maps.shape[1:3] + (3 * square[1],)],
+        0.1,
+        jnp.bfloat16,
+    )
+
 
     def forward_t(k, q0, t0, r, t, t1, rgt):
         @pl.when((k > 1) & (k < 6))
@@ -238,27 +256,32 @@
 
     (q2, hu2) = staged(second_q, stride, [r1, qa, q1, t1, both], [square] * 2, 6)
 
-    def second_fields(k, qa, fa, r1, t1, f2, rg2):
-        @pl.when((k == 2) | (k == 3))
-        def _():
-            g = summed(product(qa[...], r1[...]), fa[...])
+    def second_fields(k, qa, fa, r1, t1, f2, g2):
+        @pl.when((k == 2) | (k == 3))
+        def _():
+            g = summed(product(qa[...], r1[...]), fa[...], True)
+            g2[...] = g
             f2[...] = product(t1[...], g)
-            rg2[...] = product(r1[...], g)
-
-    (f2, rg2) = staged(second_fields, stride, [qa, fa, r1, t1], [field, field], 2)
-
-    def third_fields(k, r_late, r_next, w_came, q1, t1, both, r1, qa, fa, w4, rg4):
+
+    (f2, g2) = staged(second_fields, stride, [qa, fa, r1, t1], [field, field], 2)
+
+    def third_fields(k, r_late, r_next, w_came, q1, t1, both, r1, qa, fa, w4, g4, rc4):
         @pl.when((k == 2) | (k == 3))
         def _():
             came = jnp.where(k == 2, r_late[...], r_next[...]) + w_came[...]
             gt = summed(product(q1[...], came), t1[...], True)
             rc = r1[...] + product(both[:, : q1.shape[1]], product(came, gt))
-            g = summed(product(qa[...], rc), fa[...])
+            rc4[...] = rc
+            g = summed(product(qa[...], rc), fa[...], True)
+            g4[...] = g
             w4[...] = product(gt, g)
-            rg4[...] = product(rc, g)
-
-    (w4, rg4) = staged(
-        third_fields, stride, [r_late, r_next, w_came, q1, t1, both, r1, qa, fa], [field] * 2, 9
+
+    (w4, g4, rc4) = staged(
+        third_fields,
+        stride,
+        [r_late, r_next, w_came, q1, t1, both, r1, qa, fa],
+        [field, field, square],
+        9,
     )
     w4_came = moved(w4, [(2, 4), (3, 5)])
 
@@ -269,31 +292,49 @@
 
     (t2,) = staged(second_through, stride, [t, gt_came, gt2_came], [square], 2)
 
-    def last_fields(k, r_late, r_next, total_came, q2, f2, g6, rg6):
+    def last_fields(k, r_late, r_next, total_came, q2, f2, g6):
         @pl.when((k == 2) | (k == 3))
         def _():
             rc = jnp.where(k == 2, r_late[...], r_next[...]) + total_came[...]
-            g = summed(product(q2[...], rc), f2[...])
-            g6[...] = g
-            rg6[...] = product(rc, g)
-
-    (g6, rg6) = staged(last_fields, stride, [r_late, r_next, total_came, q2, f2], [field] * 2, 3
-    )
-    g6_came = moved(g6, [(2, 6), (3, 7)])
-
-    def all_reflected(k, ua, rg2, rg4, rg6, hu2, s2, s4, s6):
-        @pl.when((k == 2) | (k == 3))
-        def _():
-            sums = rg2[...] + product(hu2[...], rg6[...])
-            value = product(ua[:, : hu2.shape[1]], jnp.concatenate([rg2[...], rg4[...], sums], axis=1))
+            g6[...] = summed(product(q2[...], rc), f2[...])
+
+    (g6,) = staged(last_fields, stride, [r_late, r_next, total_came, q2, f2], [field], 3)
+    g6_odd = moved(g6, [(2, 6), (3, 7)], 1, 2)
+    g6_even = moved(g6, [(2, 6), (3, 7)], 0, 2)
+
+    def passed(value, choose):
+        pairs = [(i, i + 1) for i in range(length - 1) if choose(i)]
+        return lax.ppermute(value, "sec", pairs)
+
+    half = NODES // 2 * stride
+    next_low = passed(jnp.where(k < 2, f1, f2), lambda i: i < half)
+
+    def all_reflected(
+        k, ua, r1, g2, rc4, g4, r_late, r_next, total_came, g6, hu2, s2, s4, s6
+    ):
+        @pl.when((k == 2) | (k == 3))
+        def _():
+            rc = jnp.where(k == 2, r_late[...], r_next[...]) + total_came[...]
+            rg2 = product(r1[...], g2[...])
+            rg4 = product(rc4[...], g4[...])
+            sums = rg2 + product(hu2[...], product(rc, g6[...]))
+            value = product(ua[:, : hu2.shape[1]], jnp.concatenate([rg2, rg4, sums], axis=1))
             for i, out in enumerate((s2, s4, s6)):
                 out[...] = ua[:, hu2.shape[1] :] + value[:, i * width : (i + 1) * width]
 
-    (s2, s4, s6) = staged(all_reflected, stride, [ua, rg2, rg4, rg6, hu2], [field] * 3, 2)
+    (s2, s4, s6) = staged(
+        all_reflected,
+        stride,
+        [ua, r1, g2, rc4, g4, r_late, r_next, total_came, g6, hu2],
+        [field] * 3,
+        3,
+    )
     s6_came = moved(s6, [(2, 6), (3, 7)])
     s4_came = moved(s4, [(2, 4), (3, 5)])
 
-    def through(k, f1, f2, t1, w4, t2, g6, out):
+    def through_odd(d, f1, f2, t1, w4, t2, g6, out):
+        k = d // stride
+
         @pl.when(k < 2)
         def _():
             out[...] = f1[...]
@@ -306,25 +347,44 @@
         def _():
             out[...] = product(t1[...], w4[...])
 
-        @pl.when(k > 5)
+        @pl.when((k > 5) & (d % 2 == 1))
         def _():
             out[...] = product(t2[...], g6[...])
 
-    (through_field,) = staged(through, stride, [f1, f2, t1, w4_came, t2, g6_came], [field], 1
-    )
-    entering = lax.ppermute(through_field, "sec", [(i, i + 1) for i in range(length - 1)])
+    (odd,) = staged(through_odd, 1, [f1, f2, t1, w4_came, t2, g6_odd], [field], 1)
+    next_odd = passed(odd, lambda i: i >= half and i % 2 == 1)
+
+    def through_even(d, odd, t2, g6, out):
+        k = d // stride
+        late = (k > 5) & (d % 2 == 0)
+
+        @pl.when(late)
+        def _():
+            out[...] = product(t2[...], g6[...])
+
+        @pl.when(jnp.logical_not(late))
+        def _():
+            out[...] = odd[...]
+
+    (through_field,) = staged(through_even, 1, [odd, t2, g6_even], [field], 1)
+    next_even = passed(through_field, lambda i: i >= half and i % 2 == 0)
     reflected = jnp.where(
         k < 2, both[:, square[1] :], jnp.where(k < 4, s2, jnp.where(k < 6, s4_came, s6_came))
     )
 
-    def depths(place, maps, entering, incident, out):
-        value = right(jnp.where(place == 0, incident[...], entering[...]))
-        for j in range(depth_maps.shape[1]):
-            out[j] = jnp.dot(left(maps[j]), value, preferred_element_type=F32)
-
-    (depth_fields,) = staged(depths,
+    def depths(d, maps, low, odd, even, incident, out):
+        came = jnp.where(d % 2 == 1, even[...], odd[...])
+        came = jnp.where(d <= half, low[...], came)
+        value = right(jnp.where(d == 0, incident[...], came))
+
+        @pl.loop(0, depth_maps.shape[1])
+        def _(j):
+            out[j] = jnp.dot(maps[j], value, preferred_element_type=F32)
+
+    (depth_fields,) = staged(
+        depths,
         1,
-        [depth_maps[0], entering, incident],
+        [maps, next_low, next_odd, next_even, incident],
         [depth_maps.shape[1:3] + field[1:]],
         1,
     )

time: 135 us -> 135 us (level)
  the two profiles are of different devices: /device:TPU:12 before, /device:TPU:30 now
where the time goes in v5:
time: 135 us; the launch traced here: 134 us
  waiting for transfers between devices  64.5 us (48%)
  starting transfers between devices  42.9 us (32%)
  Pallas kernels  18.8 us (14%)
  local copies, waits for them, and re-layouts  5.55 us (4%)
  other arithmetic  1.66 us (1%)
    ppermute x27, waiting for transfers between devices, moved(): return lax.ppermute(value, 'sec', pairs)  64.5 us
    ppermute x27, starting transfers between devices, moved(): return lax.ppermute(value, 'sec', pairs)  39.6 us
    pallas_call x20, Pallas kernels, staged(): pl.pallas_call(kernel, out_shape=[jax.ShapeDtypeStruct(shape, dtype) for...  18.8 us
    unnamed x38, local copies, waits for them, and re-layouts  5.55 us
    ppermute x3, starting transfers between devices, passed(): return lax.ppermute(value, 'sec', pairs)  3.25 us
  transfers between devices with their start and end apart: 30, of which 7 were waited for; matrix products, arithmetic and copies ran while one was open for 1% of the time, Pallas kernels for 12%

profile of v5, /device:TPU:30, one launch (start us, length us, event | category | flops | bytes accessed | tf_op | source)
XLA Modules:
  0.0 134.4 jit_solution(3694741811584287821)
XLA Ops:
  0.6 2.4 %collective-permute-start.7 = (f32[384,384]{1,0:T(8,128)}, f32[384,384]{1,0:T(8,128)S(1)}, u32[]{:S(2)}, u32[]{:S(2)}) collective-permute-start(f32[384,384]{1,0:T(8,128)} %bitcast.refs_0_), channel_id=1, source_target_pairs={{28,24},{29,25},{30,26},{31,27},{24,28},{25,29},{26,30},{27,31},{4... | collective-permute-start | bytes 1769480 | tf_op jit(solution)/shard_map/ppermute | solution.py:73
  3.1 0.9 copy-done.9
  4.0 1.8 %shard_map.85 = (f32[384,384]{1,0:T(8,128)S(1)}, f32[384,384]{1,0:T(8,128)S(1)}, f32[384,384]{1,0:T(8,128)S(1)}, f32[384,384]{1,0:T(8,128)S(1)}, f32[384,256]{1,0:T(8,128)S(1)}) custom-call(f32[384,384]{1,0:T(8,128)} %bitcast.refs_0_, f32[384,384]{1,0:T(8,128)} %bitcast.1.refs_1_, f32[384,384]{1,0:T(8,128)} %bitcast.2.refs_2_, f32[384,384]{1,0:T(8,128)} %bitcast.3.refs_3_, ...), custom_call_target="tpu_custom_call" | custom-call | flops 339738624 | bytes 5898240 | tf_op jit(solution)/shard_map/pallas_call | solution.py:48
  6.4 0.7 collective-permute-start.1
  7.1 0.7 collective-permute-start.12
  7.8 0.7 collective-permute-start.10
  8.6 9.3 %collective-permute-done.7.refs_0_ = f32[384,384]{1,0:T(8,128)S(1)} collective-permute-done((f32[384,384]{1,0:T(8,128)}, f32[384,384]{1,0:T(8,128)S(1)}, u32[]{:S(2)}, u32[]{:S(2)}) %collective-permute-start.7) | collective-permute-done | bytes 589856 | tf_op jit(solution)/shard_map/ppermute | solution.py:73
  18.6 1.9 %collective-permute-start.8 = (f32[384,384]{1,0:T(8,128)S(1)}, f32[384,384]{1,0:T(8,128)S(1)}, u32[]{:S(2)}, u32[]{:S(2)}) collective-permute-start(f32[384,384]{1,0:T(8,128)S(1)} %get-tuple-element.41), channel_id=1, source_target_pairs={{24,28},{25,29},{26,30},{27,31},{28,20},{29,21},{30,22},{31,23},{0... | collective-permute-start | bytes 1769480 | tf_op jit(solution)/shard_map/ppermute | solution.py:73
  20.5 0.7 collective-permute-start.9
  21.2 0.7 collective-permute-start.15
  21.9 0.7 collective-permute-start.5
  22.7 0.7 collective-permute-start.13
  23.4 13.5 %collective-permute-done.8.refs_1_.refs_0_ = f32[384,384]{1,0:T(8,128)S(1)} collective-permute-done((f32[384,384]{1,0:T(8,128)S(1)}, f32[384,384]{1,0:T(8,128)S(1)}, u32[]{:S(2)}, u32[]{:S(2)}) %collective-permute-start.8) | collective-permute-done | bytes 589856 | tf_op jit(solution)/shard_map/ppermute | solution.py:73
  37.6 0.9 shard_map.87
  38.5 0.8 copy-done.13
  39.4 0.7 collective-permute-start.14
  40.1 13.2 %collective-permute-start.19 = (f32[384,384]{1,0:T(8,128)S(1)}, f32[384,384]{1,0:T(8,128)S(1)}, u32[]{:S(2)}, u32[]{:S(2)}) collective-permute-start(f32[384,384]{1,0:T(8,128)S(1)} %get-tuple-element.53), channel_id=1, source_target_pairs={{20,16},{21,17},{22,18},{23,19},{28,20},{29,21},{30,22},{31,23}} | collective-permute-start | bytes 1769480 | tf_op jit(solution)/shard_map/ppermute | solution.py:73
  53.3 0.7 collective-permute-start.6
  54.0 1.0 shard_map.93
  55.0 1.5 %collective-permute-start.2 = (f32[384,384]{1,0:T(8,128)}, f32[384,384]{1,0:T(8,128)}, u32[]{:S(2)}, u32[]{:S(2)}) collective-permute-start(f32[384,384]{1,0:T(8,128)} %get-tuple-element.40.refs_3_.refs_1_.refs_2_), channel_id=1, source_target_pairs={{0,8},{1,9},{2,10},{3,11},{4,12},{5,13},{6,14},{7,15}} | collective-permute-start | bytes 1769480 | tf_op jit(solution)/shard_map/ppermute | solution.py:73
  56.5 1.5 %collective-permute-start.16 = (f32[384,384]{1,0:T(8,128)}, f32[384,384]{1,0:T(8,128)}, u32[]{:S(2)}, u32[]{:S(2)}) collective-permute-start(f32[384,384]{1,0:T(8,128)} %get-tuple-element.48.refs_4_), channel_id=1, source_target_pairs={{16,8},{17,9},{18,10},{19,11},{20,12},{21,13},{22,14},{23,15}} | collective-permute-start | bytes 1769480 | tf_op jit(solution)/shard_map/ppermute | solution.py:73
  58.0 0.9 shard_map.90
  58.8 0.9 copy-done.7
  60.4 3.6 %collective-permute-done.19.refs_0_ = f32[384,384]{1,0:T(8,128)S(1)} collective-permute-done((f32[384,384]{1,0:T(8,128)S(1)}, f32[384,384]{1,0:T(8,128)S(1)}, u32[]{:S(2)}, u32[]{:S(2)}) %collective-permute-start.19) | collective-permute-done | bytes 589856 | tf_op jit(solution)/shard_map/ppermute | solution.py:73
  64.0 1.6 %collective-permute-start.24 = (f32[384,512]{1,0:T(8,128)}, f32[384,512]{1,0:T(8,128)}, u32[]{:S(2)}, u32[]{:S(2)}) collective-permute-start(f32[384,512]{1,0:T(8,128)} %get-tuple-element.49.refs_5_.refs_4_), channel_id=1, source_target_pairs={{0,8},{1,9},{2,10},{3,11},{4,12},{5,13},{6,14},{7,15}} | collective-permute-start | bytes 2359304 | tf_op jit(solution)/shard_map/ppermute | solution.py:73
  65.6 2.2 %shard_map.96 = (f32[384,384]{1,0:T(8,128)}, f32[384,384]{1,0:T(8,128)S(1)}) custom-call(f32[384,384]{1,0:T(8,128)S(1)} %collective-permute-done.19.refs_0_, f32[384,384]{1,0:T(8,128)} %get-tuple-element.40.refs_3_.refs_1_.refs_2_, f32[384,384]{1,0:T(8,128)S(1)} %get-tuple-element.46.refs_3_.refs_4_.refs_2_, f32[384,384]{1,0:T(8,128)S(1)} %get-tuple-element.54.refs_3_, ...), custom_call_target="tpu_custom_call" | custom-call | flops 2038431744 | bytes 4128768 | tf_op jit(solution)/shard_map/pallas_call | solution.py:48
  67.8 0.9 copy-done.17
  68.7 0.8 copy-done.5
  69.5 1.5 %collective-permute-start.21 = (f32[384,384]{1,0:T(8,128)}, f32[384,384]{1,0:T(8,128)}, u32[]{:S(2)}, u32[]{:S(2)}) collective-permute-start(f32[384,384]{1,0:T(8,128)} %get-tuple-element.56), channel_id=1, source_target_pairs={{16,8},{17,9},{18,10},{19,11},{20,12},{21,13},{22,14},{23,15}} | collective-permute-start | bytes 1769480 | tf_op jit(solution)/shard_map/ppermute | solution.py:73
  72.6 1.3 collective-permute-start.18
  73.9 1.3 collective-permute-start.20
  75.3 1.7 %shard_map.94 = (f32[384,128]{1,0:T(8,128)S(1)}, f32[384,128]{1,0:T(8,128)S(1)}, f32[384,384]{1,0:T(8,128)S(1)}) custom-call(f32[384,384]{1,0:T(8,128)S(1)} %copy-done.12, f32[384,384]{1,0:T(8,128)S(1)} %copy-done.16, f32[384,384]{1,0:T(8,128)} %collective-permute-done.16.refs_2_, f32[384,384]{1,0:T(8,128)} %get-tuple-element.40.refs_3_.refs_1_.refs_2_, ...), custom_call_target="tpu_custom_call" | custom-call | flops 3057647616 | bytes 7077888 | tf_op jit(solution)/shard_map/pallas_call | solution.py:48
  77.6 1.1 shard_map.92
  78.7 1.5 %shard_map.98 = (f32[384,384]{1,0:T(8,128)S(1)}, f32[384,384]{1,0:T(8,128)S(1)}) custom-call(f32[384,384]{1,0:T(8,128)S(1)} %shard_map.91.refs_2_.refs_6_.refs_0_.refs_1_, f32[384,384]{1,0:T(8,128)} %collective-permute-done.2.refs_0_.refs_7_.refs_1_, f32[384,384]{1,0:T(8,128)} %get-tuple-element.40.refs_3_.refs_1_.refs_2_, f32[384,384]{1,0:T(8,128)S(1)} %copy-done.2, ...), custom_call_target="tpu_custom_call" | custom-call | flops 2038431744 | bytes 4128768 | tf_op jit(solution)/shard_map/pallas_call | solution.py:48
  80.2 1.1 shard_map.99.refs_8_
  81.9 1.3 collective-permute-start.23
  83.2 1.3 shard_map.102
  84.5 2.5 %collective-permute-done.18.refs_1_ = f32[384,384]{1,0:T(8,128)S(1)} collective-permute-done((f32[384,384]{1,0:T(8,128)S(1)}, f32[384,384]{1,0:T(8,128)S(1)}, u32[]{:S(2)}, u32[]{:S(2)}) %collective-permute-start.18) | collective-permute-done | bytes 589856 | tf_op jit(solution)/shard_map/ppermute | solution.py:73
  87.7 18.7 %collective-permute-done.20.refs_2_ = f32[384,384]{1,0:T(8,128)S(1)} collective-permute-done((f32[384,384]{1,0:T(8,128)S(1)}, f32[384,384]{1,0:T(8,128)S(1)}, u32[]{:S(2)}, u32[]{:S(2)}) %collective-permute-start.20) | collective-permute-done | bytes 589856 | tf_op jit(solution)/shard_map/ppermute | solution.py:73
  106.4 1.3 collective-permute-start.26
  107.7 1.3 shard_map.97.refs_4_.refs_1_
  109.8 1.3 collective-permute-start.28
  111.1 12.2 %collective-permute-done.23.refs_2_ = f32[384,128]{1,0:T(8,128)S(1)} collective-permute-done((f32[384,128]{1,0:T(8,128)S(1)}, f32[384,128]{1,0:T(8,128)S(1)}, u32[]{:S(2)}, u32[]{:S(2)}) %collective-permute-start.23) | collective-permute-done | bytes 196640 | tf_op jit(solution)/shard_map/ppermute | solution.py:73
  123.3 1.1 shard_map.101
  124.4 1.3 collective-permute-start.29
  125.7 4.6 %collective-permute-done.26 = f32[384,128]{1,0:T(8,128)S(1)} collective-permute-done((f32[384,128]{1,0:T(8,128)S(1)}, f32[384,128]{1,0:T(8,128)S(1)}, u32[]{:S(2)}, u32[]{:S(2)}) %collective-permute-start.26) | collective-permute-done | bytes 196640 | tf_op jit(solution)/shard_map/ppermute | solution.py:73
  130.2 1.6 %select_bitcast_fusion = f32[1,384,128]{2,1,0:T(8,128)} fusion(f32[384,128]{1,0:T(8,128)S(1)} %get-tuple-element.62, f32[384,128]{1,0:T(8,128)S(1)} %collective-permute-done.25, f32[384,128]{1,0:T(8,128)S(1)} %collective-permute-done.26, f32[384,512]{1,0:T(8,128)} %get-tuple-element.49.refs_5_.refs_4_, pred[]{:T(512)S(6)} %lt.12, pred[]{:T(512)S(6)} %lt.11, ...), kind=kLoop, calls=%fused_computation | loop fusion | flops 147456 | bytes 983043 | tf_op jit(solution)/shard_map/broadcast_in_dim | solution.py:391
  131.9 2.6 %shard_map.104 = f32[4,384,128]{2,1,0:T(8,128)} custom-call(bf16[4,384,1152]{2,1,0:T(8,128)(2,1)S(1)} %shard_map.103.refs_0_, f32[384,128]{1,0:T(8,128)S(1)} %collective-permute-done.27.refs_1_, f32[384,128]{1,0:T(8,128)S(1)} %collective-permute-done.28.refs_2_, f32[384,128]{1,0:T(8,128)S(1)} %collective-permute-done.29.refs_3_, f32[384,128]{1,0:T(8,128)S(1)} %copy-done.10), custom_call_target="tpu_custom_call" | custom-call | flops 9172942848 | bytes 31850496 | tf_op jit(solution)/shard_map/pallas_call | solution.py:48
  (72 shorter events, 7.2 us)
Async XLA Ops:
  0.6 17.2 %collective-permute-start.7 = (f32[384,384]{1,0:T(8,128)}, f32[384,384]{1,0:T(8,128)S(1)}, u32[]{:S(2)}, u32[]{:S(2)}) collective-permute-start(f32[384,384]{1,0:T(8,128)} %bitcast.refs_0_), channel_id=1, source_target_pairs={{28,24},{29,25},{30,26},{31,27},{24,28},{25,29},{26,30},{27,31},{4... | collective-permute-start | bytes 1769480 | tf_op jit(solution)/shard_map/ppermute | solution.py:73
  3.1 0.9 copy-start.9
  5.7 12.8 %collective-permute-start = (f32[384,256]{1,0:T(8,128)S(1)}, f32[384,256]{1,0:T(8,128)S(1)}, u32[]{:S(2)}, u32[]{:S(2)}) collective-permute-start(f32[384,256]{1,0:T(8,128)S(1)} %get-tuple-element.34.refs_0_.refs_6_), channel_id=1, source_target_pairs={{0,4},{1,5},{2,6},{3,7}} | collective-permute-start | bytes 1179656 | tf_op jit(solution)/shard_map/ppermute | solution.py:73
  6.4 14.1 %collective-permute-start.1 = (f32[384,384]{1,0:T(8,128)}, f32[384,384]{1,0:T(8,128)S(1)}, u32[]{:S(2)}, u32[]{:S(2)}) collective-permute-start(f32[384,384]{1,0:T(8,128)} %bitcast.2.refs_2_), channel_id=1, source_target_pairs={{0,4},{1,5},{2,6},{3,7},{4,8},{5,9},{6,10},{7,11},{8,12},{9,13},{1... | collective-permute-start | bytes 1769480 | tf_op jit(solution)/shard_map/ppermute | solution.py:73
  7.1 14.1 %collective-permute-start.12 = (f32[384,384]{1,0:T(8,128)}, f32[384,384]{1,0:T(8,128)S(1)}, u32[]{:S(2)}, u32[]{:S(2)}) collective-permute-start(f32[384,384]{1,0:T(8,128)} %bitcast.1.refs_1_), channel_id=1, source_target_pairs={{4,8},{5,9},{6,10},{7,11},{8,12},{9,13},{10,14},{11,15},{12,16},{1... | collective-permute-start | bytes 1769480 | tf_op jit(solution)/shard_map/ppermute | solution.py:73
  7.8 14.8 %collective-permute-start.10 = (f32[384,384]{1,0:T(8,128)}, f32[384,384]{1,0:T(8,128)S(1)}, u32[]{:S(2)}, u32[]{:S(2)}) collective-permute-start(f32[384,384]{1,0:T(8,128)} %bitcast.3.refs_3_), channel_id=1, source_target_pairs={{4,0},{5,1},{6,2},{7,3}} | collective-permute-start | bytes 1769480 | tf_op jit(solution)/shard_map/ppermute | solution.py:73
  17.8 4.1 %collective-permute-start.4 = (f32[384,384]{1,0:T(8,128)}, f32[384,384]{1,0:T(8,128)S(1)}, u32[]{:S(2)}, u32[]{:S(2)}) collective-permute-start(f32[384,384]{1,0:T(8,128)} %bitcast.refs_0_), channel_id=1, source_target_pairs={{8,0},{9,1},{10,2},{11,3}} | collective-permute-start | bytes 1769480 | tf_op jit(solution)/shard_map/ppermute | solution.py:73
  18.6 18.3 %collective-permute-start.8 = (f32[384,384]{1,0:T(8,128)S(1)}, f32[384,384]{1,0:T(8,128)S(1)}, u32[]{:S(2)}, u32[]{:S(2)}) collective-permute-start(f32[384,384]{1,0:T(8,128)S(1)} %get-tuple-element.41), channel_id=1, source_target_pairs={{24,28},{25,29},{26,30},{27,31},{28,20},{29,21},{30,22},{31,23},{0... | collective-permute-start | bytes 1769480 | tf_op jit(solution)/shard_map/ppermute | solution.py:73
  20.5 18.8 %collective-permute-start.9 = (f32[384,384]{1,0:T(8,128)}, f32[384,384]{1,0:T(8,128)S(1)}, u32[]{:S(2)}, u32[]{:S(2)}) collective-permute-start(f32[384,384]{1,0:T(8,128)} %bitcast.3.refs_3_), channel_id=1, source_target_pairs={{0,4},{1,5},{2,6},{3,7},{8,12},{9,13},{10,14},{11,15}} | collective-permute-start | bytes 1769480 | tf_op jit(solution)/shard_map/ppermute | solution.py:73
  21.2 18.8 %collective-permute-start.15 = (f32[384,384]{1,0:T(8,128)}, f32[384,384]{1,0:T(8,128)S(1)}, u32[]{:S(2)}, u32[]{:S(2)}) collective-permute-start(f32[384,384]{1,0:T(8,128)} %bitcast.3.refs_3_), channel_id=1, source_target_pairs={{12,16},{13,17},{14,18},{15,19},{16,20},{17,21},{18,22},{19,23}} | collective-permute-start | bytes 1769480 | tf_op jit(solution)/shard_map/ppermute | solution.py:73
  21.9 31.3 %collective-permute-start.5 = (f32[384,384]{1,0:T(8,128)S(1)}, f32[384,384]{1,0:T(8,128)S(1)}, u32[]{:S(2)}, u32[]{:S(2)}) collective-permute-start(f32[384,384]{1,0:T(8,128)S(1)} %collective-permute-done.4), channel_id=1, source_target_pairs={{0,4},{1,5},{2,6},{3,7}} | collective-permute-start | bytes 1769480 | tf_op jit(solution)/shard_map/ppermute | solution.py:73
  22.7 32.3 %collective-permute-start.13 = (f32[384,384]{1,0:T(8,128)}, f32[384,384]{1,0:T(8,128)S(1)}, u32[]{:S(2)}, u32[]{:S(2)}) collective-permute-start(f32[384,384]{1,0:T(8,128)} %bitcast.refs_0_), channel_id=1, source_target_pairs={{12,8},{13,9},{14,10},{15,11}} | collective-permute-start | bytes 1769480 | tf_op jit(solution)/shard_map/ppermute | solution.py:73
  36.9 1.6 %copy-start.3 = (f32[384,384]{1,0:T(8,128)}, f32[384,384]{1,0:T(8,128)S(1)}, u32[]{:S(2)}) copy-start(f32[384,384]{1,0:T(8,128)S(1)} %collective-permute-done.8.refs_1_.refs_0_) | copy-start | bytes 1769476
  36.9 19.6 %collective-permute-start.11 = (f32[384,384]{1,0:T(8,128)S(1)}, f32[384,384]{1,0:T(8,128)S(1)}, u32[]{:S(2)}, u32[]{:S(2)}) collective-permute-start(f32[384,384]{1,0:T(8,128)S(1)} %collective-permute-done.10), channel_id=1, source_target_pairs={{0,8},{1,9},{2,10},{3,11}} | collective-permute-start | bytes 1769480 | tf_op jit(solution)/shard_map/ppermute | solution.py:73
  38.5 0.8 copy-start.13
  39.4 20.4 %collective-permute-start.14 = (f32[384,384]{1,0:T(8,128)}, f32[384,384]{1,0:T(8,128)S(1)}, u32[]{:S(2)}, u32[]{:S(2)}) collective-permute-start(f32[384,384]{1,0:T(8,128)} %bitcast.refs_0_), channel_id=1, source_target_pairs={{16,12},{17,13},{18,14},{19,15}} | collective-permute-start | bytes 1769480 | tf_op jit(solution)/shard_map/ppermute | solution.py:73
  40.1 24.0 %collective-permute-start.19 = (f32[384,384]{1,0:T(8,128)S(1)}, f32[384,384]{1,0:T(8,128)S(1)}, u32[]{:S(2)}, u32[]{:S(2)}) collective-permute-start(f32[384,384]{1,0:T(8,128)S(1)} %get-tuple-element.53), channel_id=1, source_target_pairs={{20,16},{21,17},{22,18},{23,19},{28,20},{29,21},{30,22},{31,23}} | collective-permute-start | bytes 1769480 | tf_op jit(solution)/shard_map/ppermute | solution.py:73
  53.3 12.4 %copy-start.1 = (f32[384,384]{1,0:T(8,128)}, f32[384,384]{1,0:T(8,128)S(1)}, u32[]{:S(2)}) copy-start(f32[384,384]{1,0:T(8,128)S(1)} %get-tuple-element.46.refs_3_.refs_4_.refs_2_) | copy-start | bytes 1769476
  53.3 15.5 %collective-permute-start.6 = (f32[384,384]{1,0:T(8,128)S(1)}, f32[384,384]{1,0:T(8,128)S(1)}, u32[]{:S(2)}, u32[]{:S(2)}) collective-permute-start(f32[384,384]{1,0:T(8,128)S(1)} %collective-permute-done.5), channel_id=1, source_target_pairs={{4,12},{5,13},{6,14},{7,15}} | collective-permute-start | bytes 1769480 | tf_op jit(solution)/shard_map/ppermute | solution.py:73
  55.0 12.8 %copy-start.11 = (f32[384,384]{1,0:T(8,128)}, f32[384,384]{1,0:T(8,128)S(1)}, u32[]{:S(2)}) copy-start(f32[384,384]{1,0:T(8,128)S(1)} %collective-permute-done.13.refs_0_.refs_5_) | copy-start | bytes 1769476
  55.0 18.9 %collective-permute-start.2 = (f32[384,384]{1,0:T(8,128)}, f32[384,384]{1,0:T(8,128)}, u32[]{:S(2)}, u32[]{:S(2)}) collective-permute-start(f32[384,384]{1,0:T(8,128)} %get-tuple-element.40.refs_3_.refs_1_.refs_2_), channel_id=1, source_target_pairs={{0,8},{1,9},{2,10},{3,11},{4,12},{5,13},{6,14},{7,15}} | collective-permute-start | bytes 1769480 | tf_op jit(solution)/shard_map/ppermute | solution.py:73
  56.5 18.7 %collective-permute-start.16 = (f32[384,384]{1,0:T(8,128)}, f32[384,384]{1,0:T(8,128)}, u32[]{:S(2)}, u32[]{:S(2)}) collective-permute-start(f32[384,384]{1,0:T(8,128)} %get-tuple-element.48.refs_4_), channel_id=1, source_target_pairs={{16,8},{17,9},{18,10},{19,11},{20,12},{21,13},{22,14},{23,15}} | collective-permute-start | bytes 1769480 | tf_op jit(solution)/shard_map/ppermute | solution.py:73
  58.8 0.9 copy-start.7
  59.7 8.1 %copy-start.15 = (f32[384,384]{1,0:T(8,128)}, f32[384,384]{1,0:T(8,128)S(1)}, u32[]{:S(2)}) copy-start(f32[384,384]{1,0:T(8,128)S(1)} %collective-permute-done.14.refs_1_.refs_6_) | copy-start | bytes 1769476
  59.7 12.7 %collective-permute-start.3 = (f32[384,128]{1,0:T(8,128)S(1)}, f32[384,128]{1,0:T(8,128)S(1)}, u32[]{:S(2)}, u32[]{:S(2)}) collective-permute-start(f32[384,128]{1,0:T(8,128)S(1)} %get-tuple-element.37.refs_0_), channel_id=1, source_target_pairs={{0,8},{1,9},{2,10},{3,11},{4,12},{5,13},{6,14},{7,15}} | collective-permute-start | bytes 589832 | tf_op jit(solution)/shard_map/ppermute | solution.py:73
  64.0 17.8 %collective-permute-start.24 = (f32[384,512]{1,0:T(8,128)}, f32[384,512]{1,0:T(8,128)}, u32[]{:S(2)}, u32[]{:S(2)}) collective-permute-start(f32[384,512]{1,0:T(8,128)} %get-tuple-element.49.refs_5_.refs_4_), channel_id=1, source_target_pairs={{0,8},{1,9},{2,10},{3,11},{4,12},{5,13},{6,14},{7,15}} | collective-permute-start | bytes 2359304 | tf_op jit(solution)/shard_map/ppermute | solution.py:73
  65.6 5.4 %copy-start = (f32[1,4,384,384]{3,2,1,0:T(8,128)S(1)}, f32[1,4,384,384]{3,2,1,0:T(8,128)}, u32[]{:S(2)}) copy-start(f32[1,4,384,384]{3,2,1,0:T(8,128)} %param.10) | copy-start | bytes 7077892
  67.8 0.9 copy-start.17
  69.5 10.6 %collective-permute-start.21 = (f32[384,384]{1,0:T(8,128)}, f32[384,384]{1,0:T(8,128)}, u32[]{:S(2)}, u32[]{:S(2)}) collective-permute-start(f32[384,384]{1,0:T(8,128)} %get-tuple-element.56), channel_id=1, source_target_pairs={{16,8},{17,9},{18,10},{19,11},{20,12},{21,13},{22,14},{23,15}} | collective-permute-start | bytes 1769480 | tf_op jit(solution)/shard_map/ppermute | solution.py:73
  71.0 1.1 copy-start.4
  71.0 1.2 copy-start.6
  71.0 1.4 %copy-start.8 = (f32[384,384]{1,0:T(8,128)S(1)}, f32[384,384]{1,0:T(8,128)}, u32[]{:S(2)}) copy-start(f32[384,384]{1,0:T(8,128)} %copy-done.7) | copy-start | bytes 1769476
  71.0 1.6 %copy-start.14 = (f32[384,384]{1,0:T(8,128)S(1)}, f32[384,384]{1,0:T(8,128)}, u32[]{:S(2)}) copy-start(f32[384,384]{1,0:T(8,128)} %copy-done.13) | copy-start | bytes 1769476
  71.0 2.9 %copy-start.18 = (f32[384,384]{1,0:T(8,128)S(1)}, f32[384,384]{1,0:T(8,128)}, u32[]{:S(2)}) copy-start(f32[384,384]{1,0:T(8,128)} %copy-done.17) | copy-start | bytes 1769476
  71.0 4.2 %copy-start.2 = (f32[384,384]{1,0:T(8,128)S(1)}, f32[384,384]{1,0:T(8,128)}, u32[]{:S(2)}) copy-start(f32[384,384]{1,0:T(8,128)} %copy-done.1) | copy-start | bytes 1769476
  71.0 4.2 %copy-start.12 = (f32[384,384]{1,0:T(8,128)S(1)}, f32[384,384]{1,0:T(8,128)}, u32[]{:S(2)}) copy-start(f32[384,384]{1,0:T(8,128)} %copy-done.11) | copy-start | bytes 1769476
  71.1 4.2 %copy-start.16 = (f32[384,384]{1,0:T(8,128)S(1)}, f32[384,384]{1,0:T(8,128)}, u32[]{:S(2)}) copy-start(f32[384,384]{1,0:T(8,128)} %copy-done.15) | copy-start | bytes 1769476
  72.6 14.4 %collective-permute-start.18 = (f32[384,384]{1,0:T(8,128)S(1)}, f32[384,384]{1,0:T(8,128)S(1)}, u32[]{:S(2)}, u32[]{:S(2)}) collective-permute-start(f32[384,384]{1,0:T(8,128)S(1)} %copy-done.14), channel_id=1, source_target_pairs={{20,24},{21,25},{22,26},{23,27},{24,28},{25,29},{26,30},{27,31}} | collective-permute-start | bytes 1769480 | tf_op jit(solution)/shard_map/ppermute | solution.py:73
  73.9 32.5 %collective-permute-start.20 = (f32[384,384]{1,0:T(8,128)S(1)}, f32[384,384]{1,0:T(8,128)S(1)}, u32[]{:S(2)}, u32[]{:S(2)}) collective-permute-start(f32[384,384]{1,0:T(8,128)S(1)} %copy-done.18), channel_id=1, source_target_pairs={{16,24},{17,25},{18,26},{19,27},{20,28},{21,29},{22,30},{23,31}} | collective-permute-start | bytes 1769480 | tf_op jit(solution)/shard_map/ppermute | solution.py:73
  76.9 32.1 %collective-permute-start.17 = (f32[384,128]{1,0:T(8,128)S(1)}, f32[384,128]{1,0:T(8,128)S(1)}, u32[]{:S(2)}, u32[]{:S(2)}) collective-permute-start(f32[384,128]{1,0:T(8,128)S(1)} %get-tuple-element.50), channel_id=1, source_target_pairs={{8,16},{9,17},{10,18},{11,19},{12,20},{13,21},{14,22},{15,23}} | collective-permute-start | bytes 589832 | tf_op jit(solution)/shard_map/ppermute | solution.py:73
  81.2 28.5 %collective-permute-start.22 = (f32[384,128]{1,0:T(8,128)S(1)}, f32[384,128]{1,0:T(8,128)S(1)}, u32[]{:S(2)}, u32[]{:S(2)}) collective-permute-start(f32[384,128]{1,0:T(8,128)S(1)} %shard_map.99.refs_8_), channel_id=1, source_target_pairs={{9,25},{11,27},{13,29},{15,31}} | collective-permute-start | bytes 589832 | tf_op jit(solution)/shard_map/ppermute | solution.py:73
  81.9 41.4 %collective-permute-start.23 = (f32[384,128]{1,0:T(8,128)S(1)}, f32[384,128]{1,0:T(8,128)S(1)}, u32[]{:S(2)}, u32[]{:S(2)}) collective-permute-start(f32[384,128]{1,0:T(8,128)S(1)} %shard_map.99.refs_8_), channel_id=1, source_target_pairs={{8,24},{10,26},{12,28},{14,30}} | collective-permute-start | bytes 589832 | tf_op jit(solution)/shard_map/ppermute | solution.py:73
  87.0 38.7 %collective-permute-start.25 = (f32[384,128]{1,0:T(8,128)S(1)}, f32[384,128]{1,0:T(8,128)S(1)}, u32[]{:S(2)}, u32[]{:S(2)}) collective-permute-start(f32[384,128]{1,0:T(8,128)S(1)} %get-tuple-element.63), channel_id=1, source_target_pairs={{8,16},{9,17},{10,18},{11,19},{12,20},{13,21},{14,22},{15,23}} | collective-permute-start | bytes 589832 | tf_op jit(solution)/shard_map/ppermute | solution.py:73
  106.4 23.8 %collective-permute-start.26 = (f32[384,128]{1,0:T(8,128)S(1)}, f32[384,128]{1,0:T(8,128)S(1)}, u32[]{:S(2)}, u32[]{:S(2)}) collective-permute-start(f32[384,128]{1,0:T(8,128)S(1)} %get-tuple-element.64), channel_id=1, source_target_pairs={{8,24},{9,25},{10,26},{11,27},{12,28},{13,29},{14,30},{15,31}} | collective-permute-start | bytes 589832 | tf_op jit(solution)/shard_map/ppermute | solution.py:73
  107.7 24.2 %copy-start.10 = (f32[384,128]{1,0:T(8,128)S(1)}, f32[384,128]{1,0:T(8,128)}, u32[]{:S(2)}) copy-start(f32[384,128]{1,0:T(8,128)} %refs_4_.3) | copy-start | bytes 589828
  109.0 22.9 %collective-permute-start.27 = (f32[384,128]{1,0:T(8,128)S(1)}, f32[384,128]{1,0:T(8,128)S(1)}, u32[]{:S(2)}, u32[]{:S(2)}) collective-permute-start(f32[384,128]{1,0:T(8,128)S(1)} %broadcast_select_fusion), channel_id=1, source_target_pairs={{0,1},{1,2},{2,3},{3,4},{4,5},{5,6},{6,7},{7,8},{8,9},{9,10},{10,1... | collective-permute-start | bytes 589832 | tf_op jit(solution)/shard_map/ppermute | solution.py:307
  109.8 22.1 %collective-permute-start.28 = (f32[384,128]{1,0:T(8,128)S(1)}, f32[384,128]{1,0:T(8,128)S(1)}, u32[]{:S(2)}, u32[]{:S(2)}) collective-permute-start(f32[384,128]{1,0:T(8,128)S(1)} %shard_map.100.refs_0_), channel_id=1, source_target_pairs={{17,18},{19,20},{21,22},{23,24},{25,26},{27,28},{29,30}} | collective-permute-start | bytes 589832 | tf_op jit(solution)/shard_map/ppermute | solution.py:307
  124.4 7.5 %collective-permute-start.29 = (f32[384,128]{1,0:T(8,128)}, f32[384,128]{1,0:T(8,128)S(1)}, u32[]{:S(2)}, u32[]{:S(2)}) collective-permute-start(f32[384,128]{1,0:T(8,128)} %shard_map.101), channel_id=1, source_target_pairs={{16,17},{18,19},{20,21},{22,23},{24,25},{26,27},{28,29},{30,31}} | collective-permute-start | bytes 589832 | tf_op jit(solution)/shard_map/ppermute | solution.py:307
  (1 other events, 0.8 us)

commit v6 on v5

--- a/solution.py
+++ b/solution.py
@@ -140,20 +140,7 @@
     (q1, hu) = staged(forward_q, stride, [q0, r, t, q, u], [square] * 2, 6)
     qa = moved(q1, low)
 
-    def split_maps(d, maps, out):
-        @pl.loop(0, depth_maps.shape[1])
-        def _(j):
-            out[j] = left(maps[j])
-
-    (maps,) = staged(
-        split_maps,
-        1,
-        [depth_maps[0]],
-        [depth_maps.shape[1:3] + (3 * square[1],)],
-        0.1,
-        jnp.bfloat16,
-    )
-
+    maps = depth_maps[0]
 
     def forward_t(k, q0, t0, r, t, t1, rgt):
         @pl.when((k > 1) & (k < 6))
@@ -256,14 +243,18 @@
 
     (q2, hu2) = staged(second_q, stride, [r1, qa, q1, t1, both], [square] * 2, 6)
 
-    def second_fields(k, qa, fa, r1, t1, f2, g2):
+    def second_fields(k, f1, qa, fa, r1, t1, f2, g2):
+        @pl.when(k < 2)
+        def _():
+            f2[...] = f1[...]
+
         @pl.when((k == 2) | (k == 3))
         def _():
             g = summed(product(qa[...], r1[...]), fa[...], True)
             g2[...] = g
             f2[...] = product(t1[...], g)
 
-    (f2, g2) = staged(second_fields, stride, [qa, fa, r1, t1], [field, field], 2)
+    (f2, g2) = staged(second_fields, stride, [f1, qa, fa, r1, t1], [field, field], 2)
 
     def third_fields(k, r_late, r_next, w_came, q1, t1, both, r1, qa, fa, w4, g4, rc4):
         @pl.when((k == 2) | (k == 3))
@@ -307,7 +298,7 @@
         return lax.ppermute(value, "sec", pairs)
 
     half = NODES // 2 * stride
-    next_low = passed(jnp.where(k < 2, f1, f2), lambda i: i < half)
+    next_low = passed(f2, lambda i: i < half)
 
     def all_reflected(
         k, ua, r1, g2, rc4, g4, r_late, r_next, total_came, g6, hu2, s2, s4, s6
@@ -332,14 +323,10 @@
     s6_came = moved(s6, [(2, 6), (3, 7)])
     s4_came = moved(s4, [(2, 4), (3, 5)])
 
-    def through_odd(d, f1, f2, t1, w4, t2, g6, out):
+    def through_odd(d, f2, t1, w4, t2, g6, out):
         k = d // stride
 
-        @pl.when(k < 2)
-        def _():
-            out[...] = f1[...]
-
-        @pl.when((k == 2) | (k == 3))
+        @pl.when(k < 4)
         def _():
             out[...] = f2[...]
 
@@ -351,7 +338,7 @@
         def _():
             out[...] = product(t2[...], g6[...])
 
-    (odd,) = staged(through_odd, 1, [f1, f2, t1, w4_came, t2, g6_odd], [field], 1)
+    (odd,) = staged(through_odd, 1, [f2, t1, w4_came, t2, g6_odd], [field], 1)
     next_odd = passed(odd, lambda i: i >= half and i % 2 == 1)
 
     def through_even(d, odd, t2, g6, out):
@@ -379,7 +366,7 @@
 
         @pl.loop(0, depth_maps.shape[1])
         def _(j):
-            out[j] = jnp.dot(maps[j], value, preferred_element_type=F32)
+            out[j] = jnp.dot(left(maps[j]), value, preferred_element_type=F32)
 
     (depth_fields,) = staged(
         depths,

time: 135 us -> 132 us (0.978)
  the two profiles are of different devices: /device:TPU:30 before, /device:TPU:13 now
where the time goes in v6:
time: 132 us
  starting transfers between devices  46.6 us (35%)
  waiting for transfers between devices  42.5 us (32%)
  Pallas kernels  34.7 us (26%)
  local copies, waits for them, and re-layouts  4.94 us (4%)
  other arithmetic  1.66 us (1%)
    ppermute x27, waiting for transfers between devices, moved(): return lax.ppermute(value, 'sec', pairs)  42.5 us
    ppermute x27, starting transfers between devices, moved(): return lax.ppermute(value, 'sec', pairs)  36.1 us
    pallas_call x19, Pallas kernels, staged(): pl.pallas_call(kernel, out_shape=[jax.ShapeDtypeStruct(shape, dtype) for...  34.7 us
    ppermute x3, starting transfers between devices, passed(): return lax.ppermute(value, 'sec', pairs)  10.5 us
    unnamed x14, local copies, waits for them, and re-layouts  4.94 us
  transfers between devices with their start and end apart: 30, of which 6 were waited for; matrix products, arithmetic and copies ran while one was open for 1% of the time, Pallas kernels for 24%

profile of v6, /device:TPU:13, one launch (start us, length us, event | category | flops | bytes accessed | tf_op | source)
XLA Modules:
  0.0 131.6 jit_solution(1228815068069884771)
XLA Ops:
  0.6 0.7 collective-permute-start.7
  1.3 3.1 %collective-permute-start.1 = (f32[384,384]{1,0:T(8,128)}, f32[384,384]{1,0:T(8,128)S(1)}, u32[]{:S(2)}, u32[]{:S(2)}) collective-permute-start(f32[384,384]{1,0:T(8,128)} %bitcast.10), channel_id=1, source_target_pairs={{0,4},{1,5},{2,6},{3,7},{4,8},{5,9},{6,10},{7,11},{8,12},{9,13},{1... | collective-permute-start | bytes 1769480 | tf_op jit(solution)/shard_map/ppermute | solution.py:73
  4.5 3.1 %collective-permute-start.12 = (f32[384,384]{1,0:T(8,128)}, f32[384,384]{1,0:T(8,128)S(1)}, u32[]{:S(2)}, u32[]{:S(2)}) collective-permute-start(f32[384,384]{1,0:T(8,128)} %bitcast.12), channel_id=1, source_target_pairs={{4,8},{5,9},{6,10},{7,11},{8,12},{9,13},{10,14},{11,15},{12,16},{1... | collective-permute-start | bytes 1769480 | tf_op jit(solution)/shard_map/ppermute | solution.py:73
  7.7 0.9 copy-done.1
  8.6 1.1 copy-done.3
  9.6 1.1 copy-done.4
  10.7 1.4 %shard_map.85 = (f32[384,384]{1,0:T(8,128)S(1)}, f32[384,384]{1,0:T(8,128)S(1)}, f32[384,384]{1,0:T(8,128)S(1)}, f32[384,384]{1,0:T(8,128)S(1)}, f32[384,256]{1,0:T(8,128)S(1)}) custom-call(f32[384,384]{1,0:T(8,128)} %bitcast.refs_0_, f32[384,384]{1,0:T(8,128)S(1)} %bitcast.13, f32[384,384]{1,0:T(8,128)S(1)} %bitcast.11, f32[384,384]{1,0:T(8,128)} %bitcast.3.refs_3_, ...), custom_call_target="tpu_custom_call" | custom-call | flops 339738624 | bytes 5898240 | tf_op jit(solution)/shard_map/pallas_call | solution.py:48
  12.8 0.7 collective-permute-start.4
  13.5 0.7 collective-permute-start.10
  14.3 0.7 collective-permute-start.8
  15.0 2.6 %collective-permute-done.1.refs_2_.refs_0_ = f32[384,384]{1,0:T(8,128)S(1)} collective-permute-done((f32[384,384]{1,0:T(8,128)}, f32[384,384]{1,0:T(8,128)S(1)}, u32[]{:S(2)}, u32[]{:S(2)}) %collective-permute-start.1) | collective-permute-done | bytes 589856 | tf_op jit(solution)/shard_map/ppermute | solution.py:73
  17.7 1.3 collective-permute-start.9
  18.9 11.4 %collective-permute-done.12.refs_1_ = f32[384,384]{1,0:T(8,128)S(1)} collective-permute-done((f32[384,384]{1,0:T(8,128)}, f32[384,384]{1,0:T(8,128)S(1)}, u32[]{:S(2)}, u32[]{:S(2)}) %collective-permute-start.12) | collective-permute-done | bytes 589856 | tf_op jit(solution)/shard_map/ppermute | solution.py:73
  30.3 4.1 %collective-permute-start.15 = (f32[384,384]{1,0:T(8,128)}, f32[384,384]{1,0:T(8,128)S(1)}, u32[]{:S(2)}, u32[]{:S(2)}) collective-permute-start(f32[384,384]{1,0:T(8,128)} %bitcast.3.refs_3_), channel_id=1, source_target_pairs={{12,16},{13,17},{14,18},{15,19},{16,20},{17,21},{18,22},{19,23}} | collective-permute-start | bytes 1769480 | tf_op jit(solution)/shard_map/ppermute | solution.py:73
  34.4 0.7 collective-permute-start.5
  35.1 1.3 %collective-permute-start.13 = (f32[384,384]{1,0:T(8,128)}, f32[384,384]{1,0:T(8,128)S(1)}, u32[]{:S(2)}, u32[]{:S(2)}) collective-permute-start(f32[384,384]{1,0:T(8,128)} %bitcast.refs_0_), channel_id=1, source_target_pairs={{12,8},{13,9},{14,10},{15,11}} | collective-permute-start | bytes 1769480 | tf_op jit(solution)/shard_map/ppermute | solution.py:73
  36.4 0.7 collective-permute-start.11
  37.3 5.7 %collective-permute-done.9.refs_0_ = f32[384,384]{1,0:T(8,128)S(1)} collective-permute-done((f32[384,384]{1,0:T(8,128)}, f32[384,384]{1,0:T(8,128)S(1)}, u32[]{:S(2)}, u32[]{:S(2)}) %collective-permute-start.9) | collective-permute-done | bytes 589856 | tf_op jit(solution)/shard_map/ppermute | solution.py:73
  42.9 1.3 collective-permute-start.14
  44.2 1.6 %collective-permute-done.15.refs_0_ = f32[384,384]{1,0:T(8,128)S(1)} collective-permute-done((f32[384,384]{1,0:T(8,128)}, f32[384,384]{1,0:T(8,128)S(1)}, u32[]{:S(2)}, u32[]{:S(2)}) %collective-permute-start.15) | collective-permute-done | bytes 589856 | tf_op jit(solution)/shard_map/ppermute | solution.py:73
  46.5 4.1 %shard_map.87 = (f32[384,384]{1,0:T(8,128)S(1)}, f32[384,384]{1,0:T(8,128)S(1)}) custom-call(f32[384,384]{1,0:T(8,128)S(1)} %collective-permute-done.1.refs_2_.refs_0_, f32[384,384]{1,0:T(8,128)S(1)} %get-tuple-element.35.refs_3_.refs_1_.refs_2_, f32[384,384]{1,0:T(8,128)S(1)} %get-tuple-element.36.refs_4_.refs_2_.refs_3_.refs_0_, ...), custom_call_target="tpu_custom_call" | custom-call | flops 2038431744 | bytes 4128768 | tf_op jit(solution)/shard_map/pallas_call | solution.py:48
  50.6 1.3 collective-permute-start.6
  51.9 3.9 %shard_map.89 = (f32[384,384]{1,0:T(8,128)S(1)}, f32[384,384]{1,0:T(8,128)S(1)}) custom-call(f32[384,384]{1,0:T(8,128)S(1)} %collective-permute-done.1.refs_2_.refs_0_, f32[384,384]{1,0:T(8,128)S(1)} %collective-permute-done.12.refs_1_, f32[384,384]{1,0:T(8,128)S(1)} %get-tuple-element.35.refs_3_.refs_1_.refs_2_, ...), custom_call_target="tpu_custom_call" | custom-call | flops 2038431744 | bytes 3538944 | tf_op jit(solution)/shard_map/pallas_call | solution.py:48
  56.0 1.3 collective-permute-start.2
  57.3 1.3 collective-permute-start.16
  58.7 1.3 shard_map.90
  60.0 1.3 collective-permute-start.3
  61.3 1.3 collective-permute-start.24
  62.6 5.7 %collective-permute-done.6.refs_0_ = f32[384,384]{1,0:T(8,128)S(1)} collective-permute-done((f32[384,384]{1,0:T(8,128)S(1)}, f32[384,384]{1,0:T(8,128)S(1)}, u32[]{:S(2)}, u32[]{:S(2)}) %collective-permute-start.6) | collective-permute-done | bytes 589856 | tf_op jit(solution)/shard_map/ppermute | solution.py:73
  68.4 1.3 collective-permute-start.21
  69.7 15.5 %collective-permute-done.3.refs_2_.refs_8_ = f32[384,128]{1,0:T(8,128)S(1)} collective-permute-done((f32[384,128]{1,0:T(8,128)S(1)}, f32[384,128]{1,0:T(8,128)S(1)}, u32[]{:S(2)}, u32[]{:S(2)}) %collective-permute-start.3) | collective-permute-done | bytes 196640 | tf_op jit(solution)/shard_map/ppermute | solution.py:73
  85.2 0.7 collective-permute-start.18
  85.9 0.7 collective-permute-start.20
  86.6 7.0 %shard_map.94 = (f32[384,128]{1,0:T(8,128)}, f32[384,128]{1,0:T(8,128)S(1)}, f32[384,384]{1,0:T(8,128)S(1)}) custom-call(f32[384,384]{1,0:T(8,128)S(1)} %collective-permute-done.13.refs_0_.refs_5_, f32[384,384]{1,0:T(8,128)S(1)} %collective-permute-done.14.refs_1_.refs_6_, f32[384,384]{1,0:T(8,128)S(1)} %collective-permute-done.16.refs_2_, ...), custom_call_target="tpu_custom_call" | custom-call | flops 3057647616 | bytes 7077888 | tf_op jit(solution)/shard_map/pallas_call | solution.py:48
  93.6 1.3 collective-permute-start.17
  94.9 2.5 %shard_map.92 = (f32[384,128]{1,0:T(8,128)S(1)}, f32[384,128]{1,0:T(8,128)S(1)}) custom-call(f32[384,128]{1,0:T(8,128)S(1)} %get-tuple-element.37.refs_0_, f32[384,384]{1,0:T(8,128)S(1)} %collective-permute-done.2.refs_1_.refs_7_, f32[384,128]{1,0:T(8,128)S(1)} %collective-permute-done.3.refs_2_.refs_8_, ...), custom_call_target="tpu_custom_call" | custom-call | flops 25165824 | bytes 458752 | tf_op jit(solution)/shard_map/pallas_call | solution.py:48
  97.4 4.1 %shard_map.98 = (f32[384,384]{1,0:T(8,128)S(1)}, f32[384,384]{1,0:T(8,128)S(1)}) custom-call(f32[384,384]{1,0:T(8,128)S(1)} %shard_map.91.refs_3_.refs_6_.refs_0_.refs_1_, f32[384,384]{1,0:T(8,128)S(1)} %collective-permute-done.2.refs_1_.refs_7_, f32[384,384]{1,0:T(8,128)S(1)} %get-tuple-element.40.refs_3_.refs_1_.refs_2_, ...), custom_call_target="tpu_custom_call" | custom-call | flops 2038431744 | bytes 4128768 | tf_op jit(solution)/shard_map/pallas_call | solution.py:48
  101.5 2.9 %shard_map.99.refs_8_ = f32[384,128]{1,0:T(8,128)} custom-call(f32[384,384]{1,0:T(8,128)S(1)} %collective-permute-done.13.refs_0_.refs_5_, f32[384,384]{1,0:T(8,128)S(1)} %collective-permute-done.14.refs_1_.refs_6_, f32[384,384]{1,0:T(8,128)S(1)} %collective-permute-done.21.refs_2_.refs_7_, f32[384,384]{1,0:T(8,128)S(1)} %get-tuple-element.57.refs_3_, ...), custom_call_target="tpu_custom_call" | custom-call | flops 1019215872 | bytes 3538944 | tf_op jit(solution)/shard_map/pallas_call | solution.py:48
  104.4 1.3 collective-permute-start.22
  106.4 3.7 %shard_map.102 = (f32[384,128]{1,0:T(8,128)S(1)}, f32[384,128]{1,0:T(8,128)}, f32[384,128]{1,0:T(8,128)}) custom-call(f32[384,512]{1,0:T(8,128)S(1)} %collective-permute-done.24.refs_0_, f32[384,384]{1,0:T(8,128)S(1)} %shard_map.91.refs_3_.refs_6_.refs_0_.refs_1_, f32[384,128]{1,0:T(8,128)S(1)} %get-tuple-element.58.refs_2_, ...), custom_call_target="tpu_custom_call" | custom-call | flops 2415919104 | bytes 13631488 | tf_op jit(solution)/shard_map/pallas_call | solution.py:48
  110.1 2.0 %collective-permute-start.25 = (f32[384,128]{1,0:T(8,128)}, f32[384,128]{1,0:T(8,128)}, u32[]{:S(2)}, u32[]{:S(2)}) collective-permute-start(f32[384,128]{1,0:T(8,128)} %get-tuple-element.63), channel_id=1, source_target_pairs={{8,16},{9,17},{10,18},{11,19},{12,20},{13,21},{14,22},{15,23}} | collective-permute-start | bytes 589832 | tf_op jit(solution)/shard_map/ppermute | solution.py:73
  112.1 0.8 copy-done.5
  112.9 2.0 %collective-permute-start.26 = (f32[384,128]{1,0:T(8,128)}, f32[384,128]{1,0:T(8,128)}, u32[]{:S(2)}, u32[]{:S(2)}) collective-permute-start(f32[384,128]{1,0:T(8,128)} %get-tuple-element.64), channel_id=1, source_target_pairs={{8,24},{9,25},{10,26},{11,27},{12,28},{13,29},{14,30},{15,31}} | collective-permute-start | bytes 589832 | tf_op jit(solution)/shard_map/ppermute | solution.py:73
  114.9 1.1 copy-done.6
  116.0 9.2 %collective-permute-start.27 = (f32[384,128]{1,0:T(8,128)S(1)}, f32[384,128]{1,0:T(8,128)S(1)}, u32[]{:S(2)}, u32[]{:S(2)}) collective-permute-start(f32[384,128]{1,0:T(8,128)S(1)} %get-tuple-element.47.refs_4_.refs_0_), channel_id=1, source_target_pairs={{0,1},{1,2},{2,3},{3,4},{4,5},{5,6},{6,7},{7,8},{8,9},{9,10},{10,1... | collective-permute-start | bytes 589832 | tf_op jit(solution)/shard_map/ppermute | solution.py:298
  125.9 0.7 shard_map.101
  127.3 1.7 %select_bitcast_fusion = f32[1,384,128]{2,1,0:T(8,128)} fusion(f32[384,128]{1,0:T(8,128)S(1)} %get-tuple-element.62, f32[384,128]{1,0:T(8,128)} %collective-permute-done.25, f32[384,128]{1,0:T(8,128)} %collective-permute-done.26, f32[384,512]{1,0:T(8,128)S(1)} %get-tuple-element.49.refs_5_.refs_4_, pred[]{:T(512)S(6)} %lt.11, pred[]{:T(512)S(6)} %lt.10, pred[]{:T(512)S(6)} %lt.9), kind=kLoop, calls=%fused_computation | loop fusion | flops 147456 | bytes 983043 | tf_op jit(solution)/shard_map/broadcast_in_dim | solution.py:378
  129.0 2.6 %shard_map.103 = f32[4,384,128]{2,1,0:T(8,128)} custom-call(f32[4,384,384]{2,1,0:T(8,128)S(1)} %bitcast.9, f32[384,128]{1,0:T(8,128)S(1)} %collective-permute-done.27.refs_1_, f32[384,128]{1,0:T(8,128)S(1)} %collective-permute-done.28.refs_2_, f32[384,128]{1,0:T(8,128)S(1)} %collective-permute-done.29.refs_3_, f32[384,128]{1,0:T(8,128)S(1)} %copy-done.2), custom_call_target="tpu_custom_call" | custom-call | flops 339738624 | bytes 3538944 | tf_op jit(solution)/shard_map/pallas_call | solution.py:48
  (46 shorter events, 4.0 us)
Async XLA Ops:
  0.6 12.9 %collective-permute-start.7 = (f32[384,384]{1,0:T(8,128)}, f32[384,384]{1,0:T(8,128)S(1)}, u32[]{:S(2)}, u32[]{:S(2)}) collective-permute-start(f32[384,384]{1,0:T(8,128)} %bitcast.refs_0_), channel_id=1, source_target_pairs={{28,24},{29,25},{30,26},{31,27},{24,28},{25,29},{26,30},{27,31},{4... | collective-permute-start | bytes 1769480 | tf_op jit(solution)/shard_map/ppermute | solution.py:73
  1.3 16.3 %collective-permute-start.1 = (f32[384,384]{1,0:T(8,128)}, f32[384,384]{1,0:T(8,128)S(1)}, u32[]{:S(2)}, u32[]{:S(2)}) collective-permute-start(f32[384,384]{1,0:T(8,128)} %bitcast.10), channel_id=1, source_target_pairs={{0,4},{1,5},{2,6},{3,7},{4,8},{5,9},{6,10},{7,11},{8,12},{9,13},{1... | collective-permute-start | bytes 1769480 | tf_op jit(solution)/shard_map/ppermute | solution.py:73
  4.5 25.8 %collective-permute-start.12 = (f32[384,384]{1,0:T(8,128)}, f32[384,384]{1,0:T(8,128)S(1)}, u32[]{:S(2)}, u32[]{:S(2)}) collective-permute-start(f32[384,384]{1,0:T(8,128)} %bitcast.12), channel_id=1, source_target_pairs={{4,8},{5,9},{6,10},{7,11},{8,12},{9,13},{10,14},{11,15},{12,16},{1... | collective-permute-start | bytes 1769480 | tf_op jit(solution)/shard_map/ppermute | solution.py:73
  7.6 0.9 copy-start.1
  8.6 1.1 copy-start.3
  9.6 1.1 copy-start.4
  12.1 2.2 %collective-permute-start = (f32[384,256]{1,0:T(8,128)S(1)}, f32[384,256]{1,0:T(8,128)S(1)}, u32[]{:S(2)}, u32[]{:S(2)}) collective-permute-start(f32[384,256]{1,0:T(8,128)S(1)} %get-tuple-element.34.refs_0_.refs_6_), channel_id=1, source_target_pairs={{0,4},{1,5},{2,6},{3,7}} | collective-permute-start | bytes 1179656 | tf_op jit(solution)/shard_map/ppermute | solution.py:73
  12.8 21.6 %collective-permute-start.4 = (f32[384,384]{1,0:T(8,128)}, f32[384,384]{1,0:T(8,128)S(1)}, u32[]{:S(2)}, u32[]{:S(2)}) collective-permute-start(f32[384,384]{1,0:T(8,128)} %bitcast.refs_0_), channel_id=1, source_target_pairs={{8,0},{9,1},{10,2},{11,3}} | collective-permute-start | bytes 1769480 | tf_op jit(solution)/shard_map/ppermute | solution.py:73
  13.5 21.6 %collective-permute-start.10 = (f32[384,384]{1,0:T(8,128)}, f32[384,384]{1,0:T(8,128)S(1)}, u32[]{:S(2)}, u32[]{:S(2)}) collective-permute-start(f32[384,384]{1,0:T(8,128)} %bitcast.3.refs_3_), channel_id=1, source_target_pairs={{4,0},{5,1},{6,2},{7,3}} | collective-permute-start | bytes 1769480 | tf_op jit(solution)/shard_map/ppermute | solution.py:73
  14.3 22.1 %collective-permute-start.8 = (f32[384,384]{1,0:T(8,128)S(1)}, f32[384,384]{1,0:T(8,128)S(1)}, u32[]{:S(2)}, u32[]{:S(2)}) collective-permute-start(f32[384,384]{1,0:T(8,128)S(1)} %get-tuple-element.41), channel_id=1, source_target_pairs={{24,28},{25,29},{26,30},{27,31},{28,20},{29,21},{30,22},{31,23},{0... | collective-permute-start | bytes 1769480 | tf_op jit(solution)/shard_map/ppermute | solution.py:73
  17.7 25.3 %collective-permute-start.9 = (f32[384,384]{1,0:T(8,128)}, f32[384,384]{1,0:T(8,128)S(1)}, u32[]{:S(2)}, u32[]{:S(2)}) collective-permute-start(f32[384,384]{1,0:T(8,128)} %bitcast.3.refs_3_), channel_id=1, source_target_pairs={{0,4},{1,5},{2,6},{3,7},{8,12},{9,13},{10,14},{11,15}} | collective-permute-start | bytes 1769480 | tf_op jit(solution)/shard_map/ppermute | solution.py:73
  30.3 15.5 %collective-permute-start.15 = (f32[384,384]{1,0:T(8,128)}, f32[384,384]{1,0:T(8,128)S(1)}, u32[]{:S(2)}, u32[]{:S(2)}) collective-permute-start(f32[384,384]{1,0:T(8,128)} %bitcast.3.refs_3_), channel_id=1, source_target_pairs={{12,16},{13,17},{14,18},{15,19},{16,20},{17,21},{18,22},{19,23}} | collective-permute-start | bytes 1769480 | tf_op jit(solution)/shard_map/ppermute | solution.py:73
  34.4 16.2 %collective-permute-start.5 = (f32[384,384]{1,0:T(8,128)S(1)}, f32[384,384]{1,0:T(8,128)S(1)}, u32[]{:S(2)}, u32[]{:S(2)}) collective-permute-start(f32[384,384]{1,0:T(8,128)S(1)} %collective-permute-done.4), channel_id=1, source_target_pairs={{0,4},{1,5},{2,6},{3,7}} | collective-permute-start | bytes 1769480 | tf_op jit(solution)/shard_map/ppermute | solution.py:73
  35.1 20.9 %collective-permute-start.13 = (f32[384,384]{1,0:T(8,128)}, f32[384,384]{1,0:T(8,128)S(1)}, u32[]{:S(2)}, u32[]{:S(2)}) collective-permute-start(f32[384,384]{1,0:T(8,128)} %bitcast.refs_0_), channel_id=1, source_target_pairs={{12,8},{13,9},{14,10},{15,11}} | collective-permute-start | bytes 1769480 | tf_op jit(solution)/shard_map/ppermute | solution.py:73
  36.4 20.9 %collective-permute-start.11 = (f32[384,384]{1,0:T(8,128)S(1)}, f32[384,384]{1,0:T(8,128)S(1)}, u32[]{:S(2)}, u32[]{:S(2)}) collective-permute-start(f32[384,384]{1,0:T(8,128)S(1)} %collective-permute-done.10), channel_id=1, source_target_pairs={{0,8},{1,9},{2,10},{3,11}} | collective-permute-start | bytes 1769480 | tf_op jit(solution)/shard_map/ppermute | solution.py:73
  42.9 17.1 %collective-permute-start.14 = (f32[384,384]{1,0:T(8,128)}, f32[384,384]{1,0:T(8,128)S(1)}, u32[]{:S(2)}, u32[]{:S(2)}) collective-permute-start(f32[384,384]{1,0:T(8,128)} %bitcast.refs_0_), channel_id=1, source_target_pairs={{16,12},{17,13},{18,14},{19,15}} | collective-permute-start | bytes 1769480 | tf_op jit(solution)/shard_map/ppermute | solution.py:73
  45.8 15.5 %collective-permute-start.19 = (f32[384,384]{1,0:T(8,128)S(1)}, f32[384,384]{1,0:T(8,128)S(1)}, u32[]{:S(2)}, u32[]{:S(2)}) collective-permute-start(f32[384,384]{1,0:T(8,128)S(1)} %get-tuple-element.53), channel_id=1, source_target_pairs={{20,16},{21,17},{22,18},{23,19},{28,20},{29,21},{30,22},{31,23}} | collective-permute-start | bytes 1769480 | tf_op jit(solution)/shard_map/ppermute | solution.py:73
  50.6 17.8 %collective-permute-start.6 = (f32[384,384]{1,0:T(8,128)S(1)}, f32[384,384]{1,0:T(8,128)S(1)}, u32[]{:S(2)}, u32[]{:S(2)}) collective-permute-start(f32[384,384]{1,0:T(8,128)S(1)} %collective-permute-done.5), channel_id=1, source_target_pairs={{4,12},{5,13},{6,14},{7,15}} | collective-permute-start | bytes 1769480 | tf_op jit(solution)/shard_map/ppermute | solution.py:73
  56.0 29.9 %collective-permute-start.2 = (f32[384,384]{1,0:T(8,128)S(1)}, f32[384,384]{1,0:T(8,128)S(1)}, u32[]{:S(2)}, u32[]{:S(2)}) collective-permute-start(f32[384,384]{1,0:T(8,128)S(1)} %get-tuple-element.40.refs_3_.refs_1_.refs_2_), channel_id=1, source_target_pairs={{0,8},{1,9},{2,10},{3,11},{4,12},{5,13},{6,14},{7,15}} | collective-permute-start | bytes 1769480 | tf_op jit(solution)/shard_map/ppermute | solution.py:73
  57.3 29.3 %collective-permute-start.16 = (f32[384,384]{1,0:T(8,128)S(1)}, f32[384,384]{1,0:T(8,128)S(1)}, u32[]{:S(2)}, u32[]{:S(2)}) collective-permute-start(f32[384,384]{1,0:T(8,128)S(1)} %get-tuple-element.48.refs_4_), channel_id=1, source_target_pairs={{16,8},{17,9},{18,10},{19,11},{20,12},{21,13},{22,14},{23,15}} | collective-permute-start | bytes 1769480 | tf_op jit(solution)/shard_map/ppermute | solution.py:73
  60.0 25.2 %collective-permute-start.3 = (f32[384,128]{1,0:T(8,128)S(1)}, f32[384,128]{1,0:T(8,128)S(1)}, u32[]{:S(2)}, u32[]{:S(2)}) collective-permute-start(f32[384,128]{1,0:T(8,128)S(1)} %get-tuple-element.37.refs_0_), channel_id=1, source_target_pairs={{0,8},{1,9},{2,10},{3,11},{4,12},{5,13},{6,14},{7,15}} | collective-permute-start | bytes 589832 | tf_op jit(solution)/shard_map/ppermute | solution.py:73
  61.3 44.4 %collective-permute-start.24 = (f32[384,512]{1,0:T(8,128)S(1)}, f32[384,512]{1,0:T(8,128)S(1)}, u32[]{:S(2)}, u32[]{:S(2)}) collective-permute-start(f32[384,512]{1,0:T(8,128)S(1)} %get-tuple-element.49.refs_5_.refs_4_), channel_id=1, source_target_pairs={{0,8},{1,9},{2,10},{3,11},{4,12},{5,13},{6,14},{7,15}} | collective-permute-start | bytes 2359304 | tf_op jit(solution)/shard_map/ppermute | solution.py:73
  68.4 33.2 %collective-permute-start.21 = (f32[384,384]{1,0:T(8,128)S(1)}, f32[384,384]{1,0:T(8,128)S(1)}, u32[]{:S(2)}, u32[]{:S(2)}) collective-permute-start(f32[384,384]{1,0:T(8,128)S(1)} %get-tuple-element.56), channel_id=1, source_target_pairs={{16,8},{17,9},{18,10},{19,11},{20,12},{21,13},{22,14},{23,15}} | collective-permute-start | bytes 1769480 | tf_op jit(solution)/shard_map/ppermute | solution.py:73
  85.2 24.9 %collective-permute-start.18 = (f32[384,384]{1,0:T(8,128)S(1)}, f32[384,384]{1,0:T(8,128)S(1)}, u32[]{:S(2)}, u32[]{:S(2)}) collective-permute-start(f32[384,384]{1,0:T(8,128)S(1)} %get-tuple-element.52), channel_id=1, source_target_pairs={{20,24},{21,25},{22,26},{23,27},{24,28},{25,29},{26,30},{27,31}} | collective-permute-start | bytes 1769480 | tf_op jit(solution)/shard_map/ppermute | solution.py:73
  85.9 26.2 %collective-permute-start.20 = (f32[384,384]{1,0:T(8,128)S(1)}, f32[384,384]{1,0:T(8,128)S(1)}, u32[]{:S(2)}, u32[]{:S(2)}) collective-permute-start(f32[384,384]{1,0:T(8,128)S(1)} %get-tuple-element.55), channel_id=1, source_target_pairs={{16,24},{17,25},{18,26},{19,27},{20,28},{21,29},{22,30},{23,31}} | collective-permute-start | bytes 1769480 | tf_op jit(solution)/shard_map/ppermute | solution.py:73
  93.6 22.3 %collective-permute-start.17 = (f32[384,128]{1,0:T(8,128)}, f32[384,128]{1,0:T(8,128)S(1)}, u32[]{:S(2)}, u32[]{:S(2)}) collective-permute-start(f32[384,128]{1,0:T(8,128)} %get-tuple-element.50), channel_id=1, source_target_pairs={{8,16},{9,17},{10,18},{11,19},{12,20},{13,21},{14,22},{15,23}} | collective-permute-start | bytes 589832 | tf_op jit(solution)/shard_map/ppermute | solution.py:73
  104.4 20.7 %collective-permute-start.22 = (f32[384,128]{1,0:T(8,128)}, f32[384,128]{1,0:T(8,128)S(1)}, u32[]{:S(2)}, u32[]{:S(2)}) collective-permute-start(f32[384,128]{1,0:T(8,128)} %shard_map.99.refs_8_), channel_id=1, source_target_pairs={{9,25},{11,27},{13,29},{15,31}} | collective-permute-start | bytes 589832 | tf_op jit(solution)/shard_map/ppermute | solution.py:73
  105.7 20.1 %collective-permute-start.23 = (f32[384,128]{1,0:T(8,128)}, f32[384,128]{1,0:T(8,128)S(1)}, u32[]{:S(2)}, u32[]{:S(2)}) collective-permute-start(f32[384,128]{1,0:T(8,128)} %shard_map.99.refs_8_), channel_id=1, source_target_pairs={{8,24},{10,26},{12,28},{14,30}} | collective-permute-start | bytes 589832 | tf_op jit(solution)/shard_map/ppermute | solution.py:73
  110.1 17.1 %collective-permute-start.25 = (f32[384,128]{1,0:T(8,128)}, f32[384,128]{1,0:T(8,128)}, u32[]{:S(2)}, u32[]{:S(2)}) collective-permute-start(f32[384,128]{1,0:T(8,128)} %get-tuple-element.63), channel_id=1, source_target_pairs={{8,16},{9,17},{10,18},{11,19},{12,20},{13,21},{14,22},{15,23}} | collective-permute-start | bytes 589832 | tf_op jit(solution)/shard_map/ppermute | solution.py:73
  112.1 0.8 copy-start.5
  112.9 14.4 %collective-permute-start.26 = (f32[384,128]{1,0:T(8,128)}, f32[384,128]{1,0:T(8,128)}, u32[]{:S(2)}, u32[]{:S(2)}) collective-permute-start(f32[384,128]{1,0:T(8,128)} %get-tuple-element.64), channel_id=1, source_target_pairs={{8,24},{9,25},{10,26},{11,27},{12,28},{13,29},{14,30},{15,31}} | collective-permute-start | bytes 589832 | tf_op jit(solution)/shard_map/ppermute | solution.py:73
  114.9 1.1 copy-start.6
  115.9 13.0 %copy-start = (f32[1,4,384,384]{3,2,1,0:T(8,128)S(1)}, f32[1,4,384,384]{3,2,1,0:T(8,128)}, u32[]{:S(2)}) copy-start(f32[1,4,384,384]{3,2,1,0:T(8,128)} %param.10) | copy-start | bytes 7077892
  115.9 13.0 %copy-start.2 = (f32[384,128]{1,0:T(8,128)S(1)}, f32[384,128]{1,0:T(8,128)}, u32[]{:S(2)}) copy-start(f32[384,128]{1,0:T(8,128)} %refs_4_.3) | copy-start | bytes 589828
  116.0 13.0 %collective-permute-start.27 = (f32[384,128]{1,0:T(8,128)S(1)}, f32[384,128]{1,0:T(8,128)S(1)}, u32[]{:S(2)}, u32[]{:S(2)}) collective-permute-start(f32[384,128]{1,0:T(8,128)S(1)} %get-tuple-element.47.refs_4_.refs_0_), channel_id=1, source_target_pairs={{0,1},{1,2},{2,3},{3,4},{4,5},{5,6},{6,7},{7,8},{8,9},{9,10},{10,1... | collective-permute-start | bytes 589832 | tf_op jit(solution)/shard_map/ppermute | solution.py:298
  125.2 3.8 %collective-permute-start.28 = (f32[384,128]{1,0:T(8,128)S(1)}, f32[384,128]{1,0:T(8,128)S(1)}, u32[]{:S(2)}, u32[]{:S(2)}) collective-permute-start(f32[384,128]{1,0:T(8,128)S(1)} %shard_map.100.refs_0_), channel_id=1, source_target_pairs={{17,18},{19,20},{21,22},{23,24},{25,26},{27,28},{29,30}} | collective-permute-start | bytes 589832 | tf_op jit(solution)/shard_map/ppermute | solution.py:298
  126.6 2.4 %collective-permute-start.29 = (f32[384,128]{1,0:T(8,128)}, f32[384,128]{1,0:T(8,128)S(1)}, u32[]{:S(2)}, u32[]{:S(2)}) collective-permute-start(f32[384,128]{1,0:T(8,128)} %shard_map.101), channel_id=1, source_target_pairs={{16,17},{18,19},{20,21},{22,23},{24,25},{26,27},{28,29},{30,31}} | collective-permute-start | bytes 589832 | tf_op jit(solution)/shard_map/ppermute | solution.py:298

commit v7 on v6

--- a/solution.py
+++ b/solution.py
@@ -60,8 +60,6 @@
 def per_device(front_reflect, front_through, back_reflect, back_through, depth_maps, incident):
     length = lax.axis_size("sec")
     stride = length // NODES
-    position = lax.axis_index("sec")
-    k = position // stride
     square, field = front_reflect.shape[1:], incident.shape
 
     def moved(value, routes, start=0, step=1):
@@ -355,17 +353,12 @@
 
     (through_field,) = staged(through_even, 1, [odd, t2, g6_even], [field], 1)
     next_even = passed(through_field, lambda i: i >= half and i % 2 == 0)
-    reflected = jnp.where(
-        k < 2, both[:, square[1] :], jnp.where(k < 4, s2, jnp.where(k < 6, s4_came, s6_came))
-    )
 
     def depths(d, maps, low, odd, even, incident, out):
         came = jnp.where(d % 2 == 1, even[...], odd[...])
         came = jnp.where(d <= half, low[...], came)
         value = right(jnp.where(d == 0, incident[...], came))
-
-        @pl.loop(0, depth_maps.shape[1])
-        def _(j):
+        for j in range(depth_maps.shape[1]):
             out[j] = jnp.dot(left(maps[j]), value, preferred_element_type=F32)
 
     (depth_fields,) = staged(
@@ -375,6 +368,25 @@
         [depth_maps.shape[1:3] + field[1:]],
         1,
     )
+
+    def reflected_out(k, both, s2, s4, s6, out):
+        @pl.when(k < 2)
+        def _():
+            out[...] = both[:, square[1] :]
+
+        @pl.when((k == 2) | (k == 3))
+        def _():
+            out[...] = s2[...]
+
+        @pl.when((k == 4) | (k == 5))
+        def _():
+            out[...] = s4[...]
+
+        @pl.when(k > 5)
+        def _():
+            out[...] = s6[...]
+
+    (reflected,) = staged(reflected_out, stride, [both, s2, s4_came, s6_came], [field], 0.1)
     return (through_field[None], reflected[None], depth_fields[None])
 
 

time: 132 us -> 129 us (0.977)
  the two profiles are of different devices: /device:TPU:13 before, /device:TPU:28 now
where the time goes in v7:
time: 129 us; the launch traced here: 128 us
  waiting for transfers between devices  78.4 us (61%)
  starting transfers between devices  38.1 us (30%)
  Pallas kernels  7.25 us (6%)
  local copies, waits for them, and re-layouts  3.06 us (2%)
    ppermute x27, waiting for transfers between devices, moved(): return lax.ppermute(value, 'sec', pairs)  73 us
    ppermute x27, starting transfers between devices, moved(): return lax.ppermute(value, 'sec', pairs)  34.8 us
    pallas_call x20, Pallas kernels, staged(): pl.pallas_call(kernel, out_shape=[jax.ShapeDtypeStruct(shape, dtype) for...  7.25 us
    ppermute x3, waiting for transfers between devices, passed(): return lax.ppermute(value, 'sec', pairs)  5.36 us
    ppermute x3, starting transfers between devices, passed(): return lax.ppermute(value, 'sec', pairs)  3.39 us
    unnamed x10, local copies, waits for them, and re-layouts  3.06 us
  transfers between devices with their start and end apart: 30, of which 8 were waited for; matrix products, arithmetic and copies ran while one was open for 0% of the time, Pallas kernels for 4%

profile of v7, /device:TPU:28, one launch (start us, length us, event | category | flops | bytes accessed | tf_op | source)
XLA Modules:
  0.0 128.0 jit_solution(4063140588293360849)
XLA Ops:
  0.6 2.4 %collective-permute-start.7 = (f32[384,384]{1,0:T(8,128)}, f32[384,384]{1,0:T(8,128)S(1)}, u32[]{:S(2)}, u32[]{:S(2)}) collective-permute-start(f32[384,384]{1,0:T(8,128)} %bitcast.refs_0_), channel_id=1, source_target_pairs={{28,24},{29,25},{30,26},{31,27},{24,28},{25,29},{26,30},{27,31},{4... | collective-permute-start | bytes 1769480 | tf_op jit(solution)/shard_map/ppermute | solution.py:71
  3.1 0.7 collective-permute-start.1
  3.8 0.7 collective-permute-start.12
  4.5 0.9 copy-done.1
  5.4 1.1 copy-done.3
  6.5 1.1 copy-done.4
  7.5 1.4 %shard_map.85 = (f32[384,384]{1,0:T(8,128)S(1)}, f32[384,384]{1,0:T(8,128)S(1)}, f32[384,384]{1,0:T(8,128)S(1)}, f32[384,384]{1,0:T(8,128)S(1)}, f32[384,256]{1,0:T(8,128)S(1)}) custom-call(f32[384,384]{1,0:T(8,128)} %bitcast.refs_0_, f32[384,384]{1,0:T(8,128)S(1)} %bitcast.12, f32[384,384]{1,0:T(8,128)S(1)} %bitcast.10, f32[384,384]{1,0:T(8,128)} %bitcast.3.refs_3_, ...), custom_call_target="tpu_custom_call" | custom-call | flops 339738624 | bytes 5898240 | tf_op jit(solution)/shard_map/pallas_call | solution.py:48
  8.9 0.7 collective-permute-start
  9.6 0.7 collective-permute-start.4
  10.3 7.5 %collective-permute-done.7.refs_0_ = f32[384,384]{1,0:T(8,128)S(1)} collective-permute-done((f32[384,384]{1,0:T(8,128)}, f32[384,384]{1,0:T(8,128)S(1)}, u32[]{:S(2)}, u32[]{:S(2)}) %collective-permute-start.7) | collective-permute-done | bytes 589856 | tf_op jit(solution)/shard_map/ppermute | solution.py:71
  17.8 0.7 collective-permute-start.10
  18.6 1.9 %collective-permute-start.8 = (f32[384,384]{1,0:T(8,128)S(1)}, f32[384,384]{1,0:T(8,128)S(1)}, u32[]{:S(2)}, u32[]{:S(2)}) collective-permute-start(f32[384,384]{1,0:T(8,128)S(1)} %get-tuple-element.41), channel_id=1, source_target_pairs={{24,28},{25,29},{26,30},{27,31},{28,20},{29,21},{30,22},{31,23},{0... | collective-permute-start | bytes 1769480 | tf_op jit(solution)/shard_map/ppermute | solution.py:71
  20.5 0.7 collective-permute-start.9
  21.2 0.7 collective-permute-start.15
  21.9 0.7 collective-permute-start.5
  22.7 0.7 collective-permute-start.13
  23.4 13.5 %collective-permute-done.8.refs_1_.refs_0_ = f32[384,384]{1,0:T(8,128)S(1)} collective-permute-done((f32[384,384]{1,0:T(8,128)S(1)}, f32[384,384]{1,0:T(8,128)S(1)}, u32[]{:S(2)}, u32[]{:S(2)}) %collective-permute-start.8) | collective-permute-done | bytes 589856 | tf_op jit(solution)/shard_map/ppermute | solution.py:71
  36.9 0.7 collective-permute-start.11
  37.7 0.7 collective-permute-start.14
  38.4 11.4 %collective-permute-start.19 = (f32[384,384]{1,0:T(8,128)S(1)}, f32[384,384]{1,0:T(8,128)S(1)}, u32[]{:S(2)}, u32[]{:S(2)}) collective-permute-start(f32[384,384]{1,0:T(8,128)S(1)} %get-tuple-element.53), channel_id=1, source_target_pairs={{20,16},{21,17},{22,18},{23,19},{28,20},{29,21},{30,22},{31,23}} | collective-permute-start | bytes 1769480 | tf_op jit(solution)/shard_map/ppermute | solution.py:71
  49.9 0.7 collective-permute-start.6
  50.6 0.2 shard_map.93
  50.8 0.7 collective-permute-start.2
  51.6 0.7 collective-permute-start.16
  52.3 0.7 collective-permute-start.3
  53.0 7.6 %collective-permute-done.19.refs_0_ = f32[384,384]{1,0:T(8,128)S(1)} collective-permute-done((f32[384,384]{1,0:T(8,128)S(1)}, f32[384,384]{1,0:T(8,128)S(1)}, u32[]{:S(2)}, u32[]{:S(2)}) %collective-permute-start.19) | collective-permute-done | bytes 589856 | tf_op jit(solution)/shard_map/ppermute | solution.py:71
  60.7 0.7 collective-permute-start.24
  61.4 0.7 collective-permute-start.21
  62.2 1.3 %collective-permute-start.18 = (f32[384,384]{1,0:T(8,128)S(1)}, f32[384,384]{1,0:T(8,128)S(1)}, u32[]{:S(2)}, u32[]{:S(2)}) collective-permute-start(f32[384,384]{1,0:T(8,128)S(1)} %get-tuple-element.52), channel_id=1, source_target_pairs={{20,24},{21,25},{22,26},{23,27},{24,28},{25,29},{26,30},{27,31}} | collective-permute-start | bytes 1769480 | tf_op jit(solution)/shard_map/ppermute | solution.py:71
  63.5 1.3 %collective-permute-start.20 = (f32[384,384]{1,0:T(8,128)S(1)}, f32[384,384]{1,0:T(8,128)S(1)}, u32[]{:S(2)}, u32[]{:S(2)}) collective-permute-start(f32[384,384]{1,0:T(8,128)S(1)} %get-tuple-element.55), channel_id=1, source_target_pairs={{16,24},{17,25},{18,26},{19,27},{20,28},{21,29},{22,30},{23,31}} | collective-permute-start | bytes 1769480 | tf_op jit(solution)/shard_map/ppermute | solution.py:71
  64.8 0.7 collective-permute-start.17
  65.5 0.2 shard_map.92
  65.8 0.7 collective-permute-start.22
  66.5 1.3 %collective-permute-start.23 = (f32[384,128]{1,0:T(8,128)S(1)}, f32[384,128]{1,0:T(8,128)S(1)}, u32[]{:S(2)}, u32[]{:S(2)}) collective-permute-start(f32[384,128]{1,0:T(8,128)S(1)} %shard_map.99.refs_8_), channel_id=1, source_target_pairs={{8,24},{10,26},{12,28},{14,30}} | collective-permute-start | bytes 589832 | tf_op jit(solution)/shard_map/ppermute | solution.py:71
  67.8 8.7 %collective-permute-done.18.refs_1_ = f32[384,384]{1,0:T(8,128)S(1)} collective-permute-done((f32[384,384]{1,0:T(8,128)S(1)}, f32[384,384]{1,0:T(8,128)S(1)}, u32[]{:S(2)}, u32[]{:S(2)}) %collective-permute-start.18) | collective-permute-done | bytes 589856 | tf_op jit(solution)/shard_map/ppermute | solution.py:71
  76.6 0.7 collective-permute-start.25
  77.2 21.0 %collective-permute-done.20.refs_2_ = f32[384,384]{1,0:T(8,128)S(1)} collective-permute-done((f32[384,384]{1,0:T(8,128)S(1)}, f32[384,384]{1,0:T(8,128)S(1)}, u32[]{:S(2)}, u32[]{:S(2)}) %collective-permute-start.20) | collective-permute-done | bytes 589856 | tf_op jit(solution)/shard_map/ppermute | solution.py:71
  98.2 1.3 %collective-permute-start.26 = (f32[384,128]{1,0:T(8,128)S(1)}, f32[384,128]{1,0:T(8,128)S(1)}, u32[]{:S(2)}, u32[]{:S(2)}) collective-permute-start(f32[384,128]{1,0:T(8,128)S(1)} %get-tuple-element.64), channel_id=1, source_target_pairs={{8,24},{9,25},{10,26},{11,27},{12,28},{13,29},{14,30},{15,31}} | collective-permute-start | bytes 589832 | tf_op jit(solution)/shard_map/ppermute | solution.py:71
  99.5 1.3 shard_map.97.refs_3_.refs_1_
  100.8 0.8 collective-permute-start.27
  101.7 14.1 %collective-permute-done.23.refs_2_ = f32[384,128]{1,0:T(8,128)S(1)} collective-permute-done((f32[384,128]{1,0:T(8,128)S(1)}, f32[384,128]{1,0:T(8,128)S(1)}, u32[]{:S(2)}, u32[]{:S(2)}) %collective-permute-start.23) | collective-permute-done | bytes 196640 | tf_op jit(solution)/shard_map/ppermute | solution.py:71
  115.8 1.1 shard_map.101
  116.9 1.3 %collective-permute-start.29 = (f32[384,128]{1,0:T(8,128)}, f32[384,128]{1,0:T(8,128)S(1)}, u32[]{:S(2)}, u32[]{:S(2)}) collective-permute-start(f32[384,128]{1,0:T(8,128)} %shard_map.101), channel_id=1, source_target_pairs={{16,17},{18,19},{20,21},{22,23},{24,25},{26,27},{28,29},{30,31}} | collective-permute-start | bytes 589832 | tf_op jit(solution)/shard_map/ppermute | solution.py:296
  118.2 1.3 %collective-permute-start.28 = (f32[384,128]{1,0:T(8,128)S(1)}, f32[384,128]{1,0:T(8,128)S(1)}, u32[]{:S(2)}, u32[]{:S(2)}) collective-permute-start(f32[384,128]{1,0:T(8,128)S(1)} %shard_map.100.refs_0_), channel_id=1, source_target_pairs={{17,18},{19,20},{21,22},{23,24},{25,26},{27,28},{29,30}} | collective-permute-start | bytes 589832 | tf_op jit(solution)/shard_map/ppermute | solution.py:296
  119.5 0.5 collective-permute-done.26.refs_3_
  120.0 0.7 shard_map.103
  120.7 5.4 %collective-permute-done.28.refs_2_ = f32[384,128]{1,0:T(8,128)S(1)} collective-permute-done((f32[384,128]{1,0:T(8,128)S(1)}, f32[384,128]{1,0:T(8,128)S(1)}, u32[]{:S(2)}, u32[]{:S(2)}) %collective-permute-start.28) | collective-permute-done | bytes 196640 | tf_op jit(solution)/shard_map/ppermute | solution.py:296
  126.1 2.0 %shard_map.104 = f32[4,384,128]{2,1,0:T(8,128)} custom-call(f32[4,384,384]{2,1,0:T(8,128)S(1)} %bitcast.8, f32[384,128]{1,0:T(8,128)S(1)} %collective-permute-done.27.refs_1_, f32[384,128]{1,0:T(8,128)S(1)} %collective-permute-done.28.refs_2_, f32[384,128]{1,0:T(8,128)S(1)} %collective-permute-done.29.refs_3_, f32[384,128]{1,0:T(8,128)S(1)} %copy-done.2), custom_call_target="tpu_custom_call" | custom-call | flops 339738624 | bytes 3538944 | tf_op jit(solution)/shard_map/pallas_call | solution.py:48
  (42 shorter events, 0.5 us)
Async XLA Ops:
  0.6 17.2 %collective-permute-start.7 = (f32[384,384]{1,0:T(8,128)}, f32[384,384]{1,0:T(8,128)S(1)}, u32[]{:S(2)}, u32[]{:S(2)}) collective-permute-start(f32[384,384]{1,0:T(8,128)} %bitcast.refs_0_), channel_id=1, source_target_pairs={{28,24},{29,25},{30,26},{31,27},{24,28},{25,29},{26,30},{27,31},{4... | collective-permute-start | bytes 1769480 | tf_op jit(solution)/shard_map/ppermute | solution.py:71
  3.1 17.5 %collective-permute-start.1 = (f32[384,384]{1,0:T(8,128)}, f32[384,384]{1,0:T(8,128)S(1)}, u32[]{:S(2)}, u32[]{:S(2)}) collective-permute-start(f32[384,384]{1,0:T(8,128)} %bitcast.9), channel_id=1, source_target_pairs={{0,4},{1,5},{2,6},{3,7},{4,8},{5,9},{6,10},{7,11},{8,12},{9,13},{1... | collective-permute-start | bytes 1769480 | tf_op jit(solution)/shard_map/ppermute | solution.py:71
  3.8 17.5 %collective-permute-start.12 = (f32[384,384]{1,0:T(8,128)}, f32[384,384]{1,0:T(8,128)S(1)}, u32[]{:S(2)}, u32[]{:S(2)}) collective-permute-start(f32[384,384]{1,0:T(8,128)} %bitcast.11), channel_id=1, source_target_pairs={{4,8},{5,9},{6,10},{7,11},{8,12},{9,13},{10,14},{11,15},{12,16},{1... | collective-permute-start | bytes 1769480 | tf_op jit(solution)/shard_map/ppermute | solution.py:71
  4.5 0.9 copy-start.1
  5.4 1.1 copy-start.3
  6.5 1.1 copy-start.4
  8.9 9.6 %collective-permute-start = (f32[384,256]{1,0:T(8,128)S(1)}, f32[384,256]{1,0:T(8,128)S(1)}, u32[]{:S(2)}, u32[]{:S(2)}) collective-permute-start(f32[384,256]{1,0:T(8,128)S(1)} %get-tuple-element.34.refs_0_.refs_6_), channel_id=1, source_target_pairs={{0,4},{1,5},{2,6},{3,7}} | collective-permute-start | bytes 1179656 | tf_op jit(solution)/shard_map/ppermute | solution.py:71
  9.6 12.3 %collective-permute-start.4 = (f32[384,384]{1,0:T(8,128)}, f32[384,384]{1,0:T(8,128)S(1)}, u32[]{:S(2)}, u32[]{:S(2)}) collective-permute-start(f32[384,384]{1,0:T(8,128)} %bitcast.refs_0_), channel_id=1, source_target_pairs={{8,0},{9,1},{10,2},{11,3}} | collective-permute-start | bytes 1769480 | tf_op jit(solution)/shard_map/ppermute | solution.py:71
  17.8 4.9 %collective-permute-start.10 = (f32[384,384]{1,0:T(8,128)}, f32[384,384]{1,0:T(8,128)S(1)}, u32[]{:S(2)}, u32[]{:S(2)}) collective-permute-start(f32[384,384]{1,0:T(8,128)} %bitcast.3.refs_3_), channel_id=1, source_target_pairs={{4,0},{5,1},{6,2},{7,3}} | collective-permute-start | bytes 1769480 | tf_op jit(solution)/shard_map/ppermute | solution.py:71
  18.6 18.3 %collective-permute-start.8 = (f32[384,384]{1,0:T(8,128)S(1)}, f32[384,384]{1,0:T(8,128)S(1)}, u32[]{:S(2)}, u32[]{:S(2)}) collective-permute-start(f32[384,384]{1,0:T(8,128)S(1)} %get-tuple-element.41), channel_id=1, source_target_pairs={{24,28},{25,29},{26,30},{27,31},{28,20},{29,21},{30,22},{31,23},{0... | collective-permute-start | bytes 1769480 | tf_op jit(solution)/shard_map/ppermute | solution.py:71
  20.5 17.2 %collective-permute-start.9 = (f32[384,384]{1,0:T(8,128)}, f32[384,384]{1,0:T(8,128)S(1)}, u32[]{:S(2)}, u32[]{:S(2)}) collective-permute-start(f32[384,384]{1,0:T(8,128)} %bitcast.3.refs_3_), channel_id=1, source_target_pairs={{0,4},{1,5},{2,6},{3,7},{8,12},{9,13},{10,14},{11,15}} | collective-permute-start | bytes 1769480 | tf_op jit(solution)/shard_map/ppermute | solution.py:71
  21.2 17.2 %collective-permute-start.15 = (f32[384,384]{1,0:T(8,128)}, f32[384,384]{1,0:T(8,128)S(1)}, u32[]{:S(2)}, u32[]{:S(2)}) collective-permute-start(f32[384,384]{1,0:T(8,128)} %bitcast.3.refs_3_), channel_id=1, source_target_pairs={{12,16},{13,17},{14,18},{15,19},{16,20},{17,21},{18,22},{19,23}} | collective-permute-start | bytes 1769480 | tf_op jit(solution)/shard_map/ppermute | solution.py:71
  21.9 27.9 %collective-permute-start.5 = (f32[384,384]{1,0:T(8,128)S(1)}, f32[384,384]{1,0:T(8,128)S(1)}, u32[]{:S(2)}, u32[]{:S(2)}) collective-permute-start(f32[384,384]{1,0:T(8,128)S(1)} %collective-permute-done.4), channel_id=1, source_target_pairs={{0,4},{1,5},{2,6},{3,7}} | collective-permute-start | bytes 1769480 | tf_op jit(solution)/shard_map/ppermute | solution.py:71
  22.7 28.2 %collective-permute-start.13 = (f32[384,384]{1,0:T(8,128)}, f32[384,384]{1,0:T(8,128)S(1)}, u32[]{:S(2)}, u32[]{:S(2)}) collective-permute-start(f32[384,384]{1,0:T(8,128)} %bitcast.refs_0_), channel_id=1, source_target_pairs={{12,8},{13,9},{14,10},{15,11}} | collective-permute-start | bytes 1769480 | tf_op jit(solution)/shard_map/ppermute | solution.py:71
  36.9 14.7 %collective-permute-start.11 = (f32[384,384]{1,0:T(8,128)S(1)}, f32[384,384]{1,0:T(8,128)S(1)}, u32[]{:S(2)}, u32[]{:S(2)}) collective-permute-start(f32[384,384]{1,0:T(8,128)S(1)} %collective-permute-done.10), channel_id=1, source_target_pairs={{0,8},{1,9},{2,10},{3,11}} | collective-permute-start | bytes 1769480 | tf_op jit(solution)/shard_map/ppermute | solution.py:71
  37.7 14.7 %collective-permute-start.14 = (f32[384,384]{1,0:T(8,128)}, f32[384,384]{1,0:T(8,128)S(1)}, u32[]{:S(2)}, u32[]{:S(2)}) collective-permute-start(f32[384,384]{1,0:T(8,128)} %bitcast.refs_0_), channel_id=1, source_target_pairs={{16,12},{17,13},{18,14},{19,15}} | collective-permute-start | bytes 1769480 | tf_op jit(solution)/shard_map/ppermute | solution.py:71
  38.4 22.3 %collective-permute-start.19 = (f32[384,384]{1,0:T(8,128)S(1)}, f32[384,384]{1,0:T(8,128)S(1)}, u32[]{:S(2)}, u32[]{:S(2)}) collective-permute-start(f32[384,384]{1,0:T(8,128)S(1)} %get-tuple-element.53), channel_id=1, source_target_pairs={{20,16},{21,17},{22,18},{23,19},{28,20},{29,21},{30,22},{31,23}} | collective-permute-start | bytes 1769480 | tf_op jit(solution)/shard_map/ppermute | solution.py:71
  49.9 11.5 %collective-permute-start.6 = (f32[384,384]{1,0:T(8,128)S(1)}, f32[384,384]{1,0:T(8,128)S(1)}, u32[]{:S(2)}, u32[]{:S(2)}) collective-permute-start(f32[384,384]{1,0:T(8,128)S(1)} %collective-permute-done.5), channel_id=1, source_target_pairs={{4,12},{5,13},{6,14},{7,15}} | collective-permute-start | bytes 1769480 | tf_op jit(solution)/shard_map/ppermute | solution.py:71
  50.8 12.6 %collective-permute-start.2 = (f32[384,384]{1,0:T(8,128)S(1)}, f32[384,384]{1,0:T(8,128)S(1)}, u32[]{:S(2)}, u32[]{:S(2)}) collective-permute-start(f32[384,384]{1,0:T(8,128)S(1)} %get-tuple-element.40.refs_3_.refs_1_.refs_2_), channel_id=1, source_target_pairs={{0,8},{1,9},{2,10},{3,11},{4,12},{5,13},{6,14},{7,15}} | collective-permute-start | bytes 1769480 | tf_op jit(solution)/shard_map/ppermute | solution.py:71
  51.6 13.2 %collective-permute-start.16 = (f32[384,384]{1,0:T(8,128)S(1)}, f32[384,384]{1,0:T(8,128)S(1)}, u32[]{:S(2)}, u32[]{:S(2)}) collective-permute-start(f32[384,384]{1,0:T(8,128)S(1)} %get-tuple-element.48.refs_4_), channel_id=1, source_target_pairs={{16,8},{17,9},{18,10},{19,11},{20,12},{21,13},{22,14},{23,15}} | collective-permute-start | bytes 1769480 | tf_op jit(solution)/shard_map/ppermute | solution.py:71
  52.3 9.8 %collective-permute-start.3 = (f32[384,128]{1,0:T(8,128)S(1)}, f32[384,128]{1,0:T(8,128)S(1)}, u32[]{:S(2)}, u32[]{:S(2)}) collective-permute-start(f32[384,128]{1,0:T(8,128)S(1)} %get-tuple-element.37.refs_0_), channel_id=1, source_target_pairs={{0,8},{1,9},{2,10},{3,11},{4,12},{5,13},{6,14},{7,15}} | collective-permute-start | bytes 589832 | tf_op jit(solution)/shard_map/ppermute | solution.py:71
  60.7 5.8 %collective-permute-start.24 = (f32[384,512]{1,0:T(8,128)S(1)}, f32[384,512]{1,0:T(8,128)S(1)}, u32[]{:S(2)}, u32[]{:S(2)}) collective-permute-start(f32[384,512]{1,0:T(8,128)S(1)} %get-tuple-element.49.refs_5_.refs_4_.refs_0_), channel_id=1, source_target_pairs={{0,8},{1,9},{2,10},{3,11},{4,12},{5,13},{6,14},{7,15}} | collective-permute-start | bytes 2359304 | tf_op jit(solution)/shard_map/ppermute | solution.py:71
  61.4 4.4 %collective-permute-start.21 = (f32[384,384]{1,0:T(8,128)S(1)}, f32[384,384]{1,0:T(8,128)S(1)}, u32[]{:S(2)}, u32[]{:S(2)}) collective-permute-start(f32[384,384]{1,0:T(8,128)S(1)} %get-tuple-element.56), channel_id=1, source_target_pairs={{16,8},{17,9},{18,10},{19,11},{20,12},{21,13},{22,14},{23,15}} | collective-permute-start | bytes 1769480 | tf_op jit(solution)/shard_map/ppermute | solution.py:71
  62.2 14.4 %collective-permute-start.18 = (f32[384,384]{1,0:T(8,128)S(1)}, f32[384,384]{1,0:T(8,128)S(1)}, u32[]{:S(2)}, u32[]{:S(2)}) collective-permute-start(f32[384,384]{1,0:T(8,128)S(1)} %get-tuple-element.52), channel_id=1, source_target_pairs={{20,24},{21,25},{22,26},{23,27},{24,28},{25,29},{26,30},{27,31}} | collective-permute-start | bytes 1769480 | tf_op jit(solution)/shard_map/ppermute | solution.py:71
  63.5 34.7 %collective-permute-start.20 = (f32[384,384]{1,0:T(8,128)S(1)}, f32[384,384]{1,0:T(8,128)S(1)}, u32[]{:S(2)}, u32[]{:S(2)}) collective-permute-start(f32[384,384]{1,0:T(8,128)S(1)} %get-tuple-element.55), channel_id=1, source_target_pairs={{16,24},{17,25},{18,26},{19,27},{20,28},{21,29},{22,30},{23,31}} | collective-permute-start | bytes 1769480 | tf_op jit(solution)/shard_map/ppermute | solution.py:71
  64.8 36.0 %collective-permute-start.17 = (f32[384,128]{1,0:T(8,128)S(1)}, f32[384,128]{1,0:T(8,128)S(1)}, u32[]{:S(2)}, u32[]{:S(2)}) collective-permute-start(f32[384,128]{1,0:T(8,128)S(1)} %get-tuple-element.50), channel_id=1, source_target_pairs={{8,16},{9,17},{10,18},{11,19},{12,20},{13,21},{14,22},{15,23}} | collective-permute-start | bytes 589832 | tf_op jit(solution)/shard_map/ppermute | solution.py:71
  65.8 35.8 %collective-permute-start.22 = (f32[384,128]{1,0:T(8,128)S(1)}, f32[384,128]{1,0:T(8,128)S(1)}, u32[]{:S(2)}, u32[]{:S(2)}) collective-permute-start(f32[384,128]{1,0:T(8,128)S(1)} %shard_map.99.refs_8_), channel_id=1, source_target_pairs={{9,25},{11,27},{13,29},{15,31}} | collective-permute-start | bytes 589832 | tf_op jit(solution)/shard_map/ppermute | solution.py:71
  66.5 49.3 %collective-permute-start.23 = (f32[384,128]{1,0:T(8,128)S(1)}, f32[384,128]{1,0:T(8,128)S(1)}, u32[]{:S(2)}, u32[]{:S(2)}) collective-permute-start(f32[384,128]{1,0:T(8,128)S(1)} %shard_map.99.refs_8_), channel_id=1, source_target_pairs={{8,24},{10,26},{12,28},{14,30}} | collective-permute-start | bytes 589832 | tf_op jit(solution)/shard_map/ppermute | solution.py:71
  76.6 42.9 %collective-permute-start.25 = (f32[384,128]{1,0:T(8,128)S(1)}, f32[384,128]{1,0:T(8,128)S(1)}, u32[]{:S(2)}, u32[]{:S(2)}) collective-permute-start(f32[384,128]{1,0:T(8,128)S(1)} %get-tuple-element.63), channel_id=1, source_target_pairs={{8,16},{9,17},{10,18},{11,19},{12,20},{13,21},{14,22},{15,23}} | collective-permute-start | bytes 589832 | tf_op jit(solution)/shard_map/ppermute | solution.py:71
  98.2 21.8 %collective-permute-start.26 = (f32[384,128]{1,0:T(8,128)S(1)}, f32[384,128]{1,0:T(8,128)S(1)}, u32[]{:S(2)}, u32[]{:S(2)}) collective-permute-start(f32[384,128]{1,0:T(8,128)S(1)} %get-tuple-element.64), channel_id=1, source_target_pairs={{8,24},{9,25},{10,26},{11,27},{12,28},{13,29},{14,30},{15,31}} | collective-permute-start | bytes 589832 | tf_op jit(solution)/shard_map/ppermute | solution.py:71
  100.8 25.3 %copy-start = (f32[1,4,384,384]{3,2,1,0:T(8,128)S(1)}, f32[1,4,384,384]{3,2,1,0:T(8,128)}, u32[]{:S(2)}) copy-start(f32[1,4,384,384]{3,2,1,0:T(8,128)} %param.10) | copy-start | bytes 7077892
  100.8 25.3 %copy-start.2 = (f32[384,128]{1,0:T(8,128)S(1)}, f32[384,128]{1,0:T(8,128)}, u32[]{:S(2)}) copy-start(f32[384,128]{1,0:T(8,128)} %refs_4_.3) | copy-start | bytes 589828
  100.8 19.9 %collective-permute-start.27 = (f32[384,128]{1,0:T(8,128)S(1)}, f32[384,128]{1,0:T(8,128)S(1)}, u32[]{:S(2)}, u32[]{:S(2)}) collective-permute-start(f32[384,128]{1,0:T(8,128)S(1)} %get-tuple-element.47.refs_4_.refs_0_), channel_id=1, source_target_pairs={{0,1},{1,2},{2,3},{3,4},{4,5},{5,6},{6,7},{7,8},{8,9},{9,10},{10,1... | collective-permute-start | bytes 589832 | tf_op jit(solution)/shard_map/ppermute | solution.py:296
  116.9 3.8 %collective-permute-start.29 = (f32[384,128]{1,0:T(8,128)}, f32[384,128]{1,0:T(8,128)S(1)}, u32[]{:S(2)}, u32[]{:S(2)}) collective-permute-start(f32[384,128]{1,0:T(8,128)} %shard_map.101), channel_id=1, source_target_pairs={{16,17},{18,19},{20,21},{22,23},{24,25},{26,27},{28,29},{30,31}} | collective-permute-start | bytes 589832 | tf_op jit(solution)/shard_map/ppermute | solution.py:296
  118.2 7.9 %collective-permute-start.28 = (f32[384,128]{1,0:T(8,128)S(1)}, f32[384,128]{1,0:T(8,128)S(1)}, u32[]{:S(2)}, u32[]{:S(2)}) collective-permute-start(f32[384,128]{1,0:T(8,128)S(1)} %shard_map.100.refs_0_), channel_id=1, source_target_pairs={{17,18},{19,20},{21,22},{23,24},{25,26},{27,28},{29,30}} | collective-permute-start | bytes 589832 | tf_op jit(solution)/shard_map/ppermute | solution.py:296

commit v8 on v7

--- a/solution.py
+++ b/solution.py
@@ -84,6 +84,7 @@
     u1_over = moved(u, [(1, 0)])
     u0 = moved(u, [(3, 4), (4, 5)])
     u0_low = moved(u, [(0, 1), (2, 3)])
+    qa_raw = moved(q, [(0, 2)])
     r_late = moved(r, [(3, 2)])
     r_next = moved(r, [(4, 3)])
 
@@ -136,7 +137,7 @@
             q1[...] = q[...] + product(t[...], product(q0[...], hu))
 
     (q1, hu) = staged(forward_q, stride, [q0, r, t, q, u], [square] * 2, 6)
-    qa = moved(q1, low)
+    qa = moved(q1, [(1, 3)])
 
     maps = depth_maps[0]
 
@@ -232,43 +233,45 @@
 
     (r1,) = staged(own_fields, stride, [r2_up, hopped, w_low], [square], 0.1)
 
-    def second_q(k, r1, qa, q1, t1, both, q2, hu_out):
-        @pl.when((k == 2) | (k == 3))
-        def _():
-            hu = summed(product(r1[...], qa[...]), both[:, : q1.shape[1]], True)
+    def second_q(k, r1, qa_raw, qa, q1, t1, both, q2, hu_out):
+        @pl.when((k == 2) | (k == 3))
+        def _():
+            came = jnp.where(k == 2, qa_raw[...], qa[...])
+            hu = summed(product(r1[...], came), both[:, : q1.shape[1]], True)
             hu_out[...] = hu
-            q2[...] = q1[...] + product(t1[...], product(qa[...], hu))
-
-    (q2, hu2) = staged(second_q, stride, [r1, qa, q1, t1, both], [square] * 2, 6)
-
-    def second_fields(k, f1, qa, fa, r1, t1, f2, g2):
+            q2[...] = q1[...] + product(t1[...], product(came, hu))
+
+    (q2, hu2) = staged(second_q, stride, [r1, qa_raw, qa, q1, t1, both], [square] * 2, 6)
+
+    def second_fields(k, f1, qa_raw, qa, fa, r1, t1, f2, g2):
         @pl.when(k < 2)
         def _():
             f2[...] = f1[...]
 
         @pl.when((k == 2) | (k == 3))
         def _():
-            g = summed(product(qa[...], r1[...]), fa[...], True)
+            came = jnp.where(k == 2, qa_raw[...], qa[...])
+            g = summed(product(came, r1[...]), fa[...], True)
             g2[...] = g
             f2[...] = product(t1[...], g)
 
-    (f2, g2) = staged(second_fields, stride, [f1, qa, fa, r1, t1], [field, field], 2)
-
-    def third_fields(k, r_late, r_next, w_came, q1, t1, both, r1, qa, fa, w4, g4, rc4):
+    (f2, g2) = staged(second_fields, stride, [f1, qa_raw, qa, fa, r1, t1], [field, field], 2)
+
+    def third_fields(k, r_late, r_next, w_came, q1, t1, both, r1, qa_raw, qa, fa, w4, g4, rc4):
         @pl.when((k == 2) | (k == 3))
         def _():
             came = jnp.where(k == 2, r_late[...], r_next[...]) + w_came[...]
             gt = summed(product(q1[...], came), t1[...], True)
             rc = r1[...] + product(both[:, : q1.shape[1]], product(came, gt))
             rc4[...] = rc
-            g = summed(product(qa[...], rc), fa[...], True)
+            g = summed(product(jnp.where(k == 2, qa_raw[...], qa[...]), rc), fa[...], True)
             g4[...] = g
             w4[...] = product(gt, g)
 
     (w4, g4, rc4) = staged(
         third_fields,
         stride,
-        [r_late, r_next, w_came, q1, t1, both, r1, qa, fa],
+        [r_late, r_next, w_came, q1, t1, both, r1, qa_raw, qa, fa],
         [field, field, square],
         9,
     )

time: 129 us -> 128 us (level)
  waiting for transfers between devices: 78.4 us -> 74.8 us
  local copies, waits for them, and re-layouts: 3.06 us -> 5.1 us
    ppermute x27 -> x28, waiting for transfers between devices: 73 us -> 69.4 us  [moved(): return lax.ppermute(value, 'sec', pairs)]
    unnamed x10 -> x16, local copies, waits for them, and re-layouts: 3.06 us -> 5.1 us
    ppermute x27 -> x28, starting transfers between devices: 34.8 us -> 35.2 us  [moved(): return lax.ppermute(value, 'sec', pairs)]
  transfers between devices with their start and end apart: 30 -> 31, of which waited for: 8 -> 8; matrix products, arithmetic and copies ran while one was open for 0% -> 0% of each run, Pallas kernels for 4% -> 4%
where the time goes in v8:
time: 128 us; the launch traced here: 127 us
  waiting for transfers between devices  74.8 us (58%)
  starting transfers between devices  38.6 us (30%)
  Pallas kernels  7.07 us (6%)
  local copies, waits for them, and re-layouts  5.1 us (4%)
    ppermute x28, waiting for transfers between devices, moved(): return lax.ppermute(value, 'sec', pairs)  69.4 us
    ppermute x28, starting transfers between devices, moved(): return lax.ppermute(value, 'sec', pairs)  35.2 us
    pallas_call x20, Pallas kernels, staged(): pl.pallas_call(kernel, out_shape=[jax.ShapeDtypeStruct(shape, dtype) for...  7.07 us
    ppermute x3, waiting for transfers between devices, passed(): return lax.ppermute(value, 'sec', pairs)  5.36 us
    unnamed x16, local copies, waits for them, and re-layouts  5.1 us
    ppermute x3, starting transfers between devices, passed(): return lax.ppermute(value, 'sec', pairs)  3.39 us
  transfers between devices with their start and end apart: 31, of which 8 were waited for; matrix products, arithmetic and copies ran while one was open for 0% of the time, Pallas kernels for 4%

profile of v8, /device:TPU:28, one launch (start us, length us, event | category | flops | bytes accessed | tf_op | source)
XLA Modules:
  0.0 126.8 jit_solution(3392545388139304460)
XLA Ops:
  0.6 2.4 %collective-permute-start.8 = (f32[384,384]{1,0:T(8,128)}, f32[384,384]{1,0:T(8,128)S(1)}, u32[]{:S(2)}, u32[]{:S(2)}) collective-permute-start(f32[384,384]{1,0:T(8,128)} %bitcast.refs_0_), channel_id=1, source_target_pairs={{28,24},{29,25},{30,26},{31,27},{24,28},{25,29},{26,30},{27,31},{4... | collective-permute-start | bytes 1769480 | tf_op jit(solution)/shard_map/ppermute | solution.py:71
  3.1 0.7 collective-permute-start.1
  3.8 0.7 collective-permute-start.13
  4.5 0.7 collective-permute-start.11
  5.2 0.9 copy-done.1
  6.1 1.1 copy-done.3
  7.2 1.1 copy-done.4
  8.2 1.1 copy-done.6
  9.3 1.2 shard_map.85
  10.5 0.7 collective-permute-start
  11.2 6.6 %collective-permute-done.8.refs_0_ = f32[384,384]{1,0:T(8,128)S(1)} collective-permute-done((f32[384,384]{1,0:T(8,128)}, f32[384,384]{1,0:T(8,128)S(1)}, u32[]{:S(2)}, u32[]{:S(2)}) %collective-permute-start.8) | collective-permute-done | bytes 589856 | tf_op jit(solution)/shard_map/ppermute | solution.py:71
  17.8 0.7 collective-permute-start.5
  18.6 1.0 copy-done.7
  19.6 0.7 collective-permute-start.10
  20.3 1.9 %collective-permute-start.9 = (f32[384,384]{1,0:T(8,128)S(1)}, f32[384,384]{1,0:T(8,128)S(1)}, u32[]{:S(2)}, u32[]{:S(2)}) collective-permute-start(f32[384,384]{1,0:T(8,128)S(1)} %get-tuple-element.41), channel_id=1, source_target_pairs={{24,28},{25,29},{26,30},{27,31},{28,20},{29,21},{30,22},{31,23},{0... | collective-permute-start | bytes 1769480 | tf_op jit(solution)/shard_map/ppermute | solution.py:71
  22.2 0.7 collective-permute-start.2
  22.9 0.7 collective-permute-start.16
  23.7 0.7 collective-permute-start.6
  24.4 0.7 collective-permute-start.14
  25.1 12.5 %collective-permute-done.9.refs_1_.refs_0_ = f32[384,384]{1,0:T(8,128)S(1)} collective-permute-done((f32[384,384]{1,0:T(8,128)S(1)}, f32[384,384]{1,0:T(8,128)S(1)}, u32[]{:S(2)}, u32[]{:S(2)}) %collective-permute-start.9) | collective-permute-done | bytes 589856 | tf_op jit(solution)/shard_map/ppermute | solution.py:71
  37.6 0.7 collective-permute-start.12
  38.4 0.7 collective-permute-start.15
  39.1 11.2 %collective-permute-start.20 = (f32[384,384]{1,0:T(8,128)S(1)}, f32[384,384]{1,0:T(8,128)S(1)}, u32[]{:S(2)}, u32[]{:S(2)}) collective-permute-start(f32[384,384]{1,0:T(8,128)S(1)} %get-tuple-element.53), channel_id=1, source_target_pairs={{20,16},{21,17},{22,18},{23,19},{28,20},{29,21},{30,22},{31,23}} | collective-permute-start | bytes 1769480 | tf_op jit(solution)/shard_map/ppermute | solution.py:71
  50.4 0.7 collective-permute-start.7
  51.4 0.7 collective-permute-start.3
  52.1 0.7 collective-permute-start.17
  52.9 0.7 collective-permute-start.4
  53.5 7.6 %collective-permute-done.20.refs_0_ = f32[384,384]{1,0:T(8,128)S(1)} collective-permute-done((f32[384,384]{1,0:T(8,128)S(1)}, f32[384,384]{1,0:T(8,128)S(1)}, u32[]{:S(2)}, u32[]{:S(2)}) %collective-permute-start.20) | collective-permute-done | bytes 589856 | tf_op jit(solution)/shard_map/ppermute | solution.py:71
  61.2 0.7 collective-permute-start.25
  61.9 0.7 collective-permute-start.22
  62.7 1.3 %collective-permute-start.19 = (f32[384,384]{1,0:T(8,128)S(1)}, f32[384,384]{1,0:T(8,128)S(1)}, u32[]{:S(2)}, u32[]{:S(2)}) collective-permute-start(f32[384,384]{1,0:T(8,128)S(1)} %get-tuple-element.52), channel_id=1, source_target_pairs={{20,24},{21,25},{22,26},{23,27},{24,28},{25,29},{26,30},{27,31}} | collective-permute-start | bytes 1769480 | tf_op jit(solution)/shard_map/ppermute | solution.py:71
  64.0 1.3 %collective-permute-start.21 = (f32[384,384]{1,0:T(8,128)S(1)}, f32[384,384]{1,0:T(8,128)S(1)}, u32[]{:S(2)}, u32[]{:S(2)}) collective-permute-start(f32[384,384]{1,0:T(8,128)S(1)} %get-tuple-element.55), channel_id=1, source_target_pairs={{16,24},{17,25},{18,26},{19,27},{20,28},{21,29},{22,30},{23,31}} | collective-permute-start | bytes 1769480 | tf_op jit(solution)/shard_map/ppermute | solution.py:71
  65.3 0.7 collective-permute-start.18
  66.3 0.7 collective-permute-start.23
  67.0 1.3 %collective-permute-start.24 = (f32[384,128]{1,0:T(8,128)S(1)}, f32[384,128]{1,0:T(8,128)S(1)}, u32[]{:S(2)}, u32[]{:S(2)}) collective-permute-start(f32[384,128]{1,0:T(8,128)S(1)} %shard_map.99.refs_8_), channel_id=1, source_target_pairs={{8,24},{10,26},{12,28},{14,30}} | collective-permute-start | bytes 589832 | tf_op jit(solution)/shard_map/ppermute | solution.py:71
  68.3 8.7 %collective-permute-done.19.refs_1_ = f32[384,384]{1,0:T(8,128)S(1)} collective-permute-done((f32[384,384]{1,0:T(8,128)S(1)}, f32[384,384]{1,0:T(8,128)S(1)}, u32[]{:S(2)}, u32[]{:S(2)}) %collective-permute-start.19) | collective-permute-done | bytes 589856 | tf_op jit(solution)/shard_map/ppermute | solution.py:71
  77.1 0.7 collective-permute-start.26
  77.7 19.2 %collective-permute-done.21.refs_2_ = f32[384,384]{1,0:T(8,128)S(1)} collective-permute-done((f32[384,384]{1,0:T(8,128)S(1)}, f32[384,384]{1,0:T(8,128)S(1)}, u32[]{:S(2)}, u32[]{:S(2)}) %collective-permute-start.21) | collective-permute-done | bytes 589856 | tf_op jit(solution)/shard_map/ppermute | solution.py:71
  97.0 1.3 %collective-permute-start.27 = (f32[384,128]{1,0:T(8,128)S(1)}, f32[384,128]{1,0:T(8,128)S(1)}, u32[]{:S(2)}, u32[]{:S(2)}) collective-permute-start(f32[384,128]{1,0:T(8,128)S(1)} %get-tuple-element.64), channel_id=1, source_target_pairs={{8,24},{9,25},{10,26},{11,27},{12,28},{13,29},{14,30},{15,31}} | collective-permute-start | bytes 589832 | tf_op jit(solution)/shard_map/ppermute | solution.py:71
  98.3 1.3 shard_map.97.refs_3_.refs_1_
  99.5 0.8 collective-permute-start.28
  100.4 14.1 %collective-permute-done.24.refs_2_ = f32[384,128]{1,0:T(8,128)S(1)} collective-permute-done((f32[384,128]{1,0:T(8,128)S(1)}, f32[384,128]{1,0:T(8,128)S(1)}, u32[]{:S(2)}, u32[]{:S(2)}) %collective-permute-start.24) | collective-permute-done | bytes 196640 | tf_op jit(solution)/shard_map/ppermute | solution.py:71
  114.6 1.1 shard_map.101
  115.6 1.3 %collective-permute-start.30 = (f32[384,128]{1,0:T(8,128)}, f32[384,128]{1,0:T(8,128)S(1)}, u32[]{:S(2)}, u32[]{:S(2)}) collective-permute-start(f32[384,128]{1,0:T(8,128)} %shard_map.101), channel_id=1, source_target_pairs={{16,17},{18,19},{20,21},{22,23},{24,25},{26,27},{28,29},{30,31}} | collective-permute-start | bytes 589832 | tf_op jit(solution)/shard_map/ppermute | solution.py:299
  116.9 1.3 %collective-permute-start.29 = (f32[384,128]{1,0:T(8,128)S(1)}, f32[384,128]{1,0:T(8,128)S(1)}, u32[]{:S(2)}, u32[]{:S(2)}) collective-permute-start(f32[384,128]{1,0:T(8,128)S(1)} %shard_map.100.refs_0_), channel_id=1, source_target_pairs={{17,18},{19,20},{21,22},{23,24},{25,26},{27,28},{29,30}} | collective-permute-start | bytes 589832 | tf_op jit(solution)/shard_map/ppermute | solution.py:299
  118.8 0.7 shard_map.103
  119.5 5.4 %collective-permute-done.29.refs_2_ = f32[384,128]{1,0:T(8,128)S(1)} collective-permute-done((f32[384,128]{1,0:T(8,128)S(1)}, f32[384,128]{1,0:T(8,128)S(1)}, u32[]{:S(2)}, u32[]{:S(2)}) %collective-permute-start.29) | collective-permute-done | bytes 196640 | tf_op jit(solution)/shard_map/ppermute | solution.py:299
  124.8 2.0 %shard_map.104 = f32[4,384,128]{2,1,0:T(8,128)} custom-call(f32[4,384,384]{2,1,0:T(8,128)S(1)} %bitcast.8, f32[384,128]{1,0:T(8,128)S(1)} %collective-permute-done.28.refs_1_, f32[384,128]{1,0:T(8,128)S(1)} %collective-permute-done.29.refs_2_, f32[384,128]{1,0:T(8,128)S(1)} %collective-permute-done.30.refs_3_, f32[384,128]{1,0:T(8,128)S(1)} %copy-done.2), custom_call_target="tpu_custom_call" | custom-call | flops 339738624 | bytes 3538944 | tf_op jit(solution)/shard_map/pallas_call | solution.py:48
  (50 shorter events, 1.5 us)
Async XLA Ops:
  0.6 17.2 %collective-permute-start.8 = (f32[384,384]{1,0:T(8,128)}, f32[384,384]{1,0:T(8,128)S(1)}, u32[]{:S(2)}, u32[]{:S(2)}) collective-permute-start(f32[384,384]{1,0:T(8,128)} %bitcast.refs_0_), channel_id=1, source_target_pairs={{28,24},{29,25},{30,26},{31,27},{24,28},{25,29},{26,30},{27,31},{4... | collective-permute-start | bytes 1769480 | tf_op jit(solution)/shard_map/ppermute | solution.py:71
  3.1 17.2 %collective-permute-start.1 = (f32[384,384]{1,0:T(8,128)}, f32[384,384]{1,0:T(8,128)S(1)}, u32[]{:S(2)}, u32[]{:S(2)}) collective-permute-start(f32[384,384]{1,0:T(8,128)} %bitcast.11), channel_id=1, source_target_pairs={{0,4},{1,5},{2,6},{3,7},{4,8},{5,9},{6,10},{7,11},{8,12},{9,13},{1... | collective-permute-start | bytes 1769480 | tf_op jit(solution)/shard_map/ppermute | solution.py:71
  3.8 18.4 %collective-permute-start.13 = (f32[384,384]{1,0:T(8,128)}, f32[384,384]{1,0:T(8,128)S(1)}, u32[]{:S(2)}, u32[]{:S(2)}) collective-permute-start(f32[384,384]{1,0:T(8,128)} %bitcast.9), channel_id=1, source_target_pairs={{4,8},{5,9},{6,10},{7,11},{8,12},{9,13},{10,14},{11,15},{12,16},{1... | collective-permute-start | bytes 1769480 | tf_op jit(solution)/shard_map/ppermute | solution.py:71
  4.5 18.5 %collective-permute-start.11 = (f32[384,384]{1,0:T(8,128)}, f32[384,384]{1,0:T(8,128)S(1)}, u32[]{:S(2)}, u32[]{:S(2)}) collective-permute-start(f32[384,384]{1,0:T(8,128)} %bitcast.14), channel_id=1, source_target_pairs={{4,0},{5,1},{6,2},{7,3}} | collective-permute-start | bytes 1769480 | tf_op jit(solution)/shard_map/ppermute | solution.py:71
  5.2 0.9 copy-start.1
  6.1 1.1 copy-start.3
  7.2 1.1 copy-start.4
  8.2 1.1 copy-start.6
  10.5 8.1 %collective-permute-start = (f32[384,256]{1,0:T(8,128)S(1)}, f32[384,256]{1,0:T(8,128)S(1)}, u32[]{:S(2)}, u32[]{:S(2)}) collective-permute-start(f32[384,256]{1,0:T(8,128)S(1)} %get-tuple-element.34.refs_0_.refs_6_), channel_id=1, source_target_pairs={{0,4},{1,5},{2,6},{3,7}} | collective-permute-start | bytes 1179656 | tf_op jit(solution)/shard_map/ppermute | solution.py:71
  17.8 5.8 %collective-permute-start.5 = (f32[384,384]{1,0:T(8,128)}, f32[384,384]{1,0:T(8,128)S(1)}, u32[]{:S(2)}, u32[]{:S(2)}) collective-permute-start(f32[384,384]{1,0:T(8,128)} %bitcast.refs_0_), channel_id=1, source_target_pairs={{8,0},{9,1},{10,2},{11,3}} | collective-permute-start | bytes 1769480 | tf_op jit(solution)/shard_map/ppermute | solution.py:71
  18.5 1.1 copy-start.7
  18.5 3.7 %copy-start.5 = (f32[1,384,384]{2,1,0:T(8,128)S(1)}, f32[1,384,384]{2,1,0:T(8,128)}, u32[]{:S(2)}) copy-start(f32[1,384,384]{2,1,0:T(8,128)} %param.8) | copy-start | bytes 1769476
  19.6 4.8 %collective-permute-start.10 = (f32[384,384]{1,0:T(8,128)S(1)}, f32[384,384]{1,0:T(8,128)S(1)}, u32[]{:S(2)}, u32[]{:S(2)}) collective-permute-start(f32[384,384]{1,0:T(8,128)S(1)} %bitcast.16), channel_id=1, source_target_pairs={{0,4},{1,5},{2,6},{3,7},{8,12},{9,13},{10,14},{11,15}} | collective-permute-start | bytes 1769480 | tf_op jit(solution)/shard_map/ppermute | solution.py:71
  20.3 17.3 %collective-permute-start.9 = (f32[384,384]{1,0:T(8,128)S(1)}, f32[384,384]{1,0:T(8,128)S(1)}, u32[]{:S(2)}, u32[]{:S(2)}) collective-permute-start(f32[384,384]{1,0:T(8,128)S(1)} %get-tuple-element.41), channel_id=1, source_target_pairs={{24,28},{25,29},{26,30},{27,31},{28,20},{29,21},{30,22},{31,23},{0... | collective-permute-start | bytes 1769480 | tf_op jit(solution)/shard_map/ppermute | solution.py:71
  22.2 16.2 %collective-permute-start.2 = (f32[384,384]{1,0:T(8,128)S(1)}, f32[384,384]{1,0:T(8,128)S(1)}, u32[]{:S(2)}, u32[]{:S(2)}) collective-permute-start(f32[384,384]{1,0:T(8,128)S(1)} %bitcast.13), channel_id=1, source_target_pairs={{0,8},{1,9},{2,10},{3,11}} | collective-permute-start | bytes 1769480 | tf_op jit(solution)/shard_map/ppermute | solution.py:71
  22.9 16.2 %collective-permute-start.16 = (f32[384,384]{1,0:T(8,128)S(1)}, f32[384,384]{1,0:T(8,128)S(1)}, u32[]{:S(2)}, u32[]{:S(2)}) collective-permute-start(f32[384,384]{1,0:T(8,128)S(1)} %bitcast.17), channel_id=1, source_target_pairs={{12,16},{13,17},{14,18},{15,19},{16,20},{17,21},{18,22},{19,23}} | collective-permute-start | bytes 1769480 | tf_op jit(solution)/shard_map/ppermute | solution.py:71
  23.7 26.7 %collective-permute-start.6 = (f32[384,384]{1,0:T(8,128)S(1)}, f32[384,384]{1,0:T(8,128)S(1)}, u32[]{:S(2)}, u32[]{:S(2)}) collective-permute-start(f32[384,384]{1,0:T(8,128)S(1)} %collective-permute-done.5), channel_id=1, source_target_pairs={{0,4},{1,5},{2,6},{3,7}} | collective-permute-start | bytes 1769480 | tf_op jit(solution)/shard_map/ppermute | solution.py:71
  24.4 27.0 %collective-permute-start.14 = (f32[384,384]{1,0:T(8,128)}, f32[384,384]{1,0:T(8,128)S(1)}, u32[]{:S(2)}, u32[]{:S(2)}) collective-permute-start(f32[384,384]{1,0:T(8,128)} %bitcast.refs_0_), channel_id=1, source_target_pairs={{12,8},{13,9},{14,10},{15,11}} | collective-permute-start | bytes 1769480 | tf_op jit(solution)/shard_map/ppermute | solution.py:71
  37.6 14.4 %collective-permute-start.12 = (f32[384,384]{1,0:T(8,128)S(1)}, f32[384,384]{1,0:T(8,128)S(1)}, u32[]{:S(2)}, u32[]{:S(2)}) collective-permute-start(f32[384,384]{1,0:T(8,128)S(1)} %collective-permute-done.11), channel_id=1, source_target_pairs={{0,8},{1,9},{2,10},{3,11}} | collective-permute-start | bytes 1769480 | tf_op jit(solution)/shard_map/ppermute | solution.py:71
  38.4 14.4 %collective-permute-start.15 = (f32[384,384]{1,0:T(8,128)}, f32[384,384]{1,0:T(8,128)S(1)}, u32[]{:S(2)}, u32[]{:S(2)}) collective-permute-start(f32[384,384]{1,0:T(8,128)} %bitcast.refs_0_), channel_id=1, source_target_pairs={{16,12},{17,13},{18,14},{19,15}} | collective-permute-start | bytes 1769480 | tf_op jit(solution)/shard_map/ppermute | solution.py:71
  39.1 22.0 %collective-permute-start.20 = (f32[384,384]{1,0:T(8,128)S(1)}, f32[384,384]{1,0:T(8,128)S(1)}, u32[]{:S(2)}, u32[]{:S(2)}) collective-permute-start(f32[384,384]{1,0:T(8,128)S(1)} %get-tuple-element.53), channel_id=1, source_target_pairs={{20,16},{21,17},{22,18},{23,19},{28,20},{29,21},{30,22},{31,23}} | collective-permute-start | bytes 1769480 | tf_op jit(solution)/shard_map/ppermute | solution.py:71
  50.4 11.5 %collective-permute-start.7 = (f32[384,384]{1,0:T(8,128)S(1)}, f32[384,384]{1,0:T(8,128)S(1)}, u32[]{:S(2)}, u32[]{:S(2)}) collective-permute-start(f32[384,384]{1,0:T(8,128)S(1)} %collective-permute-done.6), channel_id=1, source_target_pairs={{4,12},{5,13},{6,14},{7,15}} | collective-permute-start | bytes 1769480 | tf_op jit(solution)/shard_map/ppermute | solution.py:71
  51.4 12.6 %collective-permute-start.3 = (f32[384,384]{1,0:T(8,128)S(1)}, f32[384,384]{1,0:T(8,128)S(1)}, u32[]{:S(2)}, u32[]{:S(2)}) collective-permute-start(f32[384,384]{1,0:T(8,128)S(1)} %get-tuple-element.40.refs_3_.refs_1_), channel_id=1, source_target_pairs={{4,12},{5,13},{6,14},{7,15}} | collective-permute-start | bytes 1769480 | tf_op jit(solution)/shard_map/ppermute | solution.py:71
  52.1 13.2 %collective-permute-start.17 = (f32[384,384]{1,0:T(8,128)S(1)}, f32[384,384]{1,0:T(8,128)S(1)}, u32[]{:S(2)}, u32[]{:S(2)}) collective-permute-start(f32[384,384]{1,0:T(8,128)S(1)} %get-tuple-element.48.refs_4_), channel_id=1, source_target_pairs={{16,8},{17,9},{18,10},{19,11},{20,12},{21,13},{22,14},{23,15}} | collective-permute-start | bytes 1769480 | tf_op jit(solution)/shard_map/ppermute | solution.py:71
  52.9 9.8 %collective-permute-start.4 = (f32[384,128]{1,0:T(8,128)S(1)}, f32[384,128]{1,0:T(8,128)S(1)}, u32[]{:S(2)}, u32[]{:S(2)}) collective-permute-start(f32[384,128]{1,0:T(8,128)S(1)} %get-tuple-element.37.refs_0_), channel_id=1, source_target_pairs={{0,8},{1,9},{2,10},{3,11},{4,12},{5,13},{6,14},{7,15}} | collective-permute-start | bytes 589832 | tf_op jit(solution)/shard_map/ppermute | solution.py:71
  61.2 5.8 %collective-permute-start.25 = (f32[384,512]{1,0:T(8,128)S(1)}, f32[384,512]{1,0:T(8,128)S(1)}, u32[]{:S(2)}, u32[]{:S(2)}) collective-permute-start(f32[384,512]{1,0:T(8,128)S(1)} %get-tuple-element.49.refs_5_.refs_0_), channel_id=1, source_target_pairs={{0,8},{1,9},{2,10},{3,11},{4,12},{5,13},{6,14},{7,15}} | collective-permute-start | bytes 2359304 | tf_op jit(solution)/shard_map/ppermute | solution.py:71
  61.9 4.4 %collective-permute-start.22 = (f32[384,384]{1,0:T(8,128)S(1)}, f32[384,384]{1,0:T(8,128)S(1)}, u32[]{:S(2)}, u32[]{:S(2)}) collective-permute-start(f32[384,384]{1,0:T(8,128)S(1)} %get-tuple-element.56), channel_id=1, source_target_pairs={{16,8},{17,9},{18,10},{19,11},{20,12},{21,13},{22,14},{23,15}} | collective-permute-start | bytes 1769480 | tf_op jit(solution)/shard_map/ppermute | solution.py:71
  62.7 14.4 %collective-permute-start.19 = (f32[384,384]{1,0:T(8,128)S(1)}, f32[384,384]{1,0:T(8,128)S(1)}, u32[]{:S(2)}, u32[]{:S(2)}) collective-permute-start(f32[384,384]{1,0:T(8,128)S(1)} %get-tuple-element.52), channel_id=1, source_target_pairs={{20,24},{21,25},{22,26},{23,27},{24,28},{25,29},{26,30},{27,31}} | collective-permute-start | bytes 1769480 | tf_op jit(solution)/shard_map/ppermute | solution.py:71
  64.0 33.0 %collective-permute-start.21 = (f32[384,384]{1,0:T(8,128)S(1)}, f32[384,384]{1,0:T(8,128)S(1)}, u32[]{:S(2)}, u32[]{:S(2)}) collective-permute-start(f32[384,384]{1,0:T(8,128)S(1)} %get-tuple-element.55), channel_id=1, source_target_pairs={{16,24},{17,25},{18,26},{19,27},{20,28},{21,29},{22,30},{23,31}} | collective-permute-start | bytes 1769480 | tf_op jit(solution)/shard_map/ppermute | solution.py:71
  65.3 34.2 %collective-permute-start.18 = (f32[384,128]{1,0:T(8,128)S(1)}, f32[384,128]{1,0:T(8,128)S(1)}, u32[]{:S(2)}, u32[]{:S(2)}) collective-permute-start(f32[384,128]{1,0:T(8,128)S(1)} %get-tuple-element.50), channel_id=1, source_target_pairs={{8,16},{9,17},{10,18},{11,19},{12,20},{13,21},{14,22},{15,23}} | collective-permute-start | bytes 589832 | tf_op jit(solution)/shard_map/ppermute | solution.py:71
  66.3 34.0 %collective-permute-start.23 = (f32[384,128]{1,0:T(8,128)S(1)}, f32[384,128]{1,0:T(8,128)S(1)}, u32[]{:S(2)}, u32[]{:S(2)}) collective-permute-start(f32[384,128]{1,0:T(8,128)S(1)} %shard_map.99.refs_8_), channel_id=1, source_target_pairs={{9,25},{11,27},{13,29},{15,31}} | collective-permute-start | bytes 589832 | tf_op jit(solution)/shard_map/ppermute | solution.py:71
  67.0 47.5 %collective-permute-start.24 = (f32[384,128]{1,0:T(8,128)S(1)}, f32[384,128]{1,0:T(8,128)S(1)}, u32[]{:S(2)}, u32[]{:S(2)}) collective-permute-start(f32[384,128]{1,0:T(8,128)S(1)} %shard_map.99.refs_8_), channel_id=1, source_target_pairs={{8,24},{10,26},{12,28},{14,30}} | collective-permute-start | bytes 589832 | tf_op jit(solution)/shard_map/ppermute | solution.py:71
  77.1 41.2 %collective-permute-start.26 = (f32[384,128]{1,0:T(8,128)S(1)}, f32[384,128]{1,0:T(8,128)S(1)}, u32[]{:S(2)}, u32[]{:S(2)}) collective-permute-start(f32[384,128]{1,0:T(8,128)S(1)} %get-tuple-element.63), channel_id=1, source_target_pairs={{8,16},{9,17},{10,18},{11,19},{12,20},{13,21},{14,22},{15,23}} | collective-permute-start | bytes 589832 | tf_op jit(solution)/shard_map/ppermute | solution.py:71
  97.0 21.8 %collective-permute-start.27 = (f32[384,128]{1,0:T(8,128)S(1)}, f32[384,128]{1,0:T(8,128)S(1)}, u32[]{:S(2)}, u32[]{:S(2)}) collective-permute-start(f32[384,128]{1,0:T(8,128)S(1)} %get-tuple-element.64), channel_id=1, source_target_pairs={{8,24},{9,25},{10,26},{11,27},{12,28},{13,29},{14,30},{15,31}} | collective-permute-start | bytes 589832 | tf_op jit(solution)/shard_map/ppermute | solution.py:71
  99.5 25.3 %copy-start = (f32[1,4,384,384]{3,2,1,0:T(8,128)S(1)}, f32[1,4,384,384]{3,2,1,0:T(8,128)}, u32[]{:S(2)}) copy-start(f32[1,4,384,384]{3,2,1,0:T(8,128)} %param.10) | copy-start | bytes 7077892
  99.5 25.3 %copy-start.2 = (f32[384,128]{1,0:T(8,128)S(1)}, f32[384,128]{1,0:T(8,128)}, u32[]{:S(2)}) copy-start(f32[384,128]{1,0:T(8,128)} %refs_4_.3) | copy-start | bytes 589828
  99.5 19.9 %collective-permute-start.28 = (f32[384,128]{1,0:T(8,128)S(1)}, f32[384,128]{1,0:T(8,128)S(1)}, u32[]{:S(2)}, u32[]{:S(2)}) collective-permute-start(f32[384,128]{1,0:T(8,128)S(1)} %get-tuple-element.47.refs_4_.refs_0_), channel_id=1, source_target_pairs={{0,1},{1,2},{2,3},{3,4},{4,5},{5,6},{6,7},{7,8},{8,9},{9,10},{10,1... | collective-permute-start | bytes 589832 | tf_op jit(solution)/shard_map/ppermute | solution.py:299
  115.6 3.8 %collective-permute-start.30 = (f32[384,128]{1,0:T(8,128)}, f32[384,128]{1,0:T(8,128)S(1)}, u32[]{:S(2)}, u32[]{:S(2)}) collective-permute-start(f32[384,128]{1,0:T(8,128)} %shard_map.101), channel_id=1, source_target_pairs={{16,17},{18,19},{20,21},{22,23},{24,25},{26,27},{28,29},{30,31}} | collective-permute-start | bytes 589832 | tf_op jit(solution)/shard_map/ppermute | solution.py:299
  116.9 7.9 %collective-permute-start.29 = (f32[384,128]{1,0:T(8,128)S(1)}, f32[384,128]{1,0:T(8,128)S(1)}, u32[]{:S(2)}, u32[]{:S(2)}) collective-permute-start(f32[384,128]{1,0:T(8,128)S(1)} %shard_map.100.refs_0_), channel_id=1, source_target_pairs={{17,18},{19,20},{21,22},{23,24},{25,26},{27,28},{29,30}} | collective-permute-start | bytes 589832 | tf_op jit(solution)/shard_map/ppermute | solution.py:299

commit v9 on v8

--- a/solution.py
+++ b/solution.py
@@ -29,13 +29,20 @@
     return jnp.dot(left(former), right(latter), preferred_element_type=F32)
 
 
-def summed(bounce, value, rolled=False):
+def summed(bounce, value):
+    side = bounce.shape[1]
+    both = product(bounce, jnp.concatenate([bounce, value], axis=1))
+    total = value + both[:, side:]
+    return total + product(both[:, :side], total)
+
+
+def rolled_sum(bounce, value):
     factor = left(bounce)
 
     def step(_, total):
         return value + jnp.dot(factor, right(total), preferred_element_type=F32)
 
-    return lax.fori_loop(0, 3, step, value, unroll=not rolled)
+    return lax.fori_loop(0, 3, step, value)
 
 
 def staged(body, stride, inputs, outputs, products, dtype=F32):
@@ -107,7 +114,7 @@
 
             @pl.when(k == at)
             def _():
-                gt = summed(product(q[...], came[...]), t[...], True)
+                gt = rolled_sum(product(q[...], came[...]), t[...])
                 gt_out[...] = gt
                 out[...] = r[...] + product(u[...], product(came[...], gt))
 
@@ -132,7 +139,7 @@
 
         @pl.when((k > 0) & (k < 6))
         def _():
-            hu = summed(product(r[...], q0[...]), u[...], True)
+            hu = rolled_sum(product(r[...], q0[...]), u[...])
             hu_out[...] = hu
             q1[...] = q[...] + product(t[...], product(q0[...], hu))
 
@@ -144,7 +151,7 @@
     def forward_t(k, q0, t0, r, t, t1, rgt):
         @pl.when((k > 1) & (k < 6))
         def _():
-            gt = summed(product(q0[...], r[...]), t0[...], True)
+            gt = rolled_sum(product(q0[...], r[...]), t0[...])
             rgt[...] = product(r[...], gt)
             t1[...] = product(t[...], gt)
 
@@ -171,7 +178,7 @@
 
         @pl.when(k == 1)
         def _():
-            g = summed(product(q0[...], r[...]), came[:, :width], True)
+            g = rolled_sum(product(q0[...], r[...]), came[:, :width])
             f1[...] = product(t[...], g)
             rg[...] = product(r[...], g)
 
@@ -237,7 +244,7 @@
         @pl.when((k == 2) | (k == 3))
         def _():
             came = jnp.where(k == 2, qa_raw[...], qa[...])
-            hu = summed(product(r1[...], came), both[:, : q1.shape[1]], True)
+            hu = summed(product(r1[...], came), both[:, : q1.shape[1]])
             hu_out[...] = hu
             q2[...] = q1[...] + product(t1[...], product(came, hu))
 
@@ -251,7 +258,7 @@
         @pl.when((k == 2) | (k == 3))
         def _():
             came = jnp.where(k == 2, qa_raw[...], qa[...])
-            g = summed(product(came, r1[...]), fa[...], True)
+            g = summed(product(came, r1[...]), fa[...])
             g2[...] = g
             f2[...] = product(t1[...], g)
 
@@ -261,10 +268,10 @@
         @pl.when((k == 2) | (k == 3))
         def _():
             came = jnp.where(k == 2, r_late[...], r_next[...]) + w_came[...]
-            gt = summed(product(q1[...], came), t1[...], True)
+            gt = summed(product(q1[...], came), t1[...])
             rc = r1[...] + product(both[:, : q1.shape[1]], product(came, gt))
             rc4[...] = rc
-            g = summed(product(jnp.where(k == 2, qa_raw[...], qa[...]), rc), fa[...], True)
+            g = summed(product(jnp.where(k == 2, qa_raw[...], qa[...]), rc), fa[...])
             g4[...] = g
             w4[...] = product(gt, g)
 
@@ -324,9 +331,7 @@
     s6_came = moved(s6, [(2, 6), (3, 7)])
     s4_came = moved(s4, [(2, 4), (3, 5)])
 
-    def through_odd(d, f2, t1, w4, t2, g6, out):
-        k = d // stride
-
+    def through_mid(k, f2, t1, w4, out):
         @pl.when(k < 4)
         def _():
             out[...] = f2[...]
@@ -335,16 +340,26 @@
         def _():
             out[...] = product(t1[...], w4[...])
 
-        @pl.when((k > 5) & (d % 2 == 1))
+    (mid,) = staged(through_mid, stride, [f2, t1, w4_came], [field], 0.3)
+    top = half + half // 2
+    next_mid = passed(mid, lambda i: half <= i < top)
+
+    def through_odd(d, mid, t2, g6, out):
+        late = (d >= top) & (d % 2 == 1)
+
+        @pl.when(late)
         def _():
             out[...] = product(t2[...], g6[...])
 
-    (odd,) = staged(through_odd, 1, [f2, t1, w4_came, t2, g6_odd], [field], 1)
-    next_odd = passed(odd, lambda i: i >= half and i % 2 == 1)
+        @pl.when(jnp.logical_not(late))
+        def _():
+            out[...] = mid[...]
+
+    (odd,) = staged(through_odd, 1, [mid, t2, g6_odd], [field], 0.3)
+    next_odd = passed(odd, lambda i: i >= top and i % 2 == 1)
 
     def through_even(d, odd, t2, g6, out):
-        k = d // stride
-        late = (k > 5) & (d % 2 == 0)
+        late = (d >= top) & (d % 2 == 0)
 
         @pl.when(late)
         def _():
@@ -354,11 +369,12 @@
         def _():
             out[...] = odd[...]
 
-    (through_field,) = staged(through_even, 1, [odd, t2, g6_even], [field], 1)
-    next_even = passed(through_field, lambda i: i >= half and i % 2 == 0)
-
-    def depths(d, maps, low, odd, even, incident, out):
+    (through_field,) = staged(through_even, 1, [odd, t2, g6_even], [field], 0.3)
+    next_even = passed(through_field, lambda i: i >= top and i % 2 == 0)
+
+    def depths(d, maps, low, mid, odd, even, incident, out):
         came = jnp.where(d % 2 == 1, even[...], odd[...])
+        came = jnp.where(d <= top, mid[...], came)
         came = jnp.where(d <= half, low[...], came)
         value = right(jnp.where(d == 0, incident[...], came))
         for j in range(depth_maps.shape[1]):
@@ -367,7 +383,7 @@
     (depth_fields,) = staged(
         depths,
         1,
-        [maps, next_low, next_odd, next_even, incident],
+        [maps, next_low, next_mid, next_odd, next_even, incident],
         [depth_maps.shape[1:3] + field[1:]],
         1,
     )

time: 128 us -> 127 us (level)
  the two profiles are of different devices: /device:TPU:28 before, /device:TPU:30 now
where the time goes in v9:
time: 127 us; the launch traced here: 126 us
  waiting for transfers between devices  73.2 us (58%)
  starting transfers between devices  39.3 us (31%)
  Pallas kernels  7.1 us (6%)
  local copies, waits for them, and re-layouts  5.1 us (4%)
    ppermute x28, waiting for transfers between devices, moved(): return lax.ppermute(value, 'sec', pairs)  70.3 us
    ppermute x28, starting transfers between devices, moved(): return lax.ppermute(value, 'sec', pairs)  35.2 us
    pallas_call x21, Pallas kernels, staged(): pl.pallas_call(kernel, out_shape=[jax.ShapeDtypeStruct(shape, dtype) for...  7.1 us
    unnamed x16, local copies, waits for them, and re-layouts  5.1 us
    ppermute x4, starting transfers between devices, passed(): return lax.ppermute(value, 'sec', pairs)  4.05 us
    ppermute x4, waiting for transfers between devices, passed(): return lax.ppermute(value, 'sec', pairs)  2.9 us
  transfers between devices with their start and end apart: 32, of which 8 were waited for; matrix products, arithmetic and copies ran while one was open for 0% of the time, Pallas kernels for 4%

profile of v9, /device:TPU:30, one launch (start us, length us, event | category | flops | bytes accessed | tf_op | source)
XLA Modules:
  0.0 125.9 jit_solution(16250979580652446006)
XLA Ops:
  0.6 2.4 %collective-permute-start.8 = (f32[384,384]{1,0:T(8,128)}, f32[384,384]{1,0:T(8,128)S(1)}, u32[]{:S(2)}, u32[]{:S(2)}) collective-permute-start(f32[384,384]{1,0:T(8,128)} %bitcast.refs_0_), channel_id=1, source_target_pairs={{28,24},{29,25},{30,26},{31,27},{24,28},{25,29},{26,30},{27,31},{4... | collective-permute-start | bytes 1769480 | tf_op jit(solution)/shard_map/ppermute | solution.py:78
  3.1 0.7 collective-permute-start.1
  3.8 0.7 collective-permute-start.13
  4.5 0.7 collective-permute-start.11
  5.2 0.9 copy-done.1
  6.1 1.1 copy-done.3
  7.2 1.1 copy-done.4
  8.2 1.1 copy-done.6
  9.3 1.2 shard_map.85
  10.5 0.7 collective-permute-start
  11.2 6.6 %collective-permute-done.8.refs_0_ = f32[384,384]{1,0:T(8,128)S(1)} collective-permute-done((f32[384,384]{1,0:T(8,128)}, f32[384,384]{1,0:T(8,128)S(1)}, u32[]{:S(2)}, u32[]{:S(2)}) %collective-permute-start.8) | collective-permute-done | bytes 589856 | tf_op jit(solution)/shard_map/ppermute | solution.py:78
  17.8 0.7 collective-permute-start.5
  18.6 1.0 copy-done.7
  19.6 0.7 collective-permute-start.10
  20.3 1.9 %collective-permute-start.9 = (f32[384,384]{1,0:T(8,128)S(1)}, f32[384,384]{1,0:T(8,128)S(1)}, u32[]{:S(2)}, u32[]{:S(2)}) collective-permute-start(f32[384,384]{1,0:T(8,128)S(1)} %get-tuple-element.41), channel_id=1, source_target_pairs={{24,28},{25,29},{26,30},{27,31},{28,20},{29,21},{30,22},{31,23},{0... | collective-permute-start | bytes 1769480 | tf_op jit(solution)/shard_map/ppermute | solution.py:78
  22.2 0.7 collective-permute-start.2
  22.9 0.7 collective-permute-start.16
  23.7 0.7 collective-permute-start.6
  24.4 0.7 collective-permute-start.14
  25.1 12.5 %collective-permute-done.9.refs_1_.refs_0_ = f32[384,384]{1,0:T(8,128)S(1)} collective-permute-done((f32[384,384]{1,0:T(8,128)S(1)}, f32[384,384]{1,0:T(8,128)S(1)}, u32[]{:S(2)}, u32[]{:S(2)}) %collective-permute-start.9) | collective-permute-done | bytes 589856 | tf_op jit(solution)/shard_map/ppermute | solution.py:78
  37.6 0.7 collective-permute-start.12
  38.4 0.7 collective-permute-start.15
  39.1 11.2 %collective-permute-start.20 = (f32[384,384]{1,0:T(8,128)S(1)}, f32[384,384]{1,0:T(8,128)S(1)}, u32[]{:S(2)}, u32[]{:S(2)}) collective-permute-start(f32[384,384]{1,0:T(8,128)S(1)} %get-tuple-element.53), channel_id=1, source_target_pairs={{20,16},{21,17},{22,18},{23,19},{28,20},{29,21},{30,22},{31,23}} | collective-permute-start | bytes 1769480 | tf_op jit(solution)/shard_map/ppermute | solution.py:78
  50.4 0.7 collective-permute-start.7
  51.4 0.7 collective-permute-start.3
  52.1 0.7 collective-permute-start.17
  52.9 0.7 collective-permute-start.4
  53.5 7.6 %collective-permute-done.20.refs_0_ = f32[384,384]{1,0:T(8,128)S(1)} collective-permute-done((f32[384,384]{1,0:T(8,128)S(1)}, f32[384,384]{1,0:T(8,128)S(1)}, u32[]{:S(2)}, u32[]{:S(2)}) %collective-permute-start.20) | collective-permute-done | bytes 589856 | tf_op jit(solution)/shard_map/ppermute | solution.py:78
  61.2 0.7 collective-permute-start.25
  61.9 0.7 collective-permute-start.22
  62.7 1.3 %collective-permute-start.19 = (f32[384,384]{1,0:T(8,128)S(1)}, f32[384,384]{1,0:T(8,128)S(1)}, u32[]{:S(2)}, u32[]{:S(2)}) collective-permute-start(f32[384,384]{1,0:T(8,128)S(1)} %get-tuple-element.52), channel_id=1, source_target_pairs={{20,24},{21,25},{22,26},{23,27},{24,28},{25,29},{26,30},{27,31}} | collective-permute-start | bytes 1769480 | tf_op jit(solution)/shard_map/ppermute | solution.py:78
  64.0 1.3 %collective-permute-start.21 = (f32[384,384]{1,0:T(8,128)S(1)}, f32[384,384]{1,0:T(8,128)S(1)}, u32[]{:S(2)}, u32[]{:S(2)}) collective-permute-start(f32[384,384]{1,0:T(8,128)S(1)} %get-tuple-element.55), channel_id=1, source_target_pairs={{16,24},{17,25},{18,26},{19,27},{20,28},{21,29},{22,30},{23,31}} | collective-permute-start | bytes 1769480 | tf_op jit(solution)/shard_map/ppermute | solution.py:78
  65.3 0.7 collective-permute-start.18
  66.3 0.7 collective-permute-start.23
  67.0 1.3 %collective-permute-start.24 = (f32[384,128]{1,0:T(8,128)S(1)}, f32[384,128]{1,0:T(8,128)S(1)}, u32[]{:S(2)}, u32[]{:S(2)}) collective-permute-start(f32[384,128]{1,0:T(8,128)S(1)} %shard_map.100.refs_8_), channel_id=1, source_target_pairs={{8,24},{10,26},{12,28},{14,30}} | collective-permute-start | bytes 589832 | tf_op jit(solution)/shard_map/ppermute | solution.py:78
  69.1 8.0 %collective-permute-done.19.refs_1_ = f32[384,384]{1,0:T(8,128)S(1)} collective-permute-done((f32[384,384]{1,0:T(8,128)S(1)}, f32[384,384]{1,0:T(8,128)S(1)}, u32[]{:S(2)}, u32[]{:S(2)}) %collective-permute-start.19) | collective-permute-done | bytes 589856 | tf_op jit(solution)/shard_map/ppermute | solution.py:78
  77.7 19.8 %collective-permute-done.21.refs_2_ = f32[384,384]{1,0:T(8,128)S(1)} collective-permute-done((f32[384,384]{1,0:T(8,128)S(1)}, f32[384,384]{1,0:T(8,128)S(1)}, u32[]{:S(2)}, u32[]{:S(2)}) %collective-permute-start.21) | collective-permute-done | bytes 589856 | tf_op jit(solution)/shard_map/ppermute | solution.py:78
  97.5 1.3 %collective-permute-start.27 = (f32[384,128]{1,0:T(8,128)S(1)}, f32[384,128]{1,0:T(8,128)S(1)}, u32[]{:S(2)}, u32[]{:S(2)}) collective-permute-start(f32[384,128]{1,0:T(8,128)S(1)} %get-tuple-element.64), channel_id=1, source_target_pairs={{8,24},{9,25},{10,26},{11,27},{12,28},{13,29},{14,30},{15,31}} | collective-permute-start | bytes 589832 | tf_op jit(solution)/shard_map/ppermute | solution.py:78
  98.8 1.3 shard_map.98.refs_1_
  100.1 0.8 collective-permute-start.29
  101.0 13.5 %collective-permute-done.24.refs_2_ = f32[384,128]{1,0:T(8,128)S(1)} collective-permute-done((f32[384,128]{1,0:T(8,128)S(1)}, f32[384,128]{1,0:T(8,128)S(1)}, u32[]{:S(2)}, u32[]{:S(2)}) %collective-permute-start.24) | collective-permute-done | bytes 196640 | tf_op jit(solution)/shard_map/ppermute | solution.py:78
  114.5 1.1 shard_map.102
  115.6 1.3 %collective-permute-start.31 = (f32[384,128]{1,0:T(8,128)}, f32[384,128]{1,0:T(8,128)S(1)}, u32[]{:S(2)}, u32[]{:S(2)}) collective-permute-start(f32[384,128]{1,0:T(8,128)} %shard_map.102), channel_id=1, source_target_pairs={{24,25},{26,27},{28,29},{30,31}} | collective-permute-start | bytes 589832 | tf_op jit(solution)/shard_map/ppermute | solution.py:306
  116.9 1.3 %collective-permute-start.30 = (f32[384,128]{1,0:T(8,128)S(1)}, f32[384,128]{1,0:T(8,128)S(1)}, u32[]{:S(2)}, u32[]{:S(2)}) collective-permute-start(f32[384,128]{1,0:T(8,128)S(1)} %shard_map.101.refs_0_), channel_id=1, source_target_pairs={{25,26},{27,28},{29,30}} | collective-permute-start | bytes 589832 | tf_op jit(solution)/shard_map/ppermute | solution.py:306
  118.2 2.1 %collective-permute-done.27.refs_3_ = f32[384,128]{1,0:T(8,128)S(1)} collective-permute-done((f32[384,128]{1,0:T(8,128)S(1)}, f32[384,128]{1,0:T(8,128)S(1)}, u32[]{:S(2)}, u32[]{:S(2)}) %collective-permute-start.27) | collective-permute-done | bytes 196640 | tf_op jit(solution)/shard_map/ppermute | solution.py:78
  120.3 0.7 shard_map.104
  121.0 2.9 %collective-permute-done.30.refs_3_ = f32[384,128]{1,0:T(8,128)S(1)} collective-permute-done((f32[384,128]{1,0:T(8,128)S(1)}, f32[384,128]{1,0:T(8,128)S(1)}, u32[]{:S(2)}, u32[]{:S(2)}) %collective-permute-start.30) | collective-permute-done | bytes 196640 | tf_op jit(solution)/shard_map/ppermute | solution.py:306
  123.9 2.0 %shard_map.105 = f32[4,384,128]{2,1,0:T(8,128)} custom-call(f32[4,384,384]{2,1,0:T(8,128)S(1)} %bitcast.8, f32[384,128]{1,0:T(8,128)S(1)} %collective-permute-done.28.refs_1_, f32[384,128]{1,0:T(8,128)S(1)} %collective-permute-done.29.refs_2_, f32[384,128]{1,0:T(8,128)S(1)} %collective-permute-done.30.refs_3_, ...), custom_call_target="tpu_custom_call" | custom-call | flops 339738624 | bytes 4128768 | tf_op jit(solution)/shard_map/pallas_call | solution.py:55
  (53 shorter events, 2.3 us)
Async XLA Ops:
  0.6 17.2 %collective-permute-start.8 = (f32[384,384]{1,0:T(8,128)}, f32[384,384]{1,0:T(8,128)S(1)}, u32[]{:S(2)}, u32[]{:S(2)}) collective-permute-start(f32[384,384]{1,0:T(8,128)} %bitcast.refs_0_), channel_id=1, source_target_pairs={{28,24},{29,25},{30,26},{31,27},{24,28},{25,29},{26,30},{27,31},{4... | collective-permute-start | bytes 1769480 | tf_op jit(solution)/shard_map/ppermute | solution.py:78
  3.1 17.2 %collective-permute-start.1 = (f32[384,384]{1,0:T(8,128)}, f32[384,384]{1,0:T(8,128)S(1)}, u32[]{:S(2)}, u32[]{:S(2)}) collective-permute-start(f32[384,384]{1,0:T(8,128)} %bitcast.11), channel_id=1, source_target_pairs={{0,4},{1,5},{2,6},{3,7},{4,8},{5,9},{6,10},{7,11},{8,12},{9,13},{1... | collective-permute-start | bytes 1769480 | tf_op jit(solution)/shard_map/ppermute | solution.py:78
  3.8 18.4 %collective-permute-start.13 = (f32[384,384]{1,0:T(8,128)}, f32[384,384]{1,0:T(8,128)S(1)}, u32[]{:S(2)}, u32[]{:S(2)}) collective-permute-start(f32[384,384]{1,0:T(8,128)} %bitcast.9), channel_id=1, source_target_pairs={{4,8},{5,9},{6,10},{7,11},{8,12},{9,13},{10,14},{11,15},{12,16},{1... | collective-permute-start | bytes 1769480 | tf_op jit(solution)/shard_map/ppermute | solution.py:78
  4.5 18.5 %collective-permute-start.11 = (f32[384,384]{1,0:T(8,128)}, f32[384,384]{1,0:T(8,128)S(1)}, u32[]{:S(2)}, u32[]{:S(2)}) collective-permute-start(f32[384,384]{1,0:T(8,128)} %bitcast.14), channel_id=1, source_target_pairs={{4,0},{5,1},{6,2},{7,3}} | collective-permute-start | bytes 1769480 | tf_op jit(solution)/shard_map/ppermute | solution.py:78
  5.2 0.9 copy-start.1
  6.1 1.1 copy-start.3
  7.2 1.1 copy-start.4
  8.2 1.1 copy-start.6
  10.5 8.1 %collective-permute-start = (f32[384,256]{1,0:T(8,128)S(1)}, f32[384,256]{1,0:T(8,128)S(1)}, u32[]{:S(2)}, u32[]{:S(2)}) collective-permute-start(f32[384,256]{1,0:T(8,128)S(1)} %get-tuple-element.34.refs_0_.refs_6_), channel_id=1, source_target_pairs={{0,4},{1,5},{2,6},{3,7}} | collective-permute-start | bytes 1179656 | tf_op jit(solution)/shard_map/ppermute | solution.py:78
  17.8 5.8 %collective-permute-start.5 = (f32[384,384]{1,0:T(8,128)}, f32[384,384]{1,0:T(8,128)S(1)}, u32[]{:S(2)}, u32[]{:S(2)}) collective-permute-start(f32[384,384]{1,0:T(8,128)} %bitcast.refs_0_), channel_id=1, source_target_pairs={{8,0},{9,1},{10,2},{11,3}} | collective-permute-start | bytes 1769480 | tf_op jit(solution)/shard_map/ppermute | solution.py:78
  18.5 1.1 copy-start.7
  18.5 3.7 %copy-start.5 = (f32[1,384,384]{2,1,0:T(8,128)S(1)}, f32[1,384,384]{2,1,0:T(8,128)}, u32[]{:S(2)}) copy-start(f32[1,384,384]{2,1,0:T(8,128)} %param.8) | copy-start | bytes 1769476
  19.6 4.8 %collective-permute-start.10 = (f32[384,384]{1,0:T(8,128)S(1)}, f32[384,384]{1,0:T(8,128)S(1)}, u32[]{:S(2)}, u32[]{:S(2)}) collective-permute-start(f32[384,384]{1,0:T(8,128)S(1)} %bitcast.16), channel_id=1, source_target_pairs={{0,4},{1,5},{2,6},{3,7},{8,12},{9,13},{10,14},{11,15}} | collective-permute-start | bytes 1769480 | tf_op jit(solution)/shard_map/ppermute | solution.py:78
  20.3 17.3 %collective-permute-start.9 = (f32[384,384]{1,0:T(8,128)S(1)}, f32[384,384]{1,0:T(8,128)S(1)}, u32[]{:S(2)}, u32[]{:S(2)}) collective-permute-start(f32[384,384]{1,0:T(8,128)S(1)} %get-tuple-element.41), channel_id=1, source_target_pairs={{24,28},{25,29},{26,30},{27,31},{28,20},{29,21},{30,22},{31,23},{0... | collective-permute-start | bytes 1769480 | tf_op jit(solution)/shard_map/ppermute | solution.py:78
  22.2 16.2 %collective-permute-start.2 = (f32[384,384]{1,0:T(8,128)S(1)}, f32[384,384]{1,0:T(8,128)S(1)}, u32[]{:S(2)}, u32[]{:S(2)}) collective-permute-start(f32[384,384]{1,0:T(8,128)S(1)} %bitcast.13), channel_id=1, source_target_pairs={{0,8},{1,9},{2,10},{3,11}} | collective-permute-start | bytes 1769480 | tf_op jit(solution)/shard_map/ppermute | solution.py:78
  22.9 16.2 %collective-permute-start.16 = (f32[384,384]{1,0:T(8,128)S(1)}, f32[384,384]{1,0:T(8,128)S(1)}, u32[]{:S(2)}, u32[]{:S(2)}) collective-permute-start(f32[384,384]{1,0:T(8,128)S(1)} %bitcast.17), channel_id=1, source_target_pairs={{12,16},{13,17},{14,18},{15,19},{16,20},{17,21},{18,22},{19,23}} | collective-permute-start | bytes 1769480 | tf_op jit(solution)/shard_map/ppermute | solution.py:78
  23.7 26.7 %collective-permute-start.6 = (f32[384,384]{1,0:T(8,128)S(1)}, f32[384,384]{1,0:T(8,128)S(1)}, u32[]{:S(2)}, u32[]{:S(2)}) collective-permute-start(f32[384,384]{1,0:T(8,128)S(1)} %collective-permute-done.5), channel_id=1, source_target_pairs={{0,4},{1,5},{2,6},{3,7}} | collective-permute-start | bytes 1769480 | tf_op jit(solution)/shard_map/ppermute | solution.py:78
  24.4 27.0 %collective-permute-start.14 = (f32[384,384]{1,0:T(8,128)}, f32[384,384]{1,0:T(8,128)S(1)}, u32[]{:S(2)}, u32[]{:S(2)}) collective-permute-start(f32[384,384]{1,0:T(8,128)} %bitcast.refs_0_), channel_id=1, source_target_pairs={{12,8},{13,9},{14,10},{15,11}} | collective-permute-start | bytes 1769480 | tf_op jit(solution)/shard_map/ppermute | solution.py:78
  37.6 14.4 %collective-permute-start.12 = (f32[384,384]{1,0:T(8,128)S(1)}, f32[384,384]{1,0:T(8,128)S(1)}, u32[]{:S(2)}, u32[]{:S(2)}) collective-permute-start(f32[384,384]{1,0:T(8,128)S(1)} %collective-permute-done.11), channel_id=1, source_target_pairs={{0,8},{1,9},{2,10},{3,11}} | collective-permute-start | bytes 1769480 | tf_op jit(solution)/shard_map/ppermute | solution.py:78
  38.4 14.4 %collective-permute-start.15 = (f32[384,384]{1,0:T(8,128)}, f32[384,384]{1,0:T(8,128)S(1)}, u32[]{:S(2)}, u32[]{:S(2)}) collective-permute-start(f32[384,384]{1,0:T(8,128)} %bitcast.refs_0_), channel_id=1, source_target_pairs={{16,12},{17,13},{18,14},{19,15}} | collective-permute-start | bytes 1769480 | tf_op jit(solution)/shard_map/ppermute | solution.py:78
  39.1 22.0 %collective-permute-start.20 = (f32[384,384]{1,0:T(8,128)S(1)}, f32[384,384]{1,0:T(8,128)S(1)}, u32[]{:S(2)}, u32[]{:S(2)}) collective-permute-start(f32[384,384]{1,0:T(8,128)S(1)} %get-tuple-element.53), channel_id=1, source_target_pairs={{20,16},{21,17},{22,18},{23,19},{28,20},{29,21},{30,22},{31,23}} | collective-permute-start | bytes 1769480 | tf_op jit(solution)/shard_map/ppermute | solution.py:78
  50.4 11.5 %collective-permute-start.7 = (f32[384,384]{1,0:T(8,128)S(1)}, f32[384,384]{1,0:T(8,128)S(1)}, u32[]{:S(2)}, u32[]{:S(2)}) collective-permute-start(f32[384,384]{1,0:T(8,128)S(1)} %collective-permute-done.6), channel_id=1, source_target_pairs={{4,12},{5,13},{6,14},{7,15}} | collective-permute-start | bytes 1769480 | tf_op jit(solution)/shard_map/ppermute | solution.py:78
  51.4 12.6 %collective-permute-start.3 = (f32[384,384]{1,0:T(8,128)S(1)}, f32[384,384]{1,0:T(8,128)S(1)}, u32[]{:S(2)}, u32[]{:S(2)}) collective-permute-start(f32[384,384]{1,0:T(8,128)S(1)} %get-tuple-element.40.refs_3_.refs_1_), channel_id=1, source_target_pairs={{4,12},{5,13},{6,14},{7,15}} | collective-permute-start | bytes 1769480 | tf_op jit(solution)/shard_map/ppermute | solution.py:78
  52.1 13.2 %collective-permute-start.17 = (f32[384,384]{1,0:T(8,128)S(1)}, f32[384,384]{1,0:T(8,128)S(1)}, u32[]{:S(2)}, u32[]{:S(2)}) collective-permute-start(f32[384,384]{1,0:T(8,128)S(1)} %get-tuple-element.48.refs_4_), channel_id=1, source_target_pairs={{16,8},{17,9},{18,10},{19,11},{20,12},{21,13},{22,14},{23,15}} | collective-permute-start | bytes 1769480 | tf_op jit(solution)/shard_map/ppermute | solution.py:78
  52.9 9.8 %collective-permute-start.4 = (f32[384,128]{1,0:T(8,128)S(1)}, f32[384,128]{1,0:T(8,128)S(1)}, u32[]{:S(2)}, u32[]{:S(2)}) collective-permute-start(f32[384,128]{1,0:T(8,128)S(1)} %get-tuple-element.37.refs_0_), channel_id=1, source_target_pairs={{0,8},{1,9},{2,10},{3,11},{4,12},{5,13},{6,14},{7,15}} | collective-permute-start | bytes 589832 | tf_op jit(solution)/shard_map/ppermute | solution.py:78
  61.2 5.8 %collective-permute-start.25 = (f32[384,512]{1,0:T(8,128)S(1)}, f32[384,512]{1,0:T(8,128)S(1)}, u32[]{:S(2)}, u32[]{:S(2)}) collective-permute-start(f32[384,512]{1,0:T(8,128)S(1)} %get-tuple-element.49.refs_5_.refs_0_), channel_id=1, source_target_pairs={{0,8},{1,9},{2,10},{3,11},{4,12},{5,13},{6,14},{7,15}} | collective-permute-start | bytes 2359304 | tf_op jit(solution)/shard_map/ppermute | solution.py:78
  61.9 4.4 %collective-permute-start.22 = (f32[384,384]{1,0:T(8,128)S(1)}, f32[384,384]{1,0:T(8,128)S(1)}, u32[]{:S(2)}, u32[]{:S(2)}) collective-permute-start(f32[384,384]{1,0:T(8,128)S(1)} %get-tuple-element.56), channel_id=1, source_target_pairs={{16,8},{17,9},{18,10},{19,11},{20,12},{21,13},{22,14},{23,15}} | collective-permute-start | bytes 1769480 | tf_op jit(solution)/shard_map/ppermute | solution.py:78
  62.7 14.4 %collective-permute-start.19 = (f32[384,384]{1,0:T(8,128)S(1)}, f32[384,384]{1,0:T(8,128)S(1)}, u32[]{:S(2)}, u32[]{:S(2)}) collective-permute-start(f32[384,384]{1,0:T(8,128)S(1)} %get-tuple-element.52), channel_id=1, source_target_pairs={{20,24},{21,25},{22,26},{23,27},{24,28},{25,29},{26,30},{27,31}} | collective-permute-start | bytes 1769480 | tf_op jit(solution)/shard_map/ppermute | solution.py:78
  64.0 33.6 %collective-permute-start.21 = (f32[384,384]{1,0:T(8,128)S(1)}, f32[384,384]{1,0:T(8,128)S(1)}, u32[]{:S(2)}, u32[]{:S(2)}) collective-permute-start(f32[384,384]{1,0:T(8,128)S(1)} %get-tuple-element.55), channel_id=1, source_target_pairs={{16,24},{17,25},{18,26},{19,27},{20,28},{21,29},{22,30},{23,31}} | collective-permute-start | bytes 1769480 | tf_op jit(solution)/shard_map/ppermute | solution.py:78
  65.3 3.0 %collective-permute-start.18 = (f32[384,128]{1,0:T(8,128)S(1)}, f32[384,128]{1,0:T(8,128)S(1)}, u32[]{:S(2)}, u32[]{:S(2)}) collective-permute-start(f32[384,128]{1,0:T(8,128)S(1)} %get-tuple-element.50), channel_id=1, source_target_pairs={{8,16},{9,17},{10,18},{11,19},{12,20},{13,21},{14,22},{15,23}} | collective-permute-start | bytes 589832 | tf_op jit(solution)/shard_map/ppermute | solution.py:78
  66.3 33.8 %collective-permute-start.23 = (f32[384,128]{1,0:T(8,128)S(1)}, f32[384,128]{1,0:T(8,128)S(1)}, u32[]{:S(2)}, u32[]{:S(2)}) collective-permute-start(f32[384,128]{1,0:T(8,128)S(1)} %shard_map.100.refs_8_), channel_id=1, source_target_pairs={{9,25},{11,27},{13,29},{15,31}} | collective-permute-start | bytes 589832 | tf_op jit(solution)/shard_map/ppermute | solution.py:78
  67.0 47.5 %collective-permute-start.24 = (f32[384,128]{1,0:T(8,128)S(1)}, f32[384,128]{1,0:T(8,128)S(1)}, u32[]{:S(2)}, u32[]{:S(2)}) collective-permute-start(f32[384,128]{1,0:T(8,128)S(1)} %shard_map.100.refs_8_), channel_id=1, source_target_pairs={{8,24},{10,26},{12,28},{14,30}} | collective-permute-start | bytes 589832 | tf_op jit(solution)/shard_map/ppermute | solution.py:78
  68.4 48.5 %collective-permute-start.26 = (f32[384,128]{1,0:T(8,128)S(1)}, f32[384,128]{1,0:T(8,128)S(1)}, u32[]{:S(2)}, u32[]{:S(2)}) collective-permute-start(f32[384,128]{1,0:T(8,128)S(1)} %get-tuple-element.63), channel_id=1, source_target_pairs={{8,16},{9,17},{10,18},{11,19},{12,20},{13,21},{14,22},{15,23}} | collective-permute-start | bytes 589832 | tf_op jit(solution)/shard_map/ppermute | solution.py:78
  77.1 43.9 %collective-permute-start.28 = (f32[384,128]{1,0:T(8,128)S(1)}, f32[384,128]{1,0:T(8,128)S(1)}, u32[]{:S(2)}, u32[]{:S(2)}) collective-permute-start(f32[384,128]{1,0:T(8,128)S(1)} %get-tuple-element.47.refs_0_.refs_4_), channel_id=1, source_target_pairs={{0,1},{1,2},{2,3},{3,4},{4,5},{5,6},{6,7},{7,8},{8,9},{9,10},{10,1... | collective-permute-start | bytes 589832 | tf_op jit(solution)/shard_map/ppermute | solution.py:306
  97.5 22.8 %collective-permute-start.27 = (f32[384,128]{1,0:T(8,128)S(1)}, f32[384,128]{1,0:T(8,128)S(1)}, u32[]{:S(2)}, u32[]{:S(2)}) collective-permute-start(f32[384,128]{1,0:T(8,128)S(1)} %get-tuple-element.64), channel_id=1, source_target_pairs={{8,24},{9,25},{10,26},{11,27},{12,28},{13,29},{14,30},{15,31}} | collective-permute-start | bytes 589832 | tf_op jit(solution)/shard_map/ppermute | solution.py:78
  100.1 23.8 %copy-start = (f32[1,4,384,384]{3,2,1,0:T(8,128)S(1)}, f32[1,4,384,384]{3,2,1,0:T(8,128)}, u32[]{:S(2)}) copy-start(f32[1,4,384,384]{3,2,1,0:T(8,128)} %param.10) | copy-start | bytes 7077892
  100.1 23.8 %copy-start.2 = (f32[384,128]{1,0:T(8,128)S(1)}, f32[384,128]{1,0:T(8,128)}, u32[]{:S(2)}) copy-start(f32[384,128]{1,0:T(8,128)} %refs_5_.1) | copy-start | bytes 589828
  100.1 20.9 %collective-permute-start.29 = (f32[384,128]{1,0:T(8,128)S(1)}, f32[384,128]{1,0:T(8,128)S(1)}, u32[]{:S(2)}, u32[]{:S(2)}) collective-permute-start(f32[384,128]{1,0:T(8,128)S(1)} %shard_map.95.refs_0_), channel_id=1, source_target_pairs={{16,17},{17,18},{18,19},{19,20},{20,21},{21,22},{22,23},{23,24}} | collective-permute-start | bytes 589832 | tf_op jit(solution)/shard_map/ppermute | solution.py:306
  115.6 5.4 %collective-permute-start.31 = (f32[384,128]{1,0:T(8,128)}, f32[384,128]{1,0:T(8,128)S(1)}, u32[]{:S(2)}, u32[]{:S(2)}) collective-permute-start(f32[384,128]{1,0:T(8,128)} %shard_map.102), channel_id=1, source_target_pairs={{24,25},{26,27},{28,29},{30,31}} | collective-permute-start | bytes 589832 | tf_op jit(solution)/shard_map/ppermute | solution.py:306
  116.9 7.0 %collective-permute-start.30 = (f32[384,128]{1,0:T(8,128)S(1)}, f32[384,128]{1,0:T(8,128)S(1)}, u32[]{:S(2)}, u32[]{:S(2)}) collective-permute-start(f32[384,128]{1,0:T(8,128)S(1)} %shard_map.101.refs_0_), channel_id=1, source_target_pairs={{25,26},{27,28},{29,30}} | collective-permute-start | bytes 589832 | tf_op jit(solution)/shard_map/ppermute | solution.py:306

commit v10 on v9

--- a/solution.py
+++ b/solution.py
@@ -185,16 +185,44 @@
     (f1, rg) = staged(low_fields, stride, [first, first_came, q0, r, t], [field] * 2, 2)
     fa = moved(f1, low)
 
-    def second_reflect(k, bounced, q1, t1, u1, w, total, gt_out):
+    cut = square[1] // 3 * 2
+
+    def second_reflect(k, bounced, q1, t1, u1, w, total, gt_out, bounce_out, twice_out):
+        side = q1.shape[1]
+
         @pl.when((k == 4) | (k == 5))
         def _():
-            gt = summed(product(q1[...], bounced[...]), t1[...])
+            bounce = product(q1[...], bounced[...])
+            both = product(bounce, jnp.concatenate([bounce, t1[:, :cut]], axis=1))
+            start = t1[:, :cut] + both[:, side:]
+            gt = start + product(both[:, :side], start)
+            total[...] = w[:, :cut] + product(u1[...], product(bounced[...], gt))
             gt_out[...] = gt
-            total[...] = w[...] + product(u1[...], product(bounced[...], gt))
-
-    (total, gt2) = staged(second_reflect, stride, [bounced, q1, t1, u1, w], [square] * 2, 6
+            bounce_out[...] = bounce
+            twice_out[...] = both[:, :side]
+
+    (total, gt_cut, bounce, twice) = staged(
+        second_reflect, stride, [bounced, q1, t1, u1, w], [(square[0], cut)] * 2 + [square] * 2, 4
     )
     total_came = moved(total, back)
+
+    def second_rest(k, bounced, bounce, twice, t1, u1, w, gt_cut, total, gt_out):
+        @pl.when((k == 4) | (k == 5))
+        def _():
+            start = t1[:, cut:] + product(bounce[...], t1[:, cut:])
+            gt = start + product(twice[...], start)
+            total[...] = w[:, cut:] + product(u1[...], product(bounced[...], gt))
+            gt_out[:, :cut] = gt_cut[...]
+            gt_out[:, cut:] = gt
+
+    (total_s, gt2) = staged(
+        second_rest,
+        stride,
+        [bounced, bounce, twice, t1, u1, w, gt_cut],
+        [(square[0], square[1] - cut), square],
+        2,
+    )
+    total_s_came = moved(total_s, back)
     gt2_came = moved(gt2, [(4, 6), (5, 7)])
 
     def low_u(k, u0, u1_up, u, hu, rgt, rg, first, came, both, w):
@@ -291,13 +319,14 @@
 
     (t2,) = staged(second_through, stride, [t, gt_came, gt2_came], [square], 2)
 
-    def last_fields(k, r_late, r_next, total_came, q2, f2, g6):
-        @pl.when((k == 2) | (k == 3))
-        def _():
-            rc = jnp.where(k == 2, r_late[...], r_next[...]) + total_came[...]
+    def last_fields(k, r_late, r_next, total_came, total_s_came, q2, f2, g6):
+        @pl.when((k == 2) | (k == 3))
+        def _():
+            whole = jnp.concatenate([total_came[...], total_s_came[...]], axis=1)
+            rc = jnp.where(k == 2, r_late[...], r_next[...]) + whole
             g6[...] = summed(product(q2[...], rc), f2[...])
 
-    (g6,) = staged(last_fields, stride, [r_late, r_next, total_came, q2, f2], [field], 3)
+    (g6,) = staged(last_fields, stride, [r_late, r_next, total_came, total_s_came, q2, f2], [field], 3)
     g6_odd = moved(g6, [(2, 6), (3, 7)], 1, 2)
     g6_even = moved(g6, [(2, 6), (3, 7)], 0, 2)
 
@@ -309,11 +338,12 @@
     next_low = passed(f2, lambda i: i < half)
 
     def all_reflected(
-        k, ua, r1, g2, rc4, g4, r_late, r_next, total_came, g6, hu2, s2, s4, s6
+        k, ua, r1, g2, rc4, g4, r_late, r_next, total_came, total_s_came, g6, hu2, s2, s4, s6
     ):
         @pl.when((k == 2) | (k == 3))
         def _():
-            rc = jnp.where(k == 2, r_late[...], r_next[...]) + total_came[...]
+            whole = jnp.concatenate([total_came[...], total_s_came[...]], axis=1)
+            rc = jnp.where(k == 2, r_late[...], r_next[...]) + whole
             rg2 = product(r1[...], g2[...])
             rg4 = product(rc4[...], g4[...])
             sums = rg2 + product(hu2[...], product(rc, g6[...]))
@@ -324,7 +354,7 @@
     (s2, s4, s6) = staged(
         all_reflected,
         stride,
-        [ua, r1, g2, rc4, g4, r_late, r_next, total_came, g6, hu2],
+        [ua, r1, g2, rc4, g4, r_late, r_next, total_came, total_s_came, g6, hu2],
         [field] * 3,
         3,
     )

time: 127 us -> 143 us (1.13)
  the two profiles are of different devices: /device:TPU:30 before, /device:TPU:28 now
where the time goes in v10:
time: 143 us
  waiting for transfers between devices  93.9 us (66%)
  starting transfers between devices  37.7 us (26%)
  Pallas kernels  7.74 us (5%)
  local copies, waits for them, and re-layouts  2 us (1%)
    ppermute x29, waiting for transfers between devices, moved(): return lax.ppermute(value, 'sec', pairs)  92 us
    ppermute x29, starting transfers between devices, moved(): return lax.ppermute(value, 'sec', pairs)  33.7 us
    pallas_call x22, Pallas kernels, staged(): pl.pallas_call(kernel, out_shape=[jax.ShapeDtypeStruct(shape, dtype) for...  7.74 us
    ppermute x4, starting transfers between devices, passed(): return lax.ppermute(value, 'sec', pairs)  4.05 us
  transfers between devices with their start and end apart: 33, of which 8 were waited for; matrix products, arithmetic and copies ran while one was open for 0% of the time, Pallas kernels for 4%

profile of v10, /device:TPU:28, one launch (start us, length us, event | category | flops | bytes accessed | tf_op | source)
XLA Modules:
  0.0 142.6 jit_solution(11795864430437095632)
XLA Ops:
  0.6 2.4 %collective-permute-start.8 = (f32[384,384]{1,0:T(8,128)}, f32[384,384]{1,0:T(8,128)S(1)}, u32[]{:S(2)}, u32[]{:S(2)}) collective-permute-start(f32[384,384]{1,0:T(8,128)} %bitcast.refs_0_), channel_id=1, source_target_pairs={{28,24},{29,25},{30,26},{31,27},{24,28},{25,29},{26,30},{27,31},{4... | collective-permute-start | bytes 1769480 | tf_op jit(solution)/shard_map/ppermute | solution.py:78
  3.1 0.7 collective-permute-start.1
  3.8 0.9 copy-done.1
  4.7 1.1 copy-done.3
  5.8 1.6 %shard_map.85 = (f32[384,384]{1,0:T(8,128)S(1)}, f32[384,384]{1,0:T(8,128)S(1)}, f32[384,384]{1,0:T(8,128)S(1)}, f32[384,384]{1,0:T(8,128)S(1)}, f32[384,256]{1,0:T(8,128)S(1)}) custom-call(f32[384,384]{1,0:T(8,128)} %bitcast.refs_0_, f32[384,384]{1,0:T(8,128)} %bitcast.1.refs_1_, f32[384,384]{1,0:T(8,128)S(1)} %bitcast.10, f32[384,384]{1,0:T(8,128)} %bitcast.3.refs_3_, ...), custom_call_target="tpu_custom_call" | custom-call | flops 339738624 | bytes 5898240 | tf_op jit(solution)/shard_map/pallas_call | solution.py:55
  7.3 0.7 collective-permute-start
  8.0 0.7 collective-permute-start.13
  8.7 0.7 collective-permute-start.5
  9.4 8.4 %collective-permute-done.8.refs_0_ = f32[384,384]{1,0:T(8,128)S(1)} collective-permute-done((f32[384,384]{1,0:T(8,128)}, f32[384,384]{1,0:T(8,128)S(1)}, u32[]{:S(2)}, u32[]{:S(2)}) %collective-permute-start.8) | collective-permute-done | bytes 589856 | tf_op jit(solution)/shard_map/ppermute | solution.py:78
  17.8 0.7 collective-permute-start.11
  18.6 0.8 collective-permute-start.10
  19.4 2.5 %collective-permute-start.9 = (f32[384,384]{1,0:T(8,128)S(1)}, f32[384,384]{1,0:T(8,128)S(1)}, u32[]{:S(2)}, u32[]{:S(2)}) collective-permute-start(f32[384,384]{1,0:T(8,128)S(1)} %get-tuple-element.45), channel_id=1, source_target_pairs={{24,28},{25,29},{26,30},{27,31},{28,20},{29,21},{30,22},{31,23},{0... | collective-permute-start | bytes 1769480 | tf_op jit(solution)/shard_map/ppermute | solution.py:78
  22.0 0.7 collective-permute-start.2
  22.7 0.7 collective-permute-start.6
  23.4 0.7 collective-permute-start.16
  24.2 0.7 collective-permute-start.14
  24.9 12.7 %collective-permute-done.9.refs_1_.refs_0_ = f32[384,384]{1,0:T(8,128)S(1)} collective-permute-done((f32[384,384]{1,0:T(8,128)S(1)}, f32[384,384]{1,0:T(8,128)S(1)}, u32[]{:S(2)}, u32[]{:S(2)}) %collective-permute-start.9) | collective-permute-done | bytes 589856 | tf_op jit(solution)/shard_map/ppermute | solution.py:78
  37.6 0.7 collective-permute-start.12
  38.4 8.2 %collective-permute-start.20 = (f32[384,384]{1,0:T(8,128)S(1)}, f32[384,384]{1,0:T(8,128)S(1)}, u32[]{:S(2)}, u32[]{:S(2)}) collective-permute-start(f32[384,384]{1,0:T(8,128)S(1)} %get-tuple-element.57), channel_id=1, source_target_pairs={{20,16},{21,17},{22,18},{23,19},{28,20},{29,21},{30,22},{31,23}} | collective-permute-start | bytes 1769480 | tf_op jit(solution)/shard_map/ppermute | solution.py:78
  46.7 0.7 collective-permute-start.7
  47.5 0.7 collective-permute-start.15
  48.4 0.7 collective-permute-start.3
  49.1 0.7 collective-permute-start.17
  49.9 0.7 collective-permute-start.26
  50.6 7.0 %collective-permute-done.20.refs_0_ = f32[384,384]{1,0:T(8,128)S(1)} collective-permute-done((f32[384,384]{1,0:T(8,128)S(1)}, f32[384,384]{1,0:T(8,128)S(1)}, u32[]{:S(2)}, u32[]{:S(2)}) %collective-permute-start.20) | collective-permute-done | bytes 589856 | tf_op jit(solution)/shard_map/ppermute | solution.py:78
  57.6 0.7 collective-permute-start.4
  58.4 1.3 collective-permute-start.19
  59.7 0.7 collective-permute-start.23
  60.4 0.7 collective-permute-start.22
  61.1 1.3 collective-permute-start.21
  62.7 0.7 collective-permute-start.18
  63.4 0.7 collective-permute-start.24
  64.1 1.3 collective-permute-start.25
  65.5 0.7 collective-permute-start.27
  66.4 6.4 %collective-permute-done.19.refs_1_ = f32[384,384]{1,0:T(8,128)S(1)} collective-permute-done((f32[384,384]{1,0:T(8,128)S(1)}, f32[384,384]{1,0:T(8,128)S(1)}, u32[]{:S(2)}, u32[]{:S(2)}) %collective-permute-start.19) | collective-permute-done | bytes 589856 | tf_op jit(solution)/shard_map/ppermute | solution.py:78
  72.9 0.7 collective-permute-start.29
  73.5 46.3 %collective-permute-done.21.refs_2_ = f32[384,384]{1,0:T(8,128)S(1)} collective-permute-done((f32[384,384]{1,0:T(8,128)S(1)}, f32[384,384]{1,0:T(8,128)S(1)}, u32[]{:S(2)}, u32[]{:S(2)}) %collective-permute-start.21) | collective-permute-done | bytes 589856 | tf_op jit(solution)/shard_map/ppermute | solution.py:78
  119.8 1.3 collective-permute-start.28
  121.1 1.3 shard_map.99.refs_1_
  122.4 0.8 collective-permute-start.30
  123.3 7.1 %collective-permute-done.25.refs_2_ = f32[384,128]{1,0:T(8,128)S(1)} collective-permute-done((f32[384,128]{1,0:T(8,128)S(1)}, f32[384,128]{1,0:T(8,128)S(1)}, u32[]{:S(2)}, u32[]{:S(2)}) %collective-permute-start.25) | collective-permute-done | bytes 196640 | tf_op jit(solution)/shard_map/ppermute | solution.py:78
  130.4 1.1 shard_map.103
  131.4 1.3 collective-permute-start.32
  132.7 1.3 collective-permute-start.31
  134.0 4.0 %collective-permute-done.28.refs_3_ = f32[384,128]{1,0:T(8,128)S(1)} collective-permute-done((f32[384,128]{1,0:T(8,128)S(1)}, f32[384,128]{1,0:T(8,128)S(1)}, u32[]{:S(2)}, u32[]{:S(2)}) %collective-permute-start.28) | collective-permute-done | bytes 196640 | tf_op jit(solution)/shard_map/ppermute | solution.py:78
  138.1 0.7 shard_map.105
  138.8 1.9 %collective-permute-done.31.refs_3_ = f32[384,128]{1,0:T(8,128)S(1)} collective-permute-done((f32[384,128]{1,0:T(8,128)S(1)}, f32[384,128]{1,0:T(8,128)S(1)}, u32[]{:S(2)}, u32[]{:S(2)}) %collective-permute-start.31) | collective-permute-done | bytes 196640 | tf_op jit(solution)/shard_map/ppermute | solution.py:335
  140.6 2.0 %shard_map.106 = f32[4,384,128]{2,1,0:T(8,128)} custom-call(f32[4,384,384]{2,1,0:T(8,128)S(1)} %bitcast.8, f32[384,128]{1,0:T(8,128)S(1)} %collective-permute-done.29.refs_1_, f32[384,128]{1,0:T(8,128)S(1)} %collective-permute-done.30.refs_2_, f32[384,128]{1,0:T(8,128)S(1)} %collective-permute-done.31.refs_3_, ...), custom_call_target="tpu_custom_call" | custom-call | flops 339738624 | bytes 4128768 | tf_op jit(solution)/shard_map/pallas_call | solution.py:55
  (50 shorter events, 1.3 us)
Async XLA Ops:
  0.6 17.2 %collective-permute-start.8 = (f32[384,384]{1,0:T(8,128)}, f32[384,384]{1,0:T(8,128)S(1)}, u32[]{:S(2)}, u32[]{:S(2)}) collective-permute-start(f32[384,384]{1,0:T(8,128)} %bitcast.refs_0_), channel_id=1, source_target_pairs={{28,24},{29,25},{30,26},{31,27},{24,28},{25,29},{26,30},{27,31},{4... | collective-permute-start | bytes 1769480 | tf_op jit(solution)/shard_map/ppermute | solution.py:78
  3.1 16.4 %collective-permute-start.1 = (f32[384,384]{1,0:T(8,128)}, f32[384,384]{1,0:T(8,128)S(1)}, u32[]{:S(2)}, u32[]{:S(2)}) collective-permute-start(f32[384,384]{1,0:T(8,128)} %bitcast.9), channel_id=1, source_target_pairs={{0,4},{1,5},{2,6},{3,7},{4,8},{5,9},{6,10},{7,11},{8,12},{9,13},{1... | collective-permute-start | bytes 1769480 | tf_op jit(solution)/shard_map/ppermute | solution.py:78
  3.8 0.9 copy-start.1
  4.7 1.1 copy-start.3
  7.3 11.3 %collective-permute-start = (f32[384,256]{1,0:T(8,128)S(1)}, f32[384,256]{1,0:T(8,128)S(1)}, u32[]{:S(2)}, u32[]{:S(2)}) collective-permute-start(f32[384,256]{1,0:T(8,128)S(1)} %get-tuple-element.38.refs_0_.refs_6_), channel_id=1, source_target_pairs={{0,4},{1,5},{2,6},{3,7}} | collective-permute-start | bytes 1179656 | tf_op jit(solution)/shard_map/ppermute | solution.py:78
  8.0 14.0 %collective-permute-start.13 = (f32[384,384]{1,0:T(8,128)}, f32[384,384]{1,0:T(8,128)S(1)}, u32[]{:S(2)}, u32[]{:S(2)}) collective-permute-start(f32[384,384]{1,0:T(8,128)} %bitcast.1.refs_1_), channel_id=1, source_target_pairs={{4,8},{5,9},{6,10},{7,11},{8,12},{9,13},{10,14},{11,15},{12,16},{1... | collective-permute-start | bytes 1769480 | tf_op jit(solution)/shard_map/ppermute | solution.py:78
  8.7 14.0 %collective-permute-start.5 = (f32[384,384]{1,0:T(8,128)}, f32[384,384]{1,0:T(8,128)S(1)}, u32[]{:S(2)}, u32[]{:S(2)}) collective-permute-start(f32[384,384]{1,0:T(8,128)} %bitcast.refs_0_), channel_id=1, source_target_pairs={{8,0},{9,1},{10,2},{11,3}} | collective-permute-start | bytes 1769480 | tf_op jit(solution)/shard_map/ppermute | solution.py:78
  17.8 5.6 %collective-permute-start.11 = (f32[384,384]{1,0:T(8,128)}, f32[384,384]{1,0:T(8,128)S(1)}, u32[]{:S(2)}, u32[]{:S(2)}) collective-permute-start(f32[384,384]{1,0:T(8,128)} %bitcast.3.refs_3_), channel_id=1, source_target_pairs={{4,0},{5,1},{6,2},{7,3}} | collective-permute-start | bytes 1769480 | tf_op jit(solution)/shard_map/ppermute | solution.py:78
  18.5 3.5 %copy-start.4 = (f32[1,384,384]{2,1,0:T(8,128)S(1)}, f32[1,384,384]{2,1,0:T(8,128)}, u32[]{:S(2)}) copy-start(f32[1,384,384]{2,1,0:T(8,128)} %param.8) | copy-start | bytes 1769476
  18.6 5.6 %collective-permute-start.10 = (f32[384,384]{1,0:T(8,128)}, f32[384,384]{1,0:T(8,128)S(1)}, u32[]{:S(2)}, u32[]{:S(2)}) collective-permute-start(f32[384,384]{1,0:T(8,128)} %bitcast.3.refs_3_), channel_id=1, source_target_pairs={{0,4},{1,5},{2,6},{3,7},{8,12},{9,13},{10,14},{11,15}} | collective-permute-start | bytes 1769480 | tf_op jit(solution)/shard_map/ppermute | solution.py:78
  19.4 18.2 %collective-permute-start.9 = (f32[384,384]{1,0:T(8,128)S(1)}, f32[384,384]{1,0:T(8,128)S(1)}, u32[]{:S(2)}, u32[]{:S(2)}) collective-permute-start(f32[384,384]{1,0:T(8,128)S(1)} %get-tuple-element.45), channel_id=1, source_target_pairs={{24,28},{25,29},{26,30},{27,31},{28,20},{29,21},{30,22},{31,23},{0... | collective-permute-start | bytes 1769480 | tf_op jit(solution)/shard_map/ppermute | solution.py:78
  22.0 16.4 %collective-permute-start.2 = (f32[384,384]{1,0:T(8,128)S(1)}, f32[384,384]{1,0:T(8,128)S(1)}, u32[]{:S(2)}, u32[]{:S(2)}) collective-permute-start(f32[384,384]{1,0:T(8,128)S(1)} %bitcast.11), channel_id=1, source_target_pairs={{0,8},{1,9},{2,10},{3,11}} | collective-permute-start | bytes 1769480 | tf_op jit(solution)/shard_map/ppermute | solution.py:78
  22.7 24.0 %collective-permute-start.6 = (f32[384,384]{1,0:T(8,128)S(1)}, f32[384,384]{1,0:T(8,128)S(1)}, u32[]{:S(2)}, u32[]{:S(2)}) collective-permute-start(f32[384,384]{1,0:T(8,128)S(1)} %collective-permute-done.5), channel_id=1, source_target_pairs={{0,4},{1,5},{2,6},{3,7}} | collective-permute-start | bytes 1769480 | tf_op jit(solution)/shard_map/ppermute | solution.py:78
  23.4 24.0 %collective-permute-start.16 = (f32[384,384]{1,0:T(8,128)}, f32[384,384]{1,0:T(8,128)S(1)}, u32[]{:S(2)}, u32[]{:S(2)}) collective-permute-start(f32[384,384]{1,0:T(8,128)} %bitcast.3.refs_3_), channel_id=1, source_target_pairs={{12,16},{13,17},{14,18},{15,19},{16,20},{17,21},{18,22},{19,23}} | collective-permute-start | bytes 1769480 | tf_op jit(solution)/shard_map/ppermute | solution.py:78
  24.2 24.2 %collective-permute-start.14 = (f32[384,384]{1,0:T(8,128)}, f32[384,384]{1,0:T(8,128)S(1)}, u32[]{:S(2)}, u32[]{:S(2)}) collective-permute-start(f32[384,384]{1,0:T(8,128)} %bitcast.refs_0_), channel_id=1, source_target_pairs={{12,8},{13,9},{14,10},{15,11}} | collective-permute-start | bytes 1769480 | tf_op jit(solution)/shard_map/ppermute | solution.py:78
  37.6 11.5 %collective-permute-start.12 = (f32[384,384]{1,0:T(8,128)S(1)}, f32[384,384]{1,0:T(8,128)S(1)}, u32[]{:S(2)}, u32[]{:S(2)}) collective-permute-start(f32[384,384]{1,0:T(8,128)S(1)} %collective-permute-done.11), channel_id=1, source_target_pairs={{0,8},{1,9},{2,10},{3,11}} | collective-permute-start | bytes 1769480 | tf_op jit(solution)/shard_map/ppermute | solution.py:78
  38.4 19.2 %collective-permute-start.20 = (f32[384,384]{1,0:T(8,128)S(1)}, f32[384,384]{1,0:T(8,128)S(1)}, u32[]{:S(2)}, u32[]{:S(2)}) collective-permute-start(f32[384,384]{1,0:T(8,128)S(1)} %get-tuple-element.57), channel_id=1, source_target_pairs={{20,16},{21,17},{22,18},{23,19},{28,20},{29,21},{30,22},{31,23}} | collective-permute-start | bytes 1769480 | tf_op jit(solution)/shard_map/ppermute | solution.py:78
  46.7 3.2 %collective-permute-start.7 = (f32[384,384]{1,0:T(8,128)S(1)}, f32[384,384]{1,0:T(8,128)S(1)}, u32[]{:S(2)}, u32[]{:S(2)}) collective-permute-start(f32[384,384]{1,0:T(8,128)S(1)} %collective-permute-done.6), channel_id=1, source_target_pairs={{4,12},{5,13},{6,14},{7,15}} | collective-permute-start | bytes 1769480 | tf_op jit(solution)/shard_map/ppermute | solution.py:78
  47.5 10.9 %collective-permute-start.15 = (f32[384,384]{1,0:T(8,128)}, f32[384,384]{1,0:T(8,128)S(1)}, u32[]{:S(2)}, u32[]{:S(2)}) collective-permute-start(f32[384,384]{1,0:T(8,128)} %bitcast.refs_0_), channel_id=1, source_target_pairs={{16,12},{17,13},{18,14},{19,15}} | collective-permute-start | bytes 1769480 | tf_op jit(solution)/shard_map/ppermute | solution.py:78
  48.4 12.0 %collective-permute-start.3 = (f32[384,384]{1,0:T(8,128)S(1)}, f32[384,384]{1,0:T(8,128)S(1)}, u32[]{:S(2)}, u32[]{:S(2)}) collective-permute-start(f32[384,384]{1,0:T(8,128)S(1)} %get-tuple-element.44.refs_3_.refs_1_), channel_id=1, source_target_pairs={{4,12},{5,13},{6,14},{7,15}} | collective-permute-start | bytes 1769480 | tf_op jit(solution)/shard_map/ppermute | solution.py:78
  49.1 12.0 %collective-permute-start.17 = (f32[384,384]{1,0:T(8,128)S(1)}, f32[384,384]{1,0:T(8,128)S(1)}, u32[]{:S(2)}, u32[]{:S(2)}) collective-permute-start(f32[384,384]{1,0:T(8,128)S(1)} %get-tuple-element.52.refs_4_.refs_5_), channel_id=1, source_target_pairs={{16,8},{17,9},{18,10},{19,11},{20,12},{21,13},{22,14},{23,15}} | collective-permute-start | bytes 1769480 | tf_op jit(solution)/shard_map/ppermute | solution.py:78
  49.9 14.2 %collective-permute-start.26 = (f32[384,512]{1,0:T(8,128)S(1)}, f32[384,512]{1,0:T(8,128)S(1)}, u32[]{:S(2)}, u32[]{:S(2)}) collective-permute-start(f32[384,512]{1,0:T(8,128)S(1)} %get-tuple-element.53.refs_5_.refs_0_), channel_id=1, source_target_pairs={{0,8},{1,9},{2,10},{3,11},{4,12},{5,13},{6,14},{7,15}} | collective-permute-start | bytes 2359304 | tf_op jit(solution)/shard_map/ppermute | solution.py:78
  57.6 2.1 %collective-permute-start.4 = (f32[384,128]{1,0:T(8,128)S(1)}, f32[384,128]{1,0:T(8,128)S(1)}, u32[]{:S(2)}, u32[]{:S(2)}) collective-permute-start(f32[384,128]{1,0:T(8,128)S(1)} %get-tuple-element.41.refs_0_), channel_id=1, source_target_pairs={{0,8},{1,9},{2,10},{3,11},{4,12},{5,13},{6,14},{7,15}} | collective-permute-start | bytes 589832 | tf_op jit(solution)/shard_map/ppermute | solution.py:78
  58.4 14.5 %collective-permute-start.19 = (f32[384,384]{1,0:T(8,128)S(1)}, f32[384,384]{1,0:T(8,128)S(1)}, u32[]{:S(2)}, u32[]{:S(2)}) collective-permute-start(f32[384,384]{1,0:T(8,128)S(1)} %get-tuple-element.56), channel_id=1, source_target_pairs={{20,24},{21,25},{22,26},{23,27},{24,28},{25,29},{26,30},{27,31}} | collective-permute-start | bytes 1769480 | tf_op jit(solution)/shard_map/ppermute | solution.py:78
  59.7 3.0 %collective-permute-start.23 = (f32[384,128]{1,0:T(8,128)S(1)}, f32[384,128]{1,0:T(8,128)S(1)}, u32[]{:S(2)}, u32[]{:S(2)}) collective-permute-start(f32[384,128]{1,0:T(8,128)S(1)} %get-tuple-element.64), channel_id=1, source_target_pairs={{16,8},{17,9},{18,10},{19,11},{20,12},{21,13},{22,14},{23,15}} | collective-permute-start | bytes 589832 | tf_op jit(solution)/shard_map/ppermute | solution.py:78
  60.4 3.0 %collective-permute-start.22 = (f32[384,256]{1,0:T(8,128)S(1)}, f32[384,256]{1,0:T(8,128)S(1)}, u32[]{:S(2)}, u32[]{:S(2)}) collective-permute-start(f32[384,256]{1,0:T(8,128)S(1)} %get-tuple-element.63), channel_id=1, source_target_pairs={{16,8},{17,9},{18,10},{19,11},{20,12},{21,13},{22,14},{23,15}} | collective-permute-start | bytes 1179656 | tf_op jit(solution)/shard_map/ppermute | solution.py:78
  61.1 58.7 %collective-permute-start.21 = (f32[384,384]{1,0:T(8,128)S(1)}, f32[384,384]{1,0:T(8,128)S(1)}, u32[]{:S(2)}, u32[]{:S(2)}) collective-permute-start(f32[384,384]{1,0:T(8,128)S(1)} %get-tuple-element.62), channel_id=1, source_target_pairs={{16,24},{17,25},{18,26},{19,27},{20,28},{21,29},{22,30},{23,31}} | collective-permute-start | bytes 1769480 | tf_op jit(solution)/shard_map/ppermute | solution.py:78
  62.7 2.7 %collective-permute-start.18 = (f32[384,128]{1,0:T(8,128)S(1)}, f32[384,128]{1,0:T(8,128)S(1)}, u32[]{:S(2)}, u32[]{:S(2)}) collective-permute-start(f32[384,128]{1,0:T(8,128)S(1)} %get-tuple-element.54), channel_id=1, source_target_pairs={{8,16},{9,17},{10,18},{11,19},{12,20},{13,21},{14,22},{15,23}} | collective-permute-start | bytes 589832 | tf_op jit(solution)/shard_map/ppermute | solution.py:78
  63.4 59.0 %collective-permute-start.24 = (f32[384,128]{1,0:T(8,128)S(1)}, f32[384,128]{1,0:T(8,128)S(1)}, u32[]{:S(2)}, u32[]{:S(2)}) collective-permute-start(f32[384,128]{1,0:T(8,128)S(1)} %shard_map.101.refs_9_), channel_id=1, source_target_pairs={{9,25},{11,27},{13,29},{15,31}} | collective-permute-start | bytes 589832 | tf_op jit(solution)/shard_map/ppermute | solution.py:78
  64.1 66.2 %collective-permute-start.25 = (f32[384,128]{1,0:T(8,128)S(1)}, f32[384,128]{1,0:T(8,128)S(1)}, u32[]{:S(2)}, u32[]{:S(2)}) collective-permute-start(f32[384,128]{1,0:T(8,128)S(1)} %shard_map.101.refs_9_), channel_id=1, source_target_pairs={{8,24},{10,26},{12,28},{14,30}} | collective-permute-start | bytes 589832 | tf_op jit(solution)/shard_map/ppermute | solution.py:78
  65.5 67.3 %collective-permute-start.27 = (f32[384,128]{1,0:T(8,128)S(1)}, f32[384,128]{1,0:T(8,128)S(1)}, u32[]{:S(2)}, u32[]{:S(2)}) collective-permute-start(f32[384,128]{1,0:T(8,128)S(1)} %get-tuple-element.71), channel_id=1, source_target_pairs={{8,16},{9,17},{10,18},{11,19},{12,20},{13,21},{14,22},{15,23}} | collective-permute-start | bytes 589832 | tf_op jit(solution)/shard_map/ppermute | solution.py:78
  72.9 65.9 %collective-permute-start.29 = (f32[384,128]{1,0:T(8,128)S(1)}, f32[384,128]{1,0:T(8,128)S(1)}, u32[]{:S(2)}, u32[]{:S(2)}) collective-permute-start(f32[384,128]{1,0:T(8,128)S(1)} %get-tuple-element.51.refs_0_.refs_5_), channel_id=1, source_target_pairs={{0,1},{1,2},{2,3},{3,4},{4,5},{5,6},{6,7},{7,8},{8,9},{9,10},{10,1... | collective-permute-start | bytes 589832 | tf_op jit(solution)/shard_map/ppermute | solution.py:335
  119.8 18.2 %collective-permute-start.28 = (f32[384,128]{1,0:T(8,128)S(1)}, f32[384,128]{1,0:T(8,128)S(1)}, u32[]{:S(2)}, u32[]{:S(2)}) collective-permute-start(f32[384,128]{1,0:T(8,128)S(1)} %get-tuple-element.72), channel_id=1, source_target_pairs={{8,24},{9,25},{10,26},{11,27},{12,28},{13,29},{14,30},{15,31}} | collective-permute-start | bytes 589832 | tf_op jit(solution)/shard_map/ppermute | solution.py:78
  122.4 18.3 %copy-start = (f32[1,4,384,384]{3,2,1,0:T(8,128)S(1)}, f32[1,4,384,384]{3,2,1,0:T(8,128)}, u32[]{:S(2)}) copy-start(f32[1,4,384,384]{3,2,1,0:T(8,128)} %param.10) | copy-start | bytes 7077892
  122.4 18.3 %copy-start.2 = (f32[384,128]{1,0:T(8,128)S(1)}, f32[384,128]{1,0:T(8,128)}, u32[]{:S(2)}) copy-start(f32[384,128]{1,0:T(8,128)} %refs_5_.1) | copy-start | bytes 589828
  122.4 16.4 %collective-permute-start.30 = (f32[384,128]{1,0:T(8,128)S(1)}, f32[384,128]{1,0:T(8,128)S(1)}, u32[]{:S(2)}, u32[]{:S(2)}) collective-permute-start(f32[384,128]{1,0:T(8,128)S(1)} %shard_map.95.refs_0_), channel_id=1, source_target_pairs={{16,17},{17,18},{18,19},{19,20},{20,21},{21,22},{22,23},{23,24}} | collective-permute-start | bytes 589832 | tf_op jit(solution)/shard_map/ppermute | solution.py:335
  131.4 7.3 %collective-permute-start.32 = (f32[384,128]{1,0:T(8,128)}, f32[384,128]{1,0:T(8,128)S(1)}, u32[]{:S(2)}, u32[]{:S(2)}) collective-permute-start(f32[384,128]{1,0:T(8,128)} %shard_map.103), channel_id=1, source_target_pairs={{24,25},{26,27},{28,29},{30,31}} | collective-permute-start | bytes 589832 | tf_op jit(solution)/shard_map/ppermute | solution.py:335
  132.7 7.9 %collective-permute-start.31 = (f32[384,128]{1,0:T(8,128)S(1)}, f32[384,128]{1,0:T(8,128)S(1)}, u32[]{:S(2)}, u32[]{:S(2)}) collective-permute-start(f32[384,128]{1,0:T(8,128)S(1)} %shard_map.102.refs_0_), channel_id=1, source_target_pairs={{25,26},{27,28},{29,30}} | collective-permute-start | bytes 589832 | tf_op jit(solution)/shard_map/ppermute | solution.py:335

commit v11 on v9

--- a/solution.py
+++ b/solution.py
@@ -89,8 +89,8 @@
     q0 = moved(q, [(0, 1), (1, 2)] + middle)
     t0 = moved(t, [(1, 2)] + middle)
     u1_over = moved(u, [(1, 0)])
-    u0 = moved(u, [(3, 4), (4, 5)])
-    u0_low = moved(u, [(0, 1), (2, 3)])
+    u0 = moved(u, [(4, 5)])
+    u0_low = moved(u, [(0, 1), (2, 3), (3, 2)])
     qa_raw = moved(q, [(0, 2)])
     r_late = moved(r, [(3, 2)])
     r_next = moved(r, [(4, 3)])
@@ -120,9 +120,10 @@
 
             @pl.when(k != at)
             def _():
-                out[...] = came[...]
                 if len(rest) == 3:
                     gt_out[...] = rest[0][...]
+                else:
+                    out[...] = came[...]
 
         return body
 
@@ -158,11 +159,17 @@
     (t1, rgt) = staged(forward_t, stride, [q0, t0, r, t], [square] * 2, 6)
 
     (relay, gt) = staged(pair_reflect(5), stride, [hopped, r, t, q, u, gt], [square] * 2, 6)
-    bounced = moved(relay, [(5, 4), (7, 5)])
+    bounced = moved(relay, [(5, 4)])
+    bounced_s = moved(hopped, [(7, 5)])
     gt_came = moved(gt, [(5, 6), (6, 7)])
 
     def forward_u(k, u0, hu, rgt, u1, w):
-        @pl.when((k == 4) | (k == 5))
+        @pl.when(k == 4)
+        def _():
+            w[...] = rgt[...]
+            u1[...] = hu[...]
+
+        @pl.when(k == 5)
         def _():
             factor = left(u0[...])
             w[...] = jnp.dot(factor, right(rgt[...]), preferred_element_type=F32)
@@ -185,14 +192,15 @@
     (f1, rg) = staged(low_fields, stride, [first, first_came, q0, r, t], [field] * 2, 2)
     fa = moved(f1, low)
 
-    def second_reflect(k, bounced, q1, t1, u1, w, total, gt_out):
+    def second_reflect(k, bounced, bounced_s, q1, t1, u1, w, total, gt_out):
         @pl.when((k == 4) | (k == 5))
         def _():
-            gt = summed(product(q1[...], bounced[...]), t1[...])
+            came = jnp.where(k == 4, bounced[...], bounced_s[...])
+            gt = summed(product(q1[...], came), t1[...])
             gt_out[...] = gt
-            total[...] = w[...] + product(u1[...], product(bounced[...], gt))
-
-    (total, gt2) = staged(second_reflect, stride, [bounced, q1, t1, u1, w], [square] * 2, 6
+            total[...] = w[...] + product(u1[...], product(came, gt))
+
+    (total, gt2) = staged(second_reflect, stride, [bounced, bounced_s, q1, t1, u1, w], [square] * 2, 6
     )
     total_came = moved(total, back)
     gt2_came = moved(gt2, [(4, 6), (5, 7)])
@@ -264,10 +272,18 @@
 
     (f2, g2) = staged(second_fields, stride, [f1, qa_raw, qa, fa, r1, t1], [field, field], 2)
 
-    def third_fields(k, r_late, r_next, w_came, q1, t1, both, r1, qa_raw, qa, fa, w4, g4, rc4):
-        @pl.when((k == 2) | (k == 3))
-        def _():
-            came = jnp.where(k == 2, r_late[...], r_next[...]) + w_came[...]
+    def third_fields(k, r_late, r_next, u3, w_came, q1, t1, both, r1, qa_raw, qa, fa, w4, g4, rc4):
+        @pl.when(k == 2)
+        def _():
+            rc4[...] = r_late[...] + product(u3[...], w_came[...])
+
+        @pl.when(k == 3)
+        def _():
+            rc4[...] = r_next[...] + w_came[...]
+
+        @pl.when((k == 2) | (k == 3))
+        def _():
+            came = rc4[...]
             gt = summed(product(q1[...], came), t1[...])
             rc = r1[...] + product(both[:, : q1.shape[1]], product(came, gt))
             rc4[...] = rc
@@ -278,7 +294,7 @@
     (w4, g4, rc4) = staged(
         third_fields,
         stride,
-        [r_late, r_next, w_came, q1, t1, both, r1, qa_raw, qa, fa],
+        [r_late, r_next, u0_low, w_came, q1, t1, both, r1, qa_raw, qa, fa],
         [field, field, square],
         9,
     )
@@ -291,13 +307,22 @@
 
     (t2,) = staged(second_through, stride, [t, gt_came, gt2_came], [square], 2)
 
-    def last_fields(k, r_late, r_next, total_came, q2, f2, g6):
-        @pl.when((k == 2) | (k == 3))
-        def _():
-            rc = jnp.where(k == 2, r_late[...], r_next[...]) + total_came[...]
-            g6[...] = summed(product(q2[...], rc), f2[...])
-
-    (g6,) = staged(last_fields, stride, [r_late, r_next, total_came, q2, f2], [field], 3)
+    def last_fields(k, r_late, r_next, u3, total_came, q2, f2, g6, rc6):
+        @pl.when(k == 2)
+        def _():
+            rc6[...] = r_late[...] + product(u3[...], total_came[...])
+
+        @pl.when(k == 3)
+        def _():
+            rc6[...] = r_next[...] + total_came[...]
+
+        @pl.when((k == 2) | (k == 3))
+        def _():
+            g6[...] = summed(product(q2[...], rc6[...]), f2[...])
+
+    (g6, rc6) = staged(
+        last_fields, stride, [r_late, r_next, u0_low, total_came, q2, f2], [field, square], 3
+    )
     g6_odd = moved(g6, [(2, 6), (3, 7)], 1, 2)
     g6_even = moved(g6, [(2, 6), (3, 7)], 0, 2)
 
@@ -309,24 +334,19 @@
     next_low = passed(f2, lambda i: i < half)
 
     def all_reflected(
-        k, ua, r1, g2, rc4, g4, r_late, r_next, total_came, g6, hu2, s2, s4, s6
+        k, ua, r1, g2, rc4, g4, rc6, g6, hu2, s2, s4, s6
     ):
         @pl.when((k == 2) | (k == 3))
         def _():
-            rc = jnp.where(k == 2, r_late[...], r_next[...]) + total_came[...]
             rg2 = product(r1[...], g2[...])
             rg4 = product(rc4[...], g4[...])
-            sums = rg2 + product(hu2[...], product(rc, g6[...]))
+            sums = rg2 + product(hu2[...], product(rc6[...], g6[...]))
             value = product(ua[:, : hu2.shape[1]], jnp.concatenate([rg2, rg4, sums], axis=1))
             for i, out in enumerate((s2, s4, s6)):
                 out[...] = ua[:, hu2.shape[1] :] + value[:, i * width : (i + 1) * width]
 
     (s2, s4, s6) = staged(
-        all_reflected,
-        stride,
-        [ua, r1, g2, rc4, g4, r_late, r_next, total_came, g6, hu2],
-        [field] * 3,
-        3,
+        all_reflected, stride, [ua, r1, g2, rc4, g4, rc6, g6, hu2], [field] * 3, 3
     )
     s6_came = moved(s6, [(2, 6), (3, 7)])
     s4_came = moved(s4, [(2, 4), (3, 5)])
@@ -358,19 +378,13 @@
     (odd,) = staged(through_odd, 1, [mid, t2, g6_odd], [field], 0.3)
     next_odd = passed(odd, lambda i: i >= top and i % 2 == 1)
 
-    def through_even(d, odd, t2, g6, out):
-        late = (d >= top) & (d % 2 == 0)
-
-        @pl.when(late)
+    def through_even(d, t2, g6, out):
+        @pl.when((d >= top) & (d % 2 == 0))
         def _():
             out[...] = product(t2[...], g6[...])
 
-        @pl.when(jnp.logical_not(late))
-        def _():
-            out[...] = odd[...]
-
-    (through_field,) = staged(through_even, 1, [odd, t2, g6_even], [field], 0.3)
-    next_even = passed(through_field, lambda i: i >= top and i % 2 == 0)
+    (even,) = staged(through_even, 1, [t2, g6_even], [field], 0.3)
+    next_even = passed(even, lambda i: i >= top and i % 2 == 0)
 
     def depths(d, maps, low, mid, odd, even, incident, out):
         came = jnp.where(d % 2 == 1, even[...], odd[...])
@@ -388,24 +402,37 @@
         1,
     )
 
-    def reflected_out(k, both, s2, s4, s6, out):
+    def fields_out(d, odd, even, both, s2, s4, s6, through, reflected):
+        k = d // stride
+        late = (d >= top) & (d % 2 == 0)
+
+        @pl.when(late)
+        def _():
+            through[...] = even[...]
+
+        @pl.when(jnp.logical_not(late))
+        def _():
+            through[...] = odd[...]
+
         @pl.when(k < 2)
         def _():
-            out[...] = both[:, square[1] :]
-
-        @pl.when((k == 2) | (k == 3))
-        def _():
-            out[...] = s2[...]
+            reflected[...] = both[:, square[1] :]
+
+        @pl.when((k == 2) | (k == 3))
+        def _():
+            reflected[...] = s2[...]
 
         @pl.when((k == 4) | (k == 5))
         def _():
-            out[...] = s4[...]
+            reflected[...] = s4[...]
 
         @pl.when(k > 5)
         def _():
-            out[...] = s6[...]
-
-    (reflected,) = staged(reflected_out, stride, [both, s2, s4_came, s6_came], [field], 0.1)
+            reflected[...] = s6[...]
+
+    (through_field, reflected) = staged(
+        fields_out, 1, [odd, even, both, s2, s4_came, s6_came], [field] * 2, 0.1
+    )
     return (through_field[None], reflected[None], depth_fields[None])
 
 

time: 127 us -> 142 us (1.12)
  the two profiles are of different devices: /device:TPU:30 before, /device:TPU:28 now
where the time goes in v11:
time: 142 us; the launch traced here: 141 us
  waiting for transfers between devices  76.6 us (54%)
  starting transfers between devices  55.4 us (39%)
  Pallas kernels  6.83 us (5%)
    ppermute x29, waiting for transfers between devices, moved(): return lax.ppermute(value, 'sec', pairs)  76.5 us
    ppermute x29, starting transfers between devices, moved(): return lax.ppermute(value, 'sec', pairs)  51.5 us
    pallas_call x21, Pallas kernels, staged(): pl.pallas_call(kernel, out_shape=[jax.ShapeDtypeStruct(shape, dtype) for...  6.83 us
    ppermute x4, starting transfers between devices, passed(): return lax.ppermute(value, 'sec', pairs)  3.92 us
  transfers between devices with their start and end apart: 33, of which 8 were waited for; matrix products, arithmetic and copies ran while one was open for 0% of the time, Pallas kernels for 3%

profile of v11, /device:TPU:28, one launch (start us, length us, event | category | flops | bytes accessed | tf_op | source)
XLA Modules:
  0.0 141.1 jit_solution(5914872406323892037)
XLA Ops:
  0.6 2.4 %collective-permute-start.8 = (f32[384,384]{1,0:T(8,128)}, f32[384,384]{1,0:T(8,128)S(1)}, u32[]{:S(2)}, u32[]{:S(2)}) collective-permute-start(f32[384,384]{1,0:T(8,128)} %bitcast.refs_0_), channel_id=1, source_target_pairs={{28,24},{29,25},{30,26},{31,27},{24,28},{25,29},{26,30},{27,31},{4... | collective-permute-start | bytes 1769480 | tf_op jit(solution)/shard_map/ppermute | solution.py:78
  3.1 0.9 copy-done.1
  4.0 1.8 %shard_map.85 = (f32[384,384]{1,0:T(8,128)S(1)}, f32[384,384]{1,0:T(8,128)S(1)}, f32[384,384]{1,0:T(8,128)S(1)}, f32[384,384]{1,0:T(8,128)S(1)}, f32[384,256]{1,0:T(8,128)S(1)}) custom-call(f32[384,384]{1,0:T(8,128)} %bitcast.refs_0_, f32[384,384]{1,0:T(8,128)} %bitcast.1.refs_1_, f32[384,384]{1,0:T(8,128)} %bitcast.2.refs_2_, f32[384,384]{1,0:T(8,128)} %bitcast.3.refs_3_, ...), custom_call_target="tpu_custom_call" | custom-call | flops 339738624 | bytes 5898240 | tf_op jit(solution)/shard_map/pallas_call | solution.py:55
  5.7 0.7 collective-permute-start
  6.4 0.7 collective-permute-start.1
  7.1 0.7 collective-permute-start.13
  7.8 0.7 collective-permute-start.10
  8.6 0.7 collective-permute-start.11
  9.3 8.5 %collective-permute-done.8.refs_0_ = f32[384,384]{1,0:T(8,128)S(1)} collective-permute-done((f32[384,384]{1,0:T(8,128)}, f32[384,384]{1,0:T(8,128)S(1)}, u32[]{:S(2)}, u32[]{:S(2)}) %collective-permute-start.8) | collective-permute-done | bytes 589856 | tf_op jit(solution)/shard_map/ppermute | solution.py:78
  17.8 0.7 collective-permute-start.5
  18.6 0.7 collective-permute-start.2
  19.3 17.6 %collective-permute-start.9 = (f32[384,384]{1,0:T(8,128)S(1)}, f32[384,384]{1,0:T(8,128)S(1)}, u32[]{:S(2)}, u32[]{:S(2)}) collective-permute-start(f32[384,384]{1,0:T(8,128)S(1)} %get-tuple-element.45), channel_id=1, source_target_pairs={{24,28},{25,29},{26,30},{27,31},{28,20},{29,21},{30,22},{31,23},{0... | collective-permute-start | bytes 1769480 | tf_op jit(solution)/shard_map/ppermute | solution.py:78
  36.9 0.7 collective-permute-start.16
  37.6 0.7 collective-permute-start.14
  38.3 0.7 collective-permute-start.6
  39.0 0.7 collective-permute-start.15
  39.7 8.8 %collective-permute-done.9.refs_1_.refs_0_ = f32[384,384]{1,0:T(8,128)S(1)} collective-permute-done((f32[384,384]{1,0:T(8,128)S(1)}, f32[384,384]{1,0:T(8,128)S(1)}, u32[]{:S(2)}, u32[]{:S(2)}) %collective-permute-start.9) | collective-permute-done | bytes 589856 | tf_op jit(solution)/shard_map/ppermute | solution.py:78
  48.6 0.7 collective-permute-start.12
  49.4 0.7 collective-permute-start.20
  50.1 10.9 %collective-permute-start.21 = (f32[384,384]{1,0:T(8,128)S(1)}, f32[384,384]{1,0:T(8,128)S(1)}, u32[]{:S(2)}, u32[]{:S(2)}) collective-permute-start(f32[384,384]{1,0:T(8,128)S(1)} %collective-permute-done.9.refs_1_.refs_0_), channel_id=1, source_target_pairs={{28,20},{29,21},{30,22},{31,23}} | collective-permute-start | bytes 1769480 | tf_op jit(solution)/shard_map/ppermute | solution.py:78
  61.0 0.7 collective-permute-start.7
  61.8 0.2 shard_map.93
  62.0 0.7 collective-permute-start.3
  62.7 0.7 collective-permute-start.17
  63.5 0.7 collective-permute-start.4
  64.2 8.7 %collective-permute-done.21.refs_1_ = f32[384,384]{1,0:T(8,128)S(1)} collective-permute-done((f32[384,384]{1,0:T(8,128)S(1)}, f32[384,384]{1,0:T(8,128)S(1)}, u32[]{:S(2)}, u32[]{:S(2)}) %collective-permute-start.21) | collective-permute-done | bytes 589856 | tf_op jit(solution)/shard_map/ppermute | solution.py:78
  72.9 0.7 collective-permute-start.26
  73.6 0.7 collective-permute-start.23
  74.4 1.3 collective-permute-start.19
  75.7 1.3 collective-permute-start.22
  77.0 0.9 collective-permute-start.18
  78.0 1.3 collective-permute-start.25
  79.4 0.7 collective-permute-start.24
  80.1 0.7 collective-permute-start.27
  80.8 9.0 %collective-permute-done.19.refs_1_ = f32[384,384]{1,0:T(8,128)S(1)} collective-permute-done((f32[384,384]{1,0:T(8,128)S(1)}, f32[384,384]{1,0:T(8,128)S(1)}, u32[]{:S(2)}, u32[]{:S(2)}) %collective-permute-start.19) | collective-permute-done | bytes 589856 | tf_op jit(solution)/shard_map/ppermute | solution.py:78
  89.8 0.7 collective-permute-start.29
  90.5 23.2 %collective-permute-done.22.refs_2_ = f32[384,384]{1,0:T(8,128)S(1)} collective-permute-done((f32[384,384]{1,0:T(8,128)S(1)}, f32[384,384]{1,0:T(8,128)S(1)}, u32[]{:S(2)}, u32[]{:S(2)}) %collective-permute-start.22) | collective-permute-done | bytes 589856 | tf_op jit(solution)/shard_map/ppermute | solution.py:78
  113.7 0.7 collective-permute-start.30
  114.4 1.3 shard_map.98.refs_1_.refs_0_
  115.7 12.5 %collective-permute-done.25.refs_1_ = f32[384,128]{1,0:T(8,128)S(1)} collective-permute-done((f32[384,128]{1,0:T(8,128)S(1)}, f32[384,128]{1,0:T(8,128)S(1)}, u32[]{:S(2)}, u32[]{:S(2)}) %collective-permute-start.25) | collective-permute-done | bytes 196640 | tf_op jit(solution)/shard_map/ppermute | solution.py:78
  128.1 1.3 collective-permute-start.28
  129.4 0.4 shard_map.102.refs_1_
  129.8 1.3 collective-permute-start.32
  131.2 1.3 collective-permute-start.31
  132.5 5.7 %collective-permute-done.28.refs_5_ = f32[384,128]{1,0:T(8,128)S(1)} collective-permute-done((f32[384,128]{1,0:T(8,128)S(1)}, f32[384,128]{1,0:T(8,128)S(1)}, u32[]{:S(2)}, u32[]{:S(2)}) %collective-permute-start.28) | collective-permute-done | bytes 196640 | tf_op jit(solution)/shard_map/ppermute | solution.py:78
  138.2 0.8 shard_map.104
  139.0 0.1 collective-permute-done.31.refs_3_
  139.1 2.0 %shard_map.105 = f32[4,384,128]{2,1,0:T(8,128)} custom-call(f32[4,384,384]{2,1,0:T(8,128)S(1)} %bitcast.8, f32[384,128]{1,0:T(8,128)S(1)} %collective-permute-done.29.refs_1_, f32[384,128]{1,0:T(8,128)S(1)} %collective-permute-done.30.refs_2_, f32[384,128]{1,0:T(8,128)S(1)} %collective-permute-done.31.refs_3_, ...), custom_call_target="tpu_custom_call" | custom-call | flops 339738624 | bytes 4128768 | tf_op jit(solution)/shard_map/pallas_call | solution.py:55
  (45 shorter events, 0.5 us)
Async XLA Ops:
  0.6 17.2 %collective-permute-start.8 = (f32[384,384]{1,0:T(8,128)}, f32[384,384]{1,0:T(8,128)S(1)}, u32[]{:S(2)}, u32[]{:S(2)}) collective-permute-start(f32[384,384]{1,0:T(8,128)} %bitcast.refs_0_), channel_id=1, source_target_pairs={{28,24},{29,25},{30,26},{31,27},{24,28},{25,29},{26,30},{27,31},{4... | collective-permute-start | bytes 1769480 | tf_op jit(solution)/shard_map/ppermute | solution.py:78
  3.1 0.9 copy-start.1
  5.7 2.8 %collective-permute-start = (f32[384,256]{1,0:T(8,128)S(1)}, f32[384,256]{1,0:T(8,128)S(1)}, u32[]{:S(2)}, u32[]{:S(2)}) collective-permute-start(f32[384,256]{1,0:T(8,128)S(1)} %get-tuple-element.38.refs_0_.refs_6_), channel_id=1, source_target_pairs={{0,4},{1,5},{2,6},{3,7}} | collective-permute-start | bytes 1179656 | tf_op jit(solution)/shard_map/ppermute | solution.py:78
  6.4 12.1 %collective-permute-start.1 = (f32[384,384]{1,0:T(8,128)}, f32[384,384]{1,0:T(8,128)S(1)}, u32[]{:S(2)}, u32[]{:S(2)}) collective-permute-start(f32[384,384]{1,0:T(8,128)} %bitcast.2.refs_2_), channel_id=1, source_target_pairs={{0,4},{1,5},{2,6},{3,7},{4,8},{5,9},{6,10},{7,11},{8,12},{9,13},{1... | collective-permute-start | bytes 1769480 | tf_op jit(solution)/shard_map/ppermute | solution.py:78
  7.1 12.1 %collective-permute-start.13 = (f32[384,384]{1,0:T(8,128)}, f32[384,384]{1,0:T(8,128)S(1)}, u32[]{:S(2)}, u32[]{:S(2)}) collective-permute-start(f32[384,384]{1,0:T(8,128)} %bitcast.1.refs_1_), channel_id=1, source_target_pairs={{4,8},{5,9},{6,10},{7,11},{8,12},{9,13},{10,14},{11,15},{12,16},{1... | collective-permute-start | bytes 1769480 | tf_op jit(solution)/shard_map/ppermute | solution.py:78
  7.8 29.0 %collective-permute-start.10 = (f32[384,384]{1,0:T(8,128)}, f32[384,384]{1,0:T(8,128)S(1)}, u32[]{:S(2)}, u32[]{:S(2)}) collective-permute-start(f32[384,384]{1,0:T(8,128)} %bitcast.3.refs_3_), channel_id=1, source_target_pairs={{0,4},{1,5},{2,6},{3,7},{8,12},{9,13},{10,14},{11,15},{12,8},{13,9... | collective-permute-start | bytes 1769480 | tf_op jit(solution)/shard_map/ppermute | solution.py:78
  8.6 29.0 %collective-permute-start.11 = (f32[384,384]{1,0:T(8,128)}, f32[384,384]{1,0:T(8,128)S(1)}, u32[]{:S(2)}, u32[]{:S(2)}) collective-permute-start(f32[384,384]{1,0:T(8,128)} %bitcast.3.refs_3_), channel_id=1, source_target_pairs={{4,0},{5,1},{6,2},{7,3}} | collective-permute-start | bytes 1769480 | tf_op jit(solution)/shard_map/ppermute | solution.py:78
  17.8 20.5 %collective-permute-start.5 = (f32[384,384]{1,0:T(8,128)}, f32[384,384]{1,0:T(8,128)S(1)}, u32[]{:S(2)}, u32[]{:S(2)}) collective-permute-start(f32[384,384]{1,0:T(8,128)} %bitcast.refs_0_), channel_id=1, source_target_pairs={{8,0},{9,1},{10,2},{11,3}} | collective-permute-start | bytes 1769480 | tf_op jit(solution)/shard_map/ppermute | solution.py:78
  18.6 20.5 %collective-permute-start.2 = (f32[384,384]{1,0:T(8,128)}, f32[384,384]{1,0:T(8,128)S(1)}, u32[]{:S(2)}, u32[]{:S(2)}) collective-permute-start(f32[384,384]{1,0:T(8,128)} %bitcast.2.refs_2_), channel_id=1, source_target_pairs={{0,8},{1,9},{2,10},{3,11}} | collective-permute-start | bytes 1769480 | tf_op jit(solution)/shard_map/ppermute | solution.py:78
  19.3 29.3 %collective-permute-start.9 = (f32[384,384]{1,0:T(8,128)S(1)}, f32[384,384]{1,0:T(8,128)S(1)}, u32[]{:S(2)}, u32[]{:S(2)}) collective-permute-start(f32[384,384]{1,0:T(8,128)S(1)} %get-tuple-element.45), channel_id=1, source_target_pairs={{24,28},{25,29},{26,30},{27,31},{28,20},{29,21},{30,22},{31,23},{0... | collective-permute-start | bytes 1769480 | tf_op jit(solution)/shard_map/ppermute | solution.py:78
  36.9 12.5 %collective-permute-start.16 = (f32[384,384]{1,0:T(8,128)}, f32[384,384]{1,0:T(8,128)S(1)}, u32[]{:S(2)}, u32[]{:S(2)}) collective-permute-start(f32[384,384]{1,0:T(8,128)} %bitcast.3.refs_3_), channel_id=1, source_target_pairs={{16,20},{17,21},{18,22},{19,23}} | collective-permute-start | bytes 1769480 | tf_op jit(solution)/shard_map/ppermute | solution.py:78
  37.6 12.5 %collective-permute-start.14 = (f32[384,384]{1,0:T(8,128)}, f32[384,384]{1,0:T(8,128)S(1)}, u32[]{:S(2)}, u32[]{:S(2)}) collective-permute-start(f32[384,384]{1,0:T(8,128)} %bitcast.refs_0_), channel_id=1, source_target_pairs={{12,8},{13,9},{14,10},{15,11}} | collective-permute-start | bytes 1769480 | tf_op jit(solution)/shard_map/ppermute | solution.py:78
  38.3 22.7 %collective-permute-start.6 = (f32[384,384]{1,0:T(8,128)S(1)}, f32[384,384]{1,0:T(8,128)S(1)}, u32[]{:S(2)}, u32[]{:S(2)}) collective-permute-start(f32[384,384]{1,0:T(8,128)S(1)} %collective-permute-done.5), channel_id=1, source_target_pairs={{0,4},{1,5},{2,6},{3,7}} | collective-permute-start | bytes 1769480 | tf_op jit(solution)/shard_map/ppermute | solution.py:78
  39.0 23.0 %collective-permute-start.15 = (f32[384,384]{1,0:T(8,128)}, f32[384,384]{1,0:T(8,128)S(1)}, u32[]{:S(2)}, u32[]{:S(2)}) collective-permute-start(f32[384,384]{1,0:T(8,128)} %bitcast.refs_0_), channel_id=1, source_target_pairs={{16,12},{17,13},{18,14},{19,15}} | collective-permute-start | bytes 1769480 | tf_op jit(solution)/shard_map/ppermute | solution.py:78
  48.6 14.1 %collective-permute-start.12 = (f32[384,384]{1,0:T(8,128)S(1)}, f32[384,384]{1,0:T(8,128)S(1)}, u32[]{:S(2)}, u32[]{:S(2)}) collective-permute-start(f32[384,384]{1,0:T(8,128)S(1)} %collective-permute-done.11), channel_id=1, source_target_pairs={{0,8},{1,9},{2,10},{3,11}} | collective-permute-start | bytes 1769480 | tf_op jit(solution)/shard_map/ppermute | solution.py:78
  49.4 14.1 %collective-permute-start.20 = (f32[384,384]{1,0:T(8,128)S(1)}, f32[384,384]{1,0:T(8,128)S(1)}, u32[]{:S(2)}, u32[]{:S(2)}) collective-permute-start(f32[384,384]{1,0:T(8,128)S(1)} %get-tuple-element.57), channel_id=1, source_target_pairs={{20,16},{21,17},{22,18},{23,19}} | collective-permute-start | bytes 1769480 | tf_op jit(solution)/shard_map/ppermute | solution.py:78
  50.1 22.8 %collective-permute-start.21 = (f32[384,384]{1,0:T(8,128)S(1)}, f32[384,384]{1,0:T(8,128)S(1)}, u32[]{:S(2)}, u32[]{:S(2)}) collective-permute-start(f32[384,384]{1,0:T(8,128)S(1)} %collective-permute-done.9.refs_1_.refs_0_), channel_id=1, source_target_pairs={{28,20},{29,21},{30,22},{31,23}} | collective-permute-start | bytes 1769480 | tf_op jit(solution)/shard_map/ppermute | solution.py:78
  61.0 12.6 %collective-permute-start.7 = (f32[384,384]{1,0:T(8,128)S(1)}, f32[384,384]{1,0:T(8,128)S(1)}, u32[]{:S(2)}, u32[]{:S(2)}) collective-permute-start(f32[384,384]{1,0:T(8,128)S(1)} %collective-permute-done.6), channel_id=1, source_target_pairs={{4,12},{5,13},{6,14},{7,15}} | collective-permute-start | bytes 1769480 | tf_op jit(solution)/shard_map/ppermute | solution.py:78
  62.0 13.7 %collective-permute-start.3 = (f32[384,384]{1,0:T(8,128)S(1)}, f32[384,384]{1,0:T(8,128)S(1)}, u32[]{:S(2)}, u32[]{:S(2)}) collective-permute-start(f32[384,384]{1,0:T(8,128)S(1)} %get-tuple-element.44.refs_4_.refs_2_.refs_3_), channel_id=1, source_target_pairs={{4,12},{5,13},{6,14},{7,15}} | collective-permute-start | bytes 1769480 | tf_op jit(solution)/shard_map/ppermute | solution.py:78
  62.7 14.3 %collective-permute-start.17 = (f32[384,384]{1,0:T(8,128)S(1)}, f32[384,384]{1,0:T(8,128)S(1)}, u32[]{:S(2)}, u32[]{:S(2)}) collective-permute-start(f32[384,384]{1,0:T(8,128)S(1)} %get-tuple-element.52.refs_5_), channel_id=1, source_target_pairs={{16,8},{17,9},{18,10},{19,11},{20,12},{21,13},{22,14},{23,15}} | collective-permute-start | bytes 1769480 | tf_op jit(solution)/shard_map/ppermute | solution.py:78
  63.5 10.9 %collective-permute-start.4 = (f32[384,128]{1,0:T(8,128)S(1)}, f32[384,128]{1,0:T(8,128)S(1)}, u32[]{:S(2)}, u32[]{:S(2)}) collective-permute-start(f32[384,128]{1,0:T(8,128)S(1)} %get-tuple-element.41.refs_0_), channel_id=1, source_target_pairs={{0,8},{1,9},{2,10},{3,11},{4,12},{5,13},{6,14},{7,15}} | collective-permute-start | bytes 589832 | tf_op jit(solution)/shard_map/ppermute | solution.py:78
  72.9 6.5 %collective-permute-start.26 = (f32[384,512]{1,0:T(8,128)S(1)}, f32[384,512]{1,0:T(8,128)S(1)}, u32[]{:S(2)}, u32[]{:S(2)}) collective-permute-start(f32[384,512]{1,0:T(8,128)S(1)} %get-tuple-element.53.refs_6_.refs_5_.refs_2_), channel_id=1, source_target_pairs={{0,8},{1,9},{2,10},{3,11},{4,12},{5,13},{6,14},{7,15}} | collective-permute-start | bytes 2359304 | tf_op jit(solution)/shard_map/ppermute | solution.py:78
  73.6 4.4 %collective-permute-start.23 = (f32[384,384]{1,0:T(8,128)S(1)}, f32[384,384]{1,0:T(8,128)S(1)}, u32[]{:S(2)}, u32[]{:S(2)}) collective-permute-start(f32[384,384]{1,0:T(8,128)S(1)} %get-tuple-element.60), channel_id=1, source_target_pairs={{16,8},{17,9},{18,10},{19,11},{20,12},{21,13},{22,14},{23,15}} | collective-permute-start | bytes 1769480 | tf_op jit(solution)/shard_map/ppermute | solution.py:78
  74.4 15.4 %collective-permute-start.19 = (f32[384,384]{1,0:T(8,128)S(1)}, f32[384,384]{1,0:T(8,128)S(1)}, u32[]{:S(2)}, u32[]{:S(2)}) collective-permute-start(f32[384,384]{1,0:T(8,128)S(1)} %get-tuple-element.56), channel_id=1, source_target_pairs={{20,24},{21,25},{22,26},{23,27},{24,28},{25,29},{26,30},{27,31}} | collective-permute-start | bytes 1769480 | tf_op jit(solution)/shard_map/ppermute | solution.py:78
  75.7 38.0 %collective-permute-start.22 = (f32[384,384]{1,0:T(8,128)S(1)}, f32[384,384]{1,0:T(8,128)S(1)}, u32[]{:S(2)}, u32[]{:S(2)}) collective-permute-start(f32[384,384]{1,0:T(8,128)S(1)} %get-tuple-element.59), channel_id=1, source_target_pairs={{16,24},{17,25},{18,26},{19,27},{20,28},{21,29},{22,30},{23,31}} | collective-permute-start | bytes 1769480 | tf_op jit(solution)/shard_map/ppermute | solution.py:78
  77.0 3.0 %collective-permute-start.18 = (f32[384,128]{1,0:T(8,128)S(1)}, f32[384,128]{1,0:T(8,128)S(1)}, u32[]{:S(2)}, u32[]{:S(2)}) collective-permute-start(f32[384,128]{1,0:T(8,128)S(1)} %get-tuple-element.54), channel_id=1, source_target_pairs={{8,16},{9,17},{10,18},{11,19},{12,20},{13,21},{14,22},{15,23}} | collective-permute-start | bytes 589832 | tf_op jit(solution)/shard_map/ppermute | solution.py:78
  78.0 50.1 %collective-permute-start.25 = (f32[384,128]{1,0:T(8,128)S(1)}, f32[384,128]{1,0:T(8,128)S(1)}, u32[]{:S(2)}, u32[]{:S(2)}) collective-permute-start(f32[384,128]{1,0:T(8,128)S(1)} %get-tuple-element.62.refs_6_), channel_id=1, source_target_pairs={{8,24},{10,26},{12,28},{14,30}} | collective-permute-start | bytes 589832 | tf_op jit(solution)/shard_map/ppermute | solution.py:78
  79.4 50.5 %collective-permute-start.24 = (f32[384,128]{1,0:T(8,128)S(1)}, f32[384,128]{1,0:T(8,128)S(1)}, u32[]{:S(2)}, u32[]{:S(2)}) collective-permute-start(f32[384,128]{1,0:T(8,128)S(1)} %get-tuple-element.62.refs_6_), channel_id=1, source_target_pairs={{9,25},{11,27},{13,29},{15,31}} | collective-permute-start | bytes 589832 | tf_op jit(solution)/shard_map/ppermute | solution.py:78
  80.1 51.1 %collective-permute-start.27 = (f32[384,128]{1,0:T(8,128)S(1)}, f32[384,128]{1,0:T(8,128)S(1)}, u32[]{:S(2)}, u32[]{:S(2)}) collective-permute-start(f32[384,128]{1,0:T(8,128)S(1)} %get-tuple-element.69), channel_id=1, source_target_pairs={{8,16},{9,17},{10,18},{11,19},{12,20},{13,21},{14,22},{15,23}} | collective-permute-start | bytes 589832 | tf_op jit(solution)/shard_map/ppermute | solution.py:78
  89.8 49.2 %collective-permute-start.29 = (f32[384,128]{1,0:T(8,128)S(1)}, f32[384,128]{1,0:T(8,128)S(1)}, u32[]{:S(2)}, u32[]{:S(2)}) collective-permute-start(f32[384,128]{1,0:T(8,128)S(1)} %get-tuple-element.51.refs_0_.refs_5_), channel_id=1, source_target_pairs={{0,1},{1,2},{2,3},{3,4},{4,5},{5,6},{6,7},{7,8},{8,9},{9,10},{10,1... | collective-permute-start | bytes 589832 | tf_op jit(solution)/shard_map/ppermute | solution.py:331
  113.7 25.3 %collective-permute-start.30 = (f32[384,128]{1,0:T(8,128)S(1)}, f32[384,128]{1,0:T(8,128)S(1)}, u32[]{:S(2)}, u32[]{:S(2)}) collective-permute-start(f32[384,128]{1,0:T(8,128)S(1)} %shard_map.95.refs_0_), channel_id=1, source_target_pairs={{16,17},{17,18},{18,19},{19,20},{20,21},{21,22},{22,23},{23,24}} | collective-permute-start | bytes 589832 | tf_op jit(solution)/shard_map/ppermute | solution.py:331
  115.6 23.5 %copy-start = (f32[1,4,384,384]{3,2,1,0:T(8,128)S(1)}, f32[1,4,384,384]{3,2,1,0:T(8,128)}, u32[]{:S(2)}) copy-start(f32[1,4,384,384]{3,2,1,0:T(8,128)} %param.10) | copy-start | bytes 7077892
  115.6 23.5 %copy-start.2 = (f32[384,128]{1,0:T(8,128)S(1)}, f32[384,128]{1,0:T(8,128)}, u32[]{:S(2)}) copy-start(f32[384,128]{1,0:T(8,128)} %refs_5_.1) | copy-start | bytes 589828
  128.1 10.1 %collective-permute-start.28 = (f32[384,128]{1,0:T(8,128)S(1)}, f32[384,128]{1,0:T(8,128)S(1)}, u32[]{:S(2)}, u32[]{:S(2)}) collective-permute-start(f32[384,128]{1,0:T(8,128)S(1)} %get-tuple-element.70), channel_id=1, source_target_pairs={{8,24},{9,25},{10,26},{11,27},{12,28},{13,29},{14,30},{15,31}} | collective-permute-start | bytes 589832 | tf_op jit(solution)/shard_map/ppermute | solution.py:78
  129.8 9.2 %collective-permute-start.32 = (f32[384,128]{1,0:T(8,128)S(1)}, f32[384,128]{1,0:T(8,128)S(1)}, u32[]{:S(2)}, u32[]{:S(2)}) collective-permute-start(f32[384,128]{1,0:T(8,128)S(1)} %shard_map.102.refs_1_), channel_id=1, source_target_pairs={{24,25},{26,27},{28,29},{30,31}} | collective-permute-start | bytes 589832 | tf_op jit(solution)/shard_map/ppermute | solution.py:331
  131.2 7.9 %collective-permute-start.31 = (f32[384,128]{1,0:T(8,128)S(1)}, f32[384,128]{1,0:T(8,128)S(1)}, u32[]{:S(2)}, u32[]{:S(2)}) collective-permute-start(f32[384,128]{1,0:T(8,128)S(1)} %shard_map.101.refs_0_), channel_id=1, source_target_pairs={{25,26},{27,28},{29,30}} | collective-permute-start | bytes 589832 | tf_op jit(solution)/shard_map/ppermute | solution.py:331

commit v12 on v11

--- a/solution.py
+++ b/solution.py
@@ -323,8 +323,8 @@
     (g6, rc6) = staged(
         last_fields, stride, [r_late, r_next, u0_low, total_came, q2, f2], [field, square], 3
     )
-    g6_odd = moved(g6, [(2, 6), (3, 7)], 1, 2)
-    g6_even = moved(g6, [(2, 6), (3, 7)], 0, 2)
+    g6_one = moved(g6, [(2, 6), (3, 7)], 0, 2)
+    g6_two = moved(g6, [(2, 6), (3, 7)], 1, 2)
 
     def passed(value, choose):
         pairs = [(i, i + 1) for i in range(length - 1) if choose(i)]
@@ -364,8 +364,8 @@
     top = half + half // 2
     next_mid = passed(mid, lambda i: half <= i < top)
 
-    def through_odd(d, mid, t2, g6, out):
-        late = (d >= top) & (d % 2 == 1)
+    def through_one(d, mid, t2, g6, out):
+        late = (d >= top) & (d % 2 == 0)
 
         @pl.when(late)
         def _():
@@ -375,19 +375,19 @@
         def _():
             out[...] = mid[...]
 
-    (odd,) = staged(through_odd, 1, [mid, t2, g6_odd], [field], 0.3)
-    next_odd = passed(odd, lambda i: i >= top and i % 2 == 1)
-
-    def through_even(d, t2, g6, out):
-        @pl.when((d >= top) & (d % 2 == 0))
+    (one,) = staged(through_one, 1, [mid, t2, g6_one], [field], 0.3)
+    next_one = passed(one, lambda i: i >= top and i % 2 == 0)
+
+    def through_two(d, t2, g6, out):
+        @pl.when((d >= top) & (d % 2 == 1))
         def _():
             out[...] = product(t2[...], g6[...])
 
-    (even,) = staged(through_even, 1, [t2, g6_even], [field], 0.3)
-    next_even = passed(even, lambda i: i >= top and i % 2 == 0)
-
-    def depths(d, maps, low, mid, odd, even, incident, out):
-        came = jnp.where(d % 2 == 1, even[...], odd[...])
+    (two,) = staged(through_two, 1, [t2, g6_two], [field], 0.3)
+    next_two = passed(two, lambda i: i >= top and i % 2 == 1)
+
+    def depths(d, maps, low, mid, one, two, incident, out):
+        came = jnp.where(d % 2 == 1, one[...], two[...])
         came = jnp.where(d <= top, mid[...], came)
         came = jnp.where(d <= half, low[...], came)
         value = right(jnp.where(d == 0, incident[...], came))
@@ -397,22 +397,22 @@
     (depth_fields,) = staged(
         depths,
         1,
-        [maps, next_low, next_mid, next_odd, next_even, incident],
+        [maps, next_low, next_mid, next_one, next_two, incident],
         [depth_maps.shape[1:3] + field[1:]],
         1,
     )
 
-    def fields_out(d, odd, even, both, s2, s4, s6, through, reflected):
+    def fields_out(d, one, two, both, s2, s4, s6, through, reflected):
         k = d // stride
-        late = (d >= top) & (d % 2 == 0)
+        late = (d >= top) & (d % 2 == 1)
 
         @pl.when(late)
         def _():
-            through[...] = even[...]
+            through[...] = two[...]
 
         @pl.when(jnp.logical_not(late))
         def _():
-            through[...] = odd[...]
+            through[...] = one[...]
 
         @pl.when(k < 2)
         def _():
@@ -431,7 +431,7 @@
             reflected[...] = s6[...]
 
     (through_field, reflected) = staged(
-        fields_out, 1, [odd, even, both, s2, s4_came, s6_came], [field] * 2, 0.1
+        fields_out, 1, [one, two, both, s2, s4_came, s6_came], [field] * 2, 0.1
     )
     return (through_field[None], reflected[None], depth_fields[None])
 

time: 142 us -> 141 us (level); the launches traced: 141 us -> 138 us
  waiting for transfers between devices: 76.6 us -> 69.6 us
  starting transfers between devices: 55.4 us -> 59.6 us
    ppermute x29, waiting for transfers between devices: 76.5 us -> 69.4 us  [moved(): return lax.ppermute(value, 'sec', pairs)]
    ppermute x4, starting transfers between devices: 3.92 us -> 7.99 us  [passed(): return lax.ppermute(value, 'sec', pairs)]
  transfers between devices with their start and end apart: 33 -> 33, of which waited for: 8 -> 7; matrix products, arithmetic and copies ran while one was open for 0% -> 0% of each run, Pallas kernels for 3% -> 4%
where the time goes in v12:
time: 141 us; the launch traced here: 138 us
  waiting for transfers between devices  69.6 us (49%)
  starting transfers between devices  59.6 us (42%)
  Pallas kernels  6.84 us (5%)
    ppermute x29, waiting for transfers between devices, moved(): return lax.ppermute(value, 'sec', pairs)  69.4 us
    ppermute x29, starting transfers between devices, moved(): return lax.ppermute(value, 'sec', pairs)  51.7 us
    ppermute x4, starting transfers between devices, passed(): return lax.ppermute(value, 'sec', pairs)  7.99 us
    pallas_call x21, Pallas kernels, staged(): pl.pallas_call(kernel, out_shape=[jax.ShapeDtypeStruct(shape, dtype) for...  6.84 us
  transfers between devices with their start and end apart: 33, of which 7 were waited for; matrix products, arithmetic and copies ran while one was open for 0% of the time, Pallas kernels for 4%

profile of v12, /device:TPU:28, one launch (start us, length us, event | category | flops | bytes accessed | tf_op | source)
XLA Modules:
  0.0 138.3 jit_solution(6679661501176517585)
XLA Ops:
  0.6 2.4 %collective-permute-start.8 = (f32[384,384]{1,0:T(8,128)}, f32[384,384]{1,0:T(8,128)S(1)}, u32[]{:S(2)}, u32[]{:S(2)}) collective-permute-start(f32[384,384]{1,0:T(8,128)} %bitcast.refs_0_), channel_id=1, source_target_pairs={{28,24},{29,25},{30,26},{31,27},{24,28},{25,29},{26,30},{27,31},{4... | collective-permute-start | bytes 1769480 | tf_op jit(solution)/shard_map/ppermute | solution.py:78
  3.1 0.9 copy-done.1
  4.0 1.8 %shard_map.85 = (f32[384,384]{1,0:T(8,128)S(1)}, f32[384,384]{1,0:T(8,128)S(1)}, f32[384,384]{1,0:T(8,128)S(1)}, f32[384,384]{1,0:T(8,128)S(1)}, f32[384,256]{1,0:T(8,128)S(1)}) custom-call(f32[384,384]{1,0:T(8,128)} %bitcast.refs_0_, f32[384,384]{1,0:T(8,128)} %bitcast.1.refs_1_, f32[384,384]{1,0:T(8,128)} %bitcast.2.refs_2_, f32[384,384]{1,0:T(8,128)} %bitcast.3.refs_3_, ...), custom_call_target="tpu_custom_call" | custom-call | flops 339738624 | bytes 5898240 | tf_op jit(solution)/shard_map/pallas_call | solution.py:55
  5.7 0.7 collective-permute-start
  6.4 0.7 collective-permute-start.1
  7.1 0.7 collective-permute-start.13
  7.8 0.7 collective-permute-start.10
  8.6 0.7 collective-permute-start.11
  9.3 8.5 %collective-permute-done.8.refs_0_ = f32[384,384]{1,0:T(8,128)S(1)} collective-permute-done((f32[384,384]{1,0:T(8,128)}, f32[384,384]{1,0:T(8,128)S(1)}, u32[]{:S(2)}, u32[]{:S(2)}) %collective-permute-start.8) | collective-permute-done | bytes 589856 | tf_op jit(solution)/shard_map/ppermute | solution.py:78
  17.8 0.7 collective-permute-start.5
  18.5 0.1 shard_map.88
  18.6 0.7 collective-permute-start.2
  19.3 17.6 %collective-permute-start.9 = (f32[384,384]{1,0:T(8,128)S(1)}, f32[384,384]{1,0:T(8,128)S(1)}, u32[]{:S(2)}, u32[]{:S(2)}) collective-permute-start(f32[384,384]{1,0:T(8,128)S(1)} %get-tuple-element.45), channel_id=1, source_target_pairs={{24,28},{25,29},{26,30},{27,31},{28,20},{29,21},{30,22},{31,23},{0... | collective-permute-start | bytes 1769480 | tf_op jit(solution)/shard_map/ppermute | solution.py:78
  36.9 0.7 collective-permute-start.16
  37.6 0.7 collective-permute-start.14
  38.3 0.7 collective-permute-start.6
  39.0 0.7 collective-permute-start.15
  39.7 8.8 %collective-permute-done.9.refs_1_.refs_0_ = f32[384,384]{1,0:T(8,128)S(1)} collective-permute-done((f32[384,384]{1,0:T(8,128)S(1)}, f32[384,384]{1,0:T(8,128)S(1)}, u32[]{:S(2)}, u32[]{:S(2)}) %collective-permute-start.9) | collective-permute-done | bytes 589856 | tf_op jit(solution)/shard_map/ppermute | solution.py:78
  48.6 0.7 collective-permute-start.12
  49.4 0.7 collective-permute-start.20
  50.1 10.9 %collective-permute-start.21 = (f32[384,384]{1,0:T(8,128)S(1)}, f32[384,384]{1,0:T(8,128)S(1)}, u32[]{:S(2)}, u32[]{:S(2)}) collective-permute-start(f32[384,384]{1,0:T(8,128)S(1)} %collective-permute-done.9.refs_1_.refs_0_), channel_id=1, source_target_pairs={{28,20},{29,21},{30,22},{31,23}} | collective-permute-start | bytes 1769480 | tf_op jit(solution)/shard_map/ppermute | solution.py:78
  61.0 0.7 collective-permute-start.7
  61.8 0.2 shard_map.93
  62.0 0.7 collective-permute-start.3
  62.7 0.7 collective-permute-start.17
  63.5 0.7 collective-permute-start.4
  64.2 8.7 %collective-permute-done.21.refs_1_ = f32[384,384]{1,0:T(8,128)S(1)} collective-permute-done((f32[384,384]{1,0:T(8,128)S(1)}, f32[384,384]{1,0:T(8,128)S(1)}, u32[]{:S(2)}, u32[]{:S(2)}) %collective-permute-start.21) | collective-permute-done | bytes 589856 | tf_op jit(solution)/shard_map/ppermute | solution.py:78
  72.9 0.7 collective-permute-start.26
  73.6 0.7 collective-permute-start.23
  74.4 1.3 collective-permute-start.19
  75.7 1.3 collective-permute-start.22
  77.0 0.9 collective-permute-start.18
  78.0 0.7 collective-permute-start.25
  78.7 1.3 collective-permute-start.24
  80.1 0.7 collective-permute-start.27
  80.8 9.0 %collective-permute-done.19.refs_1_ = f32[384,384]{1,0:T(8,128)S(1)} collective-permute-done((f32[384,384]{1,0:T(8,128)S(1)}, f32[384,384]{1,0:T(8,128)S(1)}, u32[]{:S(2)}, u32[]{:S(2)}) %collective-permute-start.19) | collective-permute-done | bytes 589856 | tf_op jit(solution)/shard_map/ppermute | solution.py:78
  89.8 0.7 collective-permute-start.29
  90.5 23.2 %collective-permute-done.22.refs_2_ = f32[384,384]{1,0:T(8,128)S(1)} collective-permute-done((f32[384,384]{1,0:T(8,128)S(1)}, f32[384,384]{1,0:T(8,128)S(1)}, u32[]{:S(2)}, u32[]{:S(2)}) %collective-permute-start.22) | collective-permute-done | bytes 589856 | tf_op jit(solution)/shard_map/ppermute | solution.py:78
  113.7 0.7 collective-permute-start.30
  114.4 1.3 shard_map.98.refs_1_.refs_0_
  115.7 1.4 %collective-permute-start.28 = (f32[384,128]{1,0:T(8,128)S(1)}, f32[384,128]{1,0:T(8,128)S(1)}, u32[]{:S(2)}, u32[]{:S(2)}) collective-permute-start(f32[384,128]{1,0:T(8,128)S(1)} %get-tuple-element.70), channel_id=1, source_target_pairs={{8,24},{9,25},{10,26},{11,27},{12,28},{13,29},{14,30},{15,31}} | collective-permute-start | bytes 589832 | tf_op jit(solution)/shard_map/ppermute | solution.py:78
  117.1 11.0 %collective-permute-done.24.refs_2_ = f32[384,128]{1,0:T(8,128)S(1)} collective-permute-done((f32[384,128]{1,0:T(8,128)S(1)}, f32[384,128]{1,0:T(8,128)S(1)}, u32[]{:S(2)}, u32[]{:S(2)}) %collective-permute-start.24) | collective-permute-done | bytes 196640 | tf_op jit(solution)/shard_map/ppermute | solution.py:78
  128.1 1.3 collective-permute-start.32
  129.4 0.4 shard_map.101.refs_0_
  129.8 5.4 %collective-permute-start.31 = (f32[384,128]{1,0:T(8,128)S(1)}, f32[384,128]{1,0:T(8,128)S(1)}, u32[]{:S(2)}, u32[]{:S(2)}) collective-permute-start(f32[384,128]{1,0:T(8,128)S(1)} %shard_map.101.refs_0_), channel_id=1, source_target_pairs={{24,25},{26,27},{28,29},{30,31}} | collective-permute-start | bytes 589832 | tf_op jit(solution)/shard_map/ppermute | solution.py:331
  135.2 0.8 shard_map.104
  136.1 0.2 collective-permute-done.31.refs_3_
  136.3 2.0 %shard_map.105 = f32[4,384,128]{2,1,0:T(8,128)} custom-call(f32[4,384,384]{2,1,0:T(8,128)S(1)} %bitcast.8, f32[384,128]{1,0:T(8,128)S(1)} %collective-permute-done.29.refs_1_, f32[384,128]{1,0:T(8,128)S(1)} %collective-permute-done.30.refs_2_, f32[384,128]{1,0:T(8,128)S(1)} %collective-permute-done.31.refs_3_, ...), custom_call_target="tpu_custom_call" | custom-call | flops 339738624 | bytes 4128768 | tf_op jit(solution)/shard_map/pallas_call | solution.py:55
  (45 shorter events, 0.5 us)
Async XLA Ops:
  0.6 17.2 %collective-permute-start.8 = (f32[384,384]{1,0:T(8,128)}, f32[384,384]{1,0:T(8,128)S(1)}, u32[]{:S(2)}, u32[]{:S(2)}) collective-permute-start(f32[384,384]{1,0:T(8,128)} %bitcast.refs_0_), channel_id=1, source_target_pairs={{28,24},{29,25},{30,26},{31,27},{24,28},{25,29},{26,30},{27,31},{4... | collective-permute-start | bytes 1769480 | tf_op jit(solution)/shard_map/ppermute | solution.py:78
  3.1 0.9 copy-start.1
  5.7 2.8 %collective-permute-start = (f32[384,256]{1,0:T(8,128)S(1)}, f32[384,256]{1,0:T(8,128)S(1)}, u32[]{:S(2)}, u32[]{:S(2)}) collective-permute-start(f32[384,256]{1,0:T(8,128)S(1)} %get-tuple-element.38.refs_0_.refs_6_), channel_id=1, source_target_pairs={{0,4},{1,5},{2,6},{3,7}} | collective-permute-start | bytes 1179656 | tf_op jit(solution)/shard_map/ppermute | solution.py:78
  6.4 12.1 %collective-permute-start.1 = (f32[384,384]{1,0:T(8,128)}, f32[384,384]{1,0:T(8,128)S(1)}, u32[]{:S(2)}, u32[]{:S(2)}) collective-permute-start(f32[384,384]{1,0:T(8,128)} %bitcast.2.refs_2_), channel_id=1, source_target_pairs={{0,4},{1,5},{2,6},{3,7},{4,8},{5,9},{6,10},{7,11},{8,12},{9,13},{1... | collective-permute-start | bytes 1769480 | tf_op jit(solution)/shard_map/ppermute | solution.py:78
  7.1 12.1 %collective-permute-start.13 = (f32[384,384]{1,0:T(8,128)}, f32[384,384]{1,0:T(8,128)S(1)}, u32[]{:S(2)}, u32[]{:S(2)}) collective-permute-start(f32[384,384]{1,0:T(8,128)} %bitcast.1.refs_1_), channel_id=1, source_target_pairs={{4,8},{5,9},{6,10},{7,11},{8,12},{9,13},{10,14},{11,15},{12,16},{1... | collective-permute-start | bytes 1769480 | tf_op jit(solution)/shard_map/ppermute | solution.py:78
  7.8 29.0 %collective-permute-start.10 = (f32[384,384]{1,0:T(8,128)}, f32[384,384]{1,0:T(8,128)S(1)}, u32[]{:S(2)}, u32[]{:S(2)}) collective-permute-start(f32[384,384]{1,0:T(8,128)} %bitcast.3.refs_3_), channel_id=1, source_target_pairs={{0,4},{1,5},{2,6},{3,7},{8,12},{9,13},{10,14},{11,15},{12,8},{13,9... | collective-permute-start | bytes 1769480 | tf_op jit(solution)/shard_map/ppermute | solution.py:78
  8.6 29.0 %collective-permute-start.11 = (f32[384,384]{1,0:T(8,128)}, f32[384,384]{1,0:T(8,128)S(1)}, u32[]{:S(2)}, u32[]{:S(2)}) collective-permute-start(f32[384,384]{1,0:T(8,128)} %bitcast.3.refs_3_), channel_id=1, source_target_pairs={{4,0},{5,1},{6,2},{7,3}} | collective-permute-start | bytes 1769480 | tf_op jit(solution)/shard_map/ppermute | solution.py:78
  17.8 20.5 %collective-permute-start.5 = (f32[384,384]{1,0:T(8,128)}, f32[384,384]{1,0:T(8,128)S(1)}, u32[]{:S(2)}, u32[]{:S(2)}) collective-permute-start(f32[384,384]{1,0:T(8,128)} %bitcast.refs_0_), channel_id=1, source_target_pairs={{8,0},{9,1},{10,2},{11,3}} | collective-permute-start | bytes 1769480 | tf_op jit(solution)/shard_map/ppermute | solution.py:78
  18.6 20.5 %collective-permute-start.2 = (f32[384,384]{1,0:T(8,128)}, f32[384,384]{1,0:T(8,128)S(1)}, u32[]{:S(2)}, u32[]{:S(2)}) collective-permute-start(f32[384,384]{1,0:T(8,128)} %bitcast.2.refs_2_), channel_id=1, source_target_pairs={{0,8},{1,9},{2,10},{3,11}} | collective-permute-start | bytes 1769480 | tf_op jit(solution)/shard_map/ppermute | solution.py:78
  19.3 29.3 %collective-permute-start.9 = (f32[384,384]{1,0:T(8,128)S(1)}, f32[384,384]{1,0:T(8,128)S(1)}, u32[]{:S(2)}, u32[]{:S(2)}) collective-permute-start(f32[384,384]{1,0:T(8,128)S(1)} %get-tuple-element.45), channel_id=1, source_target_pairs={{24,28},{25,29},{26,30},{27,31},{28,20},{29,21},{30,22},{31,23},{0... | collective-permute-start | bytes 1769480 | tf_op jit(solution)/shard_map/ppermute | solution.py:78
  36.9 12.5 %collective-permute-start.16 = (f32[384,384]{1,0:T(8,128)}, f32[384,384]{1,0:T(8,128)S(1)}, u32[]{:S(2)}, u32[]{:S(2)}) collective-permute-start(f32[384,384]{1,0:T(8,128)} %bitcast.3.refs_3_), channel_id=1, source_target_pairs={{16,20},{17,21},{18,22},{19,23}} | collective-permute-start | bytes 1769480 | tf_op jit(solution)/shard_map/ppermute | solution.py:78
  37.6 12.5 %collective-permute-start.14 = (f32[384,384]{1,0:T(8,128)}, f32[384,384]{1,0:T(8,128)S(1)}, u32[]{:S(2)}, u32[]{:S(2)}) collective-permute-start(f32[384,384]{1,0:T(8,128)} %bitcast.refs_0_), channel_id=1, source_target_pairs={{12,8},{13,9},{14,10},{15,11}} | collective-permute-start | bytes 1769480 | tf_op jit(solution)/shard_map/ppermute | solution.py:78
  38.3 22.7 %collective-permute-start.6 = (f32[384,384]{1,0:T(8,128)S(1)}, f32[384,384]{1,0:T(8,128)S(1)}, u32[]{:S(2)}, u32[]{:S(2)}) collective-permute-start(f32[384,384]{1,0:T(8,128)S(1)} %collective-permute-done.5), channel_id=1, source_target_pairs={{0,4},{1,5},{2,6},{3,7}} | collective-permute-start | bytes 1769480 | tf_op jit(solution)/shard_map/ppermute | solution.py:78
  39.0 23.0 %collective-permute-start.15 = (f32[384,384]{1,0:T(8,128)}, f32[384,384]{1,0:T(8,128)S(1)}, u32[]{:S(2)}, u32[]{:S(2)}) collective-permute-start(f32[384,384]{1,0:T(8,128)} %bitcast.refs_0_), channel_id=1, source_target_pairs={{16,12},{17,13},{18,14},{19,15}} | collective-permute-start | bytes 1769480 | tf_op jit(solution)/shard_map/ppermute | solution.py:78
  48.6 14.1 %collective-permute-start.12 = (f32[384,384]{1,0:T(8,128)S(1)}, f32[384,384]{1,0:T(8,128)S(1)}, u32[]{:S(2)}, u32[]{:S(2)}) collective-permute-start(f32[384,384]{1,0:T(8,128)S(1)} %collective-permute-done.11), channel_id=1, source_target_pairs={{0,8},{1,9},{2,10},{3,11}} | collective-permute-start | bytes 1769480 | tf_op jit(solution)/shard_map/ppermute | solution.py:78
  49.4 14.1 %collective-permute-start.20 = (f32[384,384]{1,0:T(8,128)S(1)}, f32[384,384]{1,0:T(8,128)S(1)}, u32[]{:S(2)}, u32[]{:S(2)}) collective-permute-start(f32[384,384]{1,0:T(8,128)S(1)} %get-tuple-element.57), channel_id=1, source_target_pairs={{20,16},{21,17},{22,18},{23,19}} | collective-permute-start | bytes 1769480 | tf_op jit(solution)/shard_map/ppermute | solution.py:78
  50.1 22.8 %collective-permute-start.21 = (f32[384,384]{1,0:T(8,128)S(1)}, f32[384,384]{1,0:T(8,128)S(1)}, u32[]{:S(2)}, u32[]{:S(2)}) collective-permute-start(f32[384,384]{1,0:T(8,128)S(1)} %collective-permute-done.9.refs_1_.refs_0_), channel_id=1, source_target_pairs={{28,20},{29,21},{30,22},{31,23}} | collective-permute-start | bytes 1769480 | tf_op jit(solution)/shard_map/ppermute | solution.py:78
  61.0 12.6 %collective-permute-start.7 = (f32[384,384]{1,0:T(8,128)S(1)}, f32[384,384]{1,0:T(8,128)S(1)}, u32[]{:S(2)}, u32[]{:S(2)}) collective-permute-start(f32[384,384]{1,0:T(8,128)S(1)} %collective-permute-done.6), channel_id=1, source_target_pairs={{4,12},{5,13},{6,14},{7,15}} | collective-permute-start | bytes 1769480 | tf_op jit(solution)/shard_map/ppermute | solution.py:78
  62.0 13.7 %collective-permute-start.3 = (f32[384,384]{1,0:T(8,128)S(1)}, f32[384,384]{1,0:T(8,128)S(1)}, u32[]{:S(2)}, u32[]{:S(2)}) collective-permute-start(f32[384,384]{1,0:T(8,128)S(1)} %get-tuple-element.44.refs_4_.refs_2_.refs_3_), channel_id=1, source_target_pairs={{4,12},{5,13},{6,14},{7,15}} | collective-permute-start | bytes 1769480 | tf_op jit(solution)/shard_map/ppermute | solution.py:78
  62.7 14.3 %collective-permute-start.17 = (f32[384,384]{1,0:T(8,128)S(1)}, f32[384,384]{1,0:T(8,128)S(1)}, u32[]{:S(2)}, u32[]{:S(2)}) collective-permute-start(f32[384,384]{1,0:T(8,128)S(1)} %get-tuple-element.52.refs_5_), channel_id=1, source_target_pairs={{16,8},{17,9},{18,10},{19,11},{20,12},{21,13},{22,14},{23,15}} | collective-permute-start | bytes 1769480 | tf_op jit(solution)/shard_map/ppermute | solution.py:78
  63.5 10.9 %collective-permute-start.4 = (f32[384,128]{1,0:T(8,128)S(1)}, f32[384,128]{1,0:T(8,128)S(1)}, u32[]{:S(2)}, u32[]{:S(2)}) collective-permute-start(f32[384,128]{1,0:T(8,128)S(1)} %get-tuple-element.41.refs_0_), channel_id=1, source_target_pairs={{0,8},{1,9},{2,10},{3,11},{4,12},{5,13},{6,14},{7,15}} | collective-permute-start | bytes 589832 | tf_op jit(solution)/shard_map/ppermute | solution.py:78
  72.9 5.9 %collective-permute-start.26 = (f32[384,512]{1,0:T(8,128)S(1)}, f32[384,512]{1,0:T(8,128)S(1)}, u32[]{:S(2)}, u32[]{:S(2)}) collective-permute-start(f32[384,512]{1,0:T(8,128)S(1)} %get-tuple-element.53.refs_6_.refs_5_.refs_2_), channel_id=1, source_target_pairs={{0,8},{1,9},{2,10},{3,11},{4,12},{5,13},{6,14},{7,15}} | collective-permute-start | bytes 2359304 | tf_op jit(solution)/shard_map/ppermute | solution.py:78
  73.6 4.4 %collective-permute-start.23 = (f32[384,384]{1,0:T(8,128)S(1)}, f32[384,384]{1,0:T(8,128)S(1)}, u32[]{:S(2)}, u32[]{:S(2)}) collective-permute-start(f32[384,384]{1,0:T(8,128)S(1)} %get-tuple-element.60), channel_id=1, source_target_pairs={{16,8},{17,9},{18,10},{19,11},{20,12},{21,13},{22,14},{23,15}} | collective-permute-start | bytes 1769480 | tf_op jit(solution)/shard_map/ppermute | solution.py:78
  74.4 15.4 %collective-permute-start.19 = (f32[384,384]{1,0:T(8,128)S(1)}, f32[384,384]{1,0:T(8,128)S(1)}, u32[]{:S(2)}, u32[]{:S(2)}) collective-permute-start(f32[384,384]{1,0:T(8,128)S(1)} %get-tuple-element.56), channel_id=1, source_target_pairs={{20,24},{21,25},{22,26},{23,27},{24,28},{25,29},{26,30},{27,31}} | collective-permute-start | bytes 1769480 | tf_op jit(solution)/shard_map/ppermute | solution.py:78
  75.7 38.0 %collective-permute-start.22 = (f32[384,384]{1,0:T(8,128)S(1)}, f32[384,384]{1,0:T(8,128)S(1)}, u32[]{:S(2)}, u32[]{:S(2)}) collective-permute-start(f32[384,384]{1,0:T(8,128)S(1)} %get-tuple-element.59), channel_id=1, source_target_pairs={{16,24},{17,25},{18,26},{19,27},{20,28},{21,29},{22,30},{23,31}} | collective-permute-start | bytes 1769480 | tf_op jit(solution)/shard_map/ppermute | solution.py:78
  77.0 3.0 %collective-permute-start.18 = (f32[384,128]{1,0:T(8,128)S(1)}, f32[384,128]{1,0:T(8,128)S(1)}, u32[]{:S(2)}, u32[]{:S(2)}) collective-permute-start(f32[384,128]{1,0:T(8,128)S(1)} %get-tuple-element.54), channel_id=1, source_target_pairs={{8,16},{9,17},{10,18},{11,19},{12,20},{13,21},{14,22},{15,23}} | collective-permute-start | bytes 589832 | tf_op jit(solution)/shard_map/ppermute | solution.py:78
  78.0 37.6 %collective-permute-start.25 = (f32[384,128]{1,0:T(8,128)S(1)}, f32[384,128]{1,0:T(8,128)S(1)}, u32[]{:S(2)}, u32[]{:S(2)}) collective-permute-start(f32[384,128]{1,0:T(8,128)S(1)} %get-tuple-element.62.refs_6_), channel_id=1, source_target_pairs={{9,25},{11,27},{13,29},{15,31}} | collective-permute-start | bytes 589832 | tf_op jit(solution)/shard_map/ppermute | solution.py:78
  78.7 49.4 %collective-permute-start.24 = (f32[384,128]{1,0:T(8,128)S(1)}, f32[384,128]{1,0:T(8,128)S(1)}, u32[]{:S(2)}, u32[]{:S(2)}) collective-permute-start(f32[384,128]{1,0:T(8,128)S(1)} %get-tuple-element.62.refs_6_), channel_id=1, source_target_pairs={{8,24},{10,26},{12,28},{14,30}} | collective-permute-start | bytes 589832 | tf_op jit(solution)/shard_map/ppermute | solution.py:78
  80.1 49.8 %collective-permute-start.27 = (f32[384,128]{1,0:T(8,128)S(1)}, f32[384,128]{1,0:T(8,128)S(1)}, u32[]{:S(2)}, u32[]{:S(2)}) collective-permute-start(f32[384,128]{1,0:T(8,128)S(1)} %get-tuple-element.69), channel_id=1, source_target_pairs={{8,16},{9,17},{10,18},{11,19},{12,20},{13,21},{14,22},{15,23}} | collective-permute-start | bytes 589832 | tf_op jit(solution)/shard_map/ppermute | solution.py:78
  89.8 46.2 %collective-permute-start.29 = (f32[384,128]{1,0:T(8,128)S(1)}, f32[384,128]{1,0:T(8,128)S(1)}, u32[]{:S(2)}, u32[]{:S(2)}) collective-permute-start(f32[384,128]{1,0:T(8,128)S(1)} %get-tuple-element.51.refs_0_.refs_5_), channel_id=1, source_target_pairs={{0,1},{1,2},{2,3},{3,4},{4,5},{5,6},{6,7},{7,8},{8,9},{9,10},{10,1... | collective-permute-start | bytes 589832 | tf_op jit(solution)/shard_map/ppermute | solution.py:331
  113.7 22.4 %collective-permute-start.30 = (f32[384,128]{1,0:T(8,128)S(1)}, f32[384,128]{1,0:T(8,128)S(1)}, u32[]{:S(2)}, u32[]{:S(2)}) collective-permute-start(f32[384,128]{1,0:T(8,128)S(1)} %shard_map.95.refs_0_), channel_id=1, source_target_pairs={{16,17},{17,18},{18,19},{19,20},{20,21},{21,22},{22,23},{23,24}} | collective-permute-start | bytes 589832 | tf_op jit(solution)/shard_map/ppermute | solution.py:331
  115.6 20.6 %copy-start = (f32[1,4,384,384]{3,2,1,0:T(8,128)S(1)}, f32[1,4,384,384]{3,2,1,0:T(8,128)}, u32[]{:S(2)}) copy-start(f32[1,4,384,384]{3,2,1,0:T(8,128)} %param.10) | copy-start | bytes 7077892
  115.6 20.6 %copy-start.2 = (f32[384,128]{1,0:T(8,128)S(1)}, f32[384,128]{1,0:T(8,128)}, u32[]{:S(2)}) copy-start(f32[384,128]{1,0:T(8,128)} %refs_5_.1) | copy-start | bytes 589828
  115.7 19.6 %collective-permute-start.28 = (f32[384,128]{1,0:T(8,128)S(1)}, f32[384,128]{1,0:T(8,128)S(1)}, u32[]{:S(2)}, u32[]{:S(2)}) collective-permute-start(f32[384,128]{1,0:T(8,128)S(1)} %get-tuple-element.70), channel_id=1, source_target_pairs={{8,24},{9,25},{10,26},{11,27},{12,28},{13,29},{14,30},{15,31}} | collective-permute-start | bytes 589832 | tf_op jit(solution)/shard_map/ppermute | solution.py:78
  128.1 7.9 %collective-permute-start.32 = (f32[384,128]{1,0:T(8,128)S(1)}, f32[384,128]{1,0:T(8,128)S(1)}, u32[]{:S(2)}, u32[]{:S(2)}) collective-permute-start(f32[384,128]{1,0:T(8,128)S(1)} %shard_map.102.refs_1_), channel_id=1, source_target_pairs={{25,26},{27,28},{29,30}} | collective-permute-start | bytes 589832 | tf_op jit(solution)/shard_map/ppermute | solution.py:331
  129.8 6.4 %collective-permute-start.31 = (f32[384,128]{1,0:T(8,128)S(1)}, f32[384,128]{1,0:T(8,128)S(1)}, u32[]{:S(2)}, u32[]{:S(2)}) collective-permute-start(f32[384,128]{1,0:T(8,128)S(1)} %shard_map.101.refs_0_), channel_id=1, source_target_pairs={{24,25},{26,27},{28,29},{30,31}} | collective-permute-start | bytes 589832 | tf_op jit(solution)/shard_map/ppermute | solution.py:331

commit v13 on v9

--- a/solution.py
+++ b/solution.py
@@ -158,7 +158,8 @@
     (t1, rgt) = staged(forward_t, stride, [q0, t0, r, t], [square] * 2, 6)
 
     (relay, gt) = staged(pair_reflect(5), stride, [hopped, r, t, q, u, gt], [square] * 2, 6)
-    bounced = moved(relay, [(5, 4), (7, 5)])
+    bounced = moved(relay, [(5, 4)])
+    bounced_s = moved(hopped, [(7, 5)])
     gt_came = moved(gt, [(5, 6), (6, 7)])
 
     def forward_u(k, u0, hu, rgt, u1, w):
@@ -185,14 +186,15 @@
     (f1, rg) = staged(low_fields, stride, [first, first_came, q0, r, t], [field] * 2, 2)
     fa = moved(f1, low)
 
-    def second_reflect(k, bounced, q1, t1, u1, w, total, gt_out):
+    def second_reflect(k, bounced, bounced_s, q1, t1, u1, w, total, gt_out):
         @pl.when((k == 4) | (k == 5))
         def _():
-            gt = summed(product(q1[...], bounced[...]), t1[...])
+            came = jnp.where(k == 4, bounced[...], bounced_s[...])
+            gt = summed(product(q1[...], came), t1[...])
             gt_out[...] = gt
-            total[...] = w[...] + product(u1[...], product(bounced[...], gt))
-
-    (total, gt2) = staged(second_reflect, stride, [bounced, q1, t1, u1, w], [square] * 2, 6
+            total[...] = w[...] + product(u1[...], product(came, gt))
+
+    (total, gt2) = staged(second_reflect, stride, [bounced, bounced_s, q1, t1, u1, w], [square] * 2, 6
     )
     total_came = moved(total, back)
     gt2_came = moved(gt2, [(4, 6), (5, 7)])
@@ -358,19 +360,13 @@
     (odd,) = staged(through_odd, 1, [mid, t2, g6_odd], [field], 0.3)
     next_odd = passed(odd, lambda i: i >= top and i % 2 == 1)
 
-    def through_even(d, odd, t2, g6, out):
-        late = (d >= top) & (d % 2 == 0)
-
-        @pl.when(late)
+    def through_even(d, t2, g6, out):
+        @pl.when((d >= top) & (d % 2 == 0))
         def _():
             out[...] = product(t2[...], g6[...])
 
-        @pl.when(jnp.logical_not(late))
-        def _():
-            out[...] = odd[...]
-
-    (through_field,) = staged(through_even, 1, [odd, t2, g6_even], [field], 0.3)
-    next_even = passed(through_field, lambda i: i >= top and i % 2 == 0)
+    (even,) = staged(through_even, 1, [t2, g6_even], [field], 0.3)
+    next_even = passed(even, lambda i: i >= top and i % 2 == 0)
 
     def depths(d, maps, low, mid, odd, even, incident, out):
         came = jnp.where(d % 2 == 1, even[...], odd[...])
@@ -388,24 +384,37 @@
         1,
     )
 
-    def reflected_out(k, both, s2, s4, s6, out):
+    def fields_out(d, odd, even, both, s2, s4, s6, through, reflected):
+        k = d // stride
+        late = (d >= top) & (d % 2 == 0)
+
+        @pl.when(late)
+        def _():
+            through[...] = even[...]
+
+        @pl.when(jnp.logical_not(late))
+        def _():
+            through[...] = odd[...]
+
         @pl.when(k < 2)
         def _():
-            out[...] = both[:, square[1] :]
-
-        @pl.when((k == 2) | (k == 3))
-        def _():
-            out[...] = s2[...]
+            reflected[...] = both[:, square[1] :]
+
+        @pl.when((k == 2) | (k == 3))
+        def _():
+            reflected[...] = s2[...]
 
         @pl.when((k == 4) | (k == 5))
         def _():
-            out[...] = s4[...]
+            reflected[...] = s4[...]
 
         @pl.when(k > 5)
         def _():
-            out[...] = s6[...]
-
-    (reflected,) = staged(reflected_out, stride, [both, s2, s4_came, s6_came], [field], 0.1)
+            reflected[...] = s6[...]
+
+    (through_field, reflected) = staged(
+        fields_out, 1, [odd, even, both, s2, s4_came, s6_came], [field] * 2, 0.1
+    )
     return (through_field[None], reflected[None], depth_fields[None])
 
 

time: 127 us -> 137 us (1.079)
  the two profiles are of different devices: /device:TPU:30 before, /device:TPU:28 now
where the time goes in v13:
time: 137 us; the launch traced here: 135 us
  waiting for transfers between devices  72.9 us (53%)
  starting transfers between devices  53.3 us (39%)
  Pallas kernels  7.06 us (5%)
    ppermute x29, waiting for transfers between devices, moved(): return lax.ppermute(value, 'sec', pairs)  72.5 us
    ppermute x29, starting transfers between devices, moved(): return lax.ppermute(value, 'sec', pairs)  49.4 us
    pallas_call x21, Pallas kernels, staged(): pl.pallas_call(kernel, out_shape=[jax.ShapeDtypeStruct(shape, dtype) for...  7.06 us
    ppermute x4, starting transfers between devices, passed(): return lax.ppermute(value, 'sec', pairs)  3.92 us
  transfers between devices with their start and end apart: 33, of which 8 were waited for; matrix products, arithmetic and copies ran while one was open for 0% of the time, Pallas kernels for 4%

profile of v13, /device:TPU:28, one launch (start us, length us, event | category | flops | bytes accessed | tf_op | source)
XLA Modules:
  0.0 135.5 jit_solution(14123803124479956829)
XLA Ops:
  0.6 2.4 %collective-permute-start.8 = (f32[384,384]{1,0:T(8,128)}, f32[384,384]{1,0:T(8,128)S(1)}, u32[]{:S(2)}, u32[]{:S(2)}) collective-permute-start(f32[384,384]{1,0:T(8,128)} %bitcast.refs_0_), channel_id=1, source_target_pairs={{28,24},{29,25},{30,26},{31,27},{24,28},{25,29},{26,30},{27,31},{4... | collective-permute-start | bytes 1769480 | tf_op jit(solution)/shard_map/ppermute | solution.py:78
  3.1 0.9 copy-done.1
  4.0 1.8 %shard_map.85 = (f32[384,384]{1,0:T(8,128)S(1)}, f32[384,384]{1,0:T(8,128)S(1)}, f32[384,384]{1,0:T(8,128)S(1)}, f32[384,384]{1,0:T(8,128)S(1)}, f32[384,256]{1,0:T(8,128)S(1)}) custom-call(f32[384,384]{1,0:T(8,128)} %bitcast.refs_0_, f32[384,384]{1,0:T(8,128)} %bitcast.1.refs_1_, f32[384,384]{1,0:T(8,128)} %bitcast.2.refs_2_, f32[384,384]{1,0:T(8,128)} %bitcast.3.refs_3_, ...), custom_call_target="tpu_custom_call" | custom-call | flops 339738624 | bytes 5898240 | tf_op jit(solution)/shard_map/pallas_call | solution.py:55
  5.7 0.7 collective-permute-start
  6.4 0.7 collective-permute-start.1
  7.1 0.7 collective-permute-start.13
  7.8 0.7 collective-permute-start.11
  8.6 0.7 collective-permute-start.10
  9.3 8.5 %collective-permute-done.8.refs_0_ = f32[384,384]{1,0:T(8,128)S(1)} collective-permute-done((f32[384,384]{1,0:T(8,128)}, f32[384,384]{1,0:T(8,128)S(1)}, u32[]{:S(2)}, u32[]{:S(2)}) %collective-permute-start.8) | collective-permute-done | bytes 589856 | tf_op jit(solution)/shard_map/ppermute | solution.py:78
  17.8 0.7 collective-permute-start.5
  18.6 0.7 collective-permute-start.2
  19.3 17.6 %collective-permute-start.9 = (f32[384,384]{1,0:T(8,128)S(1)}, f32[384,384]{1,0:T(8,128)S(1)}, u32[]{:S(2)}, u32[]{:S(2)}) collective-permute-start(f32[384,384]{1,0:T(8,128)S(1)} %get-tuple-element.43), channel_id=1, source_target_pairs={{24,28},{25,29},{26,30},{27,31},{28,20},{29,21},{30,22},{31,23},{0... | collective-permute-start | bytes 1769480 | tf_op jit(solution)/shard_map/ppermute | solution.py:78
  36.9 0.7 collective-permute-start.16
  37.6 0.7 collective-permute-start.14
  38.3 0.7 collective-permute-start.6
  39.0 0.7 collective-permute-start.15
  39.7 8.8 %collective-permute-done.9.refs_1_.refs_0_ = f32[384,384]{1,0:T(8,128)S(1)} collective-permute-done((f32[384,384]{1,0:T(8,128)S(1)}, f32[384,384]{1,0:T(8,128)S(1)}, u32[]{:S(2)}, u32[]{:S(2)}) %collective-permute-start.9) | collective-permute-done | bytes 589856 | tf_op jit(solution)/shard_map/ppermute | solution.py:78
  48.6 0.7 collective-permute-start.12
  49.4 0.7 collective-permute-start.20
  50.1 9.0 %collective-permute-start.21 = (f32[384,384]{1,0:T(8,128)S(1)}, f32[384,384]{1,0:T(8,128)S(1)}, u32[]{:S(2)}, u32[]{:S(2)}) collective-permute-start(f32[384,384]{1,0:T(8,128)S(1)} %collective-permute-done.9.refs_1_.refs_0_), channel_id=1, source_target_pairs={{28,20},{29,21},{30,22},{31,23}} | collective-permute-start | bytes 1769480 | tf_op jit(solution)/shard_map/ppermute | solution.py:78
  59.2 0.7 collective-permute-start.7
  60.2 0.7 collective-permute-start.3
  60.9 0.7 collective-permute-start.17
  61.7 0.7 collective-permute-start.4
  62.4 7.6 %collective-permute-done.21.refs_1_ = f32[384,384]{1,0:T(8,128)S(1)} collective-permute-done((f32[384,384]{1,0:T(8,128)S(1)}, f32[384,384]{1,0:T(8,128)S(1)}, u32[]{:S(2)}, u32[]{:S(2)}) %collective-permute-start.21) | collective-permute-done | bytes 589856 | tf_op jit(solution)/shard_map/ppermute | solution.py:78
  70.0 0.7 collective-permute-start.26
  70.7 0.7 collective-permute-start.23
  71.5 1.3 collective-permute-start.19
  72.8 1.3 collective-permute-start.22
  74.1 0.7 collective-permute-start.18
  74.8 0.2 shard_map.92
  75.1 1.3 collective-permute-start.25
  76.5 0.7 collective-permute-start.24
  77.2 0.7 collective-permute-start.27
  77.9 8.0 %collective-permute-done.19.refs_1_ = f32[384,384]{1,0:T(8,128)S(1)} collective-permute-done((f32[384,384]{1,0:T(8,128)S(1)}, f32[384,384]{1,0:T(8,128)S(1)}, u32[]{:S(2)}, u32[]{:S(2)}) %collective-permute-start.19) | collective-permute-done | bytes 589856 | tf_op jit(solution)/shard_map/ppermute | solution.py:78
  85.9 0.7 collective-permute-start.29
  86.6 21.6 %collective-permute-done.22.refs_2_ = f32[384,384]{1,0:T(8,128)S(1)} collective-permute-done((f32[384,384]{1,0:T(8,128)S(1)}, f32[384,384]{1,0:T(8,128)S(1)}, u32[]{:S(2)}, u32[]{:S(2)}) %collective-permute-start.22) | collective-permute-done | bytes 589856 | tf_op jit(solution)/shard_map/ppermute | solution.py:78
  108.1 0.7 collective-permute-start.30
  108.8 1.3 shard_map.98.refs_1_.refs_0_
  110.1 12.4 %collective-permute-done.25.refs_1_ = f32[384,128]{1,0:T(8,128)S(1)} collective-permute-done((f32[384,128]{1,0:T(8,128)S(1)}, f32[384,128]{1,0:T(8,128)S(1)}, u32[]{:S(2)}, u32[]{:S(2)}) %collective-permute-start.25) | collective-permute-done | bytes 196640 | tf_op jit(solution)/shard_map/ppermute | solution.py:78
  122.5 1.3 collective-permute-start.28
  123.8 0.4 shard_map.102.refs_1_
  124.2 1.3 collective-permute-start.32
  125.6 1.3 collective-permute-start.31
  126.9 5.5 %collective-permute-done.28.refs_5_ = f32[384,128]{1,0:T(8,128)S(1)} collective-permute-done((f32[384,128]{1,0:T(8,128)S(1)}, f32[384,128]{1,0:T(8,128)S(1)}, u32[]{:S(2)}, u32[]{:S(2)}) %collective-permute-start.28) | collective-permute-done | bytes 196640 | tf_op jit(solution)/shard_map/ppermute | solution.py:78
  132.4 0.8 shard_map.104
  133.2 0.3 collective-permute-done.31.refs_3_
  133.5 2.0 %shard_map.105 = f32[4,384,128]{2,1,0:T(8,128)} custom-call(f32[4,384,384]{2,1,0:T(8,128)S(1)} %bitcast.8, f32[384,128]{1,0:T(8,128)S(1)} %collective-permute-done.29.refs_1_, f32[384,128]{1,0:T(8,128)S(1)} %collective-permute-done.30.refs_2_, f32[384,128]{1,0:T(8,128)S(1)} %collective-permute-done.31.refs_3_, ...), custom_call_target="tpu_custom_call" | custom-call | flops 339738624 | bytes 4128768 | tf_op jit(solution)/shard_map/pallas_call | solution.py:55
  (45 shorter events, 0.7 us)
Async XLA Ops:
  0.6 17.2 %collective-permute-start.8 = (f32[384,384]{1,0:T(8,128)}, f32[384,384]{1,0:T(8,128)S(1)}, u32[]{:S(2)}, u32[]{:S(2)}) collective-permute-start(f32[384,384]{1,0:T(8,128)} %bitcast.refs_0_), channel_id=1, source_target_pairs={{28,24},{29,25},{30,26},{31,27},{24,28},{25,29},{26,30},{27,31},{4... | collective-permute-start | bytes 1769480 | tf_op jit(solution)/shard_map/ppermute | solution.py:78
  3.1 0.9 copy-start.1
  5.7 2.8 %collective-permute-start = (f32[384,256]{1,0:T(8,128)S(1)}, f32[384,256]{1,0:T(8,128)S(1)}, u32[]{:S(2)}, u32[]{:S(2)}) collective-permute-start(f32[384,256]{1,0:T(8,128)S(1)} %get-tuple-element.36.refs_0_.refs_6_), channel_id=1, source_target_pairs={{0,4},{1,5},{2,6},{3,7}} | collective-permute-start | bytes 1179656 | tf_op jit(solution)/shard_map/ppermute | solution.py:78
  6.4 12.1 %collective-permute-start.1 = (f32[384,384]{1,0:T(8,128)}, f32[384,384]{1,0:T(8,128)S(1)}, u32[]{:S(2)}, u32[]{:S(2)}) collective-permute-start(f32[384,384]{1,0:T(8,128)} %bitcast.2.refs_2_), channel_id=1, source_target_pairs={{0,4},{1,5},{2,6},{3,7},{4,8},{5,9},{6,10},{7,11},{8,12},{9,13},{1... | collective-permute-start | bytes 1769480 | tf_op jit(solution)/shard_map/ppermute | solution.py:78
  7.1 12.1 %collective-permute-start.13 = (f32[384,384]{1,0:T(8,128)}, f32[384,384]{1,0:T(8,128)S(1)}, u32[]{:S(2)}, u32[]{:S(2)}) collective-permute-start(f32[384,384]{1,0:T(8,128)} %bitcast.1.refs_1_), channel_id=1, source_target_pairs={{4,8},{5,9},{6,10},{7,11},{8,12},{9,13},{10,14},{11,15},{12,16},{1... | collective-permute-start | bytes 1769480 | tf_op jit(solution)/shard_map/ppermute | solution.py:78
  7.8 29.0 %collective-permute-start.11 = (f32[384,384]{1,0:T(8,128)}, f32[384,384]{1,0:T(8,128)S(1)}, u32[]{:S(2)}, u32[]{:S(2)}) collective-permute-start(f32[384,384]{1,0:T(8,128)} %bitcast.3.refs_3_), channel_id=1, source_target_pairs={{4,0},{5,1},{6,2},{7,3}} | collective-permute-start | bytes 1769480 | tf_op jit(solution)/shard_map/ppermute | solution.py:78
  8.6 29.0 %collective-permute-start.10 = (f32[384,384]{1,0:T(8,128)}, f32[384,384]{1,0:T(8,128)S(1)}, u32[]{:S(2)}, u32[]{:S(2)}) collective-permute-start(f32[384,384]{1,0:T(8,128)} %bitcast.3.refs_3_), channel_id=1, source_target_pairs={{0,4},{1,5},{2,6},{3,7},{8,12},{9,13},{10,14},{11,15}} | collective-permute-start | bytes 1769480 | tf_op jit(solution)/shard_map/ppermute | solution.py:78
  17.8 20.5 %collective-permute-start.5 = (f32[384,384]{1,0:T(8,128)}, f32[384,384]{1,0:T(8,128)S(1)}, u32[]{:S(2)}, u32[]{:S(2)}) collective-permute-start(f32[384,384]{1,0:T(8,128)} %bitcast.refs_0_), channel_id=1, source_target_pairs={{8,0},{9,1},{10,2},{11,3}} | collective-permute-start | bytes 1769480 | tf_op jit(solution)/shard_map/ppermute | solution.py:78
  18.6 20.5 %collective-permute-start.2 = (f32[384,384]{1,0:T(8,128)}, f32[384,384]{1,0:T(8,128)S(1)}, u32[]{:S(2)}, u32[]{:S(2)}) collective-permute-start(f32[384,384]{1,0:T(8,128)} %bitcast.2.refs_2_), channel_id=1, source_target_pairs={{0,8},{1,9},{2,10},{3,11}} | collective-permute-start | bytes 1769480 | tf_op jit(solution)/shard_map/ppermute | solution.py:78
  19.3 29.3 %collective-permute-start.9 = (f32[384,384]{1,0:T(8,128)S(1)}, f32[384,384]{1,0:T(8,128)S(1)}, u32[]{:S(2)}, u32[]{:S(2)}) collective-permute-start(f32[384,384]{1,0:T(8,128)S(1)} %get-tuple-element.43), channel_id=1, source_target_pairs={{24,28},{25,29},{26,30},{27,31},{28,20},{29,21},{30,22},{31,23},{0... | collective-permute-start | bytes 1769480 | tf_op jit(solution)/shard_map/ppermute | solution.py:78
  36.9 12.5 %collective-permute-start.16 = (f32[384,384]{1,0:T(8,128)}, f32[384,384]{1,0:T(8,128)S(1)}, u32[]{:S(2)}, u32[]{:S(2)}) collective-permute-start(f32[384,384]{1,0:T(8,128)} %bitcast.3.refs_3_), channel_id=1, source_target_pairs={{12,16},{13,17},{14,18},{15,19},{16,20},{17,21},{18,22},{19,23}} | collective-permute-start | bytes 1769480 | tf_op jit(solution)/shard_map/ppermute | solution.py:78
  37.6 12.5 %collective-permute-start.14 = (f32[384,384]{1,0:T(8,128)}, f32[384,384]{1,0:T(8,128)S(1)}, u32[]{:S(2)}, u32[]{:S(2)}) collective-permute-start(f32[384,384]{1,0:T(8,128)} %bitcast.refs_0_), channel_id=1, source_target_pairs={{12,8},{13,9},{14,10},{15,11}} | collective-permute-start | bytes 1769480 | tf_op jit(solution)/shard_map/ppermute | solution.py:78
  38.3 20.9 %collective-permute-start.6 = (f32[384,384]{1,0:T(8,128)S(1)}, f32[384,384]{1,0:T(8,128)S(1)}, u32[]{:S(2)}, u32[]{:S(2)}) collective-permute-start(f32[384,384]{1,0:T(8,128)S(1)} %collective-permute-done.5), channel_id=1, source_target_pairs={{0,4},{1,5},{2,6},{3,7}} | collective-permute-start | bytes 1769480 | tf_op jit(solution)/shard_map/ppermute | solution.py:78
  39.0 21.1 %collective-permute-start.15 = (f32[384,384]{1,0:T(8,128)}, f32[384,384]{1,0:T(8,128)S(1)}, u32[]{:S(2)}, u32[]{:S(2)}) collective-permute-start(f32[384,384]{1,0:T(8,128)} %bitcast.refs_0_), channel_id=1, source_target_pairs={{16,12},{17,13},{18,14},{19,15}} | collective-permute-start | bytes 1769480 | tf_op jit(solution)/shard_map/ppermute | solution.py:78
  48.6 12.3 %collective-permute-start.12 = (f32[384,384]{1,0:T(8,128)S(1)}, f32[384,384]{1,0:T(8,128)S(1)}, u32[]{:S(2)}, u32[]{:S(2)}) collective-permute-start(f32[384,384]{1,0:T(8,128)S(1)} %collective-permute-done.11), channel_id=1, source_target_pairs={{0,8},{1,9},{2,10},{3,11}} | collective-permute-start | bytes 1769480 | tf_op jit(solution)/shard_map/ppermute | solution.py:78
  49.4 12.3 %collective-permute-start.20 = (f32[384,384]{1,0:T(8,128)S(1)}, f32[384,384]{1,0:T(8,128)S(1)}, u32[]{:S(2)}, u32[]{:S(2)}) collective-permute-start(f32[384,384]{1,0:T(8,128)S(1)} %get-tuple-element.55), channel_id=1, source_target_pairs={{20,16},{21,17},{22,18},{23,19}} | collective-permute-start | bytes 1769480 | tf_op jit(solution)/shard_map/ppermute | solution.py:78
  50.1 19.9 %collective-permute-start.21 = (f32[384,384]{1,0:T(8,128)S(1)}, f32[384,384]{1,0:T(8,128)S(1)}, u32[]{:S(2)}, u32[]{:S(2)}) collective-permute-start(f32[384,384]{1,0:T(8,128)S(1)} %collective-permute-done.9.refs_1_.refs_0_), channel_id=1, source_target_pairs={{28,20},{29,21},{30,22},{31,23}} | collective-permute-start | bytes 1769480 | tf_op jit(solution)/shard_map/ppermute | solution.py:78
  59.2 11.5 %collective-permute-start.7 = (f32[384,384]{1,0:T(8,128)S(1)}, f32[384,384]{1,0:T(8,128)S(1)}, u32[]{:S(2)}, u32[]{:S(2)}) collective-permute-start(f32[384,384]{1,0:T(8,128)S(1)} %collective-permute-done.6), channel_id=1, source_target_pairs={{4,12},{5,13},{6,14},{7,15}} | collective-permute-start | bytes 1769480 | tf_op jit(solution)/shard_map/ppermute | solution.py:78
  60.2 12.6 %collective-permute-start.3 = (f32[384,384]{1,0:T(8,128)S(1)}, f32[384,384]{1,0:T(8,128)S(1)}, u32[]{:S(2)}, u32[]{:S(2)}) collective-permute-start(f32[384,384]{1,0:T(8,128)S(1)} %get-tuple-element.42.refs_3_.refs_2_), channel_id=1, source_target_pairs={{4,12},{5,13},{6,14},{7,15}} | collective-permute-start | bytes 1769480 | tf_op jit(solution)/shard_map/ppermute | solution.py:78
  60.9 13.2 %collective-permute-start.17 = (f32[384,384]{1,0:T(8,128)S(1)}, f32[384,384]{1,0:T(8,128)S(1)}, u32[]{:S(2)}, u32[]{:S(2)}) collective-permute-start(f32[384,384]{1,0:T(8,128)S(1)} %get-tuple-element.50.refs_5_), channel_id=1, source_target_pairs={{16,8},{17,9},{18,10},{19,11},{20,12},{21,13},{22,14},{23,15}} | collective-permute-start | bytes 1769480 | tf_op jit(solution)/shard_map/ppermute | solution.py:78
  61.7 9.8 %collective-permute-start.4 = (f32[384,128]{1,0:T(8,128)S(1)}, f32[384,128]{1,0:T(8,128)S(1)}, u32[]{:S(2)}, u32[]{:S(2)}) collective-permute-start(f32[384,128]{1,0:T(8,128)S(1)} %get-tuple-element.39.refs_0_), channel_id=1, source_target_pairs={{0,8},{1,9},{2,10},{3,11},{4,12},{5,13},{6,14},{7,15}} | collective-permute-start | bytes 589832 | tf_op jit(solution)/shard_map/ppermute | solution.py:78
  70.0 6.5 %collective-permute-start.26 = (f32[384,512]{1,0:T(8,128)S(1)}, f32[384,512]{1,0:T(8,128)S(1)}, u32[]{:S(2)}, u32[]{:S(2)}) collective-permute-start(f32[384,512]{1,0:T(8,128)S(1)} %get-tuple-element.51.refs_5_.refs_2_), channel_id=1, source_target_pairs={{0,8},{1,9},{2,10},{3,11},{4,12},{5,13},{6,14},{7,15}} | collective-permute-start | bytes 2359304 | tf_op jit(solution)/shard_map/ppermute | solution.py:78
  70.7 4.4 %collective-permute-start.23 = (f32[384,384]{1,0:T(8,128)S(1)}, f32[384,384]{1,0:T(8,128)S(1)}, u32[]{:S(2)}, u32[]{:S(2)}) collective-permute-start(f32[384,384]{1,0:T(8,128)S(1)} %get-tuple-element.58), channel_id=1, source_target_pairs={{16,8},{17,9},{18,10},{19,11},{20,12},{21,13},{22,14},{23,15}} | collective-permute-start | bytes 1769480 | tf_op jit(solution)/shard_map/ppermute | solution.py:78
  71.5 14.4 %collective-permute-start.19 = (f32[384,384]{1,0:T(8,128)S(1)}, f32[384,384]{1,0:T(8,128)S(1)}, u32[]{:S(2)}, u32[]{:S(2)}) collective-permute-start(f32[384,384]{1,0:T(8,128)S(1)} %get-tuple-element.54), channel_id=1, source_target_pairs={{20,24},{21,25},{22,26},{23,27},{24,28},{25,29},{26,30},{27,31}} | collective-permute-start | bytes 1769480 | tf_op jit(solution)/shard_map/ppermute | solution.py:78
  72.8 35.3 %collective-permute-start.22 = (f32[384,384]{1,0:T(8,128)S(1)}, f32[384,384]{1,0:T(8,128)S(1)}, u32[]{:S(2)}, u32[]{:S(2)}) collective-permute-start(f32[384,384]{1,0:T(8,128)S(1)} %get-tuple-element.57), channel_id=1, source_target_pairs={{16,24},{17,25},{18,26},{19,27},{20,28},{21,29},{22,30},{23,31}} | collective-permute-start | bytes 1769480 | tf_op jit(solution)/shard_map/ppermute | solution.py:78
  74.1 3.0 %collective-permute-start.18 = (f32[384,128]{1,0:T(8,128)S(1)}, f32[384,128]{1,0:T(8,128)S(1)}, u32[]{:S(2)}, u32[]{:S(2)}) collective-permute-start(f32[384,128]{1,0:T(8,128)S(1)} %get-tuple-element.52), channel_id=1, source_target_pairs={{8,16},{9,17},{10,18},{11,19},{12,20},{13,21},{14,22},{15,23}} | collective-permute-start | bytes 589832 | tf_op jit(solution)/shard_map/ppermute | solution.py:78
  75.1 47.4 %collective-permute-start.25 = (f32[384,128]{1,0:T(8,128)S(1)}, f32[384,128]{1,0:T(8,128)S(1)}, u32[]{:S(2)}, u32[]{:S(2)}) collective-permute-start(f32[384,128]{1,0:T(8,128)S(1)} %shard_map.100.refs_8_), channel_id=1, source_target_pairs={{8,24},{10,26},{12,28},{14,30}} | collective-permute-start | bytes 589832 | tf_op jit(solution)/shard_map/ppermute | solution.py:78
  76.5 47.8 %collective-permute-start.24 = (f32[384,128]{1,0:T(8,128)S(1)}, f32[384,128]{1,0:T(8,128)S(1)}, u32[]{:S(2)}, u32[]{:S(2)}) collective-permute-start(f32[384,128]{1,0:T(8,128)S(1)} %shard_map.100.refs_8_), channel_id=1, source_target_pairs={{9,25},{11,27},{13,29},{15,31}} | collective-permute-start | bytes 589832 | tf_op jit(solution)/shard_map/ppermute | solution.py:78
  77.2 48.4 %collective-permute-start.27 = (f32[384,128]{1,0:T(8,128)S(1)}, f32[384,128]{1,0:T(8,128)S(1)}, u32[]{:S(2)}, u32[]{:S(2)}) collective-permute-start(f32[384,128]{1,0:T(8,128)S(1)} %get-tuple-element.65), channel_id=1, source_target_pairs={{8,16},{9,17},{10,18},{11,19},{12,20},{13,21},{14,22},{15,23}} | collective-permute-start | bytes 589832 | tf_op jit(solution)/shard_map/ppermute | solution.py:78
  85.9 47.3 %collective-permute-start.29 = (f32[384,128]{1,0:T(8,128)S(1)}, f32[384,128]{1,0:T(8,128)S(1)}, u32[]{:S(2)}, u32[]{:S(2)}) collective-permute-start(f32[384,128]{1,0:T(8,128)S(1)} %get-tuple-element.49.refs_0_.refs_4_), channel_id=1, source_target_pairs={{0,1},{1,2},{2,3},{3,4},{4,5},{5,6},{6,7},{7,8},{8,9},{9,10},{10,1... | collective-permute-start | bytes 589832 | tf_op jit(solution)/shard_map/ppermute | solution.py:308
  108.1 25.0 %collective-permute-start.30 = (f32[384,128]{1,0:T(8,128)S(1)}, f32[384,128]{1,0:T(8,128)S(1)}, u32[]{:S(2)}, u32[]{:S(2)}) collective-permute-start(f32[384,128]{1,0:T(8,128)S(1)} %shard_map.95.refs_0_), channel_id=1, source_target_pairs={{16,17},{17,18},{18,19},{19,20},{20,21},{21,22},{22,23},{23,24}} | collective-permute-start | bytes 589832 | tf_op jit(solution)/shard_map/ppermute | solution.py:308
  110.1 23.4 %copy-start = (f32[1,4,384,384]{3,2,1,0:T(8,128)S(1)}, f32[1,4,384,384]{3,2,1,0:T(8,128)}, u32[]{:S(2)}) copy-start(f32[1,4,384,384]{3,2,1,0:T(8,128)} %param.10) | copy-start | bytes 7077892
  110.1 23.4 %copy-start.2 = (f32[384,128]{1,0:T(8,128)S(1)}, f32[384,128]{1,0:T(8,128)}, u32[]{:S(2)}) copy-start(f32[384,128]{1,0:T(8,128)} %refs_5_.1) | copy-start | bytes 589828
  122.5 9.8 %collective-permute-start.28 = (f32[384,128]{1,0:T(8,128)S(1)}, f32[384,128]{1,0:T(8,128)S(1)}, u32[]{:S(2)}, u32[]{:S(2)}) collective-permute-start(f32[384,128]{1,0:T(8,128)S(1)} %get-tuple-element.66), channel_id=1, source_target_pairs={{8,24},{9,25},{10,26},{11,27},{12,28},{13,29},{14,30},{15,31}} | collective-permute-start | bytes 589832 | tf_op jit(solution)/shard_map/ppermute | solution.py:78
  124.2 8.9 %collective-permute-start.32 = (f32[384,128]{1,0:T(8,128)S(1)}, f32[384,128]{1,0:T(8,128)S(1)}, u32[]{:S(2)}, u32[]{:S(2)}) collective-permute-start(f32[384,128]{1,0:T(8,128)S(1)} %shard_map.102.refs_1_), channel_id=1, source_target_pairs={{24,25},{26,27},{28,29},{30,31}} | collective-permute-start | bytes 589832 | tf_op jit(solution)/shard_map/ppermute | solution.py:308
  125.6 7.9 %collective-permute-start.31 = (f32[384,128]{1,0:T(8,128)S(1)}, f32[384,128]{1,0:T(8,128)S(1)}, u32[]{:S(2)}, u32[]{:S(2)}) collective-permute-start(f32[384,128]{1,0:T(8,128)S(1)} %shard_map.101.refs_0_), channel_id=1, source_target_pairs={{25,26},{27,28},{29,30}} | collective-permute-start | bytes 589832 | tf_op jit(solution)/shard_map/ppermute | solution.py:308
